TPU v7x, 256 devices: a whole 4x4x8 slice. The times are simulated.
256 devices in a mesh: ord: 64 (over y, z, core), blk: 4 (over x).
Axes of the slice: x: 4, y: 4, z: 8, core: 2. Of those that a mesh axis runs over, the one named last changes fastest.
Arguments:
- panel: bfloat16 [2880, 64, 2880], P('ord', 'blk'), as said below
- gauss: bfloat16 [2, 16, 2880, 2880], P(None, None, 'ord', 'blk'), may hold values from -2.3841858e-06 to 2.3841858e-06
- height: float32 [16], replicated, may hold values from 0.25 to 2.5
- order_map: int32 [2880], replicated, may hold values from 0 to 2879, as said below
- cycle_map: int32 [64], P('blk'), may hold values from 360 to 2519, as said below
Outputs:
- field: bfloat16 [5760, 3072], P('ord', 'blk')
Inputs may be any that keep to these rules, and one draw needn't show every extreme that they name: `order_map`: a permutation of 0 to 2879; the 45 slots of each index of ord hold consecutive orders in ascending order. `panel`: entries at degrees below the order of their slot are zero. `cycle_map`: distinct cycle numbers.
All inputs are finite; a program needn't handle non-finite values.
Results may differ from a plain program's by a relative error of at most 0.0068.
Values may be sent and summed in bfloat16 or wider, within the bound.
No kernel may reach another device: no remote copies, remote signals or barrier semaphores. Data moves between devices by JAX's collectives and lax.ppermute only.
A program may use at most 128 MiB of HBM per device.

v0:
```python
import math

import jax
import jax.numpy as jnp
from jax import lax
from jax.sharding import PartitionSpec as P

ORDERS = 2880
TILE = 320
NLON = 5760


def cycle_angles(cycle_map):
    theta = math.pi * (cycle_map.astype(jnp.float32) + 0.5) / ORDERS
    return (jnp.cos(theta), jnp.sin(theta))


def legendre_tables(current, before, degree, orders, cosine, sine):
    deg = degree[None, None, :]
    order = orders[:, None, None]
    radial = (deg + 1.0) * current
    polar = (
        -(
            deg * cosine[None, :, None] * current
            - jnp.sqrt(jnp.maximum(deg * deg - order * order, 0.0)) * before
        )
        / sine[None, :, None]
    )
    azimuth = order * current / sine[None, :, None]
    return jnp.stack([radial, polar, azimuth], 2).astype(jnp.bfloat16)


def weighted(coef, degree, height):
    radial = jnp.exp(-(degree[None, :] + 2.0) * height[:, None] / ORDERS)
    return (coef.astype(jnp.float32) * radial[None, :, None, :]).astype(jnp.bfloat16)


def assemble(total, cycles, shells):
    count = total.shape[1]
    parts = total.reshape(2, count, cycles, 3, shells)
    g_part = parts[0]
    h_part = parts[1]
    cosine_part = jnp.concatenate([g_part[:, :, :2], -h_part[:, :, 2:]], 2)
    sine_part = jnp.concatenate([h_part[:, :, :2], g_part[:, :, 2:]], 2)
    return (
        jnp.stack([cosine_part, sine_part])
        .reshape(2, count, cycles * 3 * shells)
        .astype(jnp.bfloat16)
    )


def phase_angles(orders_int, position):
    phase = orders_int[:, None] * position[None, :] % NLON
    angle = phase.astype(jnp.float32) * (2.0 * math.pi / NLON)
    return (jnp.cos(angle), jnp.sin(angle))


def degree_sums(panel_src, edge, coef_src, orders, cosine, sine, height, base, first, last):
    count, cycles, _ = panel_src.shape
    shells = height.shape[0]

    def step(tile, total):
        offset = (tile * TILE - base).astype(jnp.int32)
        current = lax.dynamic_slice_in_dim(panel_src, offset, TILE, 2).astype(jnp.float32)
        earlier = lax.dynamic_slice_in_dim(panel_src, jnp.maximum(offset - 1, 0), TILE, 2).astype(
            jnp.float32
        )
        shifted = jnp.concatenate([edge[:, :, None].astype(jnp.float32), current[:, :, :-1]], 2)
        before = jnp.where(offset > 0, earlier, shifted)
        degree = (tile * TILE + jnp.arange(TILE)).astype(jnp.float32)
        tables = legendre_tables(current, before, degree, orders, cosine, sine).reshape(
            count, cycles * 3, TILE
        )
        weights = weighted(lax.dynamic_slice_in_dim(coef_src, offset, TILE, 3), degree, height)
        return total + jnp.einsum(
            "okl,gsol->goks", tables, weights, preferred_element_type=jnp.float32
        )

    init = jnp.zeros((2, count, cycles * 3, shells), jnp.float32)
    return lax.fori_loop(jnp.asarray(first, jnp.int32), jnp.asarray(last, jnp.int32), step, init)


def body(panel, gauss, height, order_map, cycle_map):
    count, cycles, degrees = panel.shape
    shells = height.shape[0]
    tiles = degrees // TILE
    cosine, sine = cycle_angles(cycle_map)
    coef = lax.all_gather(gauss, "blk", axis=3, tiled=True)
    here = lax.axis_index("ord")
    orders_int = lax.dynamic_slice_in_dim(order_map, here * count, count, 0)
    orders = orders_int.astype(jnp.float32)
    lowest = jnp.min(orders_int) // TILE
    zero_edge = jnp.zeros((count, cycles), jnp.bfloat16)
    total = degree_sums(panel, zero_edge, coef, orders, cosine, sine, height, 0, lowest, tiles)
    spectra = assemble(total, cycles, shells)
    spread = lax.all_to_all(spectra, "ord", split_axis=2, concat_axis=1, tiled=True)
    items = spread.shape[2]
    width = NLON // 8
    inner_cos, inner_sin = phase_angles(order_map, jnp.arange(width))
    start_cos, start_sin = phase_angles(order_map, jnp.arange(8) * width)

    def transform(block):
        block_cos = lax.dynamic_slice_in_dim(start_cos, block, 1, 1)
        block_sin = lax.dynamic_slice_in_dim(start_sin, block, 1, 1)
        table_cos = inner_cos * block_cos - inner_sin * block_sin
        table_sin = inner_sin * block_cos + inner_cos * block_sin
        tables = jnp.stack([table_cos, table_sin]).astype(jnp.bfloat16)
        return lax.dot_general(
            tables, spread, (((0, 1), (0, 1)), ((), ())), preferred_element_type=jnp.float32
        )

    field = lax.map(transform, jnp.arange(8)).reshape(NLON, items).astype(jnp.bfloat16)
    return lax.all_to_all(field, "ord", split_axis=0, concat_axis=1, tiled=True)


def solution(mesh):
    return jax.shard_map(
        body,
        mesh=mesh,
        in_specs=(P("ord", "blk", None), P(None, None, "ord", "blk"), P(), P(), P("blk")),
        out_specs=P("ord", "blk"),
        check_vma=False,
    )
```

profile of v0, /device:TPU:1, one launch (start us, length us, event | category | flops | bytes accessed | tf_op | source)
XLA Modules:
  0.0 726.7 jit_solution(5061517365681989806)
XLA Ops:
  6.5 10.8 %copy.37 = bf16[2,16,45,720]{2,1,0,3:T(8,128)(2,1)} copy(bf16[2,16,45,720]{3,1,2,0:T(8,128)(2,1)} %param.10) | data formatting | bytes 4147200 | tf_op args[1]
  20.7 5.1 copy.39
  25.9 208.9 %all-gather.2.cloned.1.call-done = bf16[2,16,45,2880]{2,1,0,3:T(8,128)(2,1)} async-done(((bf16[2,16,45,720]{2,1,0,3:T(8,128)(2,1)}), bf16[2,16,45,2880]{2,1,0,3:T(8,128)(2,1)}) %all-gather.2.cloned.1.call-update) | async-done | bytes 8294416 | tf_op jit(solution)/shard_map/all_gather | solution.py:88
  234.8 36.3 %copy.38 = bf16[2,16,45,2880]{3,1,0,2:T(8,128)(2,1)} copy(bf16[2,16,45,2880]{2,1,0,3:T(8,128)(2,1)} %all-gather.2.cloned.1.call-done) | data formatting | bytes 16588800 | tf_op jit(solution)/shard_map/while | solution.py:80
  271.2 63.9 %while.24 = (s32[]{:T(128)}, f32[2,45,48,16]{2,3,0,1:T(8,128)S(1)}, bf16[2,16,45,2880]{3,1,0,2:T(8,128)(2,1)}, f32[16]{0:T(128)S(1)}, bf16[45,16,2880]{2,0,1:T(8...) while((s32[]{:T(128)}, f32[2,45,48,16]{2,3,0,1:T(8,128)S(1)}, ...), condition=%wide.region_2.3_spmd, body=%wide.region_1.2_spmd.sunk | while | flops 50574088 | bytes 13384153 | solution.py:80
  272.8 2.5 fusion.63
  279.9 2.6 fusion.63
  294.0 2.6 fusion.63
  301.2 2.6 fusion.63
  308.3 2.7 fusion.63
  315.5 2.6 fusion.63
  322.6 2.8 fusion.63
  337.9 9.3 %all-to-all-start = ((bf16[64,2,540]{2,1,0:T(2,128)(2,1)}), bf16[64,2,540]{2,1,0:T(2,128)(2,1)S(1)}, u32[]{:S(2)}, u32[]{:S(2)}) async-start(bf16[64,2,540]{2,1,0:T(2,128)(2,1)} %reshape.318), calls=%async_computation | async-start | bytes 327680 | tf_op jit(solution)/shard_map/all_to_all | solution.py:96
  347.7 10.1 %all-to-all-done = bf16[64,2,540]{2,1,0:T(2,128)(2,1)S(1)} async-done(((bf16[64,2,540]{2,1,0:T(2,128)(2,1)}), bf16[64,2,540]{2,1,0:T(2,128)(2,1)S(1)}, u32[]{:S(2)}, u32[]{:S(2)}) %all-to-all-start) | async-done | bytes 138272 | tf_op jit(solution)/shard_map/all_to_all | solution.py:96
  359.1 342.2 %while.25 = (s32[]{:T(128)}, bf16[8,720,12]{1,2,0:T(8,128)(2,1)S(1)}, s32[8]{0:T(128)S(1)}, f32[2880,8]{0,1:T(8,128)S(1)}, f32[2880,8]{0,1:T(8,128)S(1)}, /*inde...) while((s32[]{:T(128)}, ...), condition=%wide.region_4.5_spmd.clone.clone, body=%wide.region_3.4_spmd.clone.clone.sunk | while | flops 138931200 | bytes 17091484 | solution.py:112
  361.7 37.8 %fusion.67 = (bf16[1,2880,720]{1,2,0:T(8,128)(2,1)S(1)}, bf16[1,2880,720]{1,2,0:T(8,128)(2,1)S(1)}) fusion(s32[2880]{0:T(1024)S(1)} %get-tuple-element.481, f32[2880]{0:T(1024)S(1)} %get-tuple-element.409, f32[2880]{0:T(1024)S(1)} %get-tuple-element.410), kind=kLoop, calls=%fused_computation.35.clone.1 | loop fusion | flops 35251200 | bytes 8328960 | tf_op jit(solution)/shard_map/convert
  404.5 37.8 %fusion.67 = (bf16[1,2880,720]{1,2,0:T(8,128)(2,1)S(1)}, bf16[1,2880,720]{1,2,0:T(8,128)(2,1)S(1)}) fusion(s32[2880]{0:T(1024)S(1)} %get-tuple-element.481, f32[2880]{0:T(1024)S(1)} %get-tuple-element.409, f32[2880]{0:T(1024)S(1)} %get-tuple-element.410), kind=kLoop, calls=%fused_computation.35.clone.1 | loop fusion | flops 35251200 | bytes 8328960 | tf_op jit(solution)/shard_map/convert
  447.3 37.8 %fusion.67 = (bf16[1,2880,720]{1,2,0:T(8,128)(2,1)S(1)}, bf16[1,2880,720]{1,2,0:T(8,128)(2,1)S(1)}) fusion(s32[2880]{0:T(1024)S(1)} %get-tuple-element.481, f32[2880]{0:T(1024)S(1)} %get-tuple-element.409, f32[2880]{0:T(1024)S(1)} %get-tuple-element.410), kind=kLoop, calls=%fused_computation.35.clone.1 | loop fusion | flops 35251200 | bytes 8328960 | tf_op jit(solution)/shard_map/convert
  490.0 37.8 %fusion.67 = (bf16[1,2880,720]{1,2,0:T(8,128)(2,1)S(1)}, bf16[1,2880,720]{1,2,0:T(8,128)(2,1)S(1)}) fusion(s32[2880]{0:T(1024)S(1)} %get-tuple-element.481, f32[2880]{0:T(1024)S(1)} %get-tuple-element.409, f32[2880]{0:T(1024)S(1)} %get-tuple-element.410), kind=kLoop, calls=%fused_computation.35.clone.1 | loop fusion | flops 35251200 | bytes 8328960 | tf_op jit(solution)/shard_map/convert
  532.8 37.8 %fusion.67 = (bf16[1,2880,720]{1,2,0:T(8,128)(2,1)S(1)}, bf16[1,2880,720]{1,2,0:T(8,128)(2,1)S(1)}) fusion(s32[2880]{0:T(1024)S(1)} %get-tuple-element.481, f32[2880]{0:T(1024)S(1)} %get-tuple-element.409, f32[2880]{0:T(1024)S(1)} %get-tuple-element.410), kind=kLoop, calls=%fused_computation.35.clone.1 | loop fusion | flops 35251200 | bytes 8328960 | tf_op jit(solution)/shard_map/convert
  575.6 37.8 %fusion.67 = (bf16[1,2880,720]{1,2,0:T(8,128)(2,1)S(1)}, bf16[1,2880,720]{1,2,0:T(8,128)(2,1)S(1)}) fusion(s32[2880]{0:T(1024)S(1)} %get-tuple-element.481, f32[2880]{0:T(1024)S(1)} %get-tuple-element.409, f32[2880]{0:T(1024)S(1)} %get-tuple-element.410), kind=kLoop, calls=%fused_computation.35.clone.1 | loop fusion | flops 35251200 | bytes 8328960 | tf_op jit(solution)/shard_map/convert
  618.4 37.8 %fusion.67 = (bf16[1,2880,720]{1,2,0:T(8,128)(2,1)S(1)}, bf16[1,2880,720]{1,2,0:T(8,128)(2,1)S(1)}) fusion(s32[2880]{0:T(1024)S(1)} %get-tuple-element.481, f32[2880]{0:T(1024)S(1)} %get-tuple-element.409, f32[2880]{0:T(1024)S(1)} %get-tuple-element.410), kind=kLoop, calls=%fused_computation.35.clone.1 | loop fusion | flops 35251200 | bytes 8328960 | tf_op jit(solution)/shard_map/convert
  661.2 37.8 %fusion.67 = (bf16[1,2880,720]{1,2,0:T(8,128)(2,1)S(1)}, bf16[1,2880,720]{1,2,0:T(8,128)(2,1)S(1)}) fusion(s32[2880]{0:T(1024)S(1)} %get-tuple-element.481, f32[2880]{0:T(1024)S(1)} %get-tuple-element.409, f32[2880]{0:T(1024)S(1)} %get-tuple-element.410), kind=kLoop, calls=%fused_computation.35.clone.1 | loop fusion | flops 35251200 | bytes 8328960 | tf_op jit(solution)/shard_map/convert
  701.8 17.1 %all_to_all.34 = bf16[64,90,12]{1,2,0:T(8,128)(2,1)S(1)} all-to-all(bf16[64,90,12]{1,2,0:T(8,128)(2,1)S(1)} %copy.46), channel_id=1, replica_groups=mesh['ord'=64,'blk'=4] {'ord'}, dimensions={0} | all-to-all | bytes 276480 | tf_op jit(solution)/shard_map/all_to_all | solution.py:113
  (143 shorter events, 76.5 us)
Async XLA Ops:
  6.5 228.2 %all-gather.2.cloned.1.call-start = ((), (), s32[]{:S(2)}) async-start(), calls=%async_computation.2 | async-start | bytes 29491200 | tf_op jit(solution)/shard_map/all_gather | solution.py:88
  17.3 0.7 copy-start
  20.7 5.2 copy-start.2
  25.9 245.3 %copy-start.1 = (f32[16]{0:T(128)S(1)}, f32[16]{0:T(128)}, u32[]{:S(2)}) copy-start(f32[16]{0:T(128)} %param.11) | copy-start | bytes 196
  337.9 19.9 %all-to-all-start = ((bf16[64,2,540]{2,1,0:T(2,128)(2,1)}), bf16[64,2,540]{2,1,0:T(2,128)(2,1)S(1)}, u32[]{:S(2)}, u32[]{:S(2)}) async-start(bf16[64,2,540]{2,1,0:T(2,128)(2,1)} %reshape.318), calls=%async_computation | async-start | bytes 327680 | tf_op jit(solution)/shard_map/all_to_all | solution.py:96
Sparse Core Ops, SparseCore 0:
  17.5 217.2 all-gather.1
where the time goes:
time: 728 us; the launch traced here: 727 us
  other arithmetic  346 us (48%)
  waiting for transfers between devices  219 us (30%)
  local copies, waits for them, and re-layouts  65.4 us (9%)
  matrix products  38.7 us (5%)
  blocking collectives  17.1 us (2%)
  loops' own time  16 us (2%)
  between operations  15.6 us (2%)
  starting transfers between devices  9.33 us (1%)
    another operation x9, other arithmetic  303 us
    all_gather x1, waiting for transfers between devices, body(): coef = lax.all_gather(gauss, 'blk', axis=3, tiled=True)  209 us
    while x3, local copies, waits for them, and re-layouts, degree_sums(): lax.fori_loop(jnp.asarray(first, jnp.int32), jnp.asarray(last, jnp.int32)...  42.1 us
    another operation x18, other arithmetic, legendre_tables(): return jnp.stack([radial, polar, azimuth], 2).astype(jnp.bfloat16)  27.1 us
    dot_general x9, matrix products, step(): jnp.einsum('okl,gsol->goks', tables, weights, preferred_element_type=jnp....  20.2 us
    dot_general x8, matrix products, transform(): lax.dot_general(tables, spread, (((0, 1), (0, 1)), ((), ())), preferred_e...  18.5 us
    all_to_all x1, blocking collectives, body(): return lax.all_to_all(field, 'ord', split_axis=0, concat_axis=1, tiled=True)  17.1 us
    another operation x1, loops' own time, body(): lax.map(transform, jnp.arange(8)).reshape(NLON, items).astype(jnp.bfloat16)  15.2 us
  transfers between devices with their start and end apart: 2, of which 2 were waited for; matrix products, arithmetic and copies ran while one was open for 1% of the time, Pallas kernels for 0%

commit v1 on v0

v1 whole, which is shorter than its diff:
```python
import functools
import math

import jax
import jax.numpy as jnp
from jax import lax
from jax.experimental import pallas as pl
from jax.experimental.pallas import tpu as pltpu
from jax.sharding import PartitionSpec as P

ORDERS = 2880
RUN = 45
QUARTER = 720
START = 1408
WIDE = 1536
NLON = 5760
GROUP = 5
GAUSS_PAIRS = [(0, 1), (1, 0), (2, 3), (3, 2)]
PANEL_PAIRS = [(1, 2), (2, 1), (3, 0), (0, 3)]


def sums_kernel(where_ref, order_ref, height_ref, own_ref, other_ref, near_ref, far_ref, out_ref,
                gs_ref, gn_ref, decay_ref):
    step = pl.program_id(0)
    half = where_ref[0]
    odd = where_ref[1] == 1
    first = (half * START).astype(jnp.float32)
    degree = lax.broadcasted_iota(jnp.int32, (1, WIDE), 1).astype(jnp.float32) + first

    @pl.when(step == 0)
    def _():
        gs_ref[...] = jnp.zeros_like(gs_ref)
        gn_ref[...] = jnp.zeros_like(gn_ref)
        height = height_ref[...]
        here = jnp.exp(-(degree + 2.0) * height / ORDERS)
        decay_ref[0] = here
        decay_ref[1] = here * (degree + 1.0)
        decay_ref[2] = jnp.exp(-(degree + 3.0) * height / ORDERS)

    low = jnp.where(odd, other_ref[...], own_ref[...])
    high = jnp.where(odd, own_ref[...], other_ref[...])

    @pl.when(half == 0)
    def _():
        gs_ref[:, :, :, 0:720] = low
        gs_ref[:, :, :, 720:1440] = high
        gn_ref[:, :, :, 0:719] = low[:, :, :, 1:]
        gn_ref[:, :, :, 719:1439] = high

    @pl.when(half == 1)
    def _():
        gs_ref[:, :, :, 32:752] = low
        gs_ref[:, :, :, 752:1472] = high
        gn_ref[:, :, :, 31:751] = low
        gn_ref[:, :, :, 751:1471] = high

    for o in range(GROUP):
        m = order_ref[step * GROUP + o].astype(jnp.float32)
        root = jnp.sqrt(jnp.maximum((degree + 1.0) * (degree + 1.0) - m * m, 0.0))
        slope = decay_ref[2] * root
        g = [gs_ref[k, o].astype(jnp.float32) for k in range(2)]
        n = [gn_ref[k, o].astype(jnp.float32) for k in range(2)]
        weights = jnp.concatenate(
            [g[0] * decay_ref[1], g[1] * decay_ref[1], g[0] * decay_ref[0], g[1] * decay_ref[0],
             n[0] * slope, n[1] * slope], 0).astype(jnp.bfloat16)
        table = jnp.concatenate([near_ref[o], far_ref[o]], 0)
        out_ref[o] = lax.dot_general(
            table, weights, (((1,), (1,)), ((), ())), preferred_element_type=jnp.float32)


def partial_sums(where, orders, height, own, other, near, far):
    count = near.shape[0]
    smem = pl.BlockSpec(memory_space=pltpu.SMEM)
    coef = pl.BlockSpec((2, GROUP, 16, QUARTER), lambda i: (0, i, 0, 0))
    tab = pl.BlockSpec((GROUP, 16, WIDE), lambda i: (i, 0, 0))
    return pl.pallas_call(
        sums_kernel,
        out_shape=jax.ShapeDtypeStruct((count, 32, 96), jnp.float32),
        grid=(count // GROUP,),
        in_specs=[smem, smem, pl.BlockSpec((16, 1), lambda i: (0, 0)), coef, coef, tab, tab],
        out_specs=pl.BlockSpec((GROUP, 32, 96), lambda i: (i, 0, 0)),
        scratch_shapes=[
            pltpu.VMEM((2, GROUP, 16, WIDE), jnp.bfloat16),
            pltpu.VMEM((2, GROUP, 16, WIDE), jnp.bfloat16),
            pltpu.VMEM((3, 16, WIDE), jnp.float32),
        ],
        compiler_params=pltpu.CompilerParams(vmem_limit_bytes=40 << 20),
        name="partial_sums",
    )(where, orders, height, own, other, near, far)


def turn(phase, period):
    angle = (phase % period).astype(jnp.float32) * (2.0 * math.pi / period)
    return jnp.cos(angle), jnp.sin(angle)


def body(panel, gauss, height, order_map, cycle_map):
    count, cycles, _ = panel.shape
    shells = height.shape[0]
    spot = lax.axis_index("blk")
    here = lax.axis_index("ord")
    half = spot // 2
    own = jnp.transpose(gauss, (0, 2, 1, 3))
    other = lax.ppermute(own, "blk", GAUSS_PAIRS)
    upper = jnp.pad(panel[:, :, START:], ((0, 0), (0, 0), (0, START + WIDE - ORDERS)))
    lower = panel[:, :, :WIDE]
    sent = jnp.where(half == 0, upper, lower)
    near = jnp.where(half == 0, lower, upper)
    far = lax.ppermute(sent, "blk", PANEL_PAIRS)
    orders_int = lax.dynamic_slice_in_dim(order_map, here * count, count, 0)
    where = jnp.stack([half, spot % 2]).astype(jnp.int32)
    raw = partial_sums(where, orders_int, height[:, None], own, other, near, far)
    total = raw[:, :cycles] + lax.ppermute(raw[:, cycles:], "blk", PANEL_PAIRS)
    theta = math.pi * (cycle_map.astype(jnp.float32) + 0.5) / ORDERS
    cosine = jnp.cos(theta)[None, :, None]
    sine = jnp.sin(theta)[None, :, None]
    m = orders_int.astype(jnp.float32)[:, None, None]
    s0, s2, s3 = total[:, :, 0:32], total[:, :, 32:64], total[:, :, 64:96]
    s1 = -(cosine * (s0 - s2) - s3) / sine
    s2 = m * s2 / sine
    g, h = slice(0, shells), slice(shells, 2 * shells)
    spectra = jnp.stack([
        jnp.stack([s0[..., g], s1[..., g], -s2[..., h]], 2),
        jnp.stack([s0[..., h], s1[..., h], s2[..., g]], 2),
    ]).reshape(2, count, cycles * 3 * shells).astype(jnp.bfloat16)

    parts = ORDERS // count
    items = cycles * 3 * shells // parts
    chunk = jnp.transpose(spectra.reshape(2, count, parts, items), (2, 0, 1, 3))
    spread = lax.all_to_all(chunk.reshape(parts, 2, count * items), "ord", 0, 0, tiled=True)
    spread = spread.astype(jnp.float32)
    runs = order_map[::RUN] // RUN
    b = jnp.arange(128)
    q = jnp.arange(RUN)
    cos1, sin1 = turn(b[:, None] * runs[None, :], 128)
    table = jnp.concatenate(
        [jnp.concatenate([cos1, sin1], 1), jnp.concatenate([sin1, -cos1], 1)], 0)
    flat = jnp.concatenate([spread[:, 0], spread[:, 1]], 0)
    mid = jnp.dot(table, flat, precision=lax.Precision.HIGHEST).reshape(2, 128, count, items)
    cos2, sin2 = turn(b[:, None] * q[None, :], NLON)
    cos2, sin2 = cos2[:, :, None], sin2[:, :, None]
    real = mid[0] * cos2 - mid[1] * sin2
    imag = mid[0] * sin2 + mid[1] * cos2
    cos3, sin3 = turn(q[:, None] * q[None, :], RUN)
    field = lax.dot_general(
        jnp.concatenate([cos3, -sin3], 1), jnp.concatenate([real, imag], 1),
        (((1,), (1,)), ((), ())), precision=lax.Precision.HIGHEST)
    field = field.reshape(NLON, items).astype(jnp.bfloat16)
    return lax.all_to_all(field, "ord", split_axis=0, concat_axis=1, tiled=True)


def solution(mesh):
    return jax.shard_map(
        body,
        mesh=mesh,
        in_specs=(P("ord", "blk", None), P(None, None, "ord", "blk"), P(), P(), P("blk")),
        out_specs=P("ord", "blk"),
        check_vma=False,
    )
```

time: 728 us -> 129 us (0.18)
  other arithmetic: 346 us -> 6.5 us
  waiting for transfers between devices: 219 us -> 64.8 us
  local copies, waits for them, and re-layouts: 65.4 us -> 8.38 us
  matrix products: 38.7 us -> 1.25 us
  loops' own time: 16 us -> 0 us
  between operations: 15.6 us -> 0.2 us
  Pallas kernels: 0 us -> 10.9 us
  starting transfers between devices: 9.33 us -> 19.6 us
    another operation x28 -> x6, other arithmetic: 330 us -> 0.71 us
    all_gather x1 -> x0, waiting for transfers between devices: 209 us -> none  [body(): coef = lax.all_gather(gauss, 'blk', axis=3, tiled=True)]
    ppermute x0 -> x3, waiting for transfers between devices: none -> 54.7 us  [the longest x1 47.2 us: body(): other = lax.ppermute(own, 'blk', GAUSS_PAIRS)]
    while x3 -> x0, local copies, waits for them, and re-layouts: 42.1 us -> none  [degree_sums(): lax.fori_loop(jnp.asarray(first, jnp.int32), jnp.asarray(last, jnp.int32)...]
    dot_general x17 -> x2, matrix products: 38.7 us -> 1.25 us  [the longest x1 0.78 us: body(): jnp.dot(table, flat, precision=lax.Precision.HIGHEST)]
    another operation x2 -> x0, loops' own time: 16 us -> none  [the longest x1 15.2 us: body(): lax.map(transform, jnp.arange(8)).reshape(NLON, items).astype(jnp.bfloat16)]
    unnamed x11 -> x4, local copies, waits for them, and re-layouts: 14 us -> 0.01 us
    convert_element_type x18 -> x2, other arithmetic: 12.6 us -> 0.79 us  [the longest x1 0.77 us: body(): m = orders_int.astype(jnp.float32)[:, None, None]]
  transfers between devices with their start and end apart: 2 -> 4, of which waited for: 2 -> 3; matrix products, arithmetic and copies ran while one was open for 1% -> 2% of each run, Pallas kernels for 0% -> 0%
where the time goes in v1:
time: 129 us
  waiting for transfers between devices  64.8 us (50%)
  starting transfers between devices  19.6 us (15%)
  blocking collectives  17.1 us (13%)
  Pallas kernels  10.9 us (8%)
  local copies, waits for them, and re-layouts  8.38 us (6%)
  other arithmetic  6.5 us (5%)
    ppermute x1, waiting for transfers between devices, body(): other = lax.ppermute(own, 'blk', GAUSS_PAIRS)  47.2 us
    all_to_all x1, blocking collectives, body(): return lax.all_to_all(field, 'ord', split_axis=0, concat_axis=1, tiled=True)  17.1 us
    all_to_all x1, starting transfers between devices, body(): lax.all_to_all(chunk.reshape(parts, 2, count * items), 'ord', 0, 0, tiled...  14.4 us
    pallas_call x1, Pallas kernels, partial_sums(): pl.pallas_call(sums_kernel, out_shape=jax.ShapeDtypeStruct((count, 32, 96...  10.9 us
    all_to_all x1, waiting for transfers between devices, body(): lax.all_to_all(chunk.reshape(parts, 2, count * items), 'ord', 0, 0, tiled...  10.2 us
    ppermute x1, waiting for transfers between devices, body(): total = raw[:, :cycles] + lax.ppermute(raw[:, cycles:], 'blk', PANEL_PAIRS)  7.49 us
    select_n x1, other arithmetic, body(): sent = jnp.where(half == 0, upper, lower)  4.1 us
    ppermute x1, starting transfers between devices, body(): far = lax.ppermute(sent, 'blk', PANEL_PAIRS)  3.31 us
  transfers between devices with their start and end apart: 4, of which 3 were waited for; matrix products, arithmetic and copies ran while one was open for 2% of the time, Pallas kernels for 0%

profile of v1, /device:TPU:1, one launch (start us, length us, event | category | flops | bytes accessed | tf_op | source)
XLA Modules:
  0.0 128.9 jit_solution(16837536162750951145)
XLA Ops:
  0.0 1.6 %slice-done = bf16[45,16,1472]{2,1,0:T(8,128)(2,1)S(1)} async-done(((bf16[45,16,2880]{2,1,0:T(8,128)(2,1)}), bf16[45,16,1472]{2,1,0:T(8,128)(2,1)S(1)}, s32[]{:S(2)}) %slice-start) | async-done | bytes 2119704 | tf_op jit(solution)/shard_map/slice | solution.py:105
  1.6 4.1 %broadcast_select_fusion = (bf16[45,16,1536]{2,1,0:T(8,128)(2,1)}, bf16[45,16,1536]{2,1,0:T(8,128)(2,1)S(1)}) fusion(pred[]{:T(512)S(6)} %eq.12, bf16[45,16,1472]{2,1,0:T(8,128)(2,1)S(1)} %slice-done, bf16[45,16,2880]{2,1,0:T(8,128)(2,1)} %param.5), kind=kLoop, calls=%fused_computation | loop fusion | flops 2211840 | bytes 8755201 | tf_op jit(solution)/shard_map/jit(_where)/select_n | solution.py:107
  5.7 3.3 %collective-permute-start.1 = (bf16[45,16,1536]{2,1,0:T(8,128)(2,1)}, bf16[45,16,1536]{2,1,0:T(8,128)(2,1)}, u32[]{:S(2)}, u32[]{:S(2)}) collective-permute-start(bf16[45,16,1536]{2,1,0:T(8,128)(2,1)} %get-tuple-element.9), channel_id=1, source_target_pairs={{1,2},{2,1},{3,0},{0,3},{5,6},{6,5},{7,4},{4,7},{9,10},{10,9},{11,... | collective-permute-start | bytes 6635528 | tf_op jit(solution)/shard_map/ppermute | solution.py:109
  9.1 0.8 slice.65
  10.0 0.8 fusion.50
  10.8 47.2 %collective-permute-done.other_ref = bf16[2,45,16,720]{3,2,1,0:T(8,128)(2,1)} collective-permute-done((bf16[2,45,16,720]{3,2,1,0:T(8,128)(2,1)}, bf16[2,45,16,720]{3,2,1,0:T(8,128)(2,1)}, u32[]{:S(2)}, u32[]{:S(2)}) %collective-permute-start) | collective-permute-done | bytes 2073632 | tf_op jit(solution)/shard_map/ppermute | solution.py:104
  58.0 10.9 %partial_sums.1 = f32[45,32,96]{2,1,0:T(8,128)S(1)} custom-call(s32[2]{0:T(128)S(1)} %pad_add_fusion.where_ref, s32[45]{0:T(128)S(1)} %get-tuple-element.8.order_ref, f32[16,1]{1,0:T(8,128)S(1)} %copy.48.height_ref, bf16[2,45,16,720]{3,2,1,0:T(8,128)(2,1)} %bitcast.4.own_ref, bf16[2,45,16,720]{3,2,1,0:T(8,128)(2,1)} %collective-permute-done.other_ref, ...), custom_call_target="tpu_custom_call" | custom-call | tf_op jit(solution)/shard_map/partial_sums/pallas_call | solution.py:76
  69.0 1.8 %collective-permute-start.2 = (f32[45,16,96]{2,1,0:T(8,128)S(1)}, f32[45,16,96]{2,1,0:T(8,128)S(1)}, u32[]{:S(2)}, u32[]{:S(2)}) collective-permute-start(f32[45,16,96]{2,1,0:T(8,128)S(1)} %slice.84), channel_id=1, source_target_pairs={{1,2},{2,1},{3,0},{0,3},{5,6},{6,5},{7,4},{4,7},{9,10},{10,9},{11,... | collective-permute-start | bytes 829448 | tf_op jit(solution)/shard_map/ppermute | solution.py:113
  71.0 7.5 %collective-permute-done.2 = f32[45,16,96]{2,1,0:T(8,128)S(1)} collective-permute-done((f32[45,16,96]{2,1,0:T(8,128)S(1)}, f32[45,16,96]{2,1,0:T(8,128)S(1)}, u32[]{:S(2)}, u32[]{:S(2)}) %collective-permute-start.2) | collective-permute-done | bytes 276512 | tf_op jit(solution)/shard_map/ppermute | solution.py:113
  78.5 0.3 fusion.7
  79.4 0.2 copy.51
  79.8 0.2 copy.49
  80.2 0.2 copy.53
  80.7 0.2 copy.52
  81.2 0.7 copy.55
  81.9 1.4 %copy.56 = bf16[64,2,540]{2,1,0:T(2,128)(2,1)} copy(bf16[64,2,540]{0,1,2:T(2,128)(2,1)S(1)} %bitcast.43) | data formatting | bytes 276480 | tf_op jit(solution)/shard_map/reshape | solution.py:130
  83.2 14.4 %all-to-all-start = ((bf16[64,2,540]{2,1,0:T(2,128)(2,1)}), bf16[64,2,540]{2,1,0:T(2,128)(2,1)S(1)}, u32[]{:S(2)}, u32[]{:S(2)}) async-start(bf16[64,2,540]{2,1,0:T(2,128)(2,1)} %copy.56), calls=%async_computation | async-start | bytes 327680 | tf_op jit(solution)/shard_map/all_to_all | solution.py:130
  97.8 0.3 fusion.28
  98.1 10.2 %all-to-all-done = bf16[64,2,540]{2,1,0:T(2,128)(2,1)S(1)} async-done(((bf16[64,2,540]{2,1,0:T(2,128)(2,1)}), bf16[64,2,540]{2,1,0:T(2,128)(2,1)S(1)}, u32[]{:S(2)}, u32[]{:S(2)}) %all-to-all-start) | async-done | bytes 138272 | tf_op jit(solution)/shard_map/all_to_all | solution.py:130
  108.3 0.8 fusion.8
  109.4 0.5 convolution_convert_fusion
  109.9 0.7 convert_element_type.51
  110.8 17.1 %all_to_all.21 = bf16[64,90,12]{1,2,0:T(8,128)(2,1)S(1)} all-to-all(bf16[64,90,12]{1,2,0:T(8,128)(2,1)S(1)} %copy.62), channel_id=1, replica_groups=mesh['ord'=64,'blk'=4] {'ord'}, dimensions={0} | all-to-all | bytes 276480 | tf_op jit(solution)/shard_map/all_to_all | solution.py:149
  128.0 0.8 copy.63
  (33 shorter events, 2.4 us)
Async XLA Ops:
  0.0 1.6 %slice-start = ((bf16[45,16,2880]{2,1,0:T(8,128)(2,1)}), bf16[45,16,1472]{2,1,0:T(8,128)(2,1)S(1)}, s32[]{:S(2)}) async-start(bf16[45,16,2880]{2,1,0:T(8,128)(2,1)} %param.5), calls=%async_computation.2 | async-start | bytes 4423680 | tf_op jit(solution)/shard_map/slice | solution.py:105
  1.6 7.4 %copy-start = (f32[16]{0:T(128)S(1)}, f32[16]{0:T(128)}, u32[]{:S(2)}) copy-start(f32[16]{0:T(128)} %param.7) | copy-start | bytes 196
  5.7 52.3 %collective-permute-start.1 = (bf16[45,16,1536]{2,1,0:T(8,128)(2,1)}, bf16[45,16,1536]{2,1,0:T(8,128)(2,1)}, u32[]{:S(2)}, u32[]{:S(2)}) collective-permute-start(bf16[45,16,1536]{2,1,0:T(8,128)(2,1)} %get-tuple-element.9), channel_id=1, source_target_pairs={{1,2},{2,1},{3,0},{0,3},{5,6},{6,5},{7,4},{4,7},{9,10},{10,9},{11,... | collective-permute-start | bytes 6635528 | tf_op jit(solution)/shard_map/ppermute | solution.py:109
  9.0 49.0 %collective-permute-start = (bf16[2,45,16,720]{3,2,1,0:T(8,128)(2,1)}, bf16[2,45,16,720]{3,2,1,0:T(8,128)(2,1)}, u32[]{:S(2)}, u32[]{:S(2)}) collective-permute-start(bf16[2,45,16,720]{3,2,1,0:T(8,128)(2,1)} %bitcast.4.own_ref), channel_id=1, source_target_pairs={{0,1},{1,0},{2,3},{3,2},{4,5},{5,4},{6,7},{7,6},{8,9},{9,8},{10,11... | collective-permute-start | bytes 6220808 | tf_op jit(solution)/shard_map/ppermute | solution.py:104
  58.0 12.9 %copy-start.1 = (s32[16]{0:T(128)S(1)}, s32[16]{0:T(128)}, u32[]{:S(2)}) copy-start(s32[16]{0:T(128)} %param.9) | copy-start | bytes 196
  69.0 9.5 %collective-permute-start.2 = (f32[45,16,96]{2,1,0:T(8,128)S(1)}, f32[45,16,96]{2,1,0:T(8,128)S(1)}, u32[]{:S(2)}, u32[]{:S(2)}) collective-permute-start(f32[45,16,96]{2,1,0:T(8,128)S(1)} %slice.84), channel_id=1, source_target_pairs={{1,2},{2,1},{3,0},{0,3},{5,6},{6,5},{7,4},{4,7},{9,10},{10,9},{11,... | collective-permute-start | bytes 829448 | tf_op jit(solution)/shard_map/ppermute | solution.py:113
  83.2 25.0 %all-to-all-start = ((bf16[64,2,540]{2,1,0:T(2,128)(2,1)}), bf16[64,2,540]{2,1,0:T(2,128)(2,1)S(1)}, u32[]{:S(2)}, u32[]{:S(2)}) async-start(bf16[64,2,540]{2,1,0:T(2,128)(2,1)} %copy.56), calls=%async_computation | async-start | bytes 327680 | tf_op jit(solution)/shard_map/all_to_all | solution.py:130

commit v2 on v1

--- a/solution.py
+++ b/solution.py
@@ -13,14 +13,16 @@
 QUARTER = 720
 START = 1408
 WIDE = 1536
+KEPT = 1472
 NLON = 5760
 GROUP = 5
+CHUNKS = (0, 30, 40, 45)
 GAUSS_PAIRS = [(0, 1), (1, 0), (2, 3), (3, 2)]
 PANEL_PAIRS = [(1, 2), (2, 1), (3, 0), (0, 3)]
 
 
-def sums_kernel(where_ref, order_ref, height_ref, own_ref, other_ref, near_ref, far_ref, out_ref,
-                gs_ref, gn_ref, decay_ref):
+def sums_kernel(where_ref, order_ref, height_ref, own_ref, other_ref, panel_ref, far_ref, after_ref,
+                keep_ref, send_ref, gs_ref, gn_ref, decay_ref, table_ref, *, base):
     step = pl.program_id(0)
     half = where_ref[0]
     odd = where_ref[1] == 1
@@ -31,6 +33,7 @@
     def _():
         gs_ref[...] = jnp.zeros_like(gs_ref)
         gn_ref[...] = jnp.zeros_like(gn_ref)
+        table_ref[...] = jnp.zeros_like(table_ref)
         height = height_ref[...]
         here = jnp.exp(-(degree + 2.0) * height / ORDERS)
         decay_ref[0] = here
@@ -39,9 +42,11 @@
 
     low = jnp.where(odd, other_ref[...], own_ref[...])
     high = jnp.where(odd, own_ref[...], other_ref[...])
+    table_ref[:, 16:32, 0:KEPT] = far_ref[...]
 
     @pl.when(half == 0)
     def _():
+        table_ref[:, 0:16, 0:KEPT] = panel_ref[:, :, 0:KEPT]
         gs_ref[:, :, :, 0:720] = low
         gs_ref[:, :, :, 720:1440] = high
         gn_ref[:, :, :, 0:719] = low[:, :, :, 1:]
@@ -49,13 +54,14 @@
 
     @pl.when(half == 1)
     def _():
+        table_ref[:, 0:16, 0:KEPT] = panel_ref[:, :, START:ORDERS]
         gs_ref[:, :, :, 32:752] = low
         gs_ref[:, :, :, 752:1472] = high
         gn_ref[:, :, :, 31:751] = low
         gn_ref[:, :, :, 751:1471] = high
 
     for o in range(GROUP):
-        m = order_ref[step * GROUP + o].astype(jnp.float32)
+        m = order_ref[base + step * GROUP + o].astype(jnp.float32)
         root = jnp.sqrt(jnp.maximum((degree + 1.0) * (degree + 1.0) - m * m, 0.0))
         slope = decay_ref[2] * root
         g = [gs_ref[k, o].astype(jnp.float32) for k in range(2)]
@@ -63,30 +69,42 @@
         weights = jnp.concatenate(
             [g[0] * decay_ref[1], g[1] * decay_ref[1], g[0] * decay_ref[0], g[1] * decay_ref[0],
              n[0] * slope, n[1] * slope], 0).astype(jnp.bfloat16)
-        table = jnp.concatenate([near_ref[o], far_ref[o]], 0)
-        out_ref[o] = lax.dot_general(
-            table, weights, (((1,), (1,)), ((), ())), preferred_element_type=jnp.float32)
+        sums = lax.dot_general(
+            table_ref[o], weights, (((1,), (1,)), ((), ())), preferred_element_type=jnp.float32)
+        keep_ref[o] = sums[:16]
+        send_ref[o] = sums[16:].astype(jnp.bfloat16)
 
 
-def partial_sums(where, orders, height, own, other, near, far):
-    count = near.shape[0]
+def partial_sums(where, orders, height, own, other, panel, far, after, base):
+    count = far.shape[0]
+    skip = base // GROUP
     smem = pl.BlockSpec(memory_space=pltpu.SMEM)
-    coef = pl.BlockSpec((2, GROUP, 16, QUARTER), lambda i: (0, i, 0, 0))
-    tab = pl.BlockSpec((GROUP, 16, WIDE), lambda i: (i, 0, 0))
+    out = pl.BlockSpec((GROUP, 16, 96), lambda i: (i, 0, 0))
     return pl.pallas_call(
-        sums_kernel,
-        out_shape=jax.ShapeDtypeStruct((count, 32, 96), jnp.float32),
+        functools.partial(sums_kernel, base=base),
+        out_shape=[jax.ShapeDtypeStruct((count, 16, 96), jnp.float32),
+                   jax.ShapeDtypeStruct((count, 16, 96), jnp.bfloat16)],
         grid=(count // GROUP,),
-        in_specs=[smem, smem, pl.BlockSpec((16, 1), lambda i: (0, 0)), coef, coef, tab, tab],
-        out_specs=pl.BlockSpec((GROUP, 32, 96), lambda i: (i, 0, 0)),
+        in_specs=[
+            smem, smem, pl.BlockSpec((16, 1), lambda i: (0, 0)),
+            pl.BlockSpec((2, GROUP, 16, QUARTER), lambda i: (0, i + skip, 0, 0)),
+            pl.BlockSpec((2, GROUP, 16, QUARTER), lambda i: (0, i, 0, 0)),
+            pl.BlockSpec((GROUP, 16, ORDERS), lambda i: (i + skip, 0, 0)),
+            pl.BlockSpec((GROUP, 16, KEPT), lambda i: (i, 0, 0)),
+            pl.BlockSpec(memory_space=pl.ANY),
+        ],
+        out_specs=[out, out],
         scratch_shapes=[
             pltpu.VMEM((2, GROUP, 16, WIDE), jnp.bfloat16),
             pltpu.VMEM((2, GROUP, 16, WIDE), jnp.bfloat16),
             pltpu.VMEM((3, 16, WIDE), jnp.float32),
+            pltpu.VMEM((GROUP, 32, WIDE), jnp.bfloat16),
         ],
-        compiler_params=pltpu.CompilerParams(vmem_limit_bytes=40 << 20),
+        compiler_params=pltpu.CompilerParams(vmem_limit_bytes=24 << 20),
+        cost_estimate=pl.CostEstimate(
+            flops=count * 32 * 96 * WIDE * 2, bytes_accessed=count * 200000, transcendentals=0),
         name="partial_sums",
-    )(where, orders, height, own, other, near, far)
+    )(where, orders, height, own, other, panel, far, after)
 
 
 def turn(phase, period):
@@ -101,16 +119,23 @@
     here = lax.axis_index("ord")
     half = spot // 2
     own = jnp.transpose(gauss, (0, 2, 1, 3))
-    other = lax.ppermute(own, "blk", GAUSS_PAIRS)
-    upper = jnp.pad(panel[:, :, START:], ((0, 0), (0, 0), (0, START + WIDE - ORDERS)))
-    lower = panel[:, :, :WIDE]
-    sent = jnp.where(half == 0, upper, lower)
-    near = jnp.where(half == 0, lower, upper)
-    far = lax.ppermute(sent, "blk", PANEL_PAIRS)
     orders_int = lax.dynamic_slice_in_dim(order_map, here * count, count, 0)
     where = jnp.stack([half, spot % 2]).astype(jnp.int32)
-    raw = partial_sums(where, orders_int, height[:, None], own, other, near, far)
-    total = raw[:, :cycles] + lax.ppermute(raw[:, cycles:], "blk", PANEL_PAIRS)
+    spans = list(zip(CHUNKS[:-1], CHUNKS[1:]))
+    arrived = []
+    late = jnp.zeros((), jnp.int32)
+    for a, b in spans:
+        part = lax.dynamic_slice_in_dim(own, a + late, b - a, 1)
+        other = lax.ppermute(part, "blk", GAUSS_PAIRS)
+        sent = jnp.where(half + late == 0, panel[a:b, :, START:], panel[a:b, :, :KEPT])
+        arrived.append((other, lax.ppermute(sent, "blk", PANEL_PAIRS)))
+        late = jnp.isnan(sent[0, 0, 0]).astype(jnp.int32)
+    totals = []
+    keep = own
+    for (a, b), (other, far) in zip(spans, arrived):
+        keep, send = partial_sums(where, orders_int, height[:, None], own, other, panel, far, keep, a)
+        totals.append(keep + lax.ppermute(send, "blk", PANEL_PAIRS).astype(jnp.float32))
+    total = jnp.concatenate(totals, 0)
     theta = math.pi * (cycle_map.astype(jnp.float32) + 0.5) / ORDERS
     cosine = jnp.cos(theta)[None, :, None]
     sine = jnp.sin(theta)[None, :, None]

time: 129 us -> 117 us (0.907)
  waiting for transfers between devices: 64.8 us -> 35.1 us
  starting transfers between devices: 19.6 us -> 25.5 us
  local copies, waits for them, and re-layouts: 8.38 us -> 13.5 us
  other arithmetic: 6.5 us -> 9.52 us
  between operations: 0.2 us -> 2.86 us
    ppermute x3 -> x9, waiting for transfers between devices: 54.7 us -> 24.9 us  [the longest x3 20.8 us: body(): other = lax.ppermute(part, 'blk', GAUSS_PAIRS)]
    ppermute x3 -> x9, starting transfers between devices: 5.15 us -> 10.7 us  [the longest x3 5.98 us: body(): arrived.append((other, lax.ppermute(sent, 'blk', PANEL_PAIRS)))]
    select_n x1 -> x3, other arithmetic: 4.1 us -> 7.07 us  [body(): jnp.where(half + late == 0, panel[a:b, :, START:], panel[a:b, :, :KEPT])]
    unnamed x4 -> x8, local copies, waits for them, and re-layouts: 0.01 us -> 2.21 us
    dynamic_slice x0 -> x3, local copies, waits for them, and re-layouts: none -> 2.1 us  [body(): part = lax.dynamic_slice_in_dim(own, a + late, b - a, 1)]
    pallas_call x1 -> x3, Pallas kernels: 10.9 us -> 11.7 us  [partial_sums(): pl.pallas_call(functools.partial(sums_kernel, base=base), out_shape=[jax....]
  transfers between devices with their start and end apart: 4 -> 10, of which waited for: 3 -> 6; matrix products, arithmetic and copies ran while one was open for 2% -> 9% of each run, Pallas kernels for 0% -> 9%
where the time goes in v2:
time: 117 us
  waiting for transfers between devices  35.1 us (30%)
  starting transfers between devices  25.5 us (22%)
  blocking collectives  17.1 us (15%)
  local copies, waits for them, and re-layouts  13.5 us (12%)
  Pallas kernels  11.7 us (10%)
  other arithmetic  9.52 us (8%)
  between operations  2.86 us (2%)
  matrix products  1.25 us (1%)
    ppermute x3, waiting for transfers between devices, body(): other = lax.ppermute(part, 'blk', GAUSS_PAIRS)  20.8 us
    all_to_all x1, blocking collectives, body(): return lax.all_to_all(field, 'ord', split_axis=0, concat_axis=1, tiled=True)  17.1 us
    all_to_all x1, starting transfers between devices, body(): lax.all_to_all(chunk.reshape(parts, 2, count * items), 'ord', 0, 0, tiled...  14.8 us
    pallas_call x3, Pallas kernels, partial_sums(): pl.pallas_call(functools.partial(sums_kernel, base=base), out_shape=[jax....  11.7 us
    all_to_all x1, waiting for transfers between devices, body(): lax.all_to_all(chunk.reshape(parts, 2, count * items), 'ord', 0, 0, tiled...  10.2 us
    select_n x3, other arithmetic, body(): jnp.where(half + late == 0, panel[a:b, :, START:], panel[a:b, :, :KEPT])  7.07 us
    ppermute x3, starting transfers between devices, body(): arrived.append((other, lax.ppermute(sent, 'blk', PANEL_PAIRS)))  5.98 us
    ppermute x3, waiting for transfers between devices, body(): lax.ppermute(send, 'blk', PANEL_PAIRS).astype(jnp.float32)  4.11 us
  transfers between devices with their start and end apart: 10, of which 6 were waited for; matrix products, arithmetic and copies ran while one was open for 9% of the time, Pallas kernels for 9%

profile of v2, /device:TPU:1, one launch (start us, length us, event | category | flops | bytes accessed | tf_op | source)
XLA Modules:
  0.0 116.6 jit_solution(11471363318719730952)
XLA Ops:
  0.0 3.3 %slice_select_fusion = bf16[30,16,1472]{2,1,0:T(8,128)(2,1)} fusion(bf16[45,16,2880]{2,1,0:T(8,128)(2,1)} %panel_ref.5, pred[]{:T(512)S(6)} %eq.17), kind=kLoop, calls=%fused_computation | loop fusion | flops 706560 | bytes 4239361 | tf_op jit(solution)/shard_map/jit(_where)/select_n | solution.py:130
  3.3 3.3 %collective-permute-start.1 = (bf16[30,16,1472]{2,1,0:T(8,128)(2,1)}, bf16[30,16,1472]{2,1,0:T(8,128)(2,1)}, u32[]{:S(2)}, u32[]{:S(2)}) collective-permute-start(bf16[30,16,1472]{2,1,0:T(8,128)(2,1)} %slice_select_fusion), channel_id=1, source_target_pairs={{1,2},{2,1},{3,0},{0,3},{5,6},{6,5},{7,4},{4,7},{9,10},{10,9},{11,... | collective-permute-start | bytes 4239368 | tf_op jit(solution)/shard_map/ppermute | solution.py:131
  6.6 1.2 %dynamic_slice.16 = bf16[2,30,16,720]{3,2,1,0:T(8,128)(2,1)} slice(bf16[2,45,16,720]{3,2,1,0:T(8,128)(2,1)S(1)} %bitcast.49), slice={[0:2], [0:30], [0:16], [0:720]} | slice | bytes 2764800 | tf_op jit(solution)/shard_map/dynamic_slice | solution.py:128
  7.8 1.2 %slice.99 = bf16[1,1,1]{2,1,0:T(2,128)(2,1)} slice(bf16[30,16,1472]{2,1,0:T(8,128)(2,1)} %slice_select_fusion), slice={[0:1], [0:1], [0:1]} | slice | bytes 4 | tf_op jit(solution)/shard_map/slice | solution.py:132
  10.3 0.8 dynamic-slice_bitcast_fusion
  11.2 1.4 %collective-permute-start.3 = (bf16[2,10,16,720]{3,2,1,0:T(8,128)(2,1)}, bf16[2,10,16,720]{3,2,1,0:T(8,128)(2,1)S(1)}, u32[]{:S(2)}, u32[]{:S(2)}) collective-permute-start(bf16[2,10,16,720]{3,2,1,0:T(8,128)(2,1)} %dynamic-slice_bitcast_fusion), channel_id=1, source_target_pairs={{0,1},{1,0},{2,3},{3,2},{4,5},{5,4},{6,7},{7,6},{8,9},{9,8},{10,11... | collective-permute-start | bytes 1382408 | tf_op jit(solution)/shard_map/ppermute | solution.py:129
  12.6 2.0 %slice_select_fusion.1 = bf16[10,16,1472]{2,1,0:T(8,128)(2,1)} fusion(bf16[45,16,2880]{2,1,0:T(8,128)(2,1)} %panel_ref.5, pred[]{:T(512)S(6)} %eq.18), kind=kLoop, calls=%fused_computation.6 | loop fusion | flops 235520 | bytes 1413121 | tf_op jit(solution)/shard_map/jit(_where)/select_n | solution.py:130
  14.6 1.2 %slice.100 = bf16[1,1,1]{2,1,0:T(2,128)(2,1)} slice(bf16[10,16,1472]{2,1,0:T(8,128)(2,1)} %slice_select_fusion.1), slice={[0:1], [0:1], [0:1]} | slice | bytes 4 | tf_op jit(solution)/shard_map/slice | solution.py:132
  17.2 1.8 %slice_select_fusion.2 = bf16[5,16,1472]{2,1,0:T(8,128)(2,1)} fusion(bf16[45,16,2880]{2,1,0:T(8,128)(2,1)} %panel_ref.5, pred[]{:T(512)S(6)} %eq.19), kind=kLoop, calls=%fused_computation.25 | loop fusion | flops 117760 | bytes 706561 | tf_op jit(solution)/shard_map/jit(_where)/select_n | solution.py:130
  19.0 2.7 %collective-permute-start.7 = (bf16[5,16,1472]{2,1,0:T(8,128)(2,1)}, bf16[5,16,1472]{2,1,0:T(8,128)(2,1)S(1)}, u32[]{:S(2)}, u32[]{:S(2)}) collective-permute-start(bf16[5,16,1472]{2,1,0:T(8,128)(2,1)} %slice_select_fusion.2), channel_id=1, source_target_pairs={{1,2},{2,1},{3,0},{0,3},{5,6},{6,5},{7,4},{4,7},{9,10},{10,9},{11,... | collective-permute-start | bytes 706568 | tf_op jit(solution)/shard_map/ppermute | solution.py:131
  21.7 0.8 slice.77
  23.5 17.5 %collective-permute-done.other_ref = bf16[2,30,16,720]{3,2,1,0:T(8,128)(2,1)} collective-permute-done((bf16[2,30,16,720]{3,2,1,0:T(8,128)(2,1)}, bf16[2,30,16,720]{3,2,1,0:T(8,128)(2,1)}, u32[]{:S(2)}, u32[]{:S(2)}) %collective-permute-start) | collective-permute-done | bytes 1382432 | tf_op jit(solution)/shard_map/ppermute | solution.py:129
  41.1 2.2 %copy-done = bf16[45,16,2880]{2,1,0:T(8,128)(2,1)S(1)} copy-done((bf16[45,16,2880]{2,1,0:T(8,128)(2,1)S(1)}, bf16[45,16,2880]{2,1,0:T(8,128)(2,1)}, u32[]{:S(2)}) %copy-start) | copy-done | bytes 4147224
  43.3 7.4 %partial_sums.3 = (f32[30,16,96]{2,1,0:T(8,128)S(1)}, bf16[30,16,96]{2,1,0:T(8,128)(2,1)S(1)}) custom-call(s32[2]{0:T(128)S(1)} %pad_add_fusion.where_ref, s32[45]{0:T(128)S(1)} %get-tuple-element.18.order_ref, f32[16,1]{1,0:T(8,128)S(1)} %copy.56.height_ref, bf16[2,45,16,720]{3,2,1,0:T(8,128)(2,1)S(1)} %bitcast.50, ...), custom_call_target="tpu_custom_call" | custom-call | flops 283115520 | bytes 6000000 | tf_op jit(solution)/shard_map/partial_sums/pallas_call | solution.py:83
  51.4 2.7 %partial_sums.4 = (f32[10,16,96]{2,1,0:T(8,128)S(1)}, bf16[10,16,96]{2,1,0:T(8,128)(2,1)S(1)}) custom-call(s32[2]{0:T(128)S(1)} %pad_add_fusion.where_ref, s32[45]{0:T(128)S(1)} %get-tuple-element.18.order_ref, f32[16,1]{1,0:T(8,128)S(1)} %copy.56.height_ref, bf16[2,45,16,720]{3,2,1,0:T(8,128)(2,1)S(1)} %bitcast.52, ...), custom_call_target="tpu_custom_call" | custom-call | flops 94371840 | bytes 2000000 | tf_op jit(solution)/shard_map/partial_sums/pallas_call | solution.py:83
  54.1 2.6 %collective-permute-done.6.other_ref = bf16[2,5,16,720]{3,2,1,0:T(8,128)(2,1)S(1)} collective-permute-done((bf16[2,5,16,720]{3,2,1,0:T(8,128)(2,1)S(1)}, bf16[2,5,16,720]{3,2,1,0:T(8,128)(2,1)S(1)}, u32[]{:S(2)}, u32[]{:S(2)}) %collective-permute-start.6) | collective-permute-done | bytes 230432 | tf_op jit(solution)/shard_map/ppermute | solution.py:129
  56.7 1.6 %partial_sums.5 = (f32[5,16,96]{2,1,0:T(8,128)S(1)}, bf16[5,16,96]{2,1,0:T(8,128)(2,1)S(1)}) custom-call(s32[2]{0:T(128)S(1)} %pad_add_fusion.where_ref, s32[45]{0:T(128)S(1)} %get-tuple-element.18.order_ref, f32[16,1]{1,0:T(8,128)S(1)} %copy.56.height_ref, bf16[2,45,16,720]{3,2,1,0:T(8,128)(2,1)S(1)} %bitcast.53, ...), custom_call_target="tpu_custom_call" | custom-call | flops 47185920 | bytes 1000000 | tf_op jit(solution)/shard_map/partial_sums/pallas_call | solution.py:83
  58.8 2.4 %collective-permute-start.2 = (bf16[30,16,96]{2,1,0:T(8,128)(2,1)S(1)}, bf16[30,16,96]{2,1,0:T(8,128)(2,1)S(1)}, u32[]{:S(2)}, u32[]{:S(2)}) collective-permute-start(bf16[30,16,96]{2,1,0:T(8,128)(2,1)S(1)} %get-tuple-element.12), channel_id=1, source_target_pairs={{1,2},{2,1},{3,0},{0,3},{5,6},{6,5},{7,4},{4,7},{9,10},{10,9},{11,... | collective-permute-start | bytes 276488 | tf_op jit(solution)/shard_map/ppermute | solution.py:137
  62.2 3.5 %collective-permute-done.5 = bf16[10,16,96]{2,1,0:T(8,128)(2,1)S(1)} collective-permute-done((bf16[10,16,96]{2,1,0:T(8,128)(2,1)S(1)}, bf16[10,16,96]{2,1,0:T(8,128)(2,1)S(1)}, u32[]{:S(2)}, u32[]{:S(2)}) %collective-permute-start.5) | collective-permute-done | bytes 30752 | tf_op jit(solution)/shard_map/ppermute | solution.py:137
  69.2 1.4 %copy.66 = bf16[64,2,540]{2,1,0:T(2,128)(2,1)} copy(bf16[64,2,540]{0,1,2:T(2,128)(2,1)S(1)} %bitcast.54) | data formatting | bytes 276480 | tf_op jit(solution)/shard_map/reshape | solution.py:155
  70.6 14.8 %all-to-all-start = ((bf16[64,2,540]{2,1,0:T(2,128)(2,1)}), bf16[64,2,540]{2,1,0:T(2,128)(2,1)S(1)}, u32[]{:S(2)}, u32[]{:S(2)}) async-start(bf16[64,2,540]{2,1,0:T(2,128)(2,1)} %copy.66), calls=%async_computation | async-start | bytes 327680 | tf_op jit(solution)/shard_map/all_to_all | solution.py:155
  85.8 10.2 %all-to-all-done = bf16[64,2,540]{2,1,0:T(2,128)(2,1)S(1)} async-done(((bf16[64,2,540]{2,1,0:T(2,128)(2,1)}), bf16[64,2,540]{2,1,0:T(2,128)(2,1)S(1)}, u32[]{:S(2)}, u32[]{:S(2)}) %all-to-all-start) | async-done | bytes 138272 | tf_op jit(solution)/shard_map/all_to_all | solution.py:155
  98.5 17.1 %all_to_all.21 = bf16[64,90,12]{1,2,0:T(8,128)(2,1)S(1)} all-to-all(bf16[64,90,12]{1,2,0:T(8,128)(2,1)S(1)} %copy.72), channel_id=1, replica_groups=mesh['ord'=64,'blk'=4] {'ord'}, dimensions={0} | all-to-all | bytes 276480 | tf_op jit(solution)/shard_map/all_to_all | solution.py:174
  115.7 0.8 copy.73
  (59 shorter events, 9.6 us)
Async XLA Ops:
  0.0 6.6 %copy-start.1 = (bf16[2,16,45,720]{3,1,2,0:T(8,128)(2,1)S(1)}, bf16[2,16,45,720]{3,1,2,0:T(8,128)(2,1)}, u32[]{:S(2)}) copy-start(bf16[2,16,45,720]{3,1,2,0:T(8,128)(2,1)} %param.6) | copy-start | bytes 6220804
  3.3 37.8 %collective-permute-start.1 = (bf16[30,16,1472]{2,1,0:T(8,128)(2,1)}, bf16[30,16,1472]{2,1,0:T(8,128)(2,1)}, u32[]{:S(2)}, u32[]{:S(2)}) collective-permute-start(bf16[30,16,1472]{2,1,0:T(8,128)(2,1)} %slice_select_fusion), channel_id=1, source_target_pairs={{1,2},{2,1},{3,0},{0,3},{5,6},{6,5},{7,4},{4,7},{9,10},{10,9},{11,... | collective-permute-start | bytes 4239368 | tf_op jit(solution)/shard_map/ppermute | solution.py:131
  7.8 13.8 %copy-start.2 = (f32[16]{0:T(128)S(1)}, f32[16]{0:T(128)}, u32[]{:S(2)}) copy-start(f32[16]{0:T(128)} %param.7) | copy-start | bytes 196
  7.8 15.6 %copy-start.3 = (s32[16]{0:T(128)S(1)}, s32[16]{0:T(128)}, u32[]{:S(2)}) copy-start(s32[16]{0:T(128)} %param.9) | copy-start | bytes 196
  7.8 33.2 %collective-permute-start = (bf16[2,30,16,720]{3,2,1,0:T(8,128)(2,1)}, bf16[2,30,16,720]{3,2,1,0:T(8,128)(2,1)}, u32[]{:S(2)}, u32[]{:S(2)}) collective-permute-start(bf16[2,30,16,720]{3,2,1,0:T(8,128)(2,1)} %dynamic_slice.16), channel_id=1, source_target_pairs={{0,1},{1,0},{2,3},{3,2},{4,5},{5,4},{6,7},{7,6},{8,9},{9,8},{10,11... | collective-permute-start | bytes 4147208 | tf_op jit(solution)/shard_map/ppermute | solution.py:129
  11.2 40.2 %collective-permute-start.3 = (bf16[2,10,16,720]{3,2,1,0:T(8,128)(2,1)}, bf16[2,10,16,720]{3,2,1,0:T(8,128)(2,1)S(1)}, u32[]{:S(2)}, u32[]{:S(2)}) collective-permute-start(bf16[2,10,16,720]{3,2,1,0:T(8,128)(2,1)} %dynamic-slice_bitcast_fusion), channel_id=1, source_target_pairs={{0,1},{1,0},{2,3},{3,2},{4,5},{5,4},{6,7},{7,6},{8,9},{9,8},{10,11... | collective-permute-start | bytes 1382408 | tf_op jit(solution)/shard_map/ppermute | solution.py:129
  14.6 36.8 %collective-permute-start.4 = (bf16[10,16,1472]{2,1,0:T(8,128)(2,1)}, bf16[10,16,1472]{2,1,0:T(8,128)(2,1)S(1)}, u32[]{:S(2)}, u32[]{:S(2)}) collective-permute-start(bf16[10,16,1472]{2,1,0:T(8,128)(2,1)} %slice_select_fusion.1), channel_id=1, source_target_pairs={{1,2},{2,1},{3,0},{0,3},{5,6},{6,5},{7,4},{4,7},{9,10},{10,9},{11,... | collective-permute-start | bytes 1413128 | tf_op jit(solution)/shard_map/ppermute | solution.py:131
  19.0 37.7 %collective-permute-start.7 = (bf16[5,16,1472]{2,1,0:T(8,128)(2,1)}, bf16[5,16,1472]{2,1,0:T(8,128)(2,1)S(1)}, u32[]{:S(2)}, u32[]{:S(2)}) collective-permute-start(bf16[5,16,1472]{2,1,0:T(8,128)(2,1)} %slice_select_fusion.2), channel_id=1, source_target_pairs={{1,2},{2,1},{3,0},{0,3},{5,6},{6,5},{7,4},{4,7},{9,10},{10,9},{11,... | collective-permute-start | bytes 706568 | tf_op jit(solution)/shard_map/ppermute | solution.py:131
  41.0 15.7 %collective-permute-start.6 = (bf16[2,5,16,720]{3,2,1,0:T(8,128)(2,1)S(1)}, bf16[2,5,16,720]{3,2,1,0:T(8,128)(2,1)S(1)}, u32[]{:S(2)}, u32[]{:S(2)}) collective-permute-start(bf16[2,5,16,720]{3,2,1,0:T(8,128)(2,1)S(1)} %dynamic-slice_bitcast_fusion.1), channel_id=1, source_target_pairs={{0,1},{1,0},{2,3},{3,2},{4,5},{5,4},{6,7},{7,6},{8,9},{9,8},{10,11... | collective-permute-start | bytes 691208 | tf_op jit(solution)/shard_map/ppermute | solution.py:129
  41.1 2.2 %copy-start = (bf16[45,16,2880]{2,1,0:T(8,128)(2,1)S(1)}, bf16[45,16,2880]{2,1,0:T(8,128)(2,1)}, u32[]{:S(2)}) copy-start(bf16[45,16,2880]{2,1,0:T(8,128)(2,1)} %panel_ref.5) | copy-start | bytes 12441604
  58.3 3.9 %collective-permute-start.8 = (bf16[5,16,96]{2,1,0:T(8,128)(2,1)S(1)}, bf16[5,16,96]{2,1,0:T(8,128)(2,1)S(1)}, u32[]{:S(2)}, u32[]{:S(2)}) collective-permute-start(bf16[5,16,96]{2,1,0:T(8,128)(2,1)S(1)} %get-tuple-element.16), channel_id=1, source_target_pairs={{1,2},{2,1},{3,0},{0,3},{5,6},{6,5},{7,4},{4,7},{9,10},{10,9},{11,... | collective-permute-start | bytes 46088 | tf_op jit(solution)/shard_map/ppermute | solution.py:137
  58.8 6.9 %collective-permute-start.2 = (bf16[30,16,96]{2,1,0:T(8,128)(2,1)S(1)}, bf16[30,16,96]{2,1,0:T(8,128)(2,1)S(1)}, u32[]{:S(2)}, u32[]{:S(2)}) collective-permute-start(bf16[30,16,96]{2,1,0:T(8,128)(2,1)S(1)} %get-tuple-element.12), channel_id=1, source_target_pairs={{1,2},{2,1},{3,0},{0,3},{5,6},{6,5},{7,4},{4,7},{9,10},{10,9},{11,... | collective-permute-start | bytes 276488 | tf_op jit(solution)/shard_map/ppermute | solution.py:137
  61.3 4.5 %collective-permute-start.5 = (bf16[10,16,96]{2,1,0:T(8,128)(2,1)S(1)}, bf16[10,16,96]{2,1,0:T(8,128)(2,1)S(1)}, u32[]{:S(2)}, u32[]{:S(2)}) collective-permute-start(bf16[10,16,96]{2,1,0:T(8,128)(2,1)S(1)} %get-tuple-element.14), channel_id=1, source_target_pairs={{1,2},{2,1},{3,0},{0,3},{5,6},{6,5},{7,4},{4,7},{9,10},{10,9},{11,... | collective-permute-start | bytes 92168 | tf_op jit(solution)/shard_map/ppermute | solution.py:137
  70.6 25.4 %all-to-all-start = ((bf16[64,2,540]{2,1,0:T(2,128)(2,1)}), bf16[64,2,540]{2,1,0:T(2,128)(2,1)S(1)}, u32[]{:S(2)}, u32[]{:S(2)}) async-start(bf16[64,2,540]{2,1,0:T(2,128)(2,1)} %copy.66), calls=%async_computation | async-start | bytes 327680 | tf_op jit(solution)/shard_map/all_to_all | solution.py:155

commit v3 on v2

v3 whole, which is shorter than its diff:
```python
import functools
import math

import jax
import jax.numpy as jnp
from jax import lax
from jax.experimental import pallas as pl
from jax.experimental.pallas import tpu as pltpu
from jax.sharding import PartitionSpec as P

ORDERS = 2880
RUN = 45
QUARTER = 720
START = 1408
WIDE = 1536
KEPT = 1472
NLON = 5760
GROUP = 5
CHUNKS = (0, 20, 35, 45)
GAUSS_PAIRS = [(0, 1), (1, 0), (2, 3), (3, 2)]
PANEL_PAIRS = [(1, 2), (2, 1), (3, 0), (0, 3)]


def sums_kernel(where_ref, order_ref, height_ref, angle_ref, own_ref, other_ref, panel_ref, far_ref,
                *rest, base):
    keep_ref, send_ref, gs_ref, gn_ref, decay_ref, table_ref = rest[-6:]
    step = pl.program_id(0)
    half = where_ref[0]
    odd = where_ref[1] == 1
    first = (half * START).astype(jnp.float32)
    degree = lax.broadcasted_iota(jnp.int32, (1, WIDE), 1).astype(jnp.float32) + first

    @pl.when(step == 0)
    def _():
        gs_ref[...] = jnp.zeros_like(gs_ref)
        gn_ref[...] = jnp.zeros_like(gn_ref)
        table_ref[...] = jnp.zeros_like(table_ref)
        height = height_ref[...]
        here = jnp.exp(-(degree + 2.0) * height / ORDERS)
        decay_ref[0] = here
        decay_ref[1] = here * (degree + 1.0)
        decay_ref[2] = jnp.exp(-(degree + 3.0) * height / ORDERS)

    low = jnp.where(odd, other_ref[...], own_ref[...])
    high = jnp.where(odd, own_ref[...], other_ref[...])
    table_ref[:, 16:32, 0:KEPT] = far_ref[...]

    @pl.when(half == 0)
    def _():
        table_ref[:, 0:16, 0:KEPT] = panel_ref[:, :, 0:KEPT]
        gs_ref[:, :, :, 0:720] = low
        gs_ref[:, :, :, 720:1440] = high
        gn_ref[:, :, :, 0:719] = low[:, :, :, 1:]
        gn_ref[:, :, :, 719:1439] = high

    @pl.when(half == 1)
    def _():
        table_ref[:, 0:16, 0:KEPT] = panel_ref[:, :, START:ORDERS]
        gs_ref[:, :, :, 32:752] = low
        gs_ref[:, :, :, 752:1472] = high
        gn_ref[:, :, :, 31:751] = low
        gn_ref[:, :, :, 751:1471] = high

    cosine = angle_ref[:, 0:1]
    inverse = angle_ref[:, 1:2]
    lane = lax.broadcasted_iota(jnp.int32, (32, 128), 1)
    for o in range(GROUP):
        m = order_ref[base + step * GROUP + o].astype(jnp.float32)
        root = jnp.sqrt(jnp.maximum((degree + 1.0) * (degree + 1.0) - m * m, 0.0))
        slope = decay_ref[2] * root
        g = [gs_ref[k, o].astype(jnp.float32) for k in range(2)]
        n = [gn_ref[k, o].astype(jnp.float32) for k in range(2)]
        main = [(g[k] * decay_ref[1]).astype(jnp.bfloat16) for k in range(2)]
        bare = [(g[k] * decay_ref[0]).astype(jnp.bfloat16) for k in range(2)]
        tilt = [(n[k] * slope).astype(jnp.bfloat16) for k in range(2)]
        weights = jnp.concatenate(main + bare + [-bare[1], bare[0]] + tilt, 0)
        sums = lax.dot_general(
            table_ref[o], weights, (((1,), (1,)), ((), ())), preferred_element_type=jnp.float32)
        polar = (pltpu.roll(sums, 64, 1) - cosine * (pltpu.roll(sums, 32, 1) - sums)) * inverse
        mixed = jnp.where(lane < 32, sums, jnp.where(lane < 64, polar, m * inverse * sums))
        keep_ref[o] = mixed[:16, :96]
        send_ref[o] = mixed[16:, :96].astype(jnp.bfloat16)


def partial_sums(where, orders, height, angles, own, other, panel, far, after, base):
    count = far.shape[0]
    skip = base // GROUP
    smem = pl.BlockSpec(memory_space=pltpu.SMEM)
    out = pl.BlockSpec((GROUP, 16, 96), lambda i: (i, 0, 0))
    return pl.pallas_call(
        functools.partial(sums_kernel, base=base),
        out_shape=[jax.ShapeDtypeStruct((count, 16, 96), jnp.float32),
                   jax.ShapeDtypeStruct((count, 16, 96), jnp.bfloat16)],
        grid=(count // GROUP,),
        in_specs=[
            smem, smem, pl.BlockSpec((16, 1), lambda i: (0, 0)),
            pl.BlockSpec((32, 2), lambda i: (0, 0)),
            pl.BlockSpec((2, GROUP, 16, QUARTER), lambda i: (0, i + skip, 0, 0)),
            pl.BlockSpec((2, GROUP, 16, QUARTER), lambda i: (0, i, 0, 0)),
            pl.BlockSpec((GROUP, 16, ORDERS), lambda i: (i + skip, 0, 0)),
            pl.BlockSpec((GROUP, 16, KEPT), lambda i: (i, 0, 0)),
        ] + [pl.BlockSpec(memory_space=pl.ANY)] * len(after),
        out_specs=[out, out],
        scratch_shapes=[
            pltpu.VMEM((2, GROUP, 16, WIDE), jnp.bfloat16),
            pltpu.VMEM((2, GROUP, 16, WIDE), jnp.bfloat16),
            pltpu.VMEM((3, 16, WIDE), jnp.float32),
            pltpu.VMEM((GROUP, 32, WIDE), jnp.bfloat16),
        ],
        compiler_params=pltpu.CompilerParams(vmem_limit_bytes=24 << 20),
        cost_estimate=pl.CostEstimate(
            flops=count * 32 * 96 * WIDE * 2, bytes_accessed=count * 200000, transcendentals=0),
        name="partial_sums",
    )(where, orders, height, angles, own, other, panel, far, *after)


def turn(phase, period):
    angle = (phase % period).astype(jnp.float32) * (2.0 * math.pi / period)
    return jnp.cos(angle), jnp.sin(angle)


def body(panel, gauss, height, order_map, cycle_map):
    count, cycles, _ = panel.shape
    shells = height.shape[0]
    spot = lax.axis_index("blk")
    here = lax.axis_index("ord")
    half = spot // 2
    own = jnp.transpose(gauss, (0, 2, 1, 3))
    orders_int = lax.dynamic_slice_in_dim(order_map, here * count, count, 0)
    where = jnp.stack([half, spot % 2]).astype(jnp.int32)
    spans = list(zip(CHUNKS[:-1], CHUNKS[1:]))
    arrived = []
    late, next_ = 0, 0
    for a, b in spans:
        part = lax.dynamic_slice_in_dim(own, a + next_, b - a, 1)
        other = lax.ppermute(part, "blk", GAUSS_PAIRS)
        sent = jnp.where(half + late == 0, panel[a:b, :, START:], panel[a:b, :, :KEPT])
        arrived.append((other, lax.ppermute(sent, "blk", PANEL_PAIRS)))
        late = jnp.isnan(sent[0, 0, 0]).astype(jnp.int32)
        next_ = jnp.isnan(part[0, 0, 0, 0]).astype(jnp.int32)
    facing = lax.ppermute(cycle_map, "blk", PANEL_PAIRS)
    theta = math.pi * (jnp.concatenate([cycle_map, facing]).astype(jnp.float32) + 0.5) / ORDERS
    angles = jnp.stack([jnp.cos(theta), 1.0 / jnp.sin(theta)], 1)
    kept, added = [], []
    for c, ((a, b), (other, far)) in enumerate(zip(spans, arrived)):
        after = (kept[-1:] or [own]) + (added[c - 2:c - 1] if c >= 2 else [])
        keep, send = partial_sums(
            where, orders_int, height[:, None], angles, own, other, panel, far, after, a)
        kept.append(keep)
        added.append(lax.ppermute(send, "blk", PANEL_PAIRS))
    total = jnp.concatenate(kept, 0) + jnp.concatenate(added, 0).astype(jnp.float32)
    total = lax.optimization_barrier(total.astype(jnp.bfloat16))
    split = (count, cycles, 3, 2, 4, shells // 4)
    chunk = jnp.transpose(total.reshape(split), (1, 4, 3, 2, 5, 0))

    parts = ORDERS // count
    items = cycles * 3 * shells // parts
    runs = order_map[::RUN] // RUN
    b = jnp.arange(128)
    q = jnp.arange(RUN)
    cos1, sin1 = turn(b[:, None] * runs[None, :], 128)
    table = jnp.concatenate(
        [jnp.concatenate([cos1, sin1], 1), jnp.concatenate([sin1, -cos1], 1)], 0)
    cos2, sin2 = turn(b[:, None] * q[None, :], NLON)
    cos3, sin3 = turn(q[:, None] * q[None, :], RUN)
    last = jnp.concatenate([cos3, -sin3], 1)

    chunk = chunk.reshape(parts, 2, items * count)
    chunk, table, cos2, sin2, last = lax.optimization_barrier((chunk, table, cos2, sin2, last))
    spread = lax.all_to_all(chunk, "ord", 0, 0, tiled=True).astype(jnp.float32)
    flat = jnp.concatenate([spread[:, 0], spread[:, 1]], 0)
    mid = jnp.dot(table, flat, precision=lax.Precision.HIGHEST).reshape(2, 128, items, count)
    cos2, sin2 = cos2[:, None, :], sin2[:, None, :]
    real = mid[0] * cos2 - mid[1] * sin2
    imag = mid[0] * sin2 + mid[1] * cos2
    field = lax.dot_general(
        last, jnp.concatenate([real, imag], 2),
        (((1,), (2,)), ((), ())), precision=lax.Precision.HIGHEST)
    field = field.reshape(parts, NLON // parts, items).astype(jnp.bfloat16)
    field = lax.all_to_all(field, "ord", 0, 0, tiled=True)
    field = field.reshape(cycles, 4, NLON // parts, 3, shells // 4)
    return jnp.transpose(field, (2, 0, 3, 1, 4)).reshape(NLON // parts, cycles * 3 * shells)


def solution(mesh):
    return jax.shard_map(
        body,
        mesh=mesh,
        in_specs=(P("ord", "blk", None), P(None, None, "ord", "blk"), P(), P(), P("blk")),
        out_specs=P("ord", "blk"),
        check_vma=False,
    )
```

time: 117 us -> 113 us (0.966)
  blocking collectives: 17.1 us -> 42.4 us
  waiting for transfers between devices: 35.1 us -> 14.6 us
  starting transfers between devices: 25.5 us -> 10.5 us
  Pallas kernels: 11.7 us -> 14.6 us
  between operations: 2.86 us -> 5.43 us
  local copies, waits for them, and re-layouts: 13.5 us -> 15.3 us
  other arithmetic: 9.52 us -> 8.13 us
    all_to_all x1 -> x2, blocking collectives: 17.1 us -> 42.4 us  [the longest x1 25.2 us: body(): spread = lax.all_to_all(chunk, 'ord', 0, 0, tiled=True).astype(jnp.float32)]
    all_to_all x1 -> x0, starting transfers between devices: 14.8 us -> none  [body(): lax.all_to_all(chunk.reshape(parts, 2, count * items), 'ord', 0, 0, tiled...]
    all_to_all x1 -> x0, waiting for transfers between devices: 10.2 us -> none  [body(): lax.all_to_all(chunk.reshape(parts, 2, count * items), 'ord', 0, 0, tiled...]
    ppermute x3, waiting for transfers between devices: 20.8 us -> 11.7 us  [body(): other = lax.ppermute(part, 'blk', GAUSS_PAIRS)]
    pallas_call x3, Pallas kernels: 11.7 us -> 14.6 us  [partial_sums(): pl.pallas_call(functools.partial(sums_kernel, base=base), out_shape=[jax....]
    dynamic_slice x3 -> x4, local copies, waits for them, and re-layouts: 2.1 us -> 4.84 us  [the longest x3 4.06 us: body(): part = lax.dynamic_slice_in_dim(own, a + next_, b - a, 1)]
    slice x0 -> x3, local copies, waits for them, and re-layouts: none -> 1.92 us  [the longest x2 1.69 us: body(): next_ = jnp.isnan(part[0, 0, 0, 0]).astype(jnp.int32)]
    another operation x10 -> x1, local copies, waits for them, and re-layouts: 1.86 us -> 0.09 us  [body(): angles = jnp.stack([jnp.cos(theta), 1.0 / jnp.sin(theta)], 1)]
  transfers between devices with their start and end apart: 10 -> 10, of which waited for: 6 -> 4; matrix products, arithmetic and copies ran while one was open for 9% -> 14% of each run, Pallas kernels for 9% -> 13%
where the time goes in v3:
time: 113 us; the launch traced here: 112 us
  blocking collectives  42.4 us (38%)
  local copies, waits for them, and re-layouts  15.3 us (14%)
  waiting for transfers between devices  14.6 us (13%)
  Pallas kernels  14.6 us (13%)
  starting transfers between devices  10.5 us (9%)
  other arithmetic  8.13 us (7%)
  between operations  5.43 us (5%)
  matrix products  1.2 us (1%)
    all_to_all x1, blocking collectives, body(): spread = lax.all_to_all(chunk, 'ord', 0, 0, tiled=True).astype(jnp.float32)  25.2 us
    all_to_all x1, blocking collectives, body(): field = lax.all_to_all(field, 'ord', 0, 0, tiled=True)  17.1 us
    pallas_call x3, Pallas kernels, partial_sums(): pl.pallas_call(functools.partial(sums_kernel, base=base), out_shape=[jax....  14.6 us
    ppermute x3, waiting for transfers between devices, body(): other = lax.ppermute(part, 'blk', GAUSS_PAIRS)  11.7 us
    select_n x3, other arithmetic, body(): jnp.where(half + late == 0, panel[a:b, :, START:], panel[a:b, :, :KEPT])  7.03 us
    ppermute x3, starting transfers between devices, body(): arrived.append((other, lax.ppermute(sent, 'blk', PANEL_PAIRS)))  6.33 us
    dynamic_slice x3, local copies, waits for them, and re-layouts, body(): part = lax.dynamic_slice_in_dim(own, a + next_, b - a, 1)  4.06 us
    ppermute x3, starting transfers between devices, body(): added.append(lax.ppermute(send, 'blk', PANEL_PAIRS))  3.09 us
  transfers between devices with their start and end apart: 10, of which 4 were waited for; matrix products, arithmetic and copies ran while one was open for 14% of the time, Pallas kernels for 13%

profile of v3, /device:TPU:1, one launch (start us, length us, event | category | flops | bytes accessed | tf_op | source)
XLA Modules:
  0.0 112.1 jit_solution(13886084285602294220)
XLA Ops:
  0.0 2.7 %slice_select_fusion = bf16[20,16,1472]{2,1,0:T(8,128)(2,1)} fusion(bf16[45,16,2880]{2,1,0:T(8,128)(2,1)} %panel_ref.5, pred[]{:T(512)S(6)} %eq.17), kind=kLoop, calls=%fused_computation.1 | loop fusion | flops 471040 | bytes 2826241 | tf_op jit(solution)/shard_map/jit(_where)/select_n | solution.py:137
  2.7 3.3 %collective-permute-start.2 = (bf16[20,16,1472]{2,1,0:T(8,128)(2,1)}, bf16[20,16,1472]{2,1,0:T(8,128)(2,1)S(1)}, u32[]{:S(2)}, u32[]{:S(2)}) collective-permute-start(bf16[20,16,1472]{2,1,0:T(8,128)(2,1)} %slice_select_fusion), channel_id=1, source_target_pairs={{1,2},{2,1},{3,0},{0,3},{5,6},{6,5},{7,4},{4,7},{9,10},{10,9},{11,... | collective-permute-start | bytes 2826248 | tf_op jit(solution)/shard_map/ppermute | solution.py:138
  6.0 2.2 %dynamic_slice.16 = bf16[2,20,16,720]{3,2,1,0:T(8,128)(2,1)} slice(bf16[2,45,16,720]{3,2,1,0:T(8,128)(2,1)} %bitcast.41), slice={[0:2], [0:20], [0:16], [0:720]} | slice | bytes 1843200 | tf_op jit(solution)/shard_map/dynamic_slice | solution.py:135
  9.1 1.2 %slice.66 = bf16[1,1,1]{2,1,0:T(2,128)(2,1)} slice(bf16[20,16,1472]{2,1,0:T(8,128)(2,1)} %slice_select_fusion), slice={[0:1], [0:1], [0:1]} | slice | bytes 4 | tf_op jit(solution)/shard_map/slice | solution.py:139
  11.6 2.3 %slice_select_fusion.1 = bf16[15,16,1472]{2,1,0:T(8,128)(2,1)} fusion(bf16[45,16,2880]{2,1,0:T(8,128)(2,1)} %panel_ref.5, pred[]{:T(512)S(6)} %eq.18), kind=kLoop, calls=%fused_computation.2 | loop fusion | flops 353280 | bytes 2119681 | tf_op jit(solution)/shard_map/jit(_where)/select_n | solution.py:137
  13.9 1.9 %collective-permute-start.4 = (bf16[15,16,1472]{2,1,0:T(8,128)(2,1)}, bf16[15,16,1472]{2,1,0:T(8,128)(2,1)}, u32[]{:S(2)}, u32[]{:S(2)}) collective-permute-start(bf16[15,16,1472]{2,1,0:T(8,128)(2,1)} %slice_select_fusion.1), channel_id=1, source_target_pairs={{1,2},{2,1},{3,0},{0,3},{5,6},{6,5},{7,4},{4,7},{9,10},{10,9},{11,... | collective-permute-start | bytes 2119688 | tf_op jit(solution)/shard_map/ppermute | solution.py:138
  17.5 1.0 dynamic-slice_bitcast_fusion
  18.8 1.2 %slice.68 = bf16[1,1,1]{2,1,0:T(2,128)(2,1)} slice(bf16[15,16,1472]{2,1,0:T(8,128)(2,1)} %slice_select_fusion.1), slice={[0:1], [0:1], [0:1]} | slice | bytes 4 | tf_op jit(solution)/shard_map/slice | solution.py:139
  21.3 2.0 %slice_select_fusion.2 = bf16[10,16,1472]{2,1,0:T(8,128)(2,1)} fusion(bf16[45,16,2880]{2,1,0:T(8,128)(2,1)} %panel_ref.5, pred[]{:T(512)S(6)} %eq.19), kind=kLoop, calls=%fused_computation.7 | loop fusion | flops 235520 | bytes 1413121 | tf_op jit(solution)/shard_map/jit(_where)/select_n | solution.py:137
  24.4 1.2 %slice.67 = bf16[1,1,1,1]{3,2,1,0:T(2,128)(2,1)} slice(bf16[2,15,16,720]{3,2,1,0:T(8,128)(2,1)} %dynamic-slice_bitcast_fusion), slice={[0:1], [0:1], [0:1], [0:1]} | slice | bytes 4 | tf_op jit(solution)/shard_map/slice | solution.py:140
  27.0 0.8 dynamic-slice_bitcast_fusion.1
  28.9 1.1 %collective-permute-start.6 = (bf16[10,16,1472]{2,1,0:T(8,128)(2,1)}, bf16[10,16,1472]{2,1,0:T(8,128)(2,1)}, u32[]{:S(2)}, u32[]{:S(2)}) collective-permute-start(bf16[10,16,1472]{2,1,0:T(8,128)(2,1)} %slice_select_fusion.2), channel_id=1, source_target_pairs={{1,2},{2,1},{3,0},{0,3},{5,6},{6,5},{7,4},{4,7},{9,10},{10,9},{11,... | collective-permute-start | bytes 1413128 | tf_op jit(solution)/shard_map/ppermute | solution.py:138
  31.1 2.2 %copy-done = bf16[45,16,2880]{2,1,0:T(8,128)(2,1)S(1)} copy-done((bf16[45,16,2880]{2,1,0:T(8,128)(2,1)S(1)}, bf16[45,16,2880]{2,1,0:T(8,128)(2,1)}, u32[]{:S(2)}) %copy-start) | copy-done | bytes 4147224
  33.3 6.0 %partial_sums.3 = (f32[20,16,96]{2,1,0:T(8,128)S(1)}, bf16[20,16,96]{2,1,0:T(8,128)(2,1)S(1)}) custom-call(s32[2]{0:T(128)S(1)} %pad_add_fusion.where_ref, s32[45]{0:T(128)S(1)} %dynamic_slice.12.order_ref, f32[16,1]{1,0:T(8,128)S(1)} %copy.30.height_ref, f32[32,2]{1,0:T(8,128)S(1)} %copy.31.angle_ref, bf16[2,45,16,720]{3,2,1,0:T(8,128)(2,1)S(1)} %bitcast.43, ...), custom_call_target="tpu_custom_call" | custom-call | flops 188743680 | bytes 4000000 | tf_op jit(solution)/shard_map/partial_sums/pallas_call | solution.py:90
  39.3 1.8 %collective-permute-start.7 = (bf16[20,16,96]{2,1,0:T(8,128)(2,1)S(1)}, bf16[20,16,96]{2,1,0:T(8,128)(2,1)S(1)}, u32[]{:S(2)}, u32[]{:S(2)}) collective-permute-start(bf16[20,16,96]{2,1,0:T(8,128)(2,1)S(1)} %get-tuple-element.18), channel_id=1, source_target_pairs={{1,2},{2,1},{3,0},{0,3},{5,6},{6,5},{7,4},{4,7},{9,10},{10,9},{11,... | collective-permute-start | bytes 184328 | tf_op jit(solution)/shard_map/ppermute | solution.py:150
  41.2 5.5 %collective-permute-done.3.other_ref = bf16[2,15,16,720]{3,2,1,0:T(8,128)(2,1)} collective-permute-done((bf16[2,15,16,720]{3,2,1,0:T(8,128)(2,1)}, bf16[2,15,16,720]{3,2,1,0:T(8,128)(2,1)}, u32[]{:S(2)}, u32[]{:S(2)}) %collective-permute-start.3) | collective-permute-done | bytes 691232 | tf_op jit(solution)/shard_map/ppermute | solution.py:136
  46.7 4.9 %partial_sums.4 = (f32[15,16,96]{2,1,0:T(8,128)S(1)}, bf16[15,16,96]{2,1,0:T(8,128)(2,1)S(1)}) custom-call(s32[2]{0:T(128)S(1)} %pad_add_fusion.where_ref, s32[45]{0:T(128)S(1)} %dynamic_slice.12.order_ref, f32[16,1]{1,0:T(8,128)S(1)} %copy.30.height_ref, f32[32,2]{1,0:T(8,128)S(1)} %copy.31.angle_ref, bf16[2,45,16,720]{3,2,1,0:T(8,128)(2,1)S(1)} %bitcast.45, ...), custom_call_target="tpu_custom_call" | custom-call | flops 141557760 | bytes 3000000 | tf_op jit(solution)/shard_map/partial_sums/pallas_call | solution.py:90
  51.7 5.5 %collective-permute-done.5.other_ref = bf16[2,10,16,720]{3,2,1,0:T(8,128)(2,1)} collective-permute-done((bf16[2,10,16,720]{3,2,1,0:T(8,128)(2,1)}, bf16[2,10,16,720]{3,2,1,0:T(8,128)(2,1)}, u32[]{:S(2)}, u32[]{:S(2)}) %collective-permute-start.5) | collective-permute-done | bytes 460832 | tf_op jit(solution)/shard_map/ppermute | solution.py:136
  57.2 3.7 %partial_sums.5 = (f32[10,16,96]{2,1,0:T(8,128)S(1)}, bf16[10,16,96]{2,1,0:T(8,128)(2,1)S(1)}) custom-call(s32[2]{0:T(128)S(1)} %pad_add_fusion.where_ref, s32[45]{0:T(128)S(1)} %dynamic_slice.12.order_ref, f32[16,1]{1,0:T(8,128)S(1)} %copy.30.height_ref, f32[32,2]{1,0:T(8,128)S(1)} %copy.31.angle_ref, bf16[2,45,16,720]{3,2,1,0:T(8,128)(2,1)S(1)} %bitcast.46, ...), custom_call_target="tpu_custom_call" | custom-call | flops 94371840 | bytes 2000000 | tf_op jit(solution)/shard_map/partial_sums/pallas_call | solution.py:90
  60.9 1.2 %collective-permute-start.9 = (bf16[10,16,96]{2,1,0:T(8,128)(2,1)S(1)}, bf16[10,16,96]{2,1,0:T(8,128)(2,1)S(1)}, u32[]{:S(2)}, u32[]{:S(2)}) collective-permute-start(bf16[10,16,96]{2,1,0:T(8,128)(2,1)S(1)} %get-tuple-element.21), channel_id=1, source_target_pairs={{1,2},{2,1},{3,0},{0,3},{5,6},{6,5},{7,4},{4,7},{9,10},{10,9},{11,... | collective-permute-start | bytes 92168 | tf_op jit(solution)/shard_map/ppermute | solution.py:150
  62.2 2.9 %collective-permute-done.9 = bf16[10,16,96]{2,1,0:T(8,128)(2,1)S(1)} collective-permute-done((bf16[10,16,96]{2,1,0:T(8,128)(2,1)S(1)}, bf16[10,16,96]{2,1,0:T(8,128)(2,1)S(1)}, u32[]{:S(2)}, u32[]{:S(2)}) %collective-permute-start.9) | collective-permute-done | bytes 30752 | tf_op jit(solution)/shard_map/ppermute | solution.py:150
  66.1 25.2 %all_to_all.10 = bf16[64,2,540]{2,1,0:T(2,128)(2,1)S(1)} all-to-all(bf16[64,2,540]{2,1,0:T(2,128)(2,1)S(1)} %copy.38), channel_id=1, replica_groups=mesh['ord'=64,'blk'=4] {'ord'}, dimensions={0} | all-to-all | bytes 276480 | tf_op jit(solution)/shard_map/all_to_all | solution.py:170
  93.9 17.1 %all_to_all.11 = bf16[64,90,12]{1,2,0:T(8,128)(2,1)S(1)} all-to-all(bf16[64,90,12]{1,2,0:T(8,128)(2,1)S(1)} %copy.40), channel_id=1, replica_groups=mesh['ord'=64,'blk'=4] {'ord'}, dimensions={0} | all-to-all | bytes 276480 | tf_op jit(solution)/shard_map/all_to_all | solution.py:180
  111.3 0.8 copy.43
  (52 shorter events, 8.9 us)
Async XLA Ops:
  0.0 15.7 %copy-start.1 = (bf16[2,16,45,720]{3,1,2,0:T(8,128)(2,1)S(1)}, bf16[2,16,45,720]{3,1,2,0:T(8,128)(2,1)}, u32[]{:S(2)}) copy-start(bf16[2,16,45,720]{3,1,2,0:T(8,128)(2,1)} %param.6) | copy-start | bytes 6220804
  0.0 8.3 %copy-start.3 = (s32[16]{0:T(128)S(1)}, s32[16]{0:T(128)}, u32[]{:S(2)}) copy-start(s32[16]{0:T(128)} %param.9) | copy-start | bytes 196
  2.7 28.4 %collective-permute-start.2 = (bf16[20,16,1472]{2,1,0:T(8,128)(2,1)}, bf16[20,16,1472]{2,1,0:T(8,128)(2,1)S(1)}, u32[]{:S(2)}, u32[]{:S(2)}) collective-permute-start(bf16[20,16,1472]{2,1,0:T(8,128)(2,1)} %slice_select_fusion), channel_id=1, source_target_pairs={{1,2},{2,1},{3,0},{0,3},{5,6},{6,5},{7,4},{4,7},{9,10},{10,9},{11,... | collective-permute-start | bytes 2826248 | tf_op jit(solution)/shard_map/ppermute | solution.py:138
  6.0 22.8 %copy-start.2 = (f32[16]{0:T(128)S(1)}, f32[16]{0:T(128)}, u32[]{:S(2)}) copy-start(f32[16]{0:T(128)} %param.7) | copy-start | bytes 196
  8.3 22.6 %collective-permute-start.1 = (bf16[2,20,16,720]{3,2,1,0:T(8,128)(2,1)}, bf16[2,20,16,720]{3,2,1,0:T(8,128)(2,1)}, u32[]{:S(2)}, u32[]{:S(2)}) collective-permute-start(bf16[2,20,16,720]{3,2,1,0:T(8,128)(2,1)} %dynamic_slice.16), channel_id=1, source_target_pairs={{0,1},{1,0},{2,3},{3,2},{4,5},{5,4},{6,7},{7,6},{8,9},{9,8},{10,11... | collective-permute-start | bytes 2764808 | tf_op jit(solution)/shard_map/ppermute | solution.py:136
  8.3 20.7 %collective-permute-start = (s32[16]{0:T(128)S(1)}, s32[16]{0:T(128)S(1)}, u32[]{:S(2)}, u32[]{:S(2)}) collective-permute-start(s32[16]{0:T(128)S(1)} %copy-done.3), channel_id=1, source_target_pairs={{1,2},{2,1},{3,0},{0,3},{5,6},{6,5},{7,4},{4,7},{9,10},{10,9},{11,... | collective-permute-start | bytes 200 | tf_op jit(solution)/shard_map/ppermute | solution.py:141
  13.9 32.8 %collective-permute-start.4 = (bf16[15,16,1472]{2,1,0:T(8,128)(2,1)}, bf16[15,16,1472]{2,1,0:T(8,128)(2,1)}, u32[]{:S(2)}, u32[]{:S(2)}) collective-permute-start(bf16[15,16,1472]{2,1,0:T(8,128)(2,1)} %slice_select_fusion.1), channel_id=1, source_target_pairs={{1,2},{2,1},{3,0},{0,3},{5,6},{6,5},{7,4},{4,7},{9,10},{10,9},{11,... | collective-permute-start | bytes 2119688 | tf_op jit(solution)/shard_map/ppermute | solution.py:138
  18.5 28.2 %collective-permute-start.3 = (bf16[2,15,16,720]{3,2,1,0:T(8,128)(2,1)}, bf16[2,15,16,720]{3,2,1,0:T(8,128)(2,1)}, u32[]{:S(2)}, u32[]{:S(2)}) collective-permute-start(bf16[2,15,16,720]{3,2,1,0:T(8,128)(2,1)} %dynamic-slice_bitcast_fusion), channel_id=1, source_target_pairs={{0,1},{1,0},{2,3},{3,2},{4,5},{5,4},{6,7},{7,6},{8,9},{9,8},{10,11... | collective-permute-start | bytes 2073608 | tf_op jit(solution)/shard_map/ppermute | solution.py:136
  28.9 28.3 %collective-permute-start.6 = (bf16[10,16,1472]{2,1,0:T(8,128)(2,1)}, bf16[10,16,1472]{2,1,0:T(8,128)(2,1)}, u32[]{:S(2)}, u32[]{:S(2)}) collective-permute-start(bf16[10,16,1472]{2,1,0:T(8,128)(2,1)} %slice_select_fusion.2), channel_id=1, source_target_pairs={{1,2},{2,1},{3,0},{0,3},{5,6},{6,5},{7,4},{4,7},{9,10},{10,9},{11,... | collective-permute-start | bytes 1413128 | tf_op jit(solution)/shard_map/ppermute | solution.py:138
  30.9 26.3 %collective-permute-start.5 = (bf16[2,10,16,720]{3,2,1,0:T(8,128)(2,1)}, bf16[2,10,16,720]{3,2,1,0:T(8,128)(2,1)}, u32[]{:S(2)}, u32[]{:S(2)}) collective-permute-start(bf16[2,10,16,720]{3,2,1,0:T(8,128)(2,1)} %dynamic-slice_bitcast_fusion.1), channel_id=1, source_target_pairs={{0,1},{1,0},{2,3},{3,2},{4,5},{5,4},{6,7},{7,6},{8,9},{9,8},{10,11... | collective-permute-start | bytes 1382408 | tf_op jit(solution)/shard_map/ppermute | solution.py:136
  31.1 2.2 %copy-start = (bf16[45,16,2880]{2,1,0:T(8,128)(2,1)S(1)}, bf16[45,16,2880]{2,1,0:T(8,128)(2,1)}, u32[]{:S(2)}) copy-start(bf16[45,16,2880]{2,1,0:T(8,128)(2,1)} %panel_ref.5) | copy-start | bytes 12441604
  39.3 17.9 %collective-permute-start.7 = (bf16[20,16,96]{2,1,0:T(8,128)(2,1)S(1)}, bf16[20,16,96]{2,1,0:T(8,128)(2,1)S(1)}, u32[]{:S(2)}, u32[]{:S(2)}) collective-permute-start(bf16[20,16,96]{2,1,0:T(8,128)(2,1)S(1)} %get-tuple-element.18), channel_id=1, source_target_pairs={{1,2},{2,1},{3,0},{0,3},{5,6},{6,5},{7,4},{4,7},{9,10},{10,9},{11,... | collective-permute-start | bytes 184328 | tf_op jit(solution)/shard_map/ppermute | solution.py:150
  51.6 10.6 %collective-permute-start.8 = (bf16[15,16,96]{2,1,0:T(8,128)(2,1)S(1)}, bf16[15,16,96]{2,1,0:T(8,128)(2,1)S(1)}, u32[]{:S(2)}, u32[]{:S(2)}) collective-permute-start(bf16[15,16,96]{2,1,0:T(8,128)(2,1)S(1)} %get-tuple-element.20), channel_id=1, source_target_pairs={{1,2},{2,1},{3,0},{0,3},{5,6},{6,5},{7,4},{4,7},{9,10},{10,9},{11,... | collective-permute-start | bytes 138248 | tf_op jit(solution)/shard_map/ppermute | solution.py:150
  60.9 4.2 %collective-permute-start.9 = (bf16[10,16,96]{2,1,0:T(8,128)(2,1)S(1)}, bf16[10,16,96]{2,1,0:T(8,128)(2,1)S(1)}, u32[]{:S(2)}, u32[]{:S(2)}) collective-permute-start(bf16[10,16,96]{2,1,0:T(8,128)(2,1)S(1)} %get-tuple-element.21), channel_id=1, source_target_pairs={{1,2},{2,1},{3,0},{0,3},{5,6},{6,5},{7,4},{4,7},{9,10},{10,9},{11,... | collective-permute-start | bytes 92168 | tf_op jit(solution)/shard_map/ppermute | solution.py:150

commit v4 on v3

--- a/solution.py
+++ b/solution.py
@@ -16,7 +16,7 @@
 KEPT = 1472
 NLON = 5760
 GROUP = 5
-CHUNKS = (0, 20, 35, 45)
+CHUNKS = (0, 10, 20, 30, 40, 45)
 GAUSS_PAIRS = [(0, 1), (1, 0), (2, 3), (3, 2)]
 PANEL_PAIRS = [(1, 2), (2, 1), (3, 0), (0, 3)]
 
@@ -130,6 +130,7 @@
     where = jnp.stack([half, spot % 2]).astype(jnp.int32)
     spans = list(zip(CHUNKS[:-1], CHUNKS[1:]))
     arrived = []
+    facing = lax.ppermute(cycle_map, "blk", PANEL_PAIRS)
     late, next_ = 0, 0
     for a, b in spans:
         part = lax.dynamic_slice_in_dim(own, a + next_, b - a, 1)
@@ -138,7 +139,6 @@
         arrived.append((other, lax.ppermute(sent, "blk", PANEL_PAIRS)))
         late = jnp.isnan(sent[0, 0, 0]).astype(jnp.int32)
         next_ = jnp.isnan(part[0, 0, 0, 0]).astype(jnp.int32)
-    facing = lax.ppermute(cycle_map, "blk", PANEL_PAIRS)
     theta = math.pi * (jnp.concatenate([cycle_map, facing]).astype(jnp.float32) + 0.5) / ORDERS
     angles = jnp.stack([jnp.cos(theta), 1.0 / jnp.sin(theta)], 1)
     kept, added = [], []

time: 113 us -> 136 us (1.20)
  starting transfers between devices: 10.5 us -> 18.6 us
  local copies, waits for them, and re-layouts: 15.3 us -> 22.2 us
  between operations: 5.43 us -> 11.1 us
  waiting for transfers between devices: 14.6 us -> 8.97 us
  other arithmetic: 8.13 us -> 12.3 us
  blocking collectives: 42.4 us -> 44.6 us
  Pallas kernels: 14.6 us -> 16.1 us
    ppermute x3 -> x5, waiting for transfers between devices: 11.7 us -> 0.01 us  [body(): other = lax.ppermute(part, 'blk', GAUSS_PAIRS)]
    ppermute x3 -> x5, waiting for transfers between devices: 2.86 us -> 8.95 us  [body(): added.append(lax.ppermute(send, 'blk', PANEL_PAIRS))]
    ppermute x3 -> x5, starting transfers between devices: 3.09 us -> 8.6 us  [body(): added.append(lax.ppermute(send, 'blk', PANEL_PAIRS))]
    slice x2 -> x4, local copies, waits for them, and re-layouts: 1.69 us -> 4.95 us  [body(): next_ = jnp.isnan(part[0, 0, 0, 0]).astype(jnp.int32)]
    select_n x3 -> x5, other arithmetic: 7.03 us -> 9.99 us  [body(): jnp.where(half + late == 0, panel[a:b, :, START:], panel[a:b, :, :KEPT])]
    slice x2 -> x4, local copies, waits for them, and re-layouts: 2.35 us -> 4.88 us  [body(): late = jnp.isnan(sent[0, 0, 0]).astype(jnp.int32)]
    all_to_all x1, blocking collectives: 25.2 us -> 27.4 us  [body(): spread = lax.all_to_all(chunk, 'ord', 0, 0, tiled=True).astype(jnp.float32)]
    pallas_call x3 -> x5, Pallas kernels: 14.6 us -> 16.1 us  [partial_sums(): pl.pallas_call(functools.partial(sums_kernel, base=base), out_shape=[jax....]
  transfers between devices with their start and end apart: 10 -> 16, of which waited for: 4 -> 2; matrix products, arithmetic and copies ran while one was open for 14% -> 20% of each run, Pallas kernels for 13% -> 12%
where the time goes in v4:
time: 136 us; the launch traced here: 135 us
  blocking collectives  44.6 us (33%)
  local copies, waits for them, and re-layouts  22.2 us (16%)
  starting transfers between devices  18.6 us (14%)
  Pallas kernels  16.1 us (12%)
  other arithmetic  12.3 us (9%)
  between operations  11.1 us (8%)
  waiting for transfers between devices  8.97 us (7%)
    all_to_all x1, blocking collectives, body(): spread = lax.all_to_all(chunk, 'ord', 0, 0, tiled=True).astype(jnp.float32)  27.4 us
    all_to_all x1, blocking collectives, body(): field = lax.all_to_all(field, 'ord', 0, 0, tiled=True)  17.1 us
    pallas_call x5, Pallas kernels, partial_sums(): pl.pallas_call(functools.partial(sums_kernel, base=base), out_shape=[jax....  16.1 us
    select_n x5, other arithmetic, body(): jnp.where(half + late == 0, panel[a:b, :, START:], panel[a:b, :, :KEPT])  9.99 us
    ppermute x5, waiting for transfers between devices, body(): added.append(lax.ppermute(send, 'blk', PANEL_PAIRS))  8.95 us
    ppermute x5, starting transfers between devices, body(): added.append(lax.ppermute(send, 'blk', PANEL_PAIRS))  8.6 us
    ppermute x5, starting transfers between devices, body(): arrived.append((other, lax.ppermute(sent, 'blk', PANEL_PAIRS)))  7.71 us
    dynamic_slice x5, local copies, waits for them, and re-layouts, body(): part = lax.dynamic_slice_in_dim(own, a + next_, b - a, 1)  5.06 us
  transfers between devices with their start and end apart: 16, of which 2 were waited for; matrix products, arithmetic and copies ran while one was open for 20% of the time, Pallas kernels for 12%

profile of v4, /device:TPU:1, one launch (start us, length us, event | category | flops | bytes accessed | tf_op | source)
XLA Modules:
  0.0 135.0 jit_solution(527296635939238040)
XLA Ops:
  0.0 2.2 %slice_select_fusion.3 = bf16[10,16,1472]{2,1,0:T(8,128)(2,1)} fusion(bf16[45,16,2880]{2,1,0:T(8,128)(2,1)} %panel_ref.9, pred[]{:T(512)S(6)} %eq.23), kind=kLoop, calls=%fused_computation.10 | loop fusion | flops 235520 | bytes 1413121 | tf_op jit(solution)/shard_map/jit(_where)/select_n | solution.py:138
  2.2 3.3 %collective-permute-start.2 = (bf16[10,16,1472]{2,1,0:T(8,128)(2,1)}, bf16[10,16,1472]{2,1,0:T(8,128)(2,1)S(1)}, u32[]{:S(2)}, u32[]{:S(2)}) collective-permute-start(bf16[10,16,1472]{2,1,0:T(8,128)(2,1)} %slice_select_fusion.3), channel_id=1, source_target_pairs={{1,2},{2,1},{3,0},{0,3},{5,6},{6,5},{7,4},{4,7},{9,10},{10,9},{11,... | collective-permute-start | bytes 1413128 | tf_op jit(solution)/shard_map/ppermute | solution.py:139
  5.5 1.8 %dynamic_slice.24 = bf16[2,10,16,720]{3,2,1,0:T(8,128)(2,1)} slice(bf16[2,45,16,720]{3,2,1,0:T(8,128)(2,1)} %bitcast.51), slice={[0:2], [0:10], [0:16], [0:720]} | slice | bytes 921600 | tf_op jit(solution)/shard_map/dynamic_slice | solution.py:136
  10.6 2.0 %slice_select_fusion.2 = bf16[10,16,1472]{2,1,0:T(8,128)(2,1)} fusion(bf16[45,16,2880]{2,1,0:T(8,128)(2,1)} %panel_ref.9, pred[]{:T(512)S(6)} %eq.24), kind=kLoop, calls=%fused_computation.8 | loop fusion | flops 235520 | bytes 1413121 | tf_op jit(solution)/shard_map/jit(_where)/select_n | solution.py:138
  12.7 1.9 %collective-permute-start.4 = (bf16[10,16,1472]{2,1,0:T(8,128)(2,1)}, bf16[10,16,1472]{2,1,0:T(8,128)(2,1)}, u32[]{:S(2)}, u32[]{:S(2)}) collective-permute-start(bf16[10,16,1472]{2,1,0:T(8,128)(2,1)} %slice_select_fusion.2), channel_id=1, source_target_pairs={{1,2},{2,1},{3,0},{0,3},{5,6},{6,5},{7,4},{4,7},{9,10},{10,9},{11,... | collective-permute-start | bytes 1413128 | tf_op jit(solution)/shard_map/ppermute | solution.py:139
  22.7 2.0 %slice_select_fusion.1 = bf16[10,16,1472]{2,1,0:T(8,128)(2,1)} fusion(bf16[45,16,2880]{2,1,0:T(8,128)(2,1)} %panel_ref.9, pred[]{:T(512)S(6)} %eq.25), kind=kLoop, calls=%fused_computation.6 | loop fusion | flops 235520 | bytes 1413121 | tf_op jit(solution)/shard_map/jit(_where)/select_n | solution.py:138
  26.8 1.3 slice.102
  29.5 2.0 %slice_select_fusion = bf16[10,16,1472]{2,1,0:T(8,128)(2,1)} fusion(bf16[45,16,2880]{2,1,0:T(8,128)(2,1)} %panel_ref.9, pred[]{:T(512)S(6)} %eq.26), kind=kLoop, calls=%fused_computation.4 | loop fusion | flops 235520 | bytes 1413121 | tf_op jit(solution)/shard_map/jit(_where)/select_n | solution.py:138
  34.9 1.2 slice.104
  37.5 1.8 %slice_select_fusion.4 = bf16[5,16,1472]{2,1,0:T(8,128)(2,1)} fusion(bf16[45,16,2880]{2,1,0:T(8,128)(2,1)} %panel_ref.9, pred[]{:T(512)S(6)} %eq.27), kind=kLoop, calls=%fused_computation.18 | loop fusion | flops 117760 | bytes 706561 | tf_op jit(solution)/shard_map/jit(_where)/select_n | solution.py:138
  40.5 1.3 slice.103
  47.2 1.9 %collective-permute-start.9 = (bf16[10,16,1472]{2,1,0:T(8,128)(2,1)}, bf16[10,16,1472]{2,1,0:T(8,128)(2,1)}, u32[]{:S(2)}, u32[]{:S(2)}) collective-permute-start(bf16[10,16,1472]{2,1,0:T(8,128)(2,1)} %slice_select_fusion), channel_id=1, source_target_pairs={{1,2},{2,1},{3,0},{0,3},{5,6},{6,5},{7,4},{4,7},{9,10},{10,9},{11,... | collective-permute-start | bytes 1413128 | tf_op jit(solution)/shard_map/ppermute | solution.py:139
  49.5 2.2 %copy-done = bf16[45,16,2880]{2,1,0:T(8,128)(2,1)S(1)} copy-done((bf16[45,16,2880]{2,1,0:T(8,128)(2,1)S(1)}, bf16[45,16,2880]{2,1,0:T(8,128)(2,1)}, u32[]{:S(2)}) %copy-start) | copy-done | bytes 4147224
  51.7 3.1 %partial_sums.5 = (f32[10,16,96]{2,1,0:T(8,128)S(1)}, bf16[10,16,96]{2,1,0:T(8,128)(2,1)S(1)}) custom-call(s32[2]{0:T(128)S(1)} %pad_add_fusion.where_ref, s32[45]{0:T(128)S(1)} %dynamic_slice.18.order_ref, f32[16,1]{1,0:T(8,128)S(1)} %copy.36.height_ref, f32[32,2]{1,0:T(8,128)S(1)} %copy.37.angle_ref, bf16[2,45,16,720]{3,2,1,0:T(8,128)(2,1)S(1)} %bitcast.53, ...), custom_call_target="tpu_custom_call" | custom-call | flops 94371840 | bytes 2000000 | tf_op jit(solution)/shard_map/partial_sums/pallas_call | solution.py:90
  54.9 3.8 %partial_sums.6 = (f32[10,16,96]{2,1,0:T(8,128)S(1)}, bf16[10,16,96]{2,1,0:T(8,128)(2,1)S(1)}) custom-call(s32[2]{0:T(128)S(1)} %pad_add_fusion.where_ref, s32[45]{0:T(128)S(1)} %dynamic_slice.18.order_ref, f32[16,1]{1,0:T(8,128)S(1)} %copy.36.height_ref, f32[32,2]{1,0:T(8,128)S(1)} %copy.37.angle_ref, bf16[2,45,16,720]{3,2,1,0:T(8,128)(2,1)S(1)} %bitcast.55, ...), custom_call_target="tpu_custom_call" | custom-call | flops 94371840 | bytes 2000000 | tf_op jit(solution)/shard_map/partial_sums/pallas_call | solution.py:90
  59.7 1.9 %collective-permute-start.7 = (bf16[10,16,96]{2,1,0:T(8,128)(2,1)S(1)}, bf16[10,16,96]{2,1,0:T(8,128)(2,1)S(1)}, u32[]{:S(2)}, u32[]{:S(2)}) collective-permute-start(bf16[10,16,96]{2,1,0:T(8,128)(2,1)S(1)} %get-tuple-element.22), channel_id=1, source_target_pairs={{1,2},{2,1},{3,0},{0,3},{5,6},{6,5},{7,4},{4,7},{9,10},{10,9},{11,... | collective-permute-start | bytes 92168 | tf_op jit(solution)/shard_map/ppermute | solution.py:150
  61.7 7.7 %collective-permute-done.7.rest_1_ = bf16[10,16,96]{2,1,0:T(8,128)(2,1)S(1)} collective-permute-done((bf16[10,16,96]{2,1,0:T(8,128)(2,1)S(1)}, bf16[10,16,96]{2,1,0:T(8,128)(2,1)S(1)}, u32[]{:S(2)}, u32[]{:S(2)}) %collective-permute-start.7) | collective-permute-done | bytes 30752 | tf_op jit(solution)/shard_map/ppermute | solution.py:150
  69.5 3.7 %partial_sums.7 = (f32[10,16,96]{2,1,0:T(8,128)S(1)}, bf16[10,16,96]{2,1,0:T(8,128)(2,1)S(1)}) custom-call(s32[2]{0:T(128)S(1)} %pad_add_fusion.where_ref, s32[45]{0:T(128)S(1)} %dynamic_slice.18.order_ref, f32[16,1]{1,0:T(8,128)S(1)} %copy.36.height_ref, f32[32,2]{1,0:T(8,128)S(1)} %copy.37.angle_ref, bf16[2,45,16,720]{3,2,1,0:T(8,128)(2,1)S(1)} %bitcast.56, ...), custom_call_target="tpu_custom_call" | custom-call | flops 94371840 | bytes 2000000 | tf_op jit(solution)/shard_map/partial_sums/pallas_call | solution.py:90
  73.1 2.8 %collective-permute-start.13 = (bf16[10,16,96]{2,1,0:T(8,128)(2,1)S(1)}, bf16[10,16,96]{2,1,0:T(8,128)(2,1)S(1)}, u32[]{:S(2)}, u32[]{:S(2)}) collective-permute-start(bf16[10,16,96]{2,1,0:T(8,128)(2,1)S(1)} %get-tuple-element.26), channel_id=1, source_target_pairs={{1,2},{2,1},{3,0},{0,3},{5,6},{6,5},{7,4},{4,7},{9,10},{10,9},{11,... | collective-permute-start | bytes 92168 | tf_op jit(solution)/shard_map/ppermute | solution.py:150
  76.0 3.7 %partial_sums.8 = (f32[10,16,96]{2,1,0:T(8,128)S(1)}, bf16[10,16,96]{2,1,0:T(8,128)(2,1)S(1)}) custom-call(s32[2]{0:T(128)S(1)} %pad_add_fusion.where_ref, s32[45]{0:T(128)S(1)} %dynamic_slice.18.order_ref, f32[16,1]{1,0:T(8,128)S(1)} %copy.36.height_ref, f32[32,2]{1,0:T(8,128)S(1)} %copy.37.angle_ref, bf16[2,45,16,720]{3,2,1,0:T(8,128)(2,1)S(1)} %bitcast.57, ...), custom_call_target="tpu_custom_call" | custom-call | flops 94371840 | bytes 2000000 | tf_op jit(solution)/shard_map/partial_sums/pallas_call | solution.py:90
  80.0 1.8 %partial_sums.9 = (f32[5,16,96]{2,1,0:T(8,128)S(1)}, bf16[5,16,96]{2,1,0:T(8,128)(2,1)S(1)}) custom-call(s32[2]{0:T(128)S(1)} %pad_add_fusion.where_ref, s32[45]{0:T(128)S(1)} %dynamic_slice.18.order_ref, f32[16,1]{1,0:T(8,128)S(1)} %copy.36.height_ref, f32[32,2]{1,0:T(8,128)S(1)} %copy.37.angle_ref, bf16[2,45,16,720]{3,2,1,0:T(8,128)(2,1)S(1)} %bitcast.58, ...), custom_call_target="tpu_custom_call" | custom-call | flops 47185920 | bytes 1000000 | tf_op jit(solution)/shard_map/partial_sums/pallas_call | solution.py:90
  81.8 2.7 %collective-permute-start.15 = (bf16[5,16,96]{2,1,0:T(8,128)(2,1)S(1)}, bf16[5,16,96]{2,1,0:T(8,128)(2,1)S(1)}, u32[]{:S(2)}, u32[]{:S(2)}) collective-permute-start(bf16[5,16,96]{2,1,0:T(8,128)(2,1)S(1)} %get-tuple-element.29), channel_id=1, source_target_pairs={{1,2},{2,1},{3,0},{0,3},{5,6},{6,5},{7,4},{4,7},{9,10},{10,9},{11,... | collective-permute-start | bytes 46088 | tf_op jit(solution)/shard_map/ppermute | solution.py:150
  86.8 27.4 %all_to_all.10 = bf16[64,2,540]{2,1,0:T(2,128)(2,1)S(1)} all-to-all(bf16[64,2,540]{2,1,0:T(2,128)(2,1)S(1)} %copy.48), channel_id=1, replica_groups=mesh['ord'=64,'blk'=4] {'ord'}, dimensions={0} | all-to-all | bytes 276480 | tf_op jit(solution)/shard_map/all_to_all | solution.py:170
  116.8 17.1 %all_to_all.11 = bf16[64,90,12]{1,2,0:T(8,128)(2,1)S(1)} all-to-all(bf16[64,90,12]{1,2,0:T(8,128)(2,1)S(1)} %copy.50), channel_id=1, replica_groups=mesh['ord'=64,'blk'=4] {'ord'}, dimensions={0} | all-to-all | bytes 276480 | tf_op jit(solution)/shard_map/all_to_all | solution.py:180
  (92 shorter events, 23.2 us)
Async XLA Ops:
  0.0 17.0 %copy-start.1 = (bf16[2,16,45,720]{3,1,2,0:T(8,128)(2,1)S(1)}, bf16[2,16,45,720]{3,1,2,0:T(8,128)(2,1)}, u32[]{:S(2)}) copy-start(bf16[2,16,45,720]{3,1,2,0:T(8,128)(2,1)} %param.6) | copy-start | bytes 6220804
  2.2 47.0 %collective-permute-start.2 = (bf16[10,16,1472]{2,1,0:T(8,128)(2,1)}, bf16[10,16,1472]{2,1,0:T(8,128)(2,1)S(1)}, u32[]{:S(2)}, u32[]{:S(2)}) collective-permute-start(bf16[10,16,1472]{2,1,0:T(8,128)(2,1)} %slice_select_fusion.3), channel_id=1, source_target_pairs={{1,2},{2,1},{3,0},{0,3},{5,6},{6,5},{7,4},{4,7},{9,10},{10,9},{11,... | collective-permute-start | bytes 1413128 | tf_op jit(solution)/shard_map/ppermute | solution.py:139
  7.3 39.0 %collective-permute-start.1 = (bf16[2,10,16,720]{3,2,1,0:T(8,128)(2,1)}, bf16[2,10,16,720]{3,2,1,0:T(8,128)(2,1)S(1)}, u32[]{:S(2)}, u32[]{:S(2)}) collective-permute-start(bf16[2,10,16,720]{3,2,1,0:T(8,128)(2,1)} %dynamic_slice.24), channel_id=1, source_target_pairs={{0,1},{1,0},{2,3},{3,2},{4,5},{5,4},{6,7},{7,6},{8,9},{9,8},{10,11... | collective-permute-start | bytes 1382408 | tf_op jit(solution)/shard_map/ppermute | solution.py:137
  7.3 37.7 %collective-permute-start = (s32[16]{0:T(128)}, s32[16]{0:T(128)}, u32[]{:S(2)}, u32[]{:S(2)}) collective-permute-start(s32[16]{0:T(128)} %param.9), channel_id=1, source_target_pairs={{1,2},{2,1},{3,0},{0,3},{5,6},{6,5},{7,4},{4,7},{9,10},{10,9},{11,... | collective-permute-start | bytes 200 | tf_op jit(solution)/shard_map/ppermute | solution.py:133
  12.7 32.2 %copy-start.6 = (f32[16]{0:T(128)S(1)}, f32[16]{0:T(128)}, u32[]{:S(2)}) copy-start(f32[16]{0:T(128)} %param.7) | copy-start | bytes 196
  12.7 33.0 %copy-start.7 = (s32[16]{0:T(128)S(1)}, s32[16]{0:T(128)}, u32[]{:S(2)}) copy-start(s32[16]{0:T(128)} %param.9) | copy-start | bytes 196
  12.7 42.2 %collective-permute-start.4 = (bf16[10,16,1472]{2,1,0:T(8,128)(2,1)}, bf16[10,16,1472]{2,1,0:T(8,128)(2,1)}, u32[]{:S(2)}, u32[]{:S(2)}) collective-permute-start(bf16[10,16,1472]{2,1,0:T(8,128)(2,1)} %slice_select_fusion.2), channel_id=1, source_target_pairs={{1,2},{2,1},{3,0},{0,3},{5,6},{6,5},{7,4},{4,7},{9,10},{10,9},{11,... | collective-permute-start | bytes 1413128 | tf_op jit(solution)/shard_map/ppermute | solution.py:139
  17.9 29.4 %collective-permute-start.3 = (bf16[2,10,16,720]{3,2,1,0:T(8,128)(2,1)}, bf16[2,10,16,720]{3,2,1,0:T(8,128)(2,1)}, u32[]{:S(2)}, u32[]{:S(2)}) collective-permute-start(bf16[2,10,16,720]{3,2,1,0:T(8,128)(2,1)} %dynamic-slice_bitcast_fusion.2), channel_id=1, source_target_pairs={{0,1},{1,0},{2,3},{3,2},{4,5},{5,4},{6,7},{7,6},{8,9},{9,8},{10,11... | collective-permute-start | bytes 1382408 | tf_op jit(solution)/shard_map/ppermute | solution.py:137
  45.0 16.6 %collective-permute-start.6 = (bf16[10,16,1472]{2,1,0:T(8,128)(2,1)}, bf16[10,16,1472]{2,1,0:T(8,128)(2,1)}, u32[]{:S(2)}, u32[]{:S(2)}) collective-permute-start(bf16[10,16,1472]{2,1,0:T(8,128)(2,1)} %slice_select_fusion.1), channel_id=1, source_target_pairs={{1,2},{2,1},{3,0},{0,3},{5,6},{6,5},{7,4},{4,7},{9,10},{10,9},{11,... | collective-permute-start | bytes 1413128 | tf_op jit(solution)/shard_map/ppermute | solution.py:139
  46.4 13.4 %collective-permute-start.5 = (bf16[2,10,16,720]{3,2,1,0:T(8,128)(2,1)}, bf16[2,10,16,720]{3,2,1,0:T(8,128)(2,1)}, u32[]{:S(2)}, u32[]{:S(2)}) collective-permute-start(bf16[2,10,16,720]{3,2,1,0:T(8,128)(2,1)} %dynamic-slice_bitcast_fusion.1), channel_id=1, source_target_pairs={{0,1},{1,0},{2,3},{3,2},{4,5},{5,4},{6,7},{7,6},{8,9},{9,8},{10,11... | collective-permute-start | bytes 1382408 | tf_op jit(solution)/shard_map/ppermute | solution.py:137
  47.2 28.8 %collective-permute-start.9 = (bf16[10,16,1472]{2,1,0:T(8,128)(2,1)}, bf16[10,16,1472]{2,1,0:T(8,128)(2,1)}, u32[]{:S(2)}, u32[]{:S(2)}) collective-permute-start(bf16[10,16,1472]{2,1,0:T(8,128)(2,1)} %slice_select_fusion), channel_id=1, source_target_pairs={{1,2},{2,1},{3,0},{0,3},{5,6},{6,5},{7,4},{4,7},{9,10},{10,9},{11,... | collective-permute-start | bytes 1413128 | tf_op jit(solution)/shard_map/ppermute | solution.py:139
  49.1 24.0 %collective-permute-start.8 = (bf16[2,10,16,720]{3,2,1,0:T(8,128)(2,1)}, bf16[2,10,16,720]{3,2,1,0:T(8,128)(2,1)}, u32[]{:S(2)}, u32[]{:S(2)}) collective-permute-start(bf16[2,10,16,720]{3,2,1,0:T(8,128)(2,1)} %dynamic-slice_bitcast_fusion), channel_id=1, source_target_pairs={{0,1},{1,0},{2,3},{3,2},{4,5},{5,4},{6,7},{7,6},{8,9},{9,8},{10,11... | collective-permute-start | bytes 1382408 | tf_op jit(solution)/shard_map/ppermute | solution.py:137
  49.5 2.2 %copy-start = (bf16[45,16,2880]{2,1,0:T(8,128)(2,1)S(1)}, bf16[45,16,2880]{2,1,0:T(8,128)(2,1)}, u32[]{:S(2)}) copy-start(bf16[45,16,2880]{2,1,0:T(8,128)(2,1)} %panel_ref.9) | copy-start | bytes 12441604
  54.9 6.8 %copy-start.2 = (bf16[2,5,16,720]{3,2,1,0:T(8,128)(2,1)S(1)}, bf16[2,5,16,720]{3,2,1,0:T(8,128)(2,1)}, u32[]{:S(2)}) copy-start(bf16[2,5,16,720]{3,2,1,0:T(8,128)(2,1)} %dynamic-slice_bitcast_fusion.3) | copy-start | bytes 691204
  54.9 14.6 %copy-start.3 = (bf16[5,16,1472]{2,1,0:T(8,128)(2,1)S(1)}, bf16[5,16,1472]{2,1,0:T(8,128)(2,1)}, u32[]{:S(2)}) copy-start(bf16[5,16,1472]{2,1,0:T(8,128)(2,1)} %slice_select_fusion.4) | copy-start | bytes 706564
  58.7 17.3 %collective-permute-start.10 = (bf16[10,16,96]{2,1,0:T(8,128)(2,1)S(1)}, bf16[10,16,96]{2,1,0:T(8,128)(2,1)S(1)}, u32[]{:S(2)}, u32[]{:S(2)}) collective-permute-start(bf16[10,16,96]{2,1,0:T(8,128)(2,1)S(1)} %get-tuple-element.24), channel_id=1, source_target_pairs={{1,2},{2,1},{3,0},{0,3},{5,6},{6,5},{7,4},{4,7},{9,10},{10,9},{11,... | collective-permute-start | bytes 92168 | tf_op jit(solution)/shard_map/ppermute | solution.py:150
  59.7 9.7 %collective-permute-start.7 = (bf16[10,16,96]{2,1,0:T(8,128)(2,1)S(1)}, bf16[10,16,96]{2,1,0:T(8,128)(2,1)S(1)}, u32[]{:S(2)}, u32[]{:S(2)}) collective-permute-start(bf16[10,16,96]{2,1,0:T(8,128)(2,1)S(1)} %get-tuple-element.22), channel_id=1, source_target_pairs={{1,2},{2,1},{3,0},{0,3},{5,6},{6,5},{7,4},{4,7},{9,10},{10,9},{11,... | collective-permute-start | bytes 92168 | tf_op jit(solution)/shard_map/ppermute | solution.py:150
  61.6 18.3 %collective-permute-start.11 = (bf16[2,5,16,720]{3,2,1,0:T(8,128)(2,1)S(1)}, bf16[2,5,16,720]{3,2,1,0:T(8,128)(2,1)S(1)}, u32[]{:S(2)}, u32[]{:S(2)}) collective-permute-start(bf16[2,5,16,720]{3,2,1,0:T(8,128)(2,1)S(1)} %copy-done.2), channel_id=1, source_target_pairs={{0,1},{1,0},{2,3},{3,2},{4,5},{5,4},{6,7},{7,6},{8,9},{9,8},{10,11... | collective-permute-start | bytes 691208 | tf_op jit(solution)/shard_map/ppermute | solution.py:137
  69.5 10.5 %collective-permute-start.12 = (bf16[5,16,1472]{2,1,0:T(8,128)(2,1)S(1)}, bf16[5,16,1472]{2,1,0:T(8,128)(2,1)S(1)}, u32[]{:S(2)}, u32[]{:S(2)}) collective-permute-start(bf16[5,16,1472]{2,1,0:T(8,128)(2,1)S(1)} %copy-done.3), channel_id=1, source_target_pairs={{1,2},{2,1},{3,0},{0,3},{5,6},{6,5},{7,4},{4,7},{9,10},{10,9},{11,... | collective-permute-start | bytes 706568 | tf_op jit(solution)/shard_map/ppermute | solution.py:139
  73.1 6.8 %collective-permute-start.13 = (bf16[10,16,96]{2,1,0:T(8,128)(2,1)S(1)}, bf16[10,16,96]{2,1,0:T(8,128)(2,1)S(1)}, u32[]{:S(2)}, u32[]{:S(2)}) collective-permute-start(bf16[10,16,96]{2,1,0:T(8,128)(2,1)S(1)} %get-tuple-element.26), channel_id=1, source_target_pairs={{1,2},{2,1},{3,0},{0,3},{5,6},{6,5},{7,4},{4,7},{9,10},{10,9},{11,... | collective-permute-start | bytes 92168 | tf_op jit(solution)/shard_map/ppermute | solution.py:150
  79.7 4.9 %collective-permute-start.14 = (bf16[10,16,96]{2,1,0:T(8,128)(2,1)S(1)}, bf16[10,16,96]{2,1,0:T(8,128)(2,1)S(1)}, u32[]{:S(2)}, u32[]{:S(2)}) collective-permute-start(bf16[10,16,96]{2,1,0:T(8,128)(2,1)S(1)} %get-tuple-element.28), channel_id=1, source_target_pairs={{1,2},{2,1},{3,0},{0,3},{5,6},{6,5},{7,4},{4,7},{9,10},{10,9},{11,... | collective-permute-start | bytes 92168 | tf_op jit(solution)/shard_map/ppermute | solution.py:150
  81.8 33.6 %copy-start.4 = (f32[128,45]{0,1:T(8,128)S(1)}, f32[128,45]{0,1:T(8,128)}, u32[]{:S(2)}) copy-start(f32[128,45]{0,1:T(8,128)} %get-tuple-element.34) | copy-start | bytes 69124
  81.8 33.6 %copy-start.5 = (f32[128,45]{0,1:T(8,128)S(1)}, f32[128,45]{0,1:T(8,128)}, u32[]{:S(2)}) copy-start(f32[128,45]{0,1:T(8,128)} %get-tuple-element.33) | copy-start | bytes 69124
  81.8 3.9 %collective-permute-start.15 = (bf16[5,16,96]{2,1,0:T(8,128)(2,1)S(1)}, bf16[5,16,96]{2,1,0:T(8,128)(2,1)S(1)}, u32[]{:S(2)}, u32[]{:S(2)}) collective-permute-start(bf16[5,16,96]{2,1,0:T(8,128)(2,1)S(1)} %get-tuple-element.29), channel_id=1, source_target_pairs={{1,2},{2,1},{3,0},{0,3},{5,6},{6,5},{7,4},{4,7},{9,10},{10,9},{11,... | collective-permute-start | bytes 46088 | tf_op jit(solution)/shard_map/ppermute | solution.py:150

commit v5 on v4

--- a/solution.py
+++ b/solution.py
@@ -16,17 +16,60 @@
 KEPT = 1472
 NLON = 5760
 GROUP = 5
-CHUNKS = (0, 10, 20, 30, 40, 45)
+CHUNKS = (0, 25, 40, 45)
+GAUSS_TAIL = 2 * GROUP * 640
+GAUSS_LANES = GAUSS_TAIL + 896
+PANEL_TAIL = GROUP * START
+PANEL_LANES = PANEL_TAIL + 384
 GAUSS_PAIRS = [(0, 1), (1, 0), (2, 3), (3, 2)]
 PANEL_PAIRS = [(1, 2), (2, 1), (3, 0), (0, 3)]
 
 
-def sums_kernel(where_ref, order_ref, height_ref, angle_ref, own_ref, other_ref, panel_ref, far_ref,
-                *rest, base):
-    keep_ref, send_ref, gs_ref, gn_ref, decay_ref, table_ref = rest[-6:]
+def pack_kernel(spot_ref, gauss_ref, main_ref, tail_ref, *rest):
+    gauss_out, panel_out = rest[-2:]
+    for o in range(GROUP):
+        for k in range(2):
+            j = k * GROUP + o
+            gauss_out[0, :, 640 * j:640 * (j + 1)] = gauss_ref[k, o, :, 0:640]
+            gauss_out[0, :, GAUSS_TAIL + 80 * j:GAUSS_TAIL + 80 * (j + 1)] = gauss_ref[k, o, :, 640:720]
+        panel_out[0, :, START * o:START * (o + 1)] = main_ref[o]
+        panel_out[0, :, PANEL_TAIL + 64 * o:PANEL_TAIL + 64 * (o + 1)] = tail_ref[o, :, 0:64]
+
+
+def panel_specs(skip, upper):
+    return [
+        pl.BlockSpec((GROUP, 16, START), lambda i, spot: (i + skip, 0, upper(spot[0]))),
+        pl.BlockSpec((GROUP, 16, 128), lambda i, spot: (i + skip, 0, 11 + 11 * upper(spot[0]))),
+    ]
+
+
+def pack(spot, own, panel, after, base, count):
+    skip = base // GROUP
+    steps = count // GROUP
+    return pl.pallas_call(
+        pack_kernel,
+        out_shape=[jax.ShapeDtypeStruct((steps, 16, GAUSS_LANES), jnp.bfloat16),
+                   jax.ShapeDtypeStruct((steps, 16, PANEL_LANES), jnp.bfloat16)],
+        grid_spec=pltpu.PrefetchScalarGridSpec(
+            num_scalar_prefetch=1,
+            grid=(steps,),
+            in_specs=[pl.BlockSpec((2, GROUP, 16, QUARTER), lambda i, spot: (0, i + skip, 0, 0))]
+            + panel_specs(skip, lambda blk: 1 - blk // 2)
+            + [pl.BlockSpec(memory_space=pl.ANY)] * len(after),
+            out_specs=[pl.BlockSpec((1, 16, GAUSS_LANES), lambda i, spot: (i, 0, 0)),
+                       pl.BlockSpec((1, 16, PANEL_LANES), lambda i, spot: (i, 0, 0))],
+        ),
+        cost_estimate=pl.CostEstimate(flops=0, bytes_accessed=count * 200000, transcendentals=0),
+        name="pack",
+    )(spot, own, panel, panel, *after)
+
+
+def sums_kernel(spot_ref, order_ref, height_ref, angle_ref, own_ref, other_ref, main_ref, tail_ref,
+                far_ref, *rest, base):
+    keep_ref, send_ref, gs_ref, gn_ref, decay_ref, table_ref, mate_ref = rest[-7:]
     step = pl.program_id(0)
-    half = where_ref[0]
-    odd = where_ref[1] == 1
+    half = spot_ref[0] // 2
+    odd = spot_ref[0] % 2 == 1
     first = (half * START).astype(jnp.float32)
     degree = lax.broadcasted_iota(jnp.int32, (1, WIDE), 1).astype(jnp.float32) + first
 
@@ -41,13 +84,20 @@
         decay_ref[1] = here * (degree + 1.0)
         decay_ref[2] = jnp.exp(-(degree + 3.0) * height / ORDERS)
 
-    low = jnp.where(odd, other_ref[...], own_ref[...])
-    high = jnp.where(odd, own_ref[...], other_ref[...])
-    table_ref[:, 16:32, 0:KEPT] = far_ref[...]
+    for o in range(GROUP):
+        for k in range(2):
+            j = k * GROUP + o
+            mate_ref[k, o, :, 0:640] = other_ref[0, :, 640 * j:640 * (j + 1)]
+            mate_ref[k, o, :, 640:720] = other_ref[0, :, GAUSS_TAIL + 80 * j:GAUSS_TAIL + 80 * (j + 1)]
+        table_ref[o, 0:16, 0:START] = main_ref[o]
+        table_ref[o, 0:16, START:KEPT] = tail_ref[o, :, 0:64]
+        table_ref[o, 16:32, 0:START] = far_ref[0, :, START * o:START * (o + 1)]
+        table_ref[o, 16:32, START:KEPT] = far_ref[0, :, PANEL_TAIL + 64 * o:PANEL_TAIL + 64 * (o + 1)]
+    low = jnp.where(odd, mate_ref[...], own_ref[...])
+    high = jnp.where(odd, own_ref[...], mate_ref[...])
 
     @pl.when(half == 0)
     def _():
-        table_ref[:, 0:16, 0:KEPT] = panel_ref[:, :, 0:KEPT]
         gs_ref[:, :, :, 0:720] = low
         gs_ref[:, :, :, 720:1440] = high
         gn_ref[:, :, :, 0:719] = low[:, :, :, 1:]
@@ -55,7 +105,6 @@
 
     @pl.when(half == 1)
     def _():
-        table_ref[:, 0:16, 0:KEPT] = panel_ref[:, :, START:ORDERS]
         gs_ref[:, :, :, 32:752] = low
         gs_ref[:, :, :, 752:1472] = high
         gn_ref[:, :, :, 31:751] = low
@@ -82,36 +131,39 @@
         send_ref[o] = mixed[16:, :96].astype(jnp.bfloat16)
 
 
-def partial_sums(where, orders, height, angles, own, other, panel, far, after, base):
-    count = far.shape[0]
+def partial_sums(spot, orders, height, angles, own, other, panel, far, after, base, count):
     skip = base // GROUP
     smem = pl.BlockSpec(memory_space=pltpu.SMEM)
-    out = pl.BlockSpec((GROUP, 16, 96), lambda i: (i, 0, 0))
+    out = pl.BlockSpec((GROUP, 16, 96), lambda i, spot: (i, 0, 0))
     return pl.pallas_call(
         functools.partial(sums_kernel, base=base),
         out_shape=[jax.ShapeDtypeStruct((count, 16, 96), jnp.float32),
                    jax.ShapeDtypeStruct((count, 16, 96), jnp.bfloat16)],
-        grid=(count // GROUP,),
-        in_specs=[
-            smem, smem, pl.BlockSpec((16, 1), lambda i: (0, 0)),
-            pl.BlockSpec((32, 2), lambda i: (0, 0)),
-            pl.BlockSpec((2, GROUP, 16, QUARTER), lambda i: (0, i + skip, 0, 0)),
-            pl.BlockSpec((2, GROUP, 16, QUARTER), lambda i: (0, i, 0, 0)),
-            pl.BlockSpec((GROUP, 16, ORDERS), lambda i: (i + skip, 0, 0)),
-            pl.BlockSpec((GROUP, 16, KEPT), lambda i: (i, 0, 0)),
-        ] + [pl.BlockSpec(memory_space=pl.ANY)] * len(after),
-        out_specs=[out, out],
-        scratch_shapes=[
-            pltpu.VMEM((2, GROUP, 16, WIDE), jnp.bfloat16),
-            pltpu.VMEM((2, GROUP, 16, WIDE), jnp.bfloat16),
-            pltpu.VMEM((3, 16, WIDE), jnp.float32),
-            pltpu.VMEM((GROUP, 32, WIDE), jnp.bfloat16),
-        ],
+        grid_spec=pltpu.PrefetchScalarGridSpec(
+            num_scalar_prefetch=1,
+            grid=(count // GROUP,),
+            in_specs=[
+                smem, pl.BlockSpec((16, 1), lambda i, spot: (0, 0)),
+                pl.BlockSpec((32, 2), lambda i, spot: (0, 0)),
+                pl.BlockSpec((2, GROUP, 16, QUARTER), lambda i, spot: (0, i + skip, 0, 0)),
+                pl.BlockSpec((1, 16, GAUSS_LANES), lambda i, spot: (i, 0, 0)),
+            ] + panel_specs(skip, lambda blk: blk // 2)
+            + [pl.BlockSpec((1, 16, PANEL_LANES), lambda i, spot: (i, 0, 0))]
+            + [pl.BlockSpec(memory_space=pl.ANY)] * len(after),
+            out_specs=[out, out],
+            scratch_shapes=[
+                pltpu.VMEM((2, GROUP, 16, WIDE), jnp.bfloat16),
+                pltpu.VMEM((2, GROUP, 16, WIDE), jnp.bfloat16),
+                pltpu.VMEM((3, 16, WIDE), jnp.float32),
+                pltpu.VMEM((GROUP, 32, WIDE), jnp.bfloat16),
+                pltpu.VMEM((2, GROUP, 16, QUARTER), jnp.bfloat16),
+            ],
+        ),
         compiler_params=pltpu.CompilerParams(vmem_limit_bytes=24 << 20),
         cost_estimate=pl.CostEstimate(
-            flops=count * 32 * 96 * WIDE * 2, bytes_accessed=count * 200000, transcendentals=0),
+            flops=count * 32 * 128 * WIDE * 2, bytes_accessed=count * 200000, transcendentals=0),
         name="partial_sums",
-    )(where, orders, height, angles, own, other, panel, far, *after)
+    )(spot, orders, height, angles, own, other, panel, panel, far, *after)
 
 
 def turn(phase, period):
@@ -122,30 +174,24 @@
 def body(panel, gauss, height, order_map, cycle_map):
     count, cycles, _ = panel.shape
     shells = height.shape[0]
-    spot = lax.axis_index("blk")
     here = lax.axis_index("ord")
-    half = spot // 2
+    spot = lax.axis_index("blk").astype(jnp.int32).reshape(1)
     own = jnp.transpose(gauss, (0, 2, 1, 3))
+    spans = list(zip(CHUNKS[:-1], CHUNKS[1:]))
+    arrived, packed = [], ()
+    for a, b in spans:
+        packed = pack(spot, own, panel, packed[:1], a, b - a)
+        arrived.append((lax.ppermute(packed[0], "blk", GAUSS_PAIRS),
+                        lax.ppermute(packed[1], "blk", PANEL_PAIRS)))
     orders_int = lax.dynamic_slice_in_dim(order_map, here * count, count, 0)
-    where = jnp.stack([half, spot % 2]).astype(jnp.int32)
-    spans = list(zip(CHUNKS[:-1], CHUNKS[1:]))
-    arrived = []
     facing = lax.ppermute(cycle_map, "blk", PANEL_PAIRS)
-    late, next_ = 0, 0
-    for a, b in spans:
-        part = lax.dynamic_slice_in_dim(own, a + next_, b - a, 1)
-        other = lax.ppermute(part, "blk", GAUSS_PAIRS)
-        sent = jnp.where(half + late == 0, panel[a:b, :, START:], panel[a:b, :, :KEPT])
-        arrived.append((other, lax.ppermute(sent, "blk", PANEL_PAIRS)))
-        late = jnp.isnan(sent[0, 0, 0]).astype(jnp.int32)
-        next_ = jnp.isnan(part[0, 0, 0, 0]).astype(jnp.int32)
     theta = math.pi * (jnp.concatenate([cycle_map, facing]).astype(jnp.float32) + 0.5) / ORDERS
     angles = jnp.stack([jnp.cos(theta), 1.0 / jnp.sin(theta)], 1)
     kept, added = [], []
     for c, ((a, b), (other, far)) in enumerate(zip(spans, arrived)):
         after = (kept[-1:] or [own]) + (added[c - 2:c - 1] if c >= 2 else [])
         keep, send = partial_sums(
-            where, orders_int, height[:, None], angles, own, other, panel, far, after, a)
+            spot, orders_int, height[:, None], angles, own, other, panel, far, after, a, b - a)
         kept.append(keep)
         added.append(lax.ppermute(send, "blk", PANEL_PAIRS))
     total = jnp.concatenate(kept, 0) + jnp.concatenate(added, 0).astype(jnp.float32)

time: 136 us -> 113 us (0.83)
  local copies, waits for them, and re-layouts: 22.2 us -> 7.19 us
  between operations: 11.1 us -> 0.24 us
  other arithmetic: 12.3 us -> 1.69 us
  waiting for transfers between devices: 8.97 us -> 18.9 us
  Pallas kernels: 16.1 us -> 25.7 us
  starting transfers between devices: 18.6 us -> 14.2 us
    ppermute x1, waiting for transfers between devices: 0.01 us -> 14.9 us  [body(): facing = lax.ppermute(cycle_map, 'blk', PANEL_PAIRS)]
    pallas_call x0 -> x3, Pallas kernels: none -> 10.4 us  [pack(): pl.pallas_call(pack_kernel, out_shape=[jax.ShapeDtypeStruct((steps, 16, G...]
    select_n x5 -> x0, other arithmetic: 9.99 us -> none  [body(): jnp.where(half + late == 0, panel[a:b, :, START:], panel[a:b, :, :KEPT])]
    slice x8 -> x0, local copies, waits for them, and re-layouts: 9.83 us -> none  [the longest x4 4.95 us: body(): next_ = jnp.isnan(part[0, 0, 0, 0]).astype(jnp.int32)]
    ppermute x5 -> x3, waiting for transfers between devices: 8.95 us -> 2.07 us  [body(): added.append(lax.ppermute(send, 'blk', PANEL_PAIRS))]
    dynamic_slice x5 -> x0, local copies, waits for them, and re-layouts: 5.06 us -> none  [body(): part = lax.dynamic_slice_in_dim(own, a + next_, b - a, 1)]
    ppermute x5 -> x3, starting transfers between devices: 8.6 us -> 5.47 us  [body(): added.append(lax.ppermute(send, 'blk', PANEL_PAIRS))]
    ppermute x10 -> x6, waiting for transfers between devices: 0.03 us -> 1.88 us  [the longest x3 1.88 us: body(): lax.ppermute(packed[1], 'blk', PANEL_PAIRS)]
  transfers between devices with their start and end apart: 16 -> 10, of which waited for: 2 -> 3; matrix products, arithmetic and copies ran while one was open for 20% -> 3% of each run, Pallas kernels for 12% -> 18%
where the time goes in v5:
time: 113 us
  blocking collectives  43.8 us (39%)
  Pallas kernels  25.7 us (23%)
  waiting for transfers between devices  18.9 us (17%)
  starting transfers between devices  14.2 us (13%)
  local copies, waits for them, and re-layouts  7.19 us (6%)
  other arithmetic  1.69 us (1%)
  matrix products  1.2 us (1%)
    all_to_all x1, blocking collectives, body(): spread = lax.all_to_all(chunk, 'ord', 0, 0, tiled=True).astype(jnp.float32)  26.6 us
    all_to_all x1, blocking collectives, body(): field = lax.all_to_all(field, 'ord', 0, 0, tiled=True)  17.1 us
    pallas_call x3, Pallas kernels, partial_sums(): pl.pallas_call(functools.partial(sums_kernel, base=base), out_shape=[jax....  15.3 us
    ppermute x1, waiting for transfers between devices, body(): facing = lax.ppermute(cycle_map, 'blk', PANEL_PAIRS)  14.9 us
    pallas_call x3, Pallas kernels, pack(): pl.pallas_call(pack_kernel, out_shape=[jax.ShapeDtypeStruct((steps, 16, G...  10.4 us
    ppermute x3, starting transfers between devices, body(): lax.ppermute(packed[1], 'blk', PANEL_PAIRS)  5.74 us
    ppermute x3, starting transfers between devices, body(): added.append(lax.ppermute(send, 'blk', PANEL_PAIRS))  5.47 us
  transfers between devices with their start and end apart: 10, of which 3 were waited for; matrix products, arithmetic and copies ran while one was open for 3% of the time, Pallas kernels for 18%

profile of v5, /device:TPU:1, one launch (start us, length us, event | category | flops | bytes accessed | tf_op | source)
XLA Modules:
  0.0 112.8 jit_solution(12208254344307839519)
XLA Ops:
  0.0 4.9 %pack.3 = (bf16[5,16,7296]{2,1,0:T(8,128)(2,1)}, bf16[5,16,7424]{2,1,0:T(8,128)(2,1)}) custom-call(s32[1]{0:T(128)} %bitcast.spot_ref, bf16[2,45,16,720]{3,2,1,0:T(8,128)(2,1)} %bitcast.30, bf16[45,16,2880]{2,1,0:T(8,128)(2,1)} %tail_ref.11, bf16[45,16,2880]{2,1,0:T(8,128)(2,1)} %tail_ref.11), custom_call_target="tpu_custom_call" | custom-call | bytes 5000000 | tf_op jit(solution)/shard_map/pack/pallas_call | solution.py:49
  4.9 2.0 %collective-permute-start.1 = (bf16[5,16,7296]{2,1,0:T(8,128)(2,1)}, bf16[5,16,7296]{2,1,0:T(8,128)(2,1)}, u32[]{:S(2)}, u32[]{:S(2)}) collective-permute-start(bf16[5,16,7296]{2,1,0:T(8,128)(2,1)} %get-tuple-element.22.rest_0_), channel_id=1, source_target_pairs={{0,1},{1,0},{2,3},{3,2},{4,5},{5,4},{6,7},{7,6},{8,9},{9,8},{10,11... | collective-permute-start | bytes 3502088 | tf_op jit(solution)/shard_map/ppermute | solution.py:184
  6.9 1.8 %collective-permute-start.2 = (bf16[5,16,7424]{2,1,0:T(8,128)(2,1)}, bf16[5,16,7424]{2,1,0:T(8,128)(2,1)S(1)}, u32[]{:S(2)}, u32[]{:S(2)}) collective-permute-start(bf16[5,16,7424]{2,1,0:T(8,128)(2,1)} %get-tuple-element.23), channel_id=1, source_target_pairs={{1,2},{2,1},{3,0},{0,3},{5,6},{6,5},{7,4},{4,7},{9,10},{10,9},{11,... | collective-permute-start | bytes 3563528 | tf_op jit(solution)/shard_map/ppermute | solution.py:185
  8.7 0.9 collective-permute-start
  9.6 3.4 %pack.4 = (bf16[3,16,7296]{2,1,0:T(8,128)(2,1)}, bf16[3,16,7424]{2,1,0:T(8,128)(2,1)}) custom-call(s32[1]{0:T(128)} %bitcast.spot_ref, bf16[2,45,16,720]{3,2,1,0:T(8,128)(2,1)} %bitcast.31, bf16[45,16,2880]{2,1,0:T(8,128)(2,1)} %tail_ref.11, bf16[45,16,2880]{2,1,0:T(8,128)(2,1)} %tail_ref.11, bf16[5,16,7296]{2,1,0:T(8,128)(2,1)} %get-tuple-element.22.rest_0_), custom_call_target="tpu_custom_call" | custom-call | bytes 3000000 | tf_op jit(solution)/shard_map/pack/pallas_call | solution.py:49
  13.1 1.8 %collective-permute-start.4 = (bf16[3,16,7424]{2,1,0:T(8,128)(2,1)}, bf16[3,16,7424]{2,1,0:T(8,128)(2,1)}, u32[]{:S(2)}, u32[]{:S(2)}) collective-permute-start(bf16[3,16,7424]{2,1,0:T(8,128)(2,1)} %get-tuple-element.26), channel_id=1, source_target_pairs={{1,2},{2,1},{3,0},{0,3},{5,6},{6,5},{7,4},{4,7},{9,10},{10,9},{11,... | collective-permute-start | bytes 2138120 | tf_op jit(solution)/shard_map/ppermute | solution.py:185
  14.9 0.8 slice.19
  16.0 0.8 maximum_maximum_fusion
  16.8 2.1 %pack.5 = (bf16[1,16,7296]{2,1,0:T(8,128)(2,1)}, bf16[1,16,7424]{2,1,0:T(8,128)(2,1)}) custom-call(s32[1]{0:T(128)} %bitcast.spot_ref, bf16[2,45,16,720]{3,2,1,0:T(8,128)(2,1)} %bitcast.32, bf16[45,16,2880]{2,1,0:T(8,128)(2,1)} %tail_ref.11, bf16[45,16,2880]{2,1,0:T(8,128)(2,1)} %tail_ref.11, bf16[3,16,7296]{2,1,0:T(8,128)(2,1)} %get-tuple-element.25.rest_0_), custom_call_target="tpu_custom_call" | custom-call | bytes 1000000 | tf_op jit(solution)/shard_map/pack/pallas_call | solution.py:49
  18.9 0.8 dynamic_slice.3.order_ref
  19.8 14.9 %collective-permute-done = s32[16]{0:T(128)S(1)} collective-permute-done((s32[16]{0:T(128)S(1)}, s32[16]{0:T(128)S(1)}, u32[]{:S(2)}, u32[]{:S(2)}) %collective-permute-start) | collective-permute-done | bytes 96 | tf_op jit(solution)/shard_map/ppermute | solution.py:187
  34.8 2.1 %collective-permute-start.6 = (bf16[1,16,7424]{2,1,0:T(8,128)(2,1)}, bf16[1,16,7424]{2,1,0:T(8,128)(2,1)}, u32[]{:S(2)}, u32[]{:S(2)}) collective-permute-start(bf16[1,16,7424]{2,1,0:T(8,128)(2,1)} %get-tuple-element.29), channel_id=1, source_target_pairs={{1,2},{2,1},{3,0},{0,3},{5,6},{6,5},{7,4},{4,7},{9,10},{10,9},{11,... | collective-permute-start | bytes 712712 | tf_op jit(solution)/shard_map/ppermute | solution.py:185
  37.2 2.2 %copy-done = bf16[45,16,2880]{2,1,0:T(8,128)(2,1)S(1)} copy-done((bf16[45,16,2880]{2,1,0:T(8,128)(2,1)S(1)}, bf16[45,16,2880]{2,1,0:T(8,128)(2,1)}, u32[]{:S(2)}) %copy-start) | copy-done | bytes 4147224
  39.4 7.7 %partial_sums.3 = (f32[25,16,96]{2,1,0:T(8,128)S(1)}, bf16[25,16,96]{2,1,0:T(8,128)(2,1)S(1)}) custom-call(s32[1]{0:T(128)} %bitcast.spot_ref, s32[45]{0:T(128)S(1)} %dynamic_slice.3.order_ref, f32[16,1]{1,0:T(8,128)S(1)} %copy.30.height_ref, f32[32,2]{1,0:T(8,128)S(1)} %copy.31.angle_ref, bf16[2,45,16,720]{3,2,1,0:T(8,128)(2,1)S(1)} %bitcast.33, ...), custom_call_target="tpu_custom_call" | custom-call | flops 314572800 | bytes 5000000 | tf_op jit(solution)/shard_map/partial_sums/pallas_call | solution.py:138
  47.2 1.0 collective-permute-start.7
  48.3 1.9 %collective-permute-done.4.far_ref = bf16[3,16,7424]{2,1,0:T(8,128)(2,1)} collective-permute-done((bf16[3,16,7424]{2,1,0:T(8,128)(2,1)}, bf16[3,16,7424]{2,1,0:T(8,128)(2,1)}, u32[]{:S(2)}, u32[]{:S(2)}) %collective-permute-start.4) | collective-permute-done | bytes 712736 | tf_op jit(solution)/shard_map/ppermute | solution.py:185
  50.1 5.2 %partial_sums.4 = (f32[15,16,96]{2,1,0:T(8,128)S(1)}, bf16[15,16,96]{2,1,0:T(8,128)(2,1)S(1)}) custom-call(s32[1]{0:T(128)} %bitcast.spot_ref, s32[45]{0:T(128)S(1)} %dynamic_slice.3.order_ref, f32[16,1]{1,0:T(8,128)S(1)} %copy.30.height_ref, f32[32,2]{1,0:T(8,128)S(1)} %copy.31.angle_ref, bf16[2,45,16,720]{3,2,1,0:T(8,128)(2,1)S(1)} %bitcast.35, ...), custom_call_target="tpu_custom_call" | custom-call | flops 188743680 | bytes 3000000 | tf_op jit(solution)/shard_map/partial_sums/pallas_call | solution.py:138
  55.3 2.3 %collective-permute-start.8 = (bf16[15,16,96]{2,1,0:T(8,128)(2,1)S(1)}, bf16[15,16,96]{2,1,0:T(8,128)(2,1)S(1)}, u32[]{:S(2)}, u32[]{:S(2)}) collective-permute-start(bf16[15,16,96]{2,1,0:T(8,128)(2,1)S(1)} %get-tuple-element.32), channel_id=1, source_target_pairs={{1,2},{2,1},{3,0},{0,3},{5,6},{6,5},{7,4},{4,7},{9,10},{10,9},{11,... | collective-permute-start | bytes 138248 | tf_op jit(solution)/shard_map/ppermute | solution.py:196
  57.7 2.4 %partial_sums.5 = (f32[5,16,96]{2,1,0:T(8,128)S(1)}, bf16[5,16,96]{2,1,0:T(8,128)(2,1)S(1)}) custom-call(s32[1]{0:T(128)} %bitcast.spot_ref, s32[45]{0:T(128)S(1)} %dynamic_slice.3.order_ref, f32[16,1]{1,0:T(8,128)S(1)} %copy.30.height_ref, f32[32,2]{1,0:T(8,128)S(1)} %copy.31.angle_ref, bf16[2,45,16,720]{3,2,1,0:T(8,128)(2,1)S(1)} %bitcast.36, ...), custom_call_target="tpu_custom_call" | custom-call | flops 62914560 | bytes 1000000 | tf_op jit(solution)/shard_map/partial_sums/pallas_call | solution.py:138
  60.1 2.2 %collective-permute-start.9 = (bf16[5,16,96]{2,1,0:T(8,128)(2,1)S(1)}, bf16[5,16,96]{2,1,0:T(8,128)(2,1)S(1)}, u32[]{:S(2)}, u32[]{:S(2)}) collective-permute-start(bf16[5,16,96]{2,1,0:T(8,128)(2,1)S(1)} %get-tuple-element.33), channel_id=1, source_target_pairs={{1,2},{2,1},{3,0},{0,3},{5,6},{6,5},{7,4},{4,7},{9,10},{10,9},{11,... | collective-permute-start | bytes 46088 | tf_op jit(solution)/shard_map/ppermute | solution.py:196
  62.3 2.1 %collective-permute-done.9 = bf16[5,16,96]{2,1,0:T(8,128)(2,1)S(1)} collective-permute-done((bf16[5,16,96]{2,1,0:T(8,128)(2,1)S(1)}, bf16[5,16,96]{2,1,0:T(8,128)(2,1)S(1)}, u32[]{:S(2)}, u32[]{:S(2)}) %collective-permute-start.9) | collective-permute-done | bytes 15392 | tf_op jit(solution)/shard_map/ppermute | solution.py:196
  65.5 26.6 %all_to_all.10 = bf16[64,2,540]{2,1,0:T(2,128)(2,1)S(1)} all-to-all(bf16[64,2,540]{2,1,0:T(2,128)(2,1)S(1)} %copy.38), channel_id=1, replica_groups=mesh['ord'=64,'blk'=4] {'ord'}, dimensions={0} | all-to-all | bytes 276480 | tf_op jit(solution)/shard_map/all_to_all | solution.py:216
  94.6 17.1 %all_to_all.11 = bf16[64,90,12]{1,2,0:T(8,128)(2,1)S(1)} all-to-all(bf16[64,90,12]{1,2,0:T(8,128)(2,1)S(1)} %copy.40), channel_id=1, replica_groups=mesh['ord'=64,'blk'=4] {'ord'}, dimensions={0} | all-to-all | bytes 276480 | tf_op jit(solution)/shard_map/all_to_all | solution.py:226
  112.0 0.8 copy.43
  (46 shorter events, 4.8 us)
Async XLA Ops:
  0.0 8.7 %copy-start.4 = (s32[16]{0:T(128)S(1)}, s32[16]{0:T(128)}, u32[]{:S(2)}) copy-start(s32[16]{0:T(128)} %param.9) | copy-start | bytes 196
  4.9 32.1 %collective-permute-start.1 = (bf16[5,16,7296]{2,1,0:T(8,128)(2,1)}, bf16[5,16,7296]{2,1,0:T(8,128)(2,1)}, u32[]{:S(2)}, u32[]{:S(2)}) collective-permute-start(bf16[5,16,7296]{2,1,0:T(8,128)(2,1)} %get-tuple-element.22.rest_0_), channel_id=1, source_target_pairs={{0,1},{1,0},{2,3},{3,2},{4,5},{5,4},{6,7},{7,6},{8,9},{9,8},{10,11... | collective-permute-start | bytes 3502088 | tf_op jit(solution)/shard_map/ppermute | solution.py:184
  6.9 30.3 %collective-permute-start.2 = (bf16[5,16,7424]{2,1,0:T(8,128)(2,1)}, bf16[5,16,7424]{2,1,0:T(8,128)(2,1)S(1)}, u32[]{:S(2)}, u32[]{:S(2)}) collective-permute-start(bf16[5,16,7424]{2,1,0:T(8,128)(2,1)} %get-tuple-element.23), channel_id=1, source_target_pairs={{1,2},{2,1},{3,0},{0,3},{5,6},{6,5},{7,4},{4,7},{9,10},{10,9},{11,... | collective-permute-start | bytes 3563528 | tf_op jit(solution)/shard_map/ppermute | solution.py:185
  8.7 26.0 %collective-permute-start = (s32[16]{0:T(128)S(1)}, s32[16]{0:T(128)S(1)}, u32[]{:S(2)}, u32[]{:S(2)}) collective-permute-start(s32[16]{0:T(128)S(1)} %copy-done.4), channel_id=1, source_target_pairs={{1,2},{2,1},{3,0},{0,3},{5,6},{6,5},{7,4},{4,7},{9,10},{10,9},{11,... | collective-permute-start | bytes 200 | tf_op jit(solution)/shard_map/ppermute | solution.py:187
  13.1 35.2 %collective-permute-start.3 = (bf16[3,16,7296]{2,1,0:T(8,128)(2,1)}, bf16[3,16,7296]{2,1,0:T(8,128)(2,1)}, u32[]{:S(2)}, u32[]{:S(2)}) collective-permute-start(bf16[3,16,7296]{2,1,0:T(8,128)(2,1)} %get-tuple-element.25.rest_0_), channel_id=1, source_target_pairs={{0,1},{1,0},{2,3},{3,2},{4,5},{5,4},{6,7},{7,6},{8,9},{9,8},{10,11... | collective-permute-start | bytes 2101256 | tf_op jit(solution)/shard_map/ppermute | solution.py:184
  13.1 37.1 %collective-permute-start.4 = (bf16[3,16,7424]{2,1,0:T(8,128)(2,1)}, bf16[3,16,7424]{2,1,0:T(8,128)(2,1)}, u32[]{:S(2)}, u32[]{:S(2)}) collective-permute-start(bf16[3,16,7424]{2,1,0:T(8,128)(2,1)} %get-tuple-element.26), channel_id=1, source_target_pairs={{1,2},{2,1},{3,0},{0,3},{5,6},{6,5},{7,4},{4,7},{9,10},{10,9},{11,... | collective-permute-start | bytes 2138120 | tf_op jit(solution)/shard_map/ppermute | solution.py:185
  16.8 3.0 %copy-start.3 = (f32[16]{0:T(128)S(1)}, f32[16]{0:T(128)}, u32[]{:S(2)}) copy-start(f32[16]{0:T(128)} %param.7) | copy-start | bytes 196
  16.8 20.4 %copy-start.1 = (bf16[2,16,45,720]{3,1,2,0:T(8,128)(2,1)S(1)}, bf16[2,16,45,720]{3,1,2,0:T(8,128)(2,1)}, u32[]{:S(2)}) copy-start(bf16[2,16,45,720]{3,1,2,0:T(8,128)(2,1)} %param.6) | copy-start | bytes 6220804
  34.8 22.9 %collective-permute-start.6 = (bf16[1,16,7424]{2,1,0:T(8,128)(2,1)}, bf16[1,16,7424]{2,1,0:T(8,128)(2,1)}, u32[]{:S(2)}, u32[]{:S(2)}) collective-permute-start(bf16[1,16,7424]{2,1,0:T(8,128)(2,1)} %get-tuple-element.29), channel_id=1, source_target_pairs={{1,2},{2,1},{3,0},{0,3},{5,6},{6,5},{7,4},{4,7},{9,10},{10,9},{11,... | collective-permute-start | bytes 712712 | tf_op jit(solution)/shard_map/ppermute | solution.py:185
  37.0 20.6 %collective-permute-start.5 = (bf16[1,16,7296]{2,1,0:T(8,128)(2,1)}, bf16[1,16,7296]{2,1,0:T(8,128)(2,1)}, u32[]{:S(2)}, u32[]{:S(2)}) collective-permute-start(bf16[1,16,7296]{2,1,0:T(8,128)(2,1)} %get-tuple-element.28), channel_id=1, source_target_pairs={{0,1},{1,0},{2,3},{3,2},{4,5},{5,4},{6,7},{7,6},{8,9},{9,8},{10,11... | collective-permute-start | bytes 700424 | tf_op jit(solution)/shard_map/ppermute | solution.py:184
  37.2 2.2 %copy-start = (bf16[45,16,2880]{2,1,0:T(8,128)(2,1)S(1)}, bf16[45,16,2880]{2,1,0:T(8,128)(2,1)}, u32[]{:S(2)}) copy-start(bf16[45,16,2880]{2,1,0:T(8,128)(2,1)} %tail_ref.11) | copy-start | bytes 12441604
  47.2 10.5 %collective-permute-start.7 = (bf16[25,16,96]{2,1,0:T(8,128)(2,1)S(1)}, bf16[25,16,96]{2,1,0:T(8,128)(2,1)S(1)}, u32[]{:S(2)}, u32[]{:S(2)}) collective-permute-start(bf16[25,16,96]{2,1,0:T(8,128)(2,1)S(1)} %get-tuple-element.30), channel_id=1, source_target_pairs={{1,2},{2,1},{3,0},{0,3},{5,6},{6,5},{7,4},{4,7},{9,10},{10,9},{11,... | collective-permute-start | bytes 230408 | tf_op jit(solution)/shard_map/ppermute | solution.py:196
  55.3 7.0 %collective-permute-start.8 = (bf16[15,16,96]{2,1,0:T(8,128)(2,1)S(1)}, bf16[15,16,96]{2,1,0:T(8,128)(2,1)S(1)}, u32[]{:S(2)}, u32[]{:S(2)}) collective-permute-start(bf16[15,16,96]{2,1,0:T(8,128)(2,1)S(1)} %get-tuple-element.32), channel_id=1, source_target_pairs={{1,2},{2,1},{3,0},{0,3},{5,6},{6,5},{7,4},{4,7},{9,10},{10,9},{11,... | collective-permute-start | bytes 138248 | tf_op jit(solution)/shard_map/ppermute | solution.py:196
  60.1 4.3 %collective-permute-start.9 = (bf16[5,16,96]{2,1,0:T(8,128)(2,1)S(1)}, bf16[5,16,96]{2,1,0:T(8,128)(2,1)S(1)}, u32[]{:S(2)}, u32[]{:S(2)}) collective-permute-start(bf16[5,16,96]{2,1,0:T(8,128)(2,1)S(1)} %get-tuple-element.33), channel_id=1, source_target_pairs={{1,2},{2,1},{3,0},{0,3},{5,6},{6,5},{7,4},{4,7},{9,10},{10,9},{11,... | collective-permute-start | bytes 46088 | tf_op jit(solution)/shard_map/ppermute | solution.py:196
  65.1 27.3 %copy-start.2 = (f32[256,128]{1,0:T(8,128)S(1)}, f32[256,128]{1,0:T(8,128)}, u32[]{:S(2)}) copy-start(f32[256,128]{1,0:T(8,128)} %maximum_maximum_fusion) | copy-start | bytes 393220

commit v6 on v5

--- a/solution.py
+++ b/solution.py
@@ -16,17 +16,21 @@
 KEPT = 1472
 NLON = 5760
 GROUP = 5
-CHUNKS = (0, 25, 40, 45)
+CHUNKS = (0, 15, 30, 40, 45)
 GAUSS_TAIL = 2 * GROUP * 640
 GAUSS_LANES = GAUSS_TAIL + 896
 PANEL_TAIL = GROUP * START
 PANEL_LANES = PANEL_TAIL + 384
+CYCLE_LANE = PANEL_TAIL + 320
 GAUSS_PAIRS = [(0, 1), (1, 0), (2, 3), (3, 2)]
 PANEL_PAIRS = [(1, 2), (2, 1), (3, 0), (0, 3)]
 
 
-def pack_kernel(spot_ref, gauss_ref, main_ref, tail_ref, *rest):
+def pack_kernel(spot_ref, cycle_ref, gauss_ref, main_ref, tail_ref, *rest):
     gauss_out, panel_out = rest[-2:]
+    cycle = cycle_ref[...]
+    digits = jnp.concatenate([cycle // 64, cycle % 64], 1)
+    panel_out[0, :, CYCLE_LANE:CYCLE_LANE + 2] = digits.astype(jnp.float32).astype(jnp.bfloat16)
     for o in range(GROUP):
         for k in range(2):
             j = k * GROUP + o
@@ -43,7 +47,7 @@
     ]
 
 
-def pack(spot, own, panel, after, base, count):
+def pack(spot, cycle, own, panel, after, base, count):
     skip = base // GROUP
     steps = count // GROUP
     return pl.pallas_call(
@@ -53,7 +57,8 @@
         grid_spec=pltpu.PrefetchScalarGridSpec(
             num_scalar_prefetch=1,
             grid=(steps,),
-            in_specs=[pl.BlockSpec((2, GROUP, 16, QUARTER), lambda i, spot: (0, i + skip, 0, 0))]
+            in_specs=[pl.BlockSpec((16, 1), lambda i, spot: (0, 0)),
+                      pl.BlockSpec((2, GROUP, 16, QUARTER), lambda i, spot: (0, i + skip, 0, 0))]
             + panel_specs(skip, lambda blk: 1 - blk // 2)
             + [pl.BlockSpec(memory_space=pl.ANY)] * len(after),
             out_specs=[pl.BlockSpec((1, 16, GAUSS_LANES), lambda i, spot: (i, 0, 0)),
@@ -61,12 +66,12 @@
         ),
         cost_estimate=pl.CostEstimate(flops=0, bytes_accessed=count * 200000, transcendentals=0),
         name="pack",
-    )(spot, own, panel, panel, *after)
-
-
-def sums_kernel(spot_ref, order_ref, height_ref, angle_ref, own_ref, other_ref, main_ref, tail_ref,
+    )(spot, cycle, own, panel, panel, *after)
+
+
+def sums_kernel(spot_ref, order_ref, height_ref, cycle_ref, own_ref, other_ref, main_ref, tail_ref,
                 far_ref, *rest, base):
-    keep_ref, send_ref, gs_ref, gn_ref, decay_ref, table_ref, mate_ref = rest[-7:]
+    keep_ref, send_ref, gs_ref, gn_ref, decay_ref, table_ref, mate_ref, angle_ref = rest[-8:]
     step = pl.program_id(0)
     half = spot_ref[0] // 2
     odd = spot_ref[0] % 2 == 1
@@ -83,6 +88,13 @@
         decay_ref[0] = here
         decay_ref[1] = here * (degree + 1.0)
         decay_ref[2] = jnp.exp(-(degree + 3.0) * height / ORDERS)
+        digits = far_ref[0, :, CYCLE_LANE:CYCLE_LANE + 2].astype(jnp.float32)
+        mates = digits[:, 0:1] * 64.0 + digits[:, 1:2]
+        cycles = jnp.concatenate([cycle_ref[...].astype(jnp.float32), mates], 0)
+        cycles = jnp.broadcast_to(cycles, (32, 128)).T[0:8, :]
+        theta = math.pi * (cycles + 0.5) / ORDERS
+        angle_ref[0] = jnp.cos(theta)
+        angle_ref[1] = 1.0 / jnp.sin(theta)
 
     for o in range(GROUP):
         for k in range(2):
@@ -110,28 +122,32 @@
         gn_ref[:, :, :, 31:751] = low
         gn_ref[:, :, :, 751:1471] = high
 
-    cosine = angle_ref[:, 0:1]
-    inverse = angle_ref[:, 1:2]
-    lane = lax.broadcasted_iota(jnp.int32, (32, 128), 1)
-    for o in range(GROUP):
-        m = order_ref[base + step * GROUP + o].astype(jnp.float32)
-        root = jnp.sqrt(jnp.maximum((degree + 1.0) * (degree + 1.0) - m * m, 0.0))
-        slope = decay_ref[2] * root
+    cosine = angle_ref[0, 0:1]
+    inverse = angle_ref[1, 0:1]
+    orders = [order_ref[base + step * GROUP + o].astype(jnp.float32) for o in range(GROUP)]
+    sums = []
+    for o in range(GROUP):
+        gap = jnp.maximum((degree + 1.0) * (degree + 1.0) - orders[o] * orders[o], 0.0)
+        slope = decay_ref[2] * jnp.sqrt(gap)
         g = [gs_ref[k, o].astype(jnp.float32) for k in range(2)]
         n = [gn_ref[k, o].astype(jnp.float32) for k in range(2)]
-        main = [(g[k] * decay_ref[1]).astype(jnp.bfloat16) for k in range(2)]
-        bare = [(g[k] * decay_ref[0]).astype(jnp.bfloat16) for k in range(2)]
-        tilt = [(n[k] * slope).astype(jnp.bfloat16) for k in range(2)]
-        weights = jnp.concatenate(main + bare + [-bare[1], bare[0]] + tilt, 0)
-        sums = lax.dot_general(
-            table_ref[o], weights, (((1,), (1,)), ((), ())), preferred_element_type=jnp.float32)
-        polar = (pltpu.roll(sums, 64, 1) - cosine * (pltpu.roll(sums, 32, 1) - sums)) * inverse
-        mixed = jnp.where(lane < 32, sums, jnp.where(lane < 64, polar, m * inverse * sums))
-        keep_ref[o] = mixed[:16, :96]
-        send_ref[o] = mixed[16:, :96].astype(jnp.bfloat16)
-
-
-def partial_sums(spot, orders, height, angles, own, other, panel, far, after, base, count):
+        weights = jnp.concatenate(
+            [g[0] * decay_ref[1], g[1] * decay_ref[1], g[0] * decay_ref[0], g[1] * decay_ref[0],
+             n[0] * slope, n[1] * slope], 0).astype(jnp.bfloat16)
+        sums.append(lax.dot_general(
+            weights, table_ref[o], (((1,), (1,)), ((), ())), preferred_element_type=jnp.float32))
+    mixed = []
+    for o in range(GROUP):
+        main, bare, tilt = sums[o][0:32], sums[o][32:64], sums[o][64:96]
+        polar = (tilt - cosine * (main - bare)) * inverse
+        bare = orders[o] * inverse * bare
+        mixed.append(jnp.concatenate([main, polar, -bare[16:32], bare[0:16]], 0).T)
+    for o in range(GROUP):
+        keep_ref[o] = mixed[o][:16]
+        send_ref[o] = mixed[o][16:].astype(jnp.bfloat16)
+
+
+def partial_sums(spot, orders, height, cycle, own, other, panel, far, after, base, count):
     skip = base // GROUP
     smem = pl.BlockSpec(memory_space=pltpu.SMEM)
     out = pl.BlockSpec((GROUP, 16, 96), lambda i, spot: (i, 0, 0))
@@ -144,7 +160,7 @@
             grid=(count // GROUP,),
             in_specs=[
                 smem, pl.BlockSpec((16, 1), lambda i, spot: (0, 0)),
-                pl.BlockSpec((32, 2), lambda i, spot: (0, 0)),
+                pl.BlockSpec((16, 1), lambda i, spot: (0, 0)),
                 pl.BlockSpec((2, GROUP, 16, QUARTER), lambda i, spot: (0, i + skip, 0, 0)),
                 pl.BlockSpec((1, 16, GAUSS_LANES), lambda i, spot: (i, 0, 0)),
             ] + panel_specs(skip, lambda blk: blk // 2)
@@ -157,13 +173,14 @@
                 pltpu.VMEM((3, 16, WIDE), jnp.float32),
                 pltpu.VMEM((GROUP, 32, WIDE), jnp.bfloat16),
                 pltpu.VMEM((2, GROUP, 16, QUARTER), jnp.bfloat16),
+                pltpu.VMEM((2, 8, 32), jnp.float32),
             ],
         ),
         compiler_params=pltpu.CompilerParams(vmem_limit_bytes=24 << 20),
         cost_estimate=pl.CostEstimate(
             flops=count * 32 * 128 * WIDE * 2, bytes_accessed=count * 200000, transcendentals=0),
         name="partial_sums",
-    )(spot, orders, height, angles, own, other, panel, panel, far, *after)
+    )(spot, orders, height, cycle, own, other, panel, panel, far, *after)
 
 
 def turn(phase, period):
@@ -176,22 +193,20 @@
     shells = height.shape[0]
     here = lax.axis_index("ord")
     spot = lax.axis_index("blk").astype(jnp.int32).reshape(1)
+    cycle = cycle_map[:, None]
     own = jnp.transpose(gauss, (0, 2, 1, 3))
     spans = list(zip(CHUNKS[:-1], CHUNKS[1:]))
     arrived, packed = [], ()
     for a, b in spans:
-        packed = pack(spot, own, panel, packed[:1], a, b - a)
+        packed = pack(spot, cycle, own, panel, packed[:1], a, b - a)
         arrived.append((lax.ppermute(packed[0], "blk", GAUSS_PAIRS),
                         lax.ppermute(packed[1], "blk", PANEL_PAIRS)))
     orders_int = lax.dynamic_slice_in_dim(order_map, here * count, count, 0)
-    facing = lax.ppermute(cycle_map, "blk", PANEL_PAIRS)
-    theta = math.pi * (jnp.concatenate([cycle_map, facing]).astype(jnp.float32) + 0.5) / ORDERS
-    angles = jnp.stack([jnp.cos(theta), 1.0 / jnp.sin(theta)], 1)
     kept, added = [], []
     for c, ((a, b), (other, far)) in enumerate(zip(spans, arrived)):
         after = (kept[-1:] or [own]) + (added[c - 2:c - 1] if c >= 2 else [])
         keep, send = partial_sums(
-            spot, orders_int, height[:, None], angles, own, other, panel, far, after, a, b - a)
+            spot, orders_int, height[:, None], cycle, own, other, panel, far, after, a, b - a)
         kept.append(keep)
         added.append(lax.ppermute(send, "blk", PANEL_PAIRS))
     total = jnp.concatenate(kept, 0) + jnp.concatenate(added, 0).astype(jnp.float32)

time: 113 us -> 116 us (1.027)
  starting transfers between devices: 14.2 us -> 18.9 us
  waiting for transfers between devices: 18.9 us -> 14.2 us
  local copies, waits for them, and re-layouts: 7.19 us -> 10.4 us
    ppermute x1 -> x0, waiting for transfers between devices: 14.9 us -> none  [body(): facing = lax.ppermute(cycle_map, 'blk', PANEL_PAIRS)]
    ppermute x3 -> x4, waiting for transfers between devices: 0.01 us -> 9.77 us  [body(): lax.ppermute(packed[0], 'blk', GAUSS_PAIRS)]
    ppermute x3 -> x4, starting transfers between devices: 5.74 us -> 9.97 us  [body(): lax.ppermute(packed[1], 'blk', PANEL_PAIRS)]
    ppermute x3 -> x4, waiting for transfers between devices: 2.07 us -> 4.45 us  [body(): added.append(lax.ppermute(send, 'blk', PANEL_PAIRS))]
    unnamed x12 -> x14, local copies, waits for them, and re-layouts: 2.24 us -> 4.2 us
    ppermute x3 -> x4, waiting for transfers between devices: 1.88 us -> 0.01 us  [body(): lax.ppermute(packed[1], 'blk', PANEL_PAIRS)]
    broadcast_in_dim x0 -> x1, local copies, waits for them, and re-layouts: none -> 1.32 us  [body(): cycle = cycle_map[:, None]]
    pallas_call x3 -> x4, Pallas kernels: 15.3 us -> 14 us  [partial_sums(): pl.pallas_call(functools.partial(sums_kernel, base=base), out_shape=[jax....]
  transfers between devices with their start and end apart: 10 -> 12, of which waited for: 3 -> 5; matrix products, arithmetic and copies ran while one was open for 3% -> 3% of each run, Pallas kernels for 18% -> 17%
where the time goes in v6:
time: 116 us
  blocking collectives  43.1 us (37%)
  Pallas kernels  25.3 us (22%)
  starting transfers between devices  18.9 us (16%)
  waiting for transfers between devices  14.2 us (12%)
  local copies, waits for them, and re-layouts  10.4 us (9%)
  other arithmetic  2.45 us (2%)
  matrix products  1.19 us (1%)
    all_to_all x1, blocking collectives, body(): spread = lax.all_to_all(chunk, 'ord', 0, 0, tiled=True).astype(jnp.float32)  25.9 us
    all_to_all x1, blocking collectives, body(): field = lax.all_to_all(field, 'ord', 0, 0, tiled=True)  17.1 us
    pallas_call x4, Pallas kernels, partial_sums(): pl.pallas_call(functools.partial(sums_kernel, base=base), out_shape=[jax....  14 us
    pallas_call x4, Pallas kernels, pack(): pl.pallas_call(pack_kernel, out_shape=[jax.ShapeDtypeStruct((steps, 16, G...  11.3 us
    ppermute x4, starting transfers between devices, body(): lax.ppermute(packed[1], 'blk', PANEL_PAIRS)  9.97 us
    ppermute x4, waiting for transfers between devices, body(): lax.ppermute(packed[0], 'blk', GAUSS_PAIRS)  9.77 us
    ppermute x4, starting transfers between devices, body(): added.append(lax.ppermute(send, 'blk', PANEL_PAIRS))  5.78 us
    ppermute x4, waiting for transfers between devices, body(): added.append(lax.ppermute(send, 'blk', PANEL_PAIRS))  4.45 us
  transfers between devices with their start and end apart: 12, of which 5 were waited for; matrix products, arithmetic and copies ran while one was open for 3% of the time, Pallas kernels for 17%

profile of v6, /device:TPU:1, one launch (start us, length us, event | category | flops | bytes accessed | tf_op | source)
XLA Modules:
  0.0 115.8 jit_solution(10237782626631645695)
XLA Ops:
  0.0 1.3 %copy.53.cycle_ref = s32[16,1]{1,0:T(8,128)} copy(s32[16,1]{0,1:T(1,128)} %bitcast.43) | data formatting | bytes 128 | tf_op jit(solution)/shard_map/broadcast_in_dim | solution.py:196
  1.3 3.5 %pack.4 = (bf16[3,16,7296]{2,1,0:T(8,128)(2,1)}, bf16[3,16,7424]{2,1,0:T(8,128)(2,1)}) custom-call(s32[1]{0:T(128)} %bitcast.spot_ref, s32[16,1]{1,0:T(8,128)} %copy.53.cycle_ref, bf16[2,45,16,720]{3,2,1,0:T(8,128)(2,1)} %bitcast.29, bf16[45,16,2880]{2,1,0:T(8,128)(2,1)} %tail_ref.15, bf16[45,16,2880]{2,1,0:T(8,128)(2,1)} %tail_ref.15), custom_call_target="tpu_custom_call" | custom-call | bytes 3000000 | tf_op jit(solution)/shard_map/pack/pallas_call | solution.py:53
  4.8 2.0 %collective-permute-start = (bf16[3,16,7296]{2,1,0:T(8,128)(2,1)}, bf16[3,16,7296]{2,1,0:T(8,128)(2,1)S(1)}, u32[]{:S(2)}, u32[]{:S(2)}) collective-permute-start(bf16[3,16,7296]{2,1,0:T(8,128)(2,1)} %get-tuple-element.26.rest_0_), channel_id=1, source_target_pairs={{0,1},{1,0},{2,3},{3,2},{4,5},{5,4},{6,7},{7,6},{8,9},{9,8},{10,11... | collective-permute-start | bytes 2101256 | tf_op jit(solution)/shard_map/ppermute | solution.py:202
  6.9 1.8 %collective-permute-start.1 = (bf16[3,16,7424]{2,1,0:T(8,128)(2,1)}, bf16[3,16,7424]{2,1,0:T(8,128)(2,1)}, u32[]{:S(2)}, u32[]{:S(2)}) collective-permute-start(bf16[3,16,7424]{2,1,0:T(8,128)(2,1)} %get-tuple-element.27), channel_id=1, source_target_pairs={{1,2},{2,1},{3,0},{0,3},{5,6},{6,5},{7,4},{4,7},{9,10},{10,9},{11,... | collective-permute-start | bytes 2138120 | tf_op jit(solution)/shard_map/ppermute | solution.py:203
  8.7 3.5 %pack.5 = (bf16[3,16,7296]{2,1,0:T(8,128)(2,1)}, bf16[3,16,7424]{2,1,0:T(8,128)(2,1)}) custom-call(s32[1]{0:T(128)} %bitcast.spot_ref, s32[16,1]{1,0:T(8,128)} %copy.53.cycle_ref, bf16[2,45,16,720]{3,2,1,0:T(8,128)(2,1)} %bitcast.30, bf16[45,16,2880]{2,1,0:T(8,128)(2,1)} %tail_ref.15, bf16[45,16,2880]{2,1,0:T(8,128)(2,1)} %tail_ref.15, ...), custom_call_target="tpu_custom_call" | custom-call | bytes 3000000 | tf_op jit(solution)/shard_map/pack/pallas_call | solution.py:53
  13.1 2.2 %pack.6 = (bf16[2,16,7296]{2,1,0:T(8,128)(2,1)}, bf16[2,16,7424]{2,1,0:T(8,128)(2,1)}) custom-call(s32[1]{0:T(128)} %bitcast.spot_ref, s32[16,1]{1,0:T(8,128)} %copy.53.cycle_ref, bf16[2,45,16,720]{3,2,1,0:T(8,128)(2,1)} %bitcast.31, bf16[45,16,2880]{2,1,0:T(8,128)(2,1)} %tail_ref.15, bf16[45,16,2880]{2,1,0:T(8,128)(2,1)} %tail_ref.15, ...), custom_call_target="tpu_custom_call" | custom-call | bytes 2000000 | tf_op jit(solution)/shard_map/pack/pallas_call | solution.py:53
  16.9 4.3 %collective-permute-done.other_ref = bf16[3,16,7296]{2,1,0:T(8,128)(2,1)S(1)} collective-permute-done((bf16[3,16,7296]{2,1,0:T(8,128)(2,1)}, bf16[3,16,7296]{2,1,0:T(8,128)(2,1)S(1)}, u32[]{:S(2)}, u32[]{:S(2)}) %collective-permute-start) | collective-permute-done | bytes 700448 | tf_op jit(solution)/shard_map/ppermute | solution.py:202
  22.1 3.8 %collective-permute-start.5 = (bf16[2,16,7424]{2,1,0:T(8,128)(2,1)}, bf16[2,16,7424]{2,1,0:T(8,128)(2,1)S(1)}, u32[]{:S(2)}, u32[]{:S(2)}) collective-permute-start(bf16[2,16,7424]{2,1,0:T(8,128)(2,1)} %get-tuple-element.33), channel_id=1, source_target_pairs={{1,2},{2,1},{3,0},{0,3},{5,6},{6,5},{7,4},{4,7},{9,10},{10,9},{11,... | collective-permute-start | bytes 1425416 | tf_op jit(solution)/shard_map/ppermute | solution.py:203
  26.8 2.1 %pack.7 = (bf16[1,16,7296]{2,1,0:T(8,128)(2,1)}, bf16[1,16,7424]{2,1,0:T(8,128)(2,1)}) custom-call(s32[1]{0:T(128)} %bitcast.spot_ref, s32[16,1]{1,0:T(8,128)} %copy.53.cycle_ref, bf16[2,45,16,720]{3,2,1,0:T(8,128)(2,1)} %bitcast.32, bf16[45,16,2880]{2,1,0:T(8,128)(2,1)} %tail_ref.15, bf16[45,16,2880]{2,1,0:T(8,128)(2,1)} %tail_ref.15, ...), custom_call_target="tpu_custom_call" | custom-call | bytes 1000000 | tf_op jit(solution)/shard_map/pack/pallas_call | solution.py:53
  29.8 1.0 maximum_maximum_fusion
  30.8 5.4 %collective-permute-done.2.other_ref = bf16[3,16,7296]{2,1,0:T(8,128)(2,1)} collective-permute-done((bf16[3,16,7296]{2,1,0:T(8,128)(2,1)}, bf16[3,16,7296]{2,1,0:T(8,128)(2,1)}, u32[]{:S(2)}, u32[]{:S(2)}) %collective-permute-start.2) | collective-permute-done | bytes 700448 | tf_op jit(solution)/shard_map/ppermute | solution.py:202
  36.3 3.8 %collective-permute-start.8 = (bf16[1,16,7424]{2,1,0:T(8,128)(2,1)}, bf16[1,16,7424]{2,1,0:T(8,128)(2,1)S(1)}, u32[]{:S(2)}, u32[]{:S(2)}) collective-permute-start(bf16[1,16,7424]{2,1,0:T(8,128)(2,1)} %get-tuple-element.37), channel_id=1, source_target_pairs={{1,2},{2,1},{3,0},{0,3},{5,6},{6,5},{7,4},{4,7},{9,10},{10,9},{11,... | collective-permute-start | bytes 712712 | tf_op jit(solution)/shard_map/ppermute | solution.py:203
  40.2 2.2 %copy-done = bf16[45,16,2880]{2,1,0:T(8,128)(2,1)S(1)} copy-done((bf16[45,16,2880]{2,1,0:T(8,128)(2,1)S(1)}, bf16[45,16,2880]{2,1,0:T(8,128)(2,1)}, u32[]{:S(2)}) %copy-start) | copy-done | bytes 4147224
  42.4 1.1 copy-done.3
  43.5 4.5 %partial_sums.4 = (f32[15,16,96]{2,1,0:T(8,128)S(1)}, bf16[15,16,96]{2,1,0:T(8,128)(2,1)S(1)}) custom-call(s32[1]{0:T(128)} %bitcast.spot_ref, s32[45]{0:T(128)S(1)} %dynamic_slice.3.order_ref, f32[16,1]{1,0:T(8,128)S(1)} %copy.52.height_ref, s32[16,1]{1,0:T(8,128)S(1)} %copy-done.4, bf16[2,45,16,720]{3,2,1,0:T(8,128)(2,1)S(1)} %bitcast.33, ...), custom_call_target="tpu_custom_call" | custom-call | flops 188743680 | bytes 3000000 | tf_op jit(solution)/shard_map/partial_sums/pallas_call | solution.py:154
  48.8 4.4 %partial_sums.5 = (f32[15,16,96]{2,1,0:T(8,128)S(1)}, bf16[15,16,96]{2,1,0:T(8,128)(2,1)S(1)}) custom-call(s32[1]{0:T(128)} %bitcast.spot_ref, s32[45]{0:T(128)S(1)} %dynamic_slice.3.order_ref, f32[16,1]{1,0:T(8,128)S(1)} %copy.52.height_ref, s32[16,1]{1,0:T(8,128)S(1)} %copy-done.4, bf16[2,45,16,720]{3,2,1,0:T(8,128)(2,1)S(1)} %bitcast.35, ...), custom_call_target="tpu_custom_call" | custom-call | flops 188743680 | bytes 3000000 | tf_op jit(solution)/shard_map/partial_sums/pallas_call | solution.py:154
  53.1 2.2 %collective-permute-start.9 = (bf16[15,16,96]{2,1,0:T(8,128)(2,1)S(1)}, bf16[15,16,96]{2,1,0:T(8,128)(2,1)S(1)}, u32[]{:S(2)}, u32[]{:S(2)}) collective-permute-start(bf16[15,16,96]{2,1,0:T(8,128)(2,1)S(1)} %get-tuple-element.38), channel_id=1, source_target_pairs={{1,2},{2,1},{3,0},{0,3},{5,6},{6,5},{7,4},{4,7},{9,10},{10,9},{11,... | collective-permute-start | bytes 138248 | tf_op jit(solution)/shard_map/ppermute | solution.py:211
  56.3 3.3 %partial_sums.6 = (f32[10,16,96]{2,1,0:T(8,128)S(1)}, bf16[10,16,96]{2,1,0:T(8,128)(2,1)S(1)}) custom-call(s32[1]{0:T(128)} %bitcast.spot_ref, s32[45]{0:T(128)S(1)} %dynamic_slice.3.order_ref, f32[16,1]{1,0:T(8,128)S(1)} %copy.52.height_ref, s32[16,1]{1,0:T(8,128)S(1)} %copy-done.4, bf16[2,45,16,720]{3,2,1,0:T(8,128)(2,1)S(1)} %bitcast.36, ...), custom_call_target="tpu_custom_call" | custom-call | flops 125829120 | bytes 2000000 | tf_op jit(solution)/shard_map/partial_sums/pallas_call | solution.py:154
  59.6 1.9 %partial_sums.7 = (f32[5,16,96]{2,1,0:T(8,128)S(1)}, bf16[5,16,96]{2,1,0:T(8,128)(2,1)S(1)}) custom-call(s32[1]{0:T(128)} %bitcast.spot_ref, s32[45]{0:T(128)S(1)} %dynamic_slice.3.order_ref, f32[16,1]{1,0:T(8,128)S(1)} %copy.52.height_ref, s32[16,1]{1,0:T(8,128)S(1)} %copy-done.4, bf16[2,45,16,720]{3,2,1,0:T(8,128)(2,1)S(1)} %bitcast.37, ...), custom_call_target="tpu_custom_call" | custom-call | flops 62914560 | bytes 1000000 | tf_op jit(solution)/shard_map/partial_sums/pallas_call | solution.py:154
  61.6 2.4 %collective-permute-start.11 = (bf16[5,16,96]{2,1,0:T(8,128)(2,1)S(1)}, bf16[5,16,96]{2,1,0:T(8,128)(2,1)S(1)}, u32[]{:S(2)}, u32[]{:S(2)}) collective-permute-start(bf16[5,16,96]{2,1,0:T(8,128)(2,1)S(1)} %get-tuple-element.41), channel_id=1, source_target_pairs={{1,2},{2,1},{3,0},{0,3},{5,6},{6,5},{7,4},{4,7},{9,10},{10,9},{11,... | collective-permute-start | bytes 46088 | tf_op jit(solution)/shard_map/ppermute | solution.py:211
  64.4 1.1 collective-permute-done.11
  65.5 2.5 %collective-permute-done.10 = bf16[10,16,96]{2,1,0:T(8,128)(2,1)S(1)} collective-permute-done((bf16[10,16,96]{2,1,0:T(8,128)(2,1)S(1)}, bf16[10,16,96]{2,1,0:T(8,128)(2,1)S(1)}, u32[]{:S(2)}, u32[]{:S(2)}) %collective-permute-start.10) | collective-permute-done | bytes 30752 | tf_op jit(solution)/shard_map/ppermute | solution.py:211
  69.1 25.9 %all_to_all.10 = bf16[64,2,540]{2,1,0:T(2,128)(2,1)S(1)} all-to-all(bf16[64,2,540]{2,1,0:T(2,128)(2,1)S(1)} %copy.65), channel_id=1, replica_groups=mesh['ord'=64,'blk'=4] {'ord'}, dimensions={0} | all-to-all | bytes 276480 | tf_op jit(solution)/shard_map/all_to_all | solution.py:231
  97.6 17.1 %all_to_all.11 = bf16[64,90,12]{1,2,0:T(8,128)(2,1)S(1)} all-to-all(bf16[64,90,12]{1,2,0:T(8,128)(2,1)S(1)} %copy.67), channel_id=1, replica_groups=mesh['ord'=64,'blk'=4] {'ord'}, dimensions={0} | all-to-all | bytes 276480 | tf_op jit(solution)/shard_map/all_to_all | solution.py:241
  (51 shorter events, 12.1 us)
Async XLA Ops:
  4.8 16.4 %collective-permute-start = (bf16[3,16,7296]{2,1,0:T(8,128)(2,1)}, bf16[3,16,7296]{2,1,0:T(8,128)(2,1)S(1)}, u32[]{:S(2)}, u32[]{:S(2)}) collective-permute-start(bf16[3,16,7296]{2,1,0:T(8,128)(2,1)} %get-tuple-element.26.rest_0_), channel_id=1, source_target_pairs={{0,1},{1,0},{2,3},{3,2},{4,5},{5,4},{6,7},{7,6},{8,9},{9,8},{10,11... | collective-permute-start | bytes 2101256 | tf_op jit(solution)/shard_map/ppermute | solution.py:202
  6.9 33.2 %collective-permute-start.1 = (bf16[3,16,7424]{2,1,0:T(8,128)(2,1)}, bf16[3,16,7424]{2,1,0:T(8,128)(2,1)}, u32[]{:S(2)}, u32[]{:S(2)}) collective-permute-start(bf16[3,16,7424]{2,1,0:T(8,128)(2,1)} %get-tuple-element.27), channel_id=1, source_target_pairs={{1,2},{2,1},{3,0},{0,3},{5,6},{6,5},{7,4},{4,7},{9,10},{10,9},{11,... | collective-permute-start | bytes 2138120 | tf_op jit(solution)/shard_map/ppermute | solution.py:203
  12.1 24.1 %collective-permute-start.2 = (bf16[3,16,7296]{2,1,0:T(8,128)(2,1)}, bf16[3,16,7296]{2,1,0:T(8,128)(2,1)}, u32[]{:S(2)}, u32[]{:S(2)}) collective-permute-start(bf16[3,16,7296]{2,1,0:T(8,128)(2,1)} %get-tuple-element.29.rest_0_), channel_id=1, source_target_pairs={{0,1},{1,0},{2,3},{3,2},{4,5},{5,4},{6,7},{7,6},{8,9},{9,8},{10,11... | collective-permute-start | bytes 2101256 | tf_op jit(solution)/shard_map/ppermute | solution.py:202
  12.5 35.5 %collective-permute-start.3 = (bf16[3,16,7424]{2,1,0:T(8,128)(2,1)}, bf16[3,16,7424]{2,1,0:T(8,128)(2,1)S(1)}, u32[]{:S(2)}, u32[]{:S(2)}) collective-permute-start(bf16[3,16,7424]{2,1,0:T(8,128)(2,1)} %get-tuple-element.30), channel_id=1, source_target_pairs={{1,2},{2,1},{3,0},{0,3},{5,6},{6,5},{7,4},{4,7},{9,10},{10,9},{11,... | collective-permute-start | bytes 2138120 | tf_op jit(solution)/shard_map/ppermute | solution.py:203
  15.3 37.8 %collective-permute-start.4 = (bf16[2,16,7296]{2,1,0:T(8,128)(2,1)}, bf16[2,16,7296]{2,1,0:T(8,128)(2,1)}, u32[]{:S(2)}, u32[]{:S(2)}) collective-permute-start(bf16[2,16,7296]{2,1,0:T(8,128)(2,1)} %get-tuple-element.32.rest_0_), channel_id=1, source_target_pairs={{0,1},{1,0},{2,3},{3,2},{4,5},{5,4},{6,7},{7,6},{8,9},{9,8},{10,11... | collective-permute-start | bytes 1400840 | tf_op jit(solution)/shard_map/ppermute | solution.py:202
  21.3 0.9 copy-start.2
  22.1 33.4 %collective-permute-start.5 = (bf16[2,16,7424]{2,1,0:T(8,128)(2,1)}, bf16[2,16,7424]{2,1,0:T(8,128)(2,1)S(1)}, u32[]{:S(2)}, u32[]{:S(2)}) collective-permute-start(bf16[2,16,7424]{2,1,0:T(8,128)(2,1)} %get-tuple-element.33), channel_id=1, source_target_pairs={{1,2},{2,1},{3,0},{0,3},{5,6},{6,5},{7,4},{4,7},{9,10},{10,9},{11,... | collective-permute-start | bytes 1425416 | tf_op jit(solution)/shard_map/ppermute | solution.py:203
  26.8 2.9 %copy-start.5 = (f32[16]{0:T(128)S(1)}, f32[16]{0:T(128)}, u32[]{:S(2)}) copy-start(f32[16]{0:T(128)} %param.7) | copy-start | bytes 196
  26.8 13.3 %copy-start.1 = (bf16[2,16,45,720]{3,1,2,0:T(8,128)(2,1)S(1)}, bf16[2,16,45,720]{3,1,2,0:T(8,128)(2,1)}, u32[]{:S(2)}) copy-start(bf16[2,16,45,720]{3,1,2,0:T(8,128)(2,1)} %param.6) | copy-start | bytes 6220804
  26.8 13.3 %copy-start.4 = (s32[16,1]{1,0:T(8,128)S(1)}, s32[16,1]{1,0:T(8,128)}, u32[]{:S(2)}) copy-start(s32[16,1]{1,0:T(8,128)} %copy.53.cycle_ref) | copy-start | bytes 196
  36.3 23.4 %collective-permute-start.8 = (bf16[1,16,7424]{2,1,0:T(8,128)(2,1)}, bf16[1,16,7424]{2,1,0:T(8,128)(2,1)S(1)}, u32[]{:S(2)}, u32[]{:S(2)}) collective-permute-start(bf16[1,16,7424]{2,1,0:T(8,128)(2,1)} %get-tuple-element.37), channel_id=1, source_target_pairs={{1,2},{2,1},{3,0},{0,3},{5,6},{6,5},{7,4},{4,7},{9,10},{10,9},{11,... | collective-permute-start | bytes 712712 | tf_op jit(solution)/shard_map/ppermute | solution.py:203
  40.0 19.6 %collective-permute-start.7 = (bf16[1,16,7296]{2,1,0:T(8,128)(2,1)}, bf16[1,16,7296]{2,1,0:T(8,128)(2,1)S(1)}, u32[]{:S(2)}, u32[]{:S(2)}) collective-permute-start(bf16[1,16,7296]{2,1,0:T(8,128)(2,1)} %get-tuple-element.36), channel_id=1, source_target_pairs={{0,1},{1,0},{2,3},{3,2},{4,5},{5,4},{6,7},{7,6},{8,9},{9,8},{10,11... | collective-permute-start | bytes 700424 | tf_op jit(solution)/shard_map/ppermute | solution.py:202
  40.2 2.2 %copy-start = (bf16[45,16,2880]{2,1,0:T(8,128)(2,1)S(1)}, bf16[45,16,2880]{2,1,0:T(8,128)(2,1)}, u32[]{:S(2)}) copy-start(bf16[45,16,2880]{2,1,0:T(8,128)(2,1)} %tail_ref.15) | copy-start | bytes 12441604
  42.4 1.1 copy-start.3
  48.0 8.4 %collective-permute-start.6 = (bf16[15,16,96]{2,1,0:T(8,128)(2,1)S(1)}, bf16[15,16,96]{2,1,0:T(8,128)(2,1)S(1)}, u32[]{:S(2)}, u32[]{:S(2)}) collective-permute-start(bf16[15,16,96]{2,1,0:T(8,128)(2,1)S(1)} %get-tuple-element.34), channel_id=1, source_target_pairs={{1,2},{2,1},{3,0},{0,3},{5,6},{6,5},{7,4},{4,7},{9,10},{10,9},{11,... | collective-permute-start | bytes 138248 | tf_op jit(solution)/shard_map/ppermute | solution.py:211
  53.1 6.5 %collective-permute-start.9 = (bf16[15,16,96]{2,1,0:T(8,128)(2,1)S(1)}, bf16[15,16,96]{2,1,0:T(8,128)(2,1)S(1)}, u32[]{:S(2)}, u32[]{:S(2)}) collective-permute-start(bf16[15,16,96]{2,1,0:T(8,128)(2,1)S(1)} %get-tuple-element.38), channel_id=1, source_target_pairs={{1,2},{2,1},{3,0},{0,3},{5,6},{6,5},{7,4},{4,7},{9,10},{10,9},{11,... | collective-permute-start | bytes 138248 | tf_op jit(solution)/shard_map/ppermute | solution.py:211
  61.6 3.9 %collective-permute-start.11 = (bf16[5,16,96]{2,1,0:T(8,128)(2,1)S(1)}, bf16[5,16,96]{2,1,0:T(8,128)(2,1)S(1)}, u32[]{:S(2)}, u32[]{:S(2)}) collective-permute-start(bf16[5,16,96]{2,1,0:T(8,128)(2,1)S(1)} %get-tuple-element.41), channel_id=1, source_target_pairs={{1,2},{2,1},{3,0},{0,3},{5,6},{6,5},{7,4},{4,7},{9,10},{10,9},{11,... | collective-permute-start | bytes 46088 | tf_op jit(solution)/shard_map/ppermute | solution.py:211
  64.0 4.1 %collective-permute-start.10 = (bf16[10,16,96]{2,1,0:T(8,128)(2,1)S(1)}, bf16[10,16,96]{2,1,0:T(8,128)(2,1)S(1)}, u32[]{:S(2)}, u32[]{:S(2)}) collective-permute-start(bf16[10,16,96]{2,1,0:T(8,128)(2,1)S(1)} %get-tuple-element.40), channel_id=1, source_target_pairs={{1,2},{2,1},{3,0},{0,3},{5,6},{6,5},{7,4},{4,7},{9,10},{10,9},{11,... | collective-permute-start | bytes 92168 | tf_op jit(solution)/shard_map/ppermute | solution.py:211

commit v7 on v6

--- a/solution.py
+++ b/solution.py
@@ -28,8 +28,12 @@
 
 def pack_kernel(spot_ref, cycle_ref, gauss_ref, main_ref, tail_ref, *rest):
     gauss_out, panel_out = rest[-2:]
-    cycle = cycle_ref[...]
-    digits = jnp.concatenate([cycle // 64, cycle % 64], 1)
+    row = lax.broadcasted_iota(jnp.int32, (16, 2), 0)
+    column = lax.broadcasted_iota(jnp.int32, (16, 2), 1)
+    digits = jnp.zeros((16, 2), jnp.int32)
+    for i in range(16):
+        value = jnp.where(column == 0, cycle_ref[i] // 64, cycle_ref[i] % 64)
+        digits = jnp.where(row == i, value, digits)
     panel_out[0, :, CYCLE_LANE:CYCLE_LANE + 2] = digits.astype(jnp.float32).astype(jnp.bfloat16)
     for o in range(GROUP):
         for k in range(2):
@@ -57,13 +61,14 @@
         grid_spec=pltpu.PrefetchScalarGridSpec(
             num_scalar_prefetch=1,
             grid=(steps,),
-            in_specs=[pl.BlockSpec((16, 1), lambda i, spot: (0, 0)),
+            in_specs=[pl.BlockSpec(memory_space=pltpu.SMEM),
                       pl.BlockSpec((2, GROUP, 16, QUARTER), lambda i, spot: (0, i + skip, 0, 0))]
             + panel_specs(skip, lambda blk: 1 - blk // 2)
             + [pl.BlockSpec(memory_space=pl.ANY)] * len(after),
             out_specs=[pl.BlockSpec((1, 16, GAUSS_LANES), lambda i, spot: (i, 0, 0)),
                        pl.BlockSpec((1, 16, PANEL_LANES), lambda i, spot: (i, 0, 0))],
         ),
+        compiler_params=pltpu.CompilerParams(vmem_limit_bytes=10 << 20),
         cost_estimate=pl.CostEstimate(flops=0, bytes_accessed=count * 200000, transcendentals=0),
         name="pack",
     )(spot, cycle, own, panel, panel, *after)
@@ -90,8 +95,11 @@
         decay_ref[2] = jnp.exp(-(degree + 3.0) * height / ORDERS)
         digits = far_ref[0, :, CYCLE_LANE:CYCLE_LANE + 2].astype(jnp.float32)
         mates = digits[:, 0:1] * 64.0 + digits[:, 1:2]
-        cycles = jnp.concatenate([cycle_ref[...].astype(jnp.float32), mates], 0)
-        cycles = jnp.broadcast_to(cycles, (32, 128)).T[0:8, :]
+        cycles = jnp.broadcast_to(mates, (16, 128)).T[0:8, :]
+        cycles = jnp.concatenate([jnp.zeros((8, 16), jnp.float32), cycles], 1)
+        lane = lax.broadcasted_iota(jnp.int32, (8, 32), 1)
+        for i in range(16):
+            cycles = jnp.where(lane == i, cycle_ref[i].astype(jnp.float32), cycles)
         theta = math.pi * (cycles + 0.5) / ORDERS
         angle_ref[0] = jnp.cos(theta)
         angle_ref[1] = 1.0 / jnp.sin(theta)
@@ -147,25 +155,27 @@
         send_ref[o] = mixed[o][16:].astype(jnp.bfloat16)
 
 
-def partial_sums(spot, orders, height, cycle, own, other, panel, far, after, base, count):
+def partial_sums(spot, orders, height, cycle, own, other, panel, far, after, base, count, size, begun):
     skip = base // GROUP
+    into = begun[0].shape[0] // GROUP - count // GROUP if begun else 0
+    total = begun[0].shape[0] if begun else size
     smem = pl.BlockSpec(memory_space=pltpu.SMEM)
-    out = pl.BlockSpec((GROUP, 16, 96), lambda i, spot: (i, 0, 0))
+    out = pl.BlockSpec((GROUP, 16, 96), lambda i, spot: (i + into, 0, 0))
     return pl.pallas_call(
         functools.partial(sums_kernel, base=base),
-        out_shape=[jax.ShapeDtypeStruct((count, 16, 96), jnp.float32),
-                   jax.ShapeDtypeStruct((count, 16, 96), jnp.bfloat16)],
+        out_shape=[jax.ShapeDtypeStruct((total, 16, 96), jnp.float32),
+                   jax.ShapeDtypeStruct((total, 16, 96), jnp.bfloat16)],
+        input_output_aliases={9: 0, 10: 1} if begun else {},
         grid_spec=pltpu.PrefetchScalarGridSpec(
             num_scalar_prefetch=1,
             grid=(count // GROUP,),
             in_specs=[
-                smem, pl.BlockSpec((16, 1), lambda i, spot: (0, 0)),
-                pl.BlockSpec((16, 1), lambda i, spot: (0, 0)),
+                smem, pl.BlockSpec((16, 1), lambda i, spot: (0, 0)), smem,
                 pl.BlockSpec((2, GROUP, 16, QUARTER), lambda i, spot: (0, i + skip, 0, 0)),
                 pl.BlockSpec((1, 16, GAUSS_LANES), lambda i, spot: (i, 0, 0)),
             ] + panel_specs(skip, lambda blk: blk // 2)
             + [pl.BlockSpec((1, 16, PANEL_LANES), lambda i, spot: (i, 0, 0))]
-            + [pl.BlockSpec(memory_space=pl.ANY)] * len(after),
+            + [pl.BlockSpec(memory_space=pl.ANY)] * (len(begun) + len(after)),
             out_specs=[out, out],
             scratch_shapes=[
                 pltpu.VMEM((2, GROUP, 16, WIDE), jnp.bfloat16),
@@ -176,11 +186,11 @@
                 pltpu.VMEM((2, 8, 32), jnp.float32),
             ],
         ),
-        compiler_params=pltpu.CompilerParams(vmem_limit_bytes=24 << 20),
+        compiler_params=pltpu.CompilerParams(vmem_limit_bytes=16 << 20),
         cost_estimate=pl.CostEstimate(
             flops=count * 32 * 128 * WIDE * 2, bytes_accessed=count * 200000, transcendentals=0),
         name="partial_sums",
-    )(spot, orders, height, cycle, own, other, panel, panel, far, *after)
+    )(spot, orders, height, cycle, own, other, panel, panel, far, *begun, *after)
 
 
 def turn(phase, period):
@@ -193,22 +203,35 @@
     shells = height.shape[0]
     here = lax.axis_index("ord")
     spot = lax.axis_index("blk").astype(jnp.int32).reshape(1)
-    cycle = cycle_map[:, None]
     own = jnp.transpose(gauss, (0, 2, 1, 3))
+    own = pltpu.with_memory_space_constraint(own, pltpu.HBM)
+    panel = pltpu.with_memory_space_constraint(panel, pltpu.HBM)
     spans = list(zip(CHUNKS[:-1], CHUNKS[1:]))
-    arrived, packed = [], ()
-    for a, b in spans:
-        packed = pack(spot, cycle, own, panel, packed[:1], a, b - a)
-        arrived.append((lax.ppermute(packed[0], "blk", GAUSS_PAIRS),
-                        lax.ppermute(packed[1], "blk", PANEL_PAIRS)))
     orders_int = lax.dynamic_slice_in_dim(order_map, here * count, count, 0)
-    kept, added = [], []
-    for c, ((a, b), (other, far)) in enumerate(zip(spans, arrived)):
-        after = (kept[-1:] or [own]) + (added[c - 2:c - 1] if c >= 2 else [])
+    packed, kept, sent, added = [], [], [], []
+
+    def start(c):
+        a, b = spans[c]
+        after = [[], [], kept[0:1], kept[1:2]][c] + ([packed[-1][2]] if packed else [])
+        coef, part = pack(spot, cycle_map, own, panel, after, a, b - a)
+        packed.append((lax.ppermute(coef, "blk", GAUSS_PAIRS),
+                       lax.ppermute(part, "blk", PANEL_PAIRS), coef))
+
+    start(0)
+    start(1)
+    for c, (a, b) in enumerate(spans):
+        begun = [kept.pop(), sent.pop()] if c == 3 else []
+        size = CHUNKS[4] - CHUNKS[2] if c == 2 else b - a
+        after = kept[-1:] + (added[c - 2:c - 1] if c >= 2 else [])
         keep, send = partial_sums(
-            spot, orders_int, height[:, None], cycle, own, other, panel, far, after, a, b - a)
+            spot, orders_int, height[:, None], cycle_map, own, packed[c][0], panel, packed[c][1],
+            after, a, b - a, size, begun)
         kept.append(keep)
-        added.append(lax.ppermute(send, "blk", PANEL_PAIRS))
+        sent.append(send)
+        if c != 2:
+            added.append(lax.ppermute(send, "blk", PANEL_PAIRS))
+        if c < 2:
+            start(c + 2)
     total = jnp.concatenate(kept, 0) + jnp.concatenate(added, 0).astype(jnp.float32)
     total = lax.optimization_barrier(total.astype(jnp.bfloat16))
     split = (count, cycles, 3, 2, 4, shells // 4)

time: 116 us -> 112 us (0.966)
  waiting for transfers between devices: 14.2 us -> 19.1 us
  local copies, waits for them, and re-layouts: 10.4 us -> 5.56 us
  starting transfers between devices: 18.9 us -> 16.2 us
  other arithmetic: 2.45 us -> 0.86 us
    ppermute x8, waiting for transfers between devices: 9.78 us -> 15.5 us  [the longest x4 15.5 us: start(): lax.ppermute(coef, 'blk', GAUSS_PAIRS)]
    ppermute x8, starting transfers between devices: 13.1 us -> 9.06 us  [the longest x4 8.25 us: start(): lax.ppermute(part, 'blk', PANEL_PAIRS)]
    unnamed x14 -> x8, local copies, waits for them, and re-layouts: 4.2 us -> 0.69 us
    pallas_call x4, Pallas kernels: 11.3 us -> 9.81 us  [pack(): pl.pallas_call(pack_kernel, out_shape=[jax.ShapeDtypeStruct((steps, 16, G...]
    ppermute x4 -> x3, starting transfers between devices: 5.78 us -> 7.17 us  [body(): added.append(lax.ppermute(send, 'blk', PANEL_PAIRS))]
    broadcast_in_dim x1 -> x0, local copies, waits for them, and re-layouts: 1.32 us -> none  [body(): cycle = cycle_map[:, None]]
    ppermute x4 -> x3, waiting for transfers between devices: 4.45 us -> 3.58 us  [body(): added.append(lax.ppermute(send, 'blk', PANEL_PAIRS))]
  transfers between devices with their start and end apart: 12 -> 11, of which waited for: 5 -> 4; matrix products, arithmetic and copies ran while one was open for 3% -> 2% of each run, Pallas kernels for 17% -> 17%
where the time goes in v7:
time: 112 us; the launch traced here: 111 us
  blocking collectives  43.2 us (39%)
  Pallas kernels  24.8 us (22%)
  waiting for transfers between devices  19.1 us (17%)
  starting transfers between devices  16.2 us (14%)
  local copies, waits for them, and re-layouts  5.56 us (5%)
  matrix products  1.2 us (1%)
    all_to_all x1, blocking collectives, body(): spread = lax.all_to_all(chunk, 'ord', 0, 0, tiled=True).astype(jnp.float32)  26 us
    all_to_all x1, blocking collectives, body(): field = lax.all_to_all(field, 'ord', 0, 0, tiled=True)  17.1 us
    ppermute x4, waiting for transfers between devices, start(): lax.ppermute(coef, 'blk', GAUSS_PAIRS)  15.5 us
    pallas_call x4, Pallas kernels, partial_sums(): pl.pallas_call(functools.partial(sums_kernel, base=base), out_shape=[jax....  15 us
    pallas_call x4, Pallas kernels, pack(): pl.pallas_call(pack_kernel, out_shape=[jax.ShapeDtypeStruct((steps, 16, G...  9.81 us
    ppermute x4, starting transfers between devices, start(): lax.ppermute(part, 'blk', PANEL_PAIRS)  8.25 us
    ppermute x3, starting transfers between devices, body(): added.append(lax.ppermute(send, 'blk', PANEL_PAIRS))  7.17 us
    ppermute x3, waiting for transfers between devices, body(): added.append(lax.ppermute(send, 'blk', PANEL_PAIRS))  3.58 us
  transfers between devices with their start and end apart: 11, of which 4 were waited for; matrix products, arithmetic and copies ran while one was open for 2% of the time, Pallas kernels for 17%

profile of v7, /device:TPU:1, one launch (start us, length us, event | category | flops | bytes accessed | tf_op | source)
XLA Modules:
  0.0 111.1 jit_solution(10049348808171124647)
XLA Ops:
  0.7 3.6 %pack.4 = (bf16[3,16,7296]{2,1,0:T(8,128)(2,1)}, bf16[3,16,7424]{2,1,0:T(8,128)(2,1)}) custom-call(s32[1]{0:T(128)} %bitcast.spot_ref, s32[16]{0:T(128)S(1)} %copy-done, bf16[2,45,16,720]{3,2,1,0:T(8,128)(2,1)} %bitcast.28, bf16[45,16,2880]{2,1,0:T(8,128)(2,1)} %tail_ref.15, bf16[45,16,2880]{2,1,0:T(8,128)(2,1)} %tail_ref.15), custom_call_target="tpu_custom_call" | custom-call | bytes 3000000 | tf_op jit(solution)/shard_map/pack/pallas_call | solution.py:57
  4.2 3.3 %collective-permute-start.1 = (bf16[3,16,7424]{2,1,0:T(8,128)(2,1)}, bf16[3,16,7424]{2,1,0:T(8,128)(2,1)S(1)}, u32[]{:S(2)}, u32[]{:S(2)}) collective-permute-start(bf16[3,16,7424]{2,1,0:T(8,128)(2,1)} %get-tuple-element.27), channel_id=1, source_target_pairs={{1,2},{2,1},{3,0},{0,3},{5,6},{6,5},{7,4},{4,7},{9,10},{10,9},{11,... | collective-permute-start | bytes 2138120 | tf_op jit(solution)/shard_map/ppermute | solution.py:218
  7.6 3.4 %pack.5 = (bf16[3,16,7296]{2,1,0:T(8,128)(2,1)S(1)}, bf16[3,16,7424]{2,1,0:T(8,128)(2,1)}) custom-call(s32[1]{0:T(128)} %bitcast.spot_ref, s32[16]{0:T(128)S(1)} %copy-done, bf16[2,45,16,720]{3,2,1,0:T(8,128)(2,1)} %bitcast.29, bf16[45,16,2880]{2,1,0:T(8,128)(2,1)} %tail_ref.15, bf16[45,16,2880]{2,1,0:T(8,128)(2,1)} %tail_ref.15, ...), custom_call_target="tpu_custom_call" | custom-call | bytes 3000000 | tf_op jit(solution)/shard_map/pack/pallas_call | solution.py:57
  11.0 0.8 collective-permute-start.3
  12.4 0.8 slice.19
  13.2 0.8 dynamic_slice.3.order_ref
  14.1 9.9 %collective-permute-done.other_ref = bf16[3,16,7296]{2,1,0:T(8,128)(2,1)S(1)} collective-permute-done((bf16[3,16,7296]{2,1,0:T(8,128)(2,1)}, bf16[3,16,7296]{2,1,0:T(8,128)(2,1)S(1)}, u32[]{:S(2)}, u32[]{:S(2)}) %collective-permute-start) | collective-permute-done | bytes 700448 | tf_op jit(solution)/shard_map/ppermute | solution.py:217
  24.0 4.5 %partial_sums.4 = (f32[15,16,96]{2,1,0:T(8,128)S(1)}, bf16[15,16,96]{2,1,0:T(8,128)(2,1)S(1)}) custom-call(s32[1]{0:T(128)} %bitcast.spot_ref, s32[45]{0:T(128)S(1)} %dynamic_slice.3.order_ref, f32[16,1]{1,0:T(8,128)S(1)} %copy.29.height_ref, s32[16]{0:T(128)S(1)} %copy-done.1, bf16[2,45,16,720]{3,2,1,0:T(8,128)(2,1)} %bitcast.30, ...), custom_call_target="tpu_custom_call" | custom-call | flops 188743680 | bytes 3000000 | tf_op jit(solution)/shard_map/partial_sums/pallas_call | solution.py:164
  28.5 1.6 %pack.6 = (bf16[2,16,7296]{2,1,0:T(8,128)(2,1)S(1)}, bf16[2,16,7424]{2,1,0:T(8,128)(2,1)S(1)}) custom-call(s32[1]{0:T(128)} %bitcast.spot_ref, s32[16]{0:T(128)S(1)} %copy-done.1, bf16[2,45,16,720]{3,2,1,0:T(8,128)(2,1)} %bitcast.31, bf16[45,16,2880]{2,1,0:T(8,128)(2,1)} %tail_ref.15, bf16[45,16,2880]{2,1,0:T(8,128)(2,1)} %tail_ref.15, ...), custom_call_target="tpu_custom_call" | custom-call | bytes 2000000 | tf_op jit(solution)/shard_map/pack/pallas_call | solution.py:57
  30.3 1.9 %collective-permute-start.7 = (bf16[2,16,7424]{2,1,0:T(8,128)(2,1)S(1)}, bf16[2,16,7424]{2,1,0:T(8,128)(2,1)S(1)}, u32[]{:S(2)}, u32[]{:S(2)}) collective-permute-start(bf16[2,16,7424]{2,1,0:T(8,128)(2,1)S(1)} %get-tuple-element.35), channel_id=1, source_target_pairs={{1,2},{2,1},{3,0},{0,3},{5,6},{6,5},{7,4},{4,7},{9,10},{10,9},{11,... | collective-permute-start | bytes 1425416 | tf_op jit(solution)/shard_map/ppermute | solution.py:218
  32.6 0.9 collective-permute-start.8
  33.5 5.6 %collective-permute-done.2.other_ref = bf16[3,16,7296]{2,1,0:T(8,128)(2,1)S(1)} collective-permute-done((bf16[3,16,7296]{2,1,0:T(8,128)(2,1)S(1)}, bf16[3,16,7296]{2,1,0:T(8,128)(2,1)S(1)}, u32[]{:S(2)}, u32[]{:S(2)}) %collective-permute-start.2) | collective-permute-done | bytes 700448 | tf_op jit(solution)/shard_map/ppermute | solution.py:217
  39.0 4.5 %partial_sums.5 = (f32[15,16,96]{2,1,0:T(8,128)S(1)}, bf16[15,16,96]{2,1,0:T(8,128)(2,1)S(1)}) custom-call(s32[1]{0:T(128)} %bitcast.spot_ref, s32[45]{0:T(128)S(1)} %dynamic_slice.3.order_ref, f32[16,1]{1,0:T(8,128)S(1)} %copy.29.height_ref, s32[16]{0:T(128)S(1)} %copy-done.1, bf16[2,45,16,720]{3,2,1,0:T(8,128)(2,1)} %bitcast.32, ...), custom_call_target="tpu_custom_call" | custom-call | flops 188743680 | bytes 3000000 | tf_op jit(solution)/shard_map/partial_sums/pallas_call | solution.py:164
  43.5 1.2 %pack.7 = (bf16[1,16,7296]{2,1,0:T(8,128)(2,1)S(1)}, bf16[1,16,7424]{2,1,0:T(8,128)(2,1)S(1)}) custom-call(s32[1]{0:T(128)} %bitcast.spot_ref, s32[16]{0:T(128)S(1)} %copy-done.1, bf16[2,45,16,720]{3,2,1,0:T(8,128)(2,1)} %bitcast.33, bf16[45,16,2880]{2,1,0:T(8,128)(2,1)} %tail_ref.15, bf16[45,16,2880]{2,1,0:T(8,128)(2,1)} %tail_ref.15, ...), custom_call_target="tpu_custom_call" | custom-call | bytes 1000000 | tf_op jit(solution)/shard_map/pack/pallas_call | solution.py:57
  44.8 2.2 %collective-permute-start.5 = (bf16[1,16,7424]{2,1,0:T(8,128)(2,1)S(1)}, bf16[1,16,7424]{2,1,0:T(8,128)(2,1)S(1)}, u32[]{:S(2)}, u32[]{:S(2)}) collective-permute-start(bf16[1,16,7424]{2,1,0:T(8,128)(2,1)S(1)} %get-tuple-element.34), channel_id=1, source_target_pairs={{1,2},{2,1},{3,0},{0,3},{5,6},{6,5},{7,4},{4,7},{9,10},{10,9},{11,... | collective-permute-start | bytes 712712 | tf_op jit(solution)/shard_map/ppermute | solution.py:218
  47.1 2.0 %collective-permute-done.8.rest_1_ = bf16[15,16,96]{2,1,0:T(8,128)(2,1)S(1)} collective-permute-done((bf16[15,16,96]{2,1,0:T(8,128)(2,1)S(1)}, bf16[15,16,96]{2,1,0:T(8,128)(2,1)S(1)}, u32[]{:S(2)}, u32[]{:S(2)}) %collective-permute-start.8) | collective-permute-done | bytes 46112 | tf_op jit(solution)/shard_map/ppermute | solution.py:232
  49.2 3.4 %collective-permute-start.9 = (bf16[15,16,96]{2,1,0:T(8,128)(2,1)S(1)}, bf16[15,16,96]{2,1,0:T(8,128)(2,1)S(1)}, u32[]{:S(2)}, u32[]{:S(2)}) collective-permute-start(bf16[15,16,96]{2,1,0:T(8,128)(2,1)S(1)} %get-tuple-element.39), channel_id=1, source_target_pairs={{1,2},{2,1},{3,0},{0,3},{5,6},{6,5},{7,4},{4,7},{9,10},{10,9},{11,... | collective-permute-start | bytes 138248 | tf_op jit(solution)/shard_map/ppermute | solution.py:232
  52.7 3.5 %partial_sums.6 = (f32[15,16,96]{2,1,0:T(8,128)S(1)}, bf16[15,16,96]{2,1,0:T(8,128)(2,1)S(1)}) custom-call(s32[1]{0:T(128)} %bitcast.spot_ref, s32[45]{0:T(128)S(1)} %dynamic_slice.3.order_ref, f32[16,1]{1,0:T(8,128)S(1)} %copy.29.height_ref, s32[16]{0:T(128)S(1)} %copy-done.1, bf16[2,45,16,720]{3,2,1,0:T(8,128)(2,1)} %bitcast.34, ...), custom_call_target="tpu_custom_call" | custom-call | flops 125829120 | bytes 2000000 | tf_op jit(solution)/shard_map/partial_sums/pallas_call | solution.py:164
  56.2 2.5 %partial_sums.7 = (f32[15,16,96]{2,1,0:T(8,128)S(1)}, bf16[15,16,96]{2,1,0:T(8,128)(2,1)S(1)}) custom-call(s32[1]{0:T(128)} %bitcast.spot_ref, s32[45]{0:T(128)S(1)} %dynamic_slice.3.order_ref, f32[16,1]{1,0:T(8,128)S(1)} %copy.29.height_ref, s32[16]{0:T(128)S(1)} %copy-done.1, ...), custom_call_target="tpu_custom_call", output_to_operand_aliasing={{0}: (9, {}), {1}: (10, {})} | custom-call | flops 62914560 | bytes 1000000 | tf_op jit(solution)/shard_map/partial_sums/pallas_call | solution.py:164
  58.8 2.9 %collective-permute-start.10 = (bf16[15,16,96]{2,1,0:T(8,128)(2,1)S(1)}, bf16[15,16,96]{2,1,0:T(8,128)(2,1)S(1)}, u32[]{:S(2)}, u32[]{:S(2)}) collective-permute-start(bf16[15,16,96]{2,1,0:T(8,128)(2,1)S(1)} %get-tuple-element.41), channel_id=1, source_target_pairs={{1,2},{2,1},{3,0},{0,3},{5,6},{6,5},{7,4},{4,7},{9,10},{10,9},{11,... | collective-permute-start | bytes 138248 | tf_op jit(solution)/shard_map/ppermute | solution.py:232
  61.7 1.5 %collective-permute-done.10 = bf16[15,16,96]{2,1,0:T(8,128)(2,1)S(1)} collective-permute-done((bf16[15,16,96]{2,1,0:T(8,128)(2,1)S(1)}, bf16[15,16,96]{2,1,0:T(8,128)(2,1)S(1)}, u32[]{:S(2)}, u32[]{:S(2)}) %collective-permute-start.10) | collective-permute-done | bytes 46112 | tf_op jit(solution)/shard_map/ppermute | solution.py:232
  64.3 26.0 %all_to_all.10 = bf16[64,2,540]{2,1,0:T(2,128)(2,1)S(1)} all-to-all(bf16[64,2,540]{2,1,0:T(2,128)(2,1)S(1)} %copy.35), channel_id=1, replica_groups=mesh['ord'=64,'blk'=4] {'ord'}, dimensions={0} | all-to-all | bytes 276480 | tf_op jit(solution)/shard_map/all_to_all | solution.py:254
  92.9 17.1 %all_to_all.11 = bf16[64,90,12]{1,2,0:T(8,128)(2,1)S(1)} all-to-all(bf16[64,90,12]{1,2,0:T(8,128)(2,1)S(1)} %copy.37), channel_id=1, replica_groups=mesh['ord'=64,'blk'=4] {'ord'}, dimensions={0} | all-to-all | bytes 276480 | tf_op jit(solution)/shard_map/all_to_all | solution.py:264
  110.3 0.8 copy.40
  (42 shorter events, 6.0 us)
Async XLA Ops:
  0.0 0.7 copy-start
  4.2 19.8 %collective-permute-start.1 = (bf16[3,16,7424]{2,1,0:T(8,128)(2,1)}, bf16[3,16,7424]{2,1,0:T(8,128)(2,1)S(1)}, u32[]{:S(2)}, u32[]{:S(2)}) collective-permute-start(bf16[3,16,7424]{2,1,0:T(8,128)(2,1)} %get-tuple-element.27), channel_id=1, source_target_pairs={{1,2},{2,1},{3,0},{0,3},{5,6},{6,5},{7,4},{4,7},{9,10},{10,9},{11,... | collective-permute-start | bytes 2138120 | tf_op jit(solution)/shard_map/ppermute | solution.py:218
  7.6 6.4 %copy-start.2 = (f32[16]{0:T(128)S(1)}, f32[16]{0:T(128)}, u32[]{:S(2)}) copy-start(f32[16]{0:T(128)} %param.7) | copy-start | bytes 196
  7.6 16.5 %copy-start.1 = (s32[16]{0:T(128)S(1)}, s32[16]{0:T(128)}, u32[]{:S(2)}) copy-start(s32[16]{0:T(128)} %cycle_ref.15) | copy-start | bytes 196
  7.6 16.5 %collective-permute-start = (bf16[3,16,7296]{2,1,0:T(8,128)(2,1)}, bf16[3,16,7296]{2,1,0:T(8,128)(2,1)S(1)}, u32[]{:S(2)}, u32[]{:S(2)}) collective-permute-start(bf16[3,16,7296]{2,1,0:T(8,128)(2,1)} %get-tuple-element.26.rest_0_), channel_id=1, source_target_pairs={{0,1},{1,0},{2,3},{3,2},{4,5},{5,4},{6,7},{7,6},{8,9},{9,8},{10,11... | collective-permute-start | bytes 2101256 | tf_op jit(solution)/shard_map/ppermute | solution.py:217
  11.0 28.1 %collective-permute-start.3 = (bf16[3,16,7424]{2,1,0:T(8,128)(2,1)}, bf16[3,16,7424]{2,1,0:T(8,128)(2,1)S(1)}, u32[]{:S(2)}, u32[]{:S(2)}) collective-permute-start(bf16[3,16,7424]{2,1,0:T(8,128)(2,1)} %get-tuple-element.30), channel_id=1, source_target_pairs={{1,2},{2,1},{3,0},{0,3},{5,6},{6,5},{7,4},{4,7},{9,10},{10,9},{11,... | collective-permute-start | bytes 2138120 | tf_op jit(solution)/shard_map/ppermute | solution.py:218
  11.7 27.3 %collective-permute-start.2 = (bf16[3,16,7296]{2,1,0:T(8,128)(2,1)S(1)}, bf16[3,16,7296]{2,1,0:T(8,128)(2,1)S(1)}, u32[]{:S(2)}, u32[]{:S(2)}) collective-permute-start(bf16[3,16,7296]{2,1,0:T(8,128)(2,1)S(1)} %get-tuple-element.29.rest_1_), channel_id=1, source_target_pairs={{0,1},{1,0},{2,3},{3,2},{4,5},{5,4},{6,7},{7,6},{8,9},{9,8},{10,11... | collective-permute-start | bytes 2101256 | tf_op jit(solution)/shard_map/ppermute | solution.py:217
  30.1 22.6 %collective-permute-start.6 = (bf16[2,16,7296]{2,1,0:T(8,128)(2,1)S(1)}, bf16[2,16,7296]{2,1,0:T(8,128)(2,1)S(1)}, u32[]{:S(2)}, u32[]{:S(2)}) collective-permute-start(bf16[2,16,7296]{2,1,0:T(8,128)(2,1)S(1)} %get-tuple-element.32.rest_1_), channel_id=1, source_target_pairs={{0,1},{1,0},{2,3},{3,2},{4,5},{5,4},{6,7},{7,6},{8,9},{9,8},{10,11... | collective-permute-start | bytes 1400840 | tf_op jit(solution)/shard_map/ppermute | solution.py:217
  30.3 22.4 %collective-permute-start.7 = (bf16[2,16,7424]{2,1,0:T(8,128)(2,1)S(1)}, bf16[2,16,7424]{2,1,0:T(8,128)(2,1)S(1)}, u32[]{:S(2)}, u32[]{:S(2)}) collective-permute-start(bf16[2,16,7424]{2,1,0:T(8,128)(2,1)S(1)} %get-tuple-element.35), channel_id=1, source_target_pairs={{1,2},{2,1},{3,0},{0,3},{5,6},{6,5},{7,4},{4,7},{9,10},{10,9},{11,... | collective-permute-start | bytes 1425416 | tf_op jit(solution)/shard_map/ppermute | solution.py:218
  32.6 16.6 %collective-permute-start.8 = (bf16[15,16,96]{2,1,0:T(8,128)(2,1)S(1)}, bf16[15,16,96]{2,1,0:T(8,128)(2,1)S(1)}, u32[]{:S(2)}, u32[]{:S(2)}) collective-permute-start(bf16[15,16,96]{2,1,0:T(8,128)(2,1)S(1)} %get-tuple-element.36), channel_id=1, source_target_pairs={{1,2},{2,1},{3,0},{0,3},{5,6},{6,5},{7,4},{4,7},{9,10},{10,9},{11,... | collective-permute-start | bytes 138248 | tf_op jit(solution)/shard_map/ppermute | solution.py:232
  44.8 11.5 %collective-permute-start.5 = (bf16[1,16,7424]{2,1,0:T(8,128)(2,1)S(1)}, bf16[1,16,7424]{2,1,0:T(8,128)(2,1)S(1)}, u32[]{:S(2)}, u32[]{:S(2)}) collective-permute-start(bf16[1,16,7424]{2,1,0:T(8,128)(2,1)S(1)} %get-tuple-element.34), channel_id=1, source_target_pairs={{1,2},{2,1},{3,0},{0,3},{5,6},{6,5},{7,4},{4,7},{9,10},{10,9},{11,... | collective-permute-start | bytes 712712 | tf_op jit(solution)/shard_map/ppermute | solution.py:218
  47.0 9.2 %collective-permute-start.4 = (bf16[1,16,7296]{2,1,0:T(8,128)(2,1)S(1)}, bf16[1,16,7296]{2,1,0:T(8,128)(2,1)S(1)}, u32[]{:S(2)}, u32[]{:S(2)}) collective-permute-start(bf16[1,16,7296]{2,1,0:T(8,128)(2,1)S(1)} %get-tuple-element.33), channel_id=1, source_target_pairs={{0,1},{1,0},{2,3},{3,2},{4,5},{5,4},{6,7},{7,6},{8,9},{9,8},{10,11... | collective-permute-start | bytes 700424 | tf_op jit(solution)/shard_map/ppermute | solution.py:217
  49.2 7.0 %collective-permute-start.9 = (bf16[15,16,96]{2,1,0:T(8,128)(2,1)S(1)}, bf16[15,16,96]{2,1,0:T(8,128)(2,1)S(1)}, u32[]{:S(2)}, u32[]{:S(2)}) collective-permute-start(bf16[15,16,96]{2,1,0:T(8,128)(2,1)S(1)} %get-tuple-element.39), channel_id=1, source_target_pairs={{1,2},{2,1},{3,0},{0,3},{5,6},{6,5},{7,4},{4,7},{9,10},{10,9},{11,... | collective-permute-start | bytes 138248 | tf_op jit(solution)/shard_map/ppermute | solution.py:232
  58.8 4.5 %collective-permute-start.10 = (bf16[15,16,96]{2,1,0:T(8,128)(2,1)S(1)}, bf16[15,16,96]{2,1,0:T(8,128)(2,1)S(1)}, u32[]{:S(2)}, u32[]{:S(2)}) collective-permute-start(bf16[15,16,96]{2,1,0:T(8,128)(2,1)S(1)} %get-tuple-element.41), channel_id=1, source_target_pairs={{1,2},{2,1},{3,0},{0,3},{5,6},{6,5},{7,4},{4,7},{9,10},{10,9},{11,... | collective-permute-start | bytes 138248 | tf_op jit(solution)/shard_map/ppermute | solution.py:232

commit v8 on v7

--- a/solution.py
+++ b/solution.py
@@ -26,22 +26,27 @@
 PANEL_PAIRS = [(1, 2), (2, 1), (3, 0), (0, 3)]
 
 
-def pack_kernel(spot_ref, cycle_ref, gauss_ref, main_ref, tail_ref, *rest):
-    gauss_out, panel_out = rest[-2:]
+def pack_panel(spot_ref, cycle_ref, main_ref, tail_ref, *rest):
+    out_ref = rest[-1]
     row = lax.broadcasted_iota(jnp.int32, (16, 2), 0)
     column = lax.broadcasted_iota(jnp.int32, (16, 2), 1)
     digits = jnp.zeros((16, 2), jnp.int32)
     for i in range(16):
         value = jnp.where(column == 0, cycle_ref[i] // 64, cycle_ref[i] % 64)
         digits = jnp.where(row == i, value, digits)
-    panel_out[0, :, CYCLE_LANE:CYCLE_LANE + 2] = digits.astype(jnp.float32).astype(jnp.bfloat16)
+    out_ref[0, :, CYCLE_LANE:CYCLE_LANE + 2] = digits.astype(jnp.float32).astype(jnp.bfloat16)
+    for o in range(GROUP):
+        out_ref[0, :, START * o:START * (o + 1)] = main_ref[o]
+        out_ref[0, :, PANEL_TAIL + 64 * o:PANEL_TAIL + 64 * (o + 1)] = tail_ref[o, :, 0:64]
+
+
+def pack_gauss(gauss_ref, *rest):
+    out_ref = rest[-1]
     for o in range(GROUP):
         for k in range(2):
             j = k * GROUP + o
-            gauss_out[0, :, 640 * j:640 * (j + 1)] = gauss_ref[k, o, :, 0:640]
-            gauss_out[0, :, GAUSS_TAIL + 80 * j:GAUSS_TAIL + 80 * (j + 1)] = gauss_ref[k, o, :, 640:720]
-        panel_out[0, :, START * o:START * (o + 1)] = main_ref[o]
-        panel_out[0, :, PANEL_TAIL + 64 * o:PANEL_TAIL + 64 * (o + 1)] = tail_ref[o, :, 0:64]
+            out_ref[0, :, 640 * j:640 * (j + 1)] = gauss_ref[k, o, :, 0:640]
+            out_ref[0, :, GAUSS_TAIL + 80 * j:GAUSS_TAIL + 80 * (j + 1)] = gauss_ref[k, o, :, 640:720]
 
 
 def panel_specs(skip, upper):
@@ -51,32 +56,43 @@
     ]
 
 
-def pack(spot, cycle, own, panel, after, base, count):
-    skip = base // GROUP
+def packed_panel(spot, cycle, panel, after, base, count):
     steps = count // GROUP
     return pl.pallas_call(
-        pack_kernel,
-        out_shape=[jax.ShapeDtypeStruct((steps, 16, GAUSS_LANES), jnp.bfloat16),
-                   jax.ShapeDtypeStruct((steps, 16, PANEL_LANES), jnp.bfloat16)],
+        pack_panel,
+        out_shape=jax.ShapeDtypeStruct((steps, 16, PANEL_LANES), jnp.bfloat16),
         grid_spec=pltpu.PrefetchScalarGridSpec(
             num_scalar_prefetch=1,
             grid=(steps,),
-            in_specs=[pl.BlockSpec(memory_space=pltpu.SMEM),
-                      pl.BlockSpec((2, GROUP, 16, QUARTER), lambda i, spot: (0, i + skip, 0, 0))]
-            + panel_specs(skip, lambda blk: 1 - blk // 2)
+            in_specs=[pl.BlockSpec(memory_space=pltpu.SMEM)]
+            + panel_specs(base // GROUP, lambda blk: 1 - blk // 2)
             + [pl.BlockSpec(memory_space=pl.ANY)] * len(after),
-            out_specs=[pl.BlockSpec((1, 16, GAUSS_LANES), lambda i, spot: (i, 0, 0)),
-                       pl.BlockSpec((1, 16, PANEL_LANES), lambda i, spot: (i, 0, 0))],
+            out_specs=pl.BlockSpec((1, 16, PANEL_LANES), lambda i, spot: (i, 0, 0)),
         ),
         compiler_params=pltpu.CompilerParams(vmem_limit_bytes=10 << 20),
-        cost_estimate=pl.CostEstimate(flops=0, bytes_accessed=count * 200000, transcendentals=0),
-        name="pack",
-    )(spot, cycle, own, panel, panel, *after)
-
-
-def sums_kernel(spot_ref, order_ref, height_ref, cycle_ref, own_ref, other_ref, main_ref, tail_ref,
+        cost_estimate=pl.CostEstimate(flops=0, bytes_accessed=count * 100000, transcendentals=0),
+        name="pack_panel",
+    )(spot, cycle, panel, panel, *after)
+
+
+def packed_gauss(own, after, base, count):
+    steps, skip = count // GROUP, base // GROUP
+    return pl.pallas_call(
+        pack_gauss,
+        out_shape=jax.ShapeDtypeStruct((steps, 16, GAUSS_LANES), jnp.bfloat16),
+        grid=(steps,),
+        in_specs=[pl.BlockSpec((2, GROUP, 16, QUARTER), lambda i: (0, i + skip, 0, 0))]
+        + [pl.BlockSpec(memory_space=pl.ANY)] * len(after),
+        out_specs=pl.BlockSpec((1, 16, GAUSS_LANES), lambda i: (i, 0, 0)),
+        compiler_params=pltpu.CompilerParams(vmem_limit_bytes=10 << 20),
+        cost_estimate=pl.CostEstimate(flops=0, bytes_accessed=count * 100000, transcendentals=0),
+        name="pack_gauss",
+    )(own, *after)
+
+
+def sums_kernel(spot_ref, order_ref, decay_ref, cycle_ref, own_ref, other_ref, main_ref, tail_ref,
                 far_ref, *rest, base):
-    keep_ref, send_ref, gs_ref, gn_ref, decay_ref, table_ref, mate_ref, angle_ref = rest[-8:]
+    keep_ref, send_ref, gs_ref, gn_ref, table_ref, mate_ref, angle_ref = rest[-7:]
     step = pl.program_id(0)
     half = spot_ref[0] // 2
     odd = spot_ref[0] % 2 == 1
@@ -88,11 +104,6 @@
         gs_ref[...] = jnp.zeros_like(gs_ref)
         gn_ref[...] = jnp.zeros_like(gn_ref)
         table_ref[...] = jnp.zeros_like(table_ref)
-        height = height_ref[...]
-        here = jnp.exp(-(degree + 2.0) * height / ORDERS)
-        decay_ref[0] = here
-        decay_ref[1] = here * (degree + 1.0)
-        decay_ref[2] = jnp.exp(-(degree + 3.0) * height / ORDERS)
         digits = far_ref[0, :, CYCLE_LANE:CYCLE_LANE + 2].astype(jnp.float32)
         mates = digits[:, 0:1] * 64.0 + digits[:, 1:2]
         cycles = jnp.broadcast_to(mates, (16, 128)).T[0:8, :]
@@ -155,9 +166,9 @@
         send_ref[o] = mixed[o][16:].astype(jnp.bfloat16)
 
 
-def partial_sums(spot, orders, height, cycle, own, other, panel, far, after, base, count, size, begun):
+def partial_sums(spot, orders, decay, cycle, own, other, panel, far, after, base, count, place, size, begun):
     skip = base // GROUP
-    into = begun[0].shape[0] // GROUP - count // GROUP if begun else 0
+    into = place // GROUP
     total = begun[0].shape[0] if begun else size
     smem = pl.BlockSpec(memory_space=pltpu.SMEM)
     out = pl.BlockSpec((GROUP, 16, 96), lambda i, spot: (i + into, 0, 0))
@@ -170,7 +181,7 @@
             num_scalar_prefetch=1,
             grid=(count // GROUP,),
             in_specs=[
-                smem, pl.BlockSpec((16, 1), lambda i, spot: (0, 0)), smem,
+                smem, pl.BlockSpec((3, 16, WIDE), lambda i, spot: (0, 0, 0)), smem,
                 pl.BlockSpec((2, GROUP, 16, QUARTER), lambda i, spot: (0, i + skip, 0, 0)),
                 pl.BlockSpec((1, 16, GAUSS_LANES), lambda i, spot: (i, 0, 0)),
             ] + panel_specs(skip, lambda blk: blk // 2)
@@ -180,7 +191,6 @@
             scratch_shapes=[
                 pltpu.VMEM((2, GROUP, 16, WIDE), jnp.bfloat16),
                 pltpu.VMEM((2, GROUP, 16, WIDE), jnp.bfloat16),
-                pltpu.VMEM((3, 16, WIDE), jnp.float32),
                 pltpu.VMEM((GROUP, 32, WIDE), jnp.bfloat16),
                 pltpu.VMEM((2, GROUP, 16, QUARTER), jnp.bfloat16),
                 pltpu.VMEM((2, 8, 32), jnp.float32),
@@ -190,7 +200,7 @@
         cost_estimate=pl.CostEstimate(
             flops=count * 32 * 128 * WIDE * 2, bytes_accessed=count * 200000, transcendentals=0),
         name="partial_sums",
-    )(spot, orders, height, cycle, own, other, panel, panel, far, *begun, *after)
+    )(spot, orders, decay, cycle, own, other, panel, panel, far, *begun, *after)
 
 
 def turn(phase, period):
@@ -208,27 +218,32 @@
     panel = pltpu.with_memory_space_constraint(panel, pltpu.HBM)
     spans = list(zip(CHUNKS[:-1], CHUNKS[1:]))
     orders_int = lax.dynamic_slice_in_dim(order_map, here * count, count, 0)
+    degree = (spot // 2 * START + jnp.arange(WIDE)).astype(jnp.float32)[None, :]
+    here_ = jnp.exp(-(degree + 2.0) * height[:, None] / ORDERS)
+    next_ = jnp.exp(-(degree + 3.0) * height[:, None] / ORDERS)
+    decay = jnp.stack([here_, here_ * (degree + 1.0), next_])
     packed, kept, sent, added = [], [], [], []
 
     def start(c):
         a, b = spans[c]
-        after = [[], [], kept[0:1], kept[1:2]][c] + ([packed[-1][2]] if packed else [])
-        coef, part = pack(spot, cycle_map, own, panel, after, a, b - a)
-        packed.append((lax.ppermute(coef, "blk", GAUSS_PAIRS),
-                       lax.ppermute(part, "blk", PANEL_PAIRS), coef))
+        after = (kept[-1:] if c >= 2 else []) + ([packed[-1][2]] if packed else [])
+        part = packed_panel(spot, cycle_map, panel, after, a, b - a)
+        far = lax.ppermute(part, "blk", PANEL_PAIRS)
+        coef = packed_gauss(own, [part], a, b - a)
+        packed.append((lax.ppermute(coef, "blk", GAUSS_PAIRS), far, coef))
 
     start(0)
     start(1)
     for c, (a, b) in enumerate(spans):
-        begun = [kept.pop(), sent.pop()] if c == 3 else []
-        size = CHUNKS[4] - CHUNKS[2] if c == 2 else b - a
-        after = kept[-1:] + (added[c - 2:c - 1] if c >= 2 else [])
+        begun = [kept.pop(), sent.pop()] if c >= 2 else []
+        size = CHUNKS[4] - CHUNKS[1] if c == 1 else b - a
+        after = kept[-1:] + (added if c == 3 else [])
         keep, send = partial_sums(
-            spot, orders_int, height[:, None], cycle_map, own, packed[c][0], panel, packed[c][1],
-            after, a, b - a, size, begun)
+            spot, orders_int, decay, cycle_map, own, packed[c][0], panel, packed[c][1],
+            after, a, b - a, a - CHUNKS[1] if c else 0, size, begun)
         kept.append(keep)
         sent.append(send)
-        if c != 2:
+        if c in (0, 3):
             added.append(lax.ppermute(send, "blk", PANEL_PAIRS))
         if c < 2:
             start(c + 2)

time: 112 us -> 111 us (level)
  starting transfers between devices: 16.2 us -> 9.27 us
  other arithmetic: 0.86 us -> 5.25 us
  waiting for transfers between devices: 19.1 us -> 15.1 us
  Pallas kernels: 24.8 us -> 28.7 us
  blocking collectives: 43.2 us -> 44.8 us
    ppermute x8, waiting for transfers between devices: 15.5 us -> 10.6 us  [the longest x4 10.6 us: start(): packed.append((lax.ppermute(coef, 'blk', GAUSS_PAIRS), far, coef))]
    pallas_call x4 -> x8, Pallas kernels: 9.81 us -> 13.3 us  [the longest x4 6.95 us: packed_panel(): pl.pallas_call(pack_panel, out_shape=jax.ShapeDtypeStruct((steps, 16, PAN...]
    ppermute x3 -> x2, starting transfers between devices: 7.17 us -> 3.68 us  [body(): added.append(lax.ppermute(send, 'blk', PANEL_PAIRS))]
    ppermute x8, starting transfers between devices: 9.06 us -> 5.59 us  [the longest x4 4.4 us: start(): far = lax.ppermute(part, 'blk', PANEL_PAIRS)]
    all_to_all x1, blocking collectives: 26 us -> 27.7 us  [body(): spread = lax.all_to_all(chunk, 'ord', 0, 0, tiled=True).astype(jnp.float32)]
    exp x0 -> x1, other arithmetic: none -> 1.5 us  [body(): here_ = jnp.exp(-(degree + 2.0) * height[:, None] / ORDERS)]
    ppermute x3 -> x2, waiting for transfers between devices: 3.58 us -> 4.42 us  [body(): added.append(lax.ppermute(send, 'blk', PANEL_PAIRS))]
  transfers between devices with their start and end apart: 11 -> 10, of which waited for: 4 -> 4; matrix products, arithmetic and copies ran while one was open for 2% -> 7% of each run, Pallas kernels for 17% -> 22%
where the time goes in v8:
time: 111 us
  blocking collectives  44.8 us (40%)
  Pallas kernels  28.7 us (26%)
  waiting for transfers between devices  15.1 us (14%)
  starting transfers between devices  9.27 us (8%)
  local copies, waits for them, and re-layouts  6.07 us (5%)
  other arithmetic  5.25 us (5%)
  matrix products  1.2 us (1%)
    all_to_all x1, blocking collectives, body(): spread = lax.all_to_all(chunk, 'ord', 0, 0, tiled=True).astype(jnp.float32)  27.7 us
    all_to_all x1, blocking collectives, body(): field = lax.all_to_all(field, 'ord', 0, 0, tiled=True)  17.1 us
    pallas_call x4, Pallas kernels, partial_sums(): pl.pallas_call(functools.partial(sums_kernel, base=base), out_shape=[jax....  15.4 us
    ppermute x4, waiting for transfers between devices, start(): packed.append((lax.ppermute(coef, 'blk', GAUSS_PAIRS), far, coef))  10.6 us
    pallas_call x4, Pallas kernels, packed_panel(): pl.pallas_call(pack_panel, out_shape=jax.ShapeDtypeStruct((steps, 16, PAN...  6.95 us
    pallas_call x4, Pallas kernels, packed_gauss(): pl.pallas_call(pack_gauss, out_shape=jax.ShapeDtypeStruct((steps, 16, GAU...  6.4 us
    ppermute x2, waiting for transfers between devices, body(): added.append(lax.ppermute(send, 'blk', PANEL_PAIRS))  4.42 us
    ppermute x4, starting transfers between devices, start(): far = lax.ppermute(part, 'blk', PANEL_PAIRS)  4.4 us
  transfers between devices with their start and end apart: 10, of which 4 were waited for; matrix products, arithmetic and copies ran while one was open for 7% of the time, Pallas kernels for 22%

profile of v8, /device:TPU:1, one launch (start us, length us, event | category | flops | bytes accessed | tf_op | source)
XLA Modules:
  0.0 110.6 jit_solution(4239322758911879444)
XLA Ops:
  0.7 2.2 %pack_panel.4.rest_0_ = bf16[3,16,7424]{2,1,0:T(8,128)(2,1)S(1)} custom-call(s32[1]{0:T(128)} %bitcast.spot_ref, s32[16]{0:T(128)S(1)} %copy-done, bf16[45,16,2880]{2,1,0:T(8,128)(2,1)} %tail_ref.15, bf16[45,16,2880]{2,1,0:T(8,128)(2,1)} %tail_ref.15), custom_call_target="tpu_custom_call" | custom-call | bytes 1500000 | tf_op jit(solution)/shard_map/pack_panel/pallas_call | solution.py:61
  2.9 3.4 %collective-permute-start.1 = (bf16[3,16,7424]{2,1,0:T(8,128)(2,1)S(1)}, bf16[3,16,7424]{2,1,0:T(8,128)(2,1)}, u32[]{:S(2)}, u32[]{:S(2)}) collective-permute-start(bf16[3,16,7424]{2,1,0:T(8,128)(2,1)S(1)} %pack_panel.4.rest_0_), channel_id=1, source_target_pairs={{1,2},{2,1},{3,0},{0,3},{5,6},{6,5},{7,4},{4,7},{9,10},{10,9},{11,... | collective-permute-start | bytes 2138120 | tf_op jit(solution)/shard_map/ppermute | solution.py:231
  6.3 2.1 %pack_gauss.4.rest_0_ = bf16[3,16,7296]{2,1,0:T(8,128)(2,1)S(1)} custom-call(bf16[2,45,16,720]{3,2,1,0:T(8,128)(2,1)} %bitcast.28, bf16[3,16,7424]{2,1,0:T(8,128)(2,1)S(1)} %pack_panel.4.rest_0_), custom_call_target="tpu_custom_call" | custom-call | bytes 1500000 | tf_op jit(solution)/shard_map/pack_gauss/pallas_call | solution.py:80
  8.5 2.3 %pack_panel.5.rest_0_ = bf16[3,16,7424]{2,1,0:T(8,128)(2,1)S(1)} custom-call(s32[1]{0:T(128)} %bitcast.spot_ref, s32[16]{0:T(128)S(1)} %copy-done, bf16[45,16,2880]{2,1,0:T(8,128)(2,1)} %tail_ref.15, bf16[45,16,2880]{2,1,0:T(8,128)(2,1)} %tail_ref.15, bf16[3,16,7296]{2,1,0:T(8,128)(2,1)S(1)} %pack_gauss.4.rest_0_), custom_call_target="tpu_custom_call" | custom-call | bytes 1500000 | tf_op jit(solution)/shard_map/pack_panel/pallas_call | solution.py:61
  10.7 0.8 collective-permute-start.3
  11.6 2.1 %pack_gauss.5.rest_1_ = bf16[3,16,7296]{2,1,0:T(8,128)(2,1)S(1)} custom-call(bf16[2,45,16,720]{3,2,1,0:T(8,128)(2,1)} %bitcast.29, bf16[3,16,7424]{2,1,0:T(8,128)(2,1)S(1)} %pack_panel.5.rest_0_), custom_call_target="tpu_custom_call" | custom-call | bytes 1500000 | tf_op jit(solution)/shard_map/pack_gauss/pallas_call | solution.py:80
  15.7 1.4 %slice.19 = s32[64]{0:T(128)} slice(s32[2880]{0:T(1024)} %param.8), slice={[0:2880:45]} | slice | bytes 512 | tf_op jit(solution)/shard_map/slice | solution.py:257
  17.1 1.5 %multiply_exponential_fusion.1 = (f32[1,16,1536]{2,1,0:T(8,128)}, f32[1,16,1536]{2,1,0:T(8,128)}, f32[1,16,1536]{2,1,0:T(8,128)}) fusion(f32[16]{0:T(128)S(1)} %copy-done.2, f32[1536]{0:T(1024)} %get-tuple-element.44, f32[1536]{0:T(1024)} %convert_add_fusion, f32[1536]{0:T(1024)S(1)} %get-tuple-element.43), kind=kLoop, calls=%fused_computation.20 | loop fusion | flops 122880 | bytes 313408 | tf_op jit(solution)/shard_map/exp | solution.py:222
  20.1 1.0 pad_maximum_fusion.decay_ref
  21.1 3.8 %collective-permute-done.other_ref = bf16[3,16,7296]{2,1,0:T(8,128)(2,1)} collective-permute-done((bf16[3,16,7296]{2,1,0:T(8,128)(2,1)S(1)}, bf16[3,16,7296]{2,1,0:T(8,128)(2,1)}, u32[]{:S(2)}, u32[]{:S(2)}) %collective-permute-start) | collective-permute-done | bytes 700448 | tf_op jit(solution)/shard_map/ppermute | solution.py:233
  24.8 5.0 %partial_sums.4 = (f32[15,16,96]{2,1,0:T(8,128)S(1)}, bf16[15,16,96]{2,1,0:T(8,128)(2,1)S(1)}) custom-call(s32[1]{0:T(128)} %bitcast.spot_ref, s32[45]{0:T(128)S(1)} %dynamic_slice.3.order_ref, f32[3,16,1536]{2,1,0:T(8,128)S(1)} %pad_maximum_fusion.decay_ref, s32[16]{0:T(128)S(1)} %copy-done.1, bf16[2,45,16,720]{3,2,1,0:T(8,128)(2,1)} %bitcast.30, ...), custom_call_target="tpu_custom_call" | custom-call | flops 188743680 | bytes 3000000 | tf_op jit(solution)/shard_map/partial_sums/pallas_call | solution.py:175
  29.8 1.3 %pack_panel.6.rest_0_ = bf16[2,16,7424]{2,1,0:T(8,128)(2,1)S(1)} custom-call(s32[1]{0:T(128)} %bitcast.spot_ref, s32[16]{0:T(128)S(1)} %copy-done.1, bf16[45,16,2880]{2,1,0:T(8,128)(2,1)} %tail_ref.15, bf16[45,16,2880]{2,1,0:T(8,128)(2,1)} %tail_ref.15, f32[15,16,96]{2,1,0:T(8,128)S(1)} %get-tuple-element.18.rest_0_.rest_2_, ...), custom_call_target="tpu_custom_call" | custom-call | bytes 1000000 | tf_op jit(solution)/shard_map/pack_panel/pallas_call | solution.py:61
  31.1 1.2 %pack_gauss.6.rest_1_ = bf16[2,16,7296]{2,1,0:T(8,128)(2,1)S(1)} custom-call(bf16[2,45,16,720]{3,2,1,0:T(8,128)(2,1)} %bitcast.31, bf16[2,16,7424]{2,1,0:T(8,128)(2,1)S(1)} %pack_panel.6.rest_0_), custom_call_target="tpu_custom_call" | custom-call | bytes 1000000 | tf_op jit(solution)/shard_map/pack_gauss/pallas_call | solution.py:80
  33.0 6.9 %collective-permute-done.2.other_ref = bf16[3,16,7296]{2,1,0:T(8,128)(2,1)} collective-permute-done((bf16[3,16,7296]{2,1,0:T(8,128)(2,1)S(1)}, bf16[3,16,7296]{2,1,0:T(8,128)(2,1)}, u32[]{:S(2)}, u32[]{:S(2)}) %collective-permute-start.2) | collective-permute-done | bytes 700448 | tf_op jit(solution)/shard_map/ppermute | solution.py:233
  39.8 4.7 %partial_sums.5 = (f32[30,16,96]{2,1,0:T(8,128)S(1)}, bf16[30,16,96]{2,1,0:T(8,128)(2,1)S(1)}) custom-call(s32[1]{0:T(128)} %bitcast.spot_ref, s32[45]{0:T(128)S(1)} %dynamic_slice.3.order_ref, f32[3,16,1536]{2,1,0:T(8,128)S(1)} %pad_maximum_fusion.decay_ref, s32[16]{0:T(128)S(1)} %copy-done.1, bf16[2,45,16,720]{3,2,1,0:T(8,128)(2,1)} %bitcast.32, ...), custom_call_target="tpu_custom_call" | custom-call | flops 188743680 | bytes 3000000 | tf_op jit(solution)/shard_map/partial_sums/pallas_call | solution.py:175
  44.5 1.1 %pack_panel.7.rest_0_ = bf16[1,16,7424]{2,1,0:T(8,128)(2,1)S(1)} custom-call(s32[1]{0:T(128)} %bitcast.spot_ref, s32[16]{0:T(128)S(1)} %copy-done.1, bf16[45,16,2880]{2,1,0:T(8,128)(2,1)} %tail_ref.15, bf16[45,16,2880]{2,1,0:T(8,128)(2,1)} %tail_ref.15, f32[30,16,96]{2,1,0:T(8,128)S(1)} %get-tuple-element.19.rest_0_, bf16[2,16,7296]{2,1,0:T(8,128)(2,1)S(1)} %pack_gauss.6.rest_1_), custom_call_target="tpu_custom_call" | custom-call | bytes 500000 | tf_op jit(solution)/shard_map/pack_panel/pallas_call | solution.py:61
  45.6 1.0 pack_gauss.7
  47.1 2.6 %collective-permute-start.8 = (bf16[15,16,96]{2,1,0:T(8,128)(2,1)S(1)}, bf16[15,16,96]{2,1,0:T(8,128)(2,1)S(1)}, u32[]{:S(2)}, u32[]{:S(2)}) collective-permute-start(bf16[15,16,96]{2,1,0:T(8,128)(2,1)S(1)} %get-tuple-element.23), channel_id=1, source_target_pairs={{1,2},{2,1},{3,0},{0,3},{5,6},{6,5},{7,4},{4,7},{9,10},{10,9},{11,... | collective-permute-start | bytes 138248 | tf_op jit(solution)/shard_map/ppermute | solution.py:247
  49.8 3.4 %partial_sums.6 = (f32[30,16,96]{2,1,0:T(8,128)S(1)}, bf16[30,16,96]{2,1,0:T(8,128)(2,1)S(1)}) custom-call(s32[1]{0:T(128)} %bitcast.spot_ref, s32[45]{0:T(128)S(1)} %dynamic_slice.3.order_ref, f32[3,16,1536]{2,1,0:T(8,128)S(1)} %pad_maximum_fusion.decay_ref, s32[16]{0:T(128)S(1)} %copy-done.1, ...), custom_call_target="tpu_custom_call", output_to_operand_aliasing={{0}: (9, {}), {1}: (10, {})} | custom-call | flops 125829120 | bytes 2000000 | tf_op jit(solution)/shard_map/partial_sums/pallas_call | solution.py:175
  53.6 2.3 %partial_sums.7 = (f32[30,16,96]{2,1,0:T(8,128)S(1)}, bf16[30,16,96]{2,1,0:T(8,128)(2,1)S(1)}) custom-call(s32[1]{0:T(128)} %bitcast.spot_ref, s32[45]{0:T(128)S(1)} %dynamic_slice.3.order_ref, f32[3,16,1536]{2,1,0:T(8,128)S(1)} %pad_maximum_fusion.decay_ref, s32[16]{0:T(128)S(1)} %copy-done.1, ...), custom_call_target="tpu_custom_call", output_to_operand_aliasing={{0}: (9, {}), {1}: (10, {})} | custom-call | flops 62914560 | bytes 1000000 | tf_op jit(solution)/shard_map/partial_sums/pallas_call | solution.py:175
  55.9 1.1 collective-permute-start.9
  57.1 4.0 %collective-permute-done.9 = bf16[30,16,96]{2,1,0:T(8,128)(2,1)S(1)} collective-permute-done((bf16[30,16,96]{2,1,0:T(8,128)(2,1)S(1)}, bf16[30,16,96]{2,1,0:T(8,128)(2,1)S(1)}, u32[]{:S(2)}, u32[]{:S(2)}) %collective-permute-start.9) | collective-permute-done | bytes 92192 | tf_op jit(solution)/shard_map/ppermute | solution.py:247
  62.2 27.7 %all_to_all.10 = bf16[64,2,540]{2,1,0:T(2,128)(2,1)S(1)} all-to-all(bf16[64,2,540]{2,1,0:T(2,128)(2,1)S(1)} %copy.21), channel_id=1, replica_groups=mesh['ord'=64,'blk'=4] {'ord'}, dimensions={0} | all-to-all | bytes 276480 | tf_op jit(solution)/shard_map/all_to_all | solution.py:269
  92.4 17.1 %all_to_all.11 = bf16[64,90,12]{1,2,0:T(8,128)(2,1)S(1)} all-to-all(bf16[64,90,12]{1,2,0:T(8,128)(2,1)S(1)} %copy.23), channel_id=1, replica_groups=mesh['ord'=64,'blk'=4] {'ord'}, dimensions={0} | all-to-all | bytes 276480 | tf_op jit(solution)/shard_map/all_to_all | solution.py:279
  (47 shorter events, 10.4 us)
Async XLA Ops:
  0.0 0.7 copy-start
  2.9 21.9 %collective-permute-start.1 = (bf16[3,16,7424]{2,1,0:T(8,128)(2,1)S(1)}, bf16[3,16,7424]{2,1,0:T(8,128)(2,1)}, u32[]{:S(2)}, u32[]{:S(2)}) collective-permute-start(bf16[3,16,7424]{2,1,0:T(8,128)(2,1)S(1)} %pack_panel.4.rest_0_), channel_id=1, source_target_pairs={{1,2},{2,1},{3,0},{0,3},{5,6},{6,5},{7,4},{4,7},{9,10},{10,9},{11,... | collective-permute-start | bytes 2138120 | tf_op jit(solution)/shard_map/ppermute | solution.py:231
  8.4 8.7 %copy-start.2 = (f32[16]{0:T(128)S(1)}, f32[16]{0:T(128)}, u32[]{:S(2)}) copy-start(f32[16]{0:T(128)} %param.7) | copy-start | bytes 196
  8.4 16.4 %collective-permute-start = (bf16[3,16,7296]{2,1,0:T(8,128)(2,1)S(1)}, bf16[3,16,7296]{2,1,0:T(8,128)(2,1)}, u32[]{:S(2)}, u32[]{:S(2)}) collective-permute-start(bf16[3,16,7296]{2,1,0:T(8,128)(2,1)S(1)} %pack_gauss.4.rest_0_), channel_id=1, source_target_pairs={{0,1},{1,0},{2,3},{3,2},{4,5},{5,4},{6,7},{7,6},{8,9},{9,8},{10,11... | collective-permute-start | bytes 2101256 | tf_op jit(solution)/shard_map/ppermute | solution.py:233
  10.7 14.1 %copy-start.1 = (s32[16]{0:T(128)S(1)}, s32[16]{0:T(128)}, u32[]{:S(2)}) copy-start(s32[16]{0:T(128)} %cycle_ref.15) | copy-start | bytes 196
  10.7 29.1 %collective-permute-start.3 = (bf16[3,16,7424]{2,1,0:T(8,128)(2,1)S(1)}, bf16[3,16,7424]{2,1,0:T(8,128)(2,1)S(1)}, u32[]{:S(2)}, u32[]{:S(2)}) collective-permute-start(bf16[3,16,7424]{2,1,0:T(8,128)(2,1)S(1)} %pack_panel.5.rest_0_), channel_id=1, source_target_pairs={{1,2},{2,1},{3,0},{0,3},{5,6},{6,5},{7,4},{4,7},{9,10},{10,9},{11,... | collective-permute-start | bytes 2138120 | tf_op jit(solution)/shard_map/ppermute | solution.py:231
  13.7 26.1 %collective-permute-start.2 = (bf16[3,16,7296]{2,1,0:T(8,128)(2,1)S(1)}, bf16[3,16,7296]{2,1,0:T(8,128)(2,1)}, u32[]{:S(2)}, u32[]{:S(2)}) collective-permute-start(bf16[3,16,7296]{2,1,0:T(8,128)(2,1)S(1)} %pack_gauss.5.rest_1_), channel_id=1, source_target_pairs={{0,1},{1,0},{2,3},{3,2},{4,5},{5,4},{6,7},{7,6},{8,9},{9,8},{10,11... | collective-permute-start | bytes 2101256 | tf_op jit(solution)/shard_map/ppermute | solution.py:233
  32.3 17.5 %collective-permute-start.7 = (bf16[2,16,7424]{2,1,0:T(8,128)(2,1)S(1)}, bf16[2,16,7424]{2,1,0:T(8,128)(2,1)S(1)}, u32[]{:S(2)}, u32[]{:S(2)}) collective-permute-start(bf16[2,16,7424]{2,1,0:T(8,128)(2,1)S(1)} %pack_panel.6.rest_0_), channel_id=1, source_target_pairs={{1,2},{2,1},{3,0},{0,3},{5,6},{6,5},{7,4},{4,7},{9,10},{10,9},{11,... | collective-permute-start | bytes 1425416 | tf_op jit(solution)/shard_map/ppermute | solution.py:231
  32.4 17.4 %collective-permute-start.6 = (bf16[2,16,7296]{2,1,0:T(8,128)(2,1)S(1)}, bf16[2,16,7296]{2,1,0:T(8,128)(2,1)S(1)}, u32[]{:S(2)}, u32[]{:S(2)}) collective-permute-start(bf16[2,16,7296]{2,1,0:T(8,128)(2,1)S(1)} %pack_gauss.6.rest_1_), channel_id=1, source_target_pairs={{0,1},{1,0},{2,3},{3,2},{4,5},{5,4},{6,7},{7,6},{8,9},{9,8},{10,11... | collective-permute-start | bytes 1400840 | tf_op jit(solution)/shard_map/ppermute | solution.py:233
  46.7 6.9 %collective-permute-start.5 = (bf16[1,16,7424]{2,1,0:T(8,128)(2,1)S(1)}, bf16[1,16,7424]{2,1,0:T(8,128)(2,1)S(1)}, u32[]{:S(2)}, u32[]{:S(2)}) collective-permute-start(bf16[1,16,7424]{2,1,0:T(8,128)(2,1)S(1)} %pack_panel.7.rest_0_), channel_id=1, source_target_pairs={{1,2},{2,1},{3,0},{0,3},{5,6},{6,5},{7,4},{4,7},{9,10},{10,9},{11,... | collective-permute-start | bytes 712712 | tf_op jit(solution)/shard_map/ppermute | solution.py:231
  46.8 6.8 %collective-permute-start.4 = (bf16[1,16,7296]{2,1,0:T(8,128)(2,1)S(1)}, bf16[1,16,7296]{2,1,0:T(8,128)(2,1)S(1)}, u32[]{:S(2)}, u32[]{:S(2)}) collective-permute-start(bf16[1,16,7296]{2,1,0:T(8,128)(2,1)S(1)} %pack_gauss.7), channel_id=1, source_target_pairs={{0,1},{1,0},{2,3},{3,2},{4,5},{5,4},{6,7},{7,6},{8,9},{9,8},{10,11... | collective-permute-start | bytes 700424 | tf_op jit(solution)/shard_map/ppermute | solution.py:233
  47.1 6.5 %collective-permute-start.8 = (bf16[15,16,96]{2,1,0:T(8,128)(2,1)S(1)}, bf16[15,16,96]{2,1,0:T(8,128)(2,1)S(1)}, u32[]{:S(2)}, u32[]{:S(2)}) collective-permute-start(bf16[15,16,96]{2,1,0:T(8,128)(2,1)S(1)} %get-tuple-element.23), channel_id=1, source_target_pairs={{1,2},{2,1},{3,0},{0,3},{5,6},{6,5},{7,4},{4,7},{9,10},{10,9},{11,... | collective-permute-start | bytes 138248 | tf_op jit(solution)/shard_map/ppermute | solution.py:247
  55.9 5.2 %collective-permute-start.9 = (bf16[30,16,96]{2,1,0:T(8,128)(2,1)S(1)}, bf16[30,16,96]{2,1,0:T(8,128)(2,1)S(1)}, u32[]{:S(2)}, u32[]{:S(2)}) collective-permute-start(bf16[30,16,96]{2,1,0:T(8,128)(2,1)S(1)} %get-tuple-element.25), channel_id=1, source_target_pairs={{1,2},{2,1},{3,0},{0,3},{5,6},{6,5},{7,4},{4,7},{9,10},{10,9},{11,... | collective-permute-start | bytes 276488 | tf_op jit(solution)/shard_map/ppermute | solution.py:247

commit v9 on v8

--- a/solution.py
+++ b/solution.py
@@ -226,7 +226,7 @@
 
     def start(c):
         a, b = spans[c]
-        after = (kept[-1:] if c >= 2 else []) + ([packed[-1][2]] if packed else [])
+        after = (kept[0:1] if c >= 2 else []) + ([packed[-1][2]] if packed else [])
         part = packed_panel(spot, cycle_map, panel, after, a, b - a)
         far = lax.ppermute(part, "blk", PANEL_PAIRS)
         coef = packed_gauss(own, [part], a, b - a)
@@ -275,10 +275,11 @@
     field = lax.dot_general(
         last, jnp.concatenate([real, imag], 2),
         (((1,), (2,)), ((), ())), precision=lax.Precision.HIGHEST)
-    field = field.reshape(parts, NLON // parts, items).astype(jnp.bfloat16)
+    field = field.reshape(parts, NLON // parts, 3, shells // 4).astype(jnp.bfloat16)
+    field = jnp.transpose(field, (0, 2, 3, 1)).reshape(parts * 3, shells // 4, NLON // parts)
     field = lax.all_to_all(field, "ord", 0, 0, tiled=True)
-    field = field.reshape(cycles, 4, NLON // parts, 3, shells // 4)
-    return jnp.transpose(field, (2, 0, 3, 1, 4)).reshape(NLON // parts, cycles * 3 * shells)
+    field = field.reshape(cycles, 4, 3, shells // 4, NLON // parts)
+    return jnp.transpose(field, (4, 0, 2, 1, 3)).reshape(NLON // parts, cycles * 3 * shells)
 
 
 def solution(mesh):

time: 111 us -> 109 us (0.982)
  blocking collectives: 44.8 us -> 41.1 us
    all_to_all x1, blocking collectives: 27.7 us -> 25.1 us  [body(): spread = lax.all_to_all(chunk, 'ord', 0, 0, tiled=True).astype(jnp.float32)]
    ppermute x4, starting transfers between devices: 4.4 us -> 6.9 us  [start(): far = lax.ppermute(part, 'blk', PANEL_PAIRS)]
    ppermute x2, starting transfers between devices: 3.68 us -> 1.52 us  [body(): added.append(lax.ppermute(send, 'blk', PANEL_PAIRS))]
    ppermute x4, waiting for transfers between devices: 10.6 us -> 12.2 us  [start(): packed.append((lax.ppermute(coef, 'blk', GAUSS_PAIRS), far, coef))]
  transfers between devices with their start and end apart: 10 -> 10, of which waited for: 4 -> 5; matrix products, arithmetic and copies ran while one was open for 7% -> 7% of each run, Pallas kernels for 22% -> 22%
where the time goes in v9:
time: 109 us; the launch traced here: 108 us
  blocking collectives  41.1 us (38%)
  Pallas kernels  28.7 us (26%)
  waiting for transfers between devices  15.9 us (15%)
  starting transfers between devices  9.53 us (9%)
  local copies, waits for them, and re-layouts  5.95 us (5%)
  other arithmetic  5.25 us (5%)
  matrix products  1.2 us (1%)
    all_to_all x1, blocking collectives, body(): spread = lax.all_to_all(chunk, 'ord', 0, 0, tiled=True).astype(jnp.float32)  25.1 us
    all_to_all x1, blocking collectives, body(): field = lax.all_to_all(field, 'ord', 0, 0, tiled=True)  16.1 us
    pallas_call x4, Pallas kernels, partial_sums(): pl.pallas_call(functools.partial(sums_kernel, base=base), out_shape=[jax....  15.3 us
    ppermute x4, waiting for transfers between devices, start(): packed.append((lax.ppermute(coef, 'blk', GAUSS_PAIRS), far, coef))  12.2 us
    pallas_call x4, Pallas kernels, packed_panel(): pl.pallas_call(pack_panel, out_shape=jax.ShapeDtypeStruct((steps, 16, PAN...  6.95 us
    ppermute x4, starting transfers between devices, start(): far = lax.ppermute(part, 'blk', PANEL_PAIRS)  6.9 us
    pallas_call x4, Pallas kernels, packed_gauss(): pl.pallas_call(pack_gauss, out_shape=jax.ShapeDtypeStruct((steps, 16, GAU...  6.4 us
    ppermute x2, waiting for transfers between devices, body(): added.append(lax.ppermute(send, 'blk', PANEL_PAIRS))  3.7 us
  transfers between devices with their start and end apart: 10, of which 5 were waited for; matrix products, arithmetic and copies ran while one was open for 7% of the time, Pallas kernels for 22%

profile of v9, /device:TPU:1, one launch (start us, length us, event | category | flops | bytes accessed | tf_op | source)
XLA Modules:
  0.0 107.9 jit_solution(7952511736407901640)
XLA Ops:
  0.7 2.2 %pack_panel.4.rest_0_ = bf16[3,16,7424]{2,1,0:T(8,128)(2,1)S(1)} custom-call(s32[1]{0:T(128)} %bitcast.spot_ref, s32[16]{0:T(128)S(1)} %copy-done, bf16[45,16,2880]{2,1,0:T(8,128)(2,1)} %tail_ref.15, bf16[45,16,2880]{2,1,0:T(8,128)(2,1)} %tail_ref.15), custom_call_target="tpu_custom_call" | custom-call | bytes 1500000 | tf_op jit(solution)/shard_map/pack_panel/pallas_call | solution.py:61
  2.9 3.4 %collective-permute-start.1 = (bf16[3,16,7424]{2,1,0:T(8,128)(2,1)S(1)}, bf16[3,16,7424]{2,1,0:T(8,128)(2,1)}, u32[]{:S(2)}, u32[]{:S(2)}) collective-permute-start(bf16[3,16,7424]{2,1,0:T(8,128)(2,1)S(1)} %pack_panel.4.rest_0_), channel_id=1, source_target_pairs={{1,2},{2,1},{3,0},{0,3},{5,6},{6,5},{7,4},{4,7},{9,10},{10,9},{11,... | collective-permute-start | bytes 2138120 | tf_op jit(solution)/shard_map/ppermute | solution.py:231
  6.3 2.1 %pack_gauss.4.rest_0_ = bf16[3,16,7296]{2,1,0:T(8,128)(2,1)S(1)} custom-call(bf16[2,45,16,720]{3,2,1,0:T(8,128)(2,1)} %bitcast.31, bf16[3,16,7424]{2,1,0:T(8,128)(2,1)S(1)} %pack_panel.4.rest_0_), custom_call_target="tpu_custom_call" | custom-call | bytes 1500000 | tf_op jit(solution)/shard_map/pack_gauss/pallas_call | solution.py:80
  8.5 2.3 %pack_panel.5.rest_0_ = bf16[3,16,7424]{2,1,0:T(8,128)(2,1)S(1)} custom-call(s32[1]{0:T(128)} %bitcast.spot_ref, s32[16]{0:T(128)S(1)} %copy-done, bf16[45,16,2880]{2,1,0:T(8,128)(2,1)} %tail_ref.15, bf16[45,16,2880]{2,1,0:T(8,128)(2,1)} %tail_ref.15, bf16[3,16,7296]{2,1,0:T(8,128)(2,1)S(1)} %pack_gauss.4.rest_0_), custom_call_target="tpu_custom_call" | custom-call | bytes 1500000 | tf_op jit(solution)/shard_map/pack_panel/pallas_call | solution.py:61
  11.6 2.1 %pack_gauss.5.rest_1_ = bf16[3,16,7296]{2,1,0:T(8,128)(2,1)S(1)} custom-call(bf16[2,45,16,720]{3,2,1,0:T(8,128)(2,1)} %bitcast.32, bf16[3,16,7424]{2,1,0:T(8,128)(2,1)S(1)} %pack_panel.5.rest_0_), custom_call_target="tpu_custom_call" | custom-call | bytes 1500000 | tf_op jit(solution)/shard_map/pack_gauss/pallas_call | solution.py:80
  15.7 1.4 %slice.19 = s32[64]{0:T(128)} slice(s32[2880]{0:T(1024)} %param.8), slice={[0:2880:45]} | slice | bytes 512 | tf_op jit(solution)/shard_map/slice | solution.py:257
  17.1 1.5 %multiply_exponential_fusion.1 = (f32[1,16,1536]{2,1,0:T(8,128)}, f32[1,16,1536]{2,1,0:T(8,128)}, f32[1,16,1536]{2,1,0:T(8,128)}) fusion(f32[16]{0:T(128)S(1)} %copy-done.2, f32[1536]{0:T(1024)} %get-tuple-element.44, f32[1536]{0:T(1024)} %convert_add_fusion, f32[1536]{0:T(1024)S(1)} %get-tuple-element.43), kind=kLoop, calls=%fused_computation.20 | loop fusion | flops 122880 | bytes 313408 | tf_op jit(solution)/shard_map/exp | solution.py:222
  21.1 3.8 %collective-permute-done.other_ref = bf16[3,16,7296]{2,1,0:T(8,128)(2,1)} collective-permute-done((bf16[3,16,7296]{2,1,0:T(8,128)(2,1)S(1)}, bf16[3,16,7296]{2,1,0:T(8,128)(2,1)}, u32[]{:S(2)}, u32[]{:S(2)}) %collective-permute-start) | collective-permute-done | bytes 700448 | tf_op jit(solution)/shard_map/ppermute | solution.py:233
  24.8 5.0 %partial_sums.4 = (f32[15,16,96]{2,1,0:T(8,128)S(1)}, bf16[15,16,96]{2,1,0:T(8,128)(2,1)S(1)}) custom-call(s32[1]{0:T(128)} %bitcast.spot_ref, s32[45]{0:T(128)S(1)} %dynamic_slice.3.order_ref, f32[3,16,1536]{2,1,0:T(8,128)S(1)} %pad_maximum_fusion.decay_ref, s32[16]{0:T(128)S(1)} %copy-done.1, bf16[2,45,16,720]{3,2,1,0:T(8,128)(2,1)} %bitcast.33, ...), custom_call_target="tpu_custom_call" | custom-call | flops 188743680 | bytes 3000000 | tf_op jit(solution)/shard_map/partial_sums/pallas_call | solution.py:175
  29.8 1.3 %pack_panel.6.rest_0_ = bf16[2,16,7424]{2,1,0:T(8,128)(2,1)S(1)} custom-call(s32[1]{0:T(128)} %bitcast.spot_ref, s32[16]{0:T(128)S(1)} %copy-done.1, bf16[45,16,2880]{2,1,0:T(8,128)(2,1)} %tail_ref.15, bf16[45,16,2880]{2,1,0:T(8,128)(2,1)} %tail_ref.15, f32[15,16,96]{2,1,0:T(8,128)S(1)} %get-tuple-element.18.rest_0_.rest_2_, ...), custom_call_target="tpu_custom_call" | custom-call | bytes 1000000 | tf_op jit(solution)/shard_map/pack_panel/pallas_call | solution.py:61
  31.1 1.2 %pack_gauss.6.rest_1_ = bf16[2,16,7296]{2,1,0:T(8,128)(2,1)S(1)} custom-call(bf16[2,45,16,720]{3,2,1,0:T(8,128)(2,1)} %bitcast.34, bf16[2,16,7424]{2,1,0:T(8,128)(2,1)S(1)} %pack_panel.6.rest_0_), custom_call_target="tpu_custom_call" | custom-call | bytes 1000000 | tf_op jit(solution)/shard_map/pack_gauss/pallas_call | solution.py:80
  33.0 1.1 %pack_panel.7.rest_0_ = bf16[1,16,7424]{2,1,0:T(8,128)(2,1)S(1)} custom-call(s32[1]{0:T(128)} %bitcast.spot_ref, s32[16]{0:T(128)S(1)} %copy-done.1, bf16[45,16,2880]{2,1,0:T(8,128)(2,1)} %tail_ref.15, bf16[45,16,2880]{2,1,0:T(8,128)(2,1)} %tail_ref.15, f32[15,16,96]{2,1,0:T(8,128)S(1)} %get-tuple-element.18.rest_0_.rest_2_, ...), custom_call_target="tpu_custom_call" | custom-call | bytes 500000 | tf_op jit(solution)/shard_map/pack_panel/pallas_call | solution.py:61
  34.1 1.0 pack_gauss.7
  35.1 2.6 %collective-permute-start.3 = (bf16[1,16,7424]{2,1,0:T(8,128)(2,1)S(1)}, bf16[1,16,7424]{2,1,0:T(8,128)(2,1)S(1)}, u32[]{:S(2)}, u32[]{:S(2)}) collective-permute-start(bf16[1,16,7424]{2,1,0:T(8,128)(2,1)S(1)} %pack_panel.7.rest_0_), channel_id=1, source_target_pairs={{1,2},{2,1},{3,0},{0,3},{5,6},{6,5},{7,4},{4,7},{9,10},{10,9},{11,... | collective-permute-start | bytes 712712 | tf_op jit(solution)/shard_map/ppermute | solution.py:231
  37.7 2.1 %collective-permute-done.6.other_ref = bf16[3,16,7296]{2,1,0:T(8,128)(2,1)} collective-permute-done((bf16[3,16,7296]{2,1,0:T(8,128)(2,1)S(1)}, bf16[3,16,7296]{2,1,0:T(8,128)(2,1)}, u32[]{:S(2)}, u32[]{:S(2)}) %collective-permute-start.6) | collective-permute-done | bytes 700448 | tf_op jit(solution)/shard_map/ppermute | solution.py:233
  40.3 4.7 %partial_sums.5 = (f32[30,16,96]{2,1,0:T(8,128)S(1)}, bf16[30,16,96]{2,1,0:T(8,128)(2,1)S(1)}) custom-call(s32[1]{0:T(128)} %bitcast.spot_ref, s32[45]{0:T(128)S(1)} %dynamic_slice.3.order_ref, f32[3,16,1536]{2,1,0:T(8,128)S(1)} %pad_maximum_fusion.decay_ref, s32[16]{0:T(128)S(1)} %copy-done.1, bf16[2,45,16,720]{3,2,1,0:T(8,128)(2,1)} %bitcast.36, ...), custom_call_target="tpu_custom_call" | custom-call | flops 188743680 | bytes 3000000 | tf_op jit(solution)/shard_map/partial_sums/pallas_call | solution.py:175
  45.0 4.7 %collective-permute-done.4.other_ref = bf16[2,16,7296]{2,1,0:T(8,128)(2,1)S(1)} collective-permute-done((bf16[2,16,7296]{2,1,0:T(8,128)(2,1)S(1)}, bf16[2,16,7296]{2,1,0:T(8,128)(2,1)S(1)}, u32[]{:S(2)}, u32[]{:S(2)}) %collective-permute-start.4) | collective-permute-done | bytes 466976 | tf_op jit(solution)/shard_map/ppermute | solution.py:233
  49.7 3.4 %partial_sums.6 = (f32[30,16,96]{2,1,0:T(8,128)S(1)}, bf16[30,16,96]{2,1,0:T(8,128)(2,1)S(1)}) custom-call(s32[1]{0:T(128)} %bitcast.spot_ref, s32[45]{0:T(128)S(1)} %dynamic_slice.3.order_ref, f32[3,16,1536]{2,1,0:T(8,128)S(1)} %pad_maximum_fusion.decay_ref, s32[16]{0:T(128)S(1)} %copy-done.1, ...), custom_call_target="tpu_custom_call", output_to_operand_aliasing={{0}: (9, {}), {1}: (10, {})} | custom-call | flops 125829120 | bytes 2000000 | tf_op jit(solution)/shard_map/partial_sums/pallas_call | solution.py:175
  53.1 1.6 %collective-permute-done.2.other_ref = bf16[1,16,7296]{2,1,0:T(8,128)(2,1)S(1)} collective-permute-done((bf16[1,16,7296]{2,1,0:T(8,128)(2,1)S(1)}, bf16[1,16,7296]{2,1,0:T(8,128)(2,1)S(1)}, u32[]{:S(2)}, u32[]{:S(2)}) %collective-permute-start.2) | collective-permute-done | bytes 233504 | tf_op jit(solution)/shard_map/ppermute | solution.py:233
  54.7 2.3 %partial_sums.7 = (f32[30,16,96]{2,1,0:T(8,128)S(1)}, bf16[30,16,96]{2,1,0:T(8,128)(2,1)S(1)}) custom-call(s32[1]{0:T(128)} %bitcast.spot_ref, s32[45]{0:T(128)S(1)} %dynamic_slice.3.order_ref, f32[3,16,1536]{2,1,0:T(8,128)S(1)} %pad_maximum_fusion.decay_ref, s32[16]{0:T(128)S(1)} %copy-done.1, ...), custom_call_target="tpu_custom_call", output_to_operand_aliasing={{0}: (9, {}), {1}: (10, {})} | custom-call | flops 62914560 | bytes 1000000 | tf_op jit(solution)/shard_map/partial_sums/pallas_call | solution.py:175
  57.0 1.4 %collective-permute-start.9 = (bf16[30,16,96]{2,1,0:T(8,128)(2,1)S(1)}, bf16[30,16,96]{2,1,0:T(8,128)(2,1)S(1)}, u32[]{:S(2)}, u32[]{:S(2)}) collective-permute-start(bf16[30,16,96]{2,1,0:T(8,128)(2,1)S(1)} %get-tuple-element.25), channel_id=1, source_target_pairs={{1,2},{2,1},{3,0},{0,3},{5,6},{6,5},{7,4},{4,7},{9,10},{10,9},{11,... | collective-permute-start | bytes 276488 | tf_op jit(solution)/shard_map/ppermute | solution.py:247
  58.6 3.7 %collective-permute-done.9 = bf16[30,16,96]{2,1,0:T(8,128)(2,1)S(1)} collective-permute-done((bf16[30,16,96]{2,1,0:T(8,128)(2,1)S(1)}, bf16[30,16,96]{2,1,0:T(8,128)(2,1)S(1)}, u32[]{:S(2)}, u32[]{:S(2)}) %collective-permute-start.9) | collective-permute-done | bytes 92192 | tf_op jit(solution)/shard_map/ppermute | solution.py:247
  63.3 25.1 %all_to_all.10 = bf16[64,2,540]{2,1,0:T(2,128)(2,1)S(1)} all-to-all(bf16[64,2,540]{2,1,0:T(2,128)(2,1)S(1)} %copy.18), channel_id=1, replica_groups=mesh['ord'=64,'blk'=4] {'ord'}, dimensions={0} | all-to-all | bytes 276480 | tf_op jit(solution)/shard_map/all_to_all | solution.py:269
  91.0 16.1 %all_to_all.11 = bf16[192,4,90]{2,1,0:T(4,128)(2,1)S(1)} all-to-all(bf16[192,4,90]{2,1,0:T(4,128)(2,1)S(1)} %bitcast.40), channel_id=1, replica_groups=mesh['ord'=64,'blk'=4] {'ord'}, dimensions={0} | all-to-all | bytes 276480 | tf_op jit(solution)/shard_map/all_to_all | solution.py:280
  (46 shorter events, 11.6 us)
Async XLA Ops:
  0.0 0.7 copy-start
  2.9 21.9 %collective-permute-start.1 = (bf16[3,16,7424]{2,1,0:T(8,128)(2,1)S(1)}, bf16[3,16,7424]{2,1,0:T(8,128)(2,1)}, u32[]{:S(2)}, u32[]{:S(2)}) collective-permute-start(bf16[3,16,7424]{2,1,0:T(8,128)(2,1)S(1)} %pack_panel.4.rest_0_), channel_id=1, source_target_pairs={{1,2},{2,1},{3,0},{0,3},{5,6},{6,5},{7,4},{4,7},{9,10},{10,9},{11,... | collective-permute-start | bytes 2138120 | tf_op jit(solution)/shard_map/ppermute | solution.py:231
  8.4 8.7 %copy-start.2 = (f32[16]{0:T(128)S(1)}, f32[16]{0:T(128)}, u32[]{:S(2)}) copy-start(f32[16]{0:T(128)} %param.7) | copy-start | bytes 196
  8.4 16.4 %collective-permute-start = (bf16[3,16,7296]{2,1,0:T(8,128)(2,1)S(1)}, bf16[3,16,7296]{2,1,0:T(8,128)(2,1)}, u32[]{:S(2)}, u32[]{:S(2)}) collective-permute-start(bf16[3,16,7296]{2,1,0:T(8,128)(2,1)S(1)} %pack_gauss.4.rest_0_), channel_id=1, source_target_pairs={{0,1},{1,0},{2,3},{3,2},{4,5},{5,4},{6,7},{7,6},{8,9},{9,8},{10,11... | collective-permute-start | bytes 2101256 | tf_op jit(solution)/shard_map/ppermute | solution.py:233
  10.7 14.1 %copy-start.1 = (s32[16]{0:T(128)S(1)}, s32[16]{0:T(128)}, u32[]{:S(2)}) copy-start(s32[16]{0:T(128)} %cycle_ref.15) | copy-start | bytes 196
  10.7 29.3 %collective-permute-start.7 = (bf16[3,16,7424]{2,1,0:T(8,128)(2,1)S(1)}, bf16[3,16,7424]{2,1,0:T(8,128)(2,1)S(1)}, u32[]{:S(2)}, u32[]{:S(2)}) collective-permute-start(bf16[3,16,7424]{2,1,0:T(8,128)(2,1)S(1)} %pack_panel.5.rest_0_), channel_id=1, source_target_pairs={{1,2},{2,1},{3,0},{0,3},{5,6},{6,5},{7,4},{4,7},{9,10},{10,9},{11,... | collective-permute-start | bytes 2138120 | tf_op jit(solution)/shard_map/ppermute | solution.py:231
  13.7 26.1 %collective-permute-start.6 = (bf16[3,16,7296]{2,1,0:T(8,128)(2,1)S(1)}, bf16[3,16,7296]{2,1,0:T(8,128)(2,1)}, u32[]{:S(2)}, u32[]{:S(2)}) collective-permute-start(bf16[3,16,7296]{2,1,0:T(8,128)(2,1)S(1)} %pack_gauss.5.rest_1_), channel_id=1, source_target_pairs={{0,1},{1,0},{2,3},{3,2},{4,5},{5,4},{6,7},{7,6},{8,9},{9,8},{10,11... | collective-permute-start | bytes 2101256 | tf_op jit(solution)/shard_map/ppermute | solution.py:233
  32.3 17.4 %collective-permute-start.5 = (bf16[2,16,7424]{2,1,0:T(8,128)(2,1)S(1)}, bf16[2,16,7424]{2,1,0:T(8,128)(2,1)S(1)}, u32[]{:S(2)}, u32[]{:S(2)}) collective-permute-start(bf16[2,16,7424]{2,1,0:T(8,128)(2,1)S(1)} %pack_panel.6.rest_0_), channel_id=1, source_target_pairs={{1,2},{2,1},{3,0},{0,3},{5,6},{6,5},{7,4},{4,7},{9,10},{10,9},{11,... | collective-permute-start | bytes 1425416 | tf_op jit(solution)/shard_map/ppermute | solution.py:231
  32.4 17.3 %collective-permute-start.4 = (bf16[2,16,7296]{2,1,0:T(8,128)(2,1)S(1)}, bf16[2,16,7296]{2,1,0:T(8,128)(2,1)S(1)}, u32[]{:S(2)}, u32[]{:S(2)}) collective-permute-start(bf16[2,16,7296]{2,1,0:T(8,128)(2,1)S(1)} %pack_gauss.6.rest_1_), channel_id=1, source_target_pairs={{0,1},{1,0},{2,3},{3,2},{4,5},{5,4},{6,7},{7,6},{8,9},{9,8},{10,11... | collective-permute-start | bytes 1400840 | tf_op jit(solution)/shard_map/ppermute | solution.py:233
  35.1 19.6 %collective-permute-start.3 = (bf16[1,16,7424]{2,1,0:T(8,128)(2,1)S(1)}, bf16[1,16,7424]{2,1,0:T(8,128)(2,1)S(1)}, u32[]{:S(2)}, u32[]{:S(2)}) collective-permute-start(bf16[1,16,7424]{2,1,0:T(8,128)(2,1)S(1)} %pack_panel.7.rest_0_), channel_id=1, source_target_pairs={{1,2},{2,1},{3,0},{0,3},{5,6},{6,5},{7,4},{4,7},{9,10},{10,9},{11,... | collective-permute-start | bytes 712712 | tf_op jit(solution)/shard_map/ppermute | solution.py:231
  39.8 14.9 %collective-permute-start.2 = (bf16[1,16,7296]{2,1,0:T(8,128)(2,1)S(1)}, bf16[1,16,7296]{2,1,0:T(8,128)(2,1)S(1)}, u32[]{:S(2)}, u32[]{:S(2)}) collective-permute-start(bf16[1,16,7296]{2,1,0:T(8,128)(2,1)S(1)} %pack_gauss.7), channel_id=1, source_target_pairs={{0,1},{1,0},{2,3},{3,2},{4,5},{5,4},{6,7},{7,6},{8,9},{9,8},{10,11... | collective-permute-start | bytes 700424 | tf_op jit(solution)/shard_map/ppermute | solution.py:233
  40.0 13.1 %collective-permute-start.8 = (bf16[15,16,96]{2,1,0:T(8,128)(2,1)S(1)}, bf16[15,16,96]{2,1,0:T(8,128)(2,1)S(1)}, u32[]{:S(2)}, u32[]{:S(2)}) collective-permute-start(bf16[15,16,96]{2,1,0:T(8,128)(2,1)S(1)} %get-tuple-element.23), channel_id=1, source_target_pairs={{1,2},{2,1},{3,0},{0,3},{5,6},{6,5},{7,4},{4,7},{9,10},{10,9},{11,... | collective-permute-start | bytes 138248 | tf_op jit(solution)/shard_map/ppermute | solution.py:247
  57.0 5.2 %collective-permute-start.9 = (bf16[30,16,96]{2,1,0:T(8,128)(2,1)S(1)}, bf16[30,16,96]{2,1,0:T(8,128)(2,1)S(1)}, u32[]{:S(2)}, u32[]{:S(2)}) collective-permute-start(bf16[30,16,96]{2,1,0:T(8,128)(2,1)S(1)} %get-tuple-element.25), channel_id=1, source_target_pairs={{1,2},{2,1},{3,0},{0,3},{5,6},{6,5},{7,4},{4,7},{9,10},{10,9},{11,... | collective-permute-start | bytes 276488 | tf_op jit(solution)/shard_map/ppermute | solution.py:247

commit v10 on v9

--- a/solution.py
+++ b/solution.py
@@ -26,27 +26,36 @@
 PANEL_PAIRS = [(1, 2), (2, 1), (3, 0), (0, 3)]
 
 
-def pack_panel(spot_ref, cycle_ref, main_ref, tail_ref, *rest):
-    out_ref = rest[-1]
+def pack_panel(spot_ref, cycle_hbm, *rest, steps):
+    out_ref, cycle_ref, sem = rest[-3:]
+    copy = pltpu.make_async_copy(cycle_hbm, cycle_ref, sem)
+    copy.start()
+    for g in range(steps):
+        main_ref, tail_ref = rest[2 * g:2 * g + 2]
+        for o in range(GROUP):
+            out_ref[g, :, START * o:START * (o + 1)] = main_ref[o]
+            out_ref[g, :, PANEL_TAIL + 64 * o:PANEL_TAIL + 64 * (o + 1)] = tail_ref[o, :, 0:64]
+    copy.wait()
     row = lax.broadcasted_iota(jnp.int32, (16, 2), 0)
     column = lax.broadcasted_iota(jnp.int32, (16, 2), 1)
     digits = jnp.zeros((16, 2), jnp.int32)
     for i in range(16):
         value = jnp.where(column == 0, cycle_ref[i] // 64, cycle_ref[i] % 64)
         digits = jnp.where(row == i, value, digits)
-    out_ref[0, :, CYCLE_LANE:CYCLE_LANE + 2] = digits.astype(jnp.float32).astype(jnp.bfloat16)
-    for o in range(GROUP):
-        out_ref[0, :, START * o:START * (o + 1)] = main_ref[o]
-        out_ref[0, :, PANEL_TAIL + 64 * o:PANEL_TAIL + 64 * (o + 1)] = tail_ref[o, :, 0:64]
-
-
-def pack_gauss(gauss_ref, *rest):
+    digits = digits.astype(jnp.float32).astype(jnp.bfloat16)
+    for g in range(steps):
+        out_ref[g, :, CYCLE_LANE:CYCLE_LANE + 2] = digits
+
+
+def pack_gauss(*rest, steps):
     out_ref = rest[-1]
-    for o in range(GROUP):
+    for g in range(steps):
         for k in range(2):
-            j = k * GROUP + o
-            out_ref[0, :, 640 * j:640 * (j + 1)] = gauss_ref[k, o, :, 0:640]
-            out_ref[0, :, GAUSS_TAIL + 80 * j:GAUSS_TAIL + 80 * (j + 1)] = gauss_ref[k, o, :, 640:720]
+            for o in range(GROUP):
+                j = k * GROUP + o
+                plane = rest[2 * g + k]
+                out_ref[g, :, 640 * j:640 * (j + 1)] = plane[0, o, :, 0:640]
+                out_ref[g, :, GAUSS_TAIL + 80 * j:GAUSS_TAIL + 80 * (j + 1)] = plane[0, o, :, 640:720]
 
 
 def panel_specs(skip, upper):
@@ -58,36 +67,43 @@
 
 def packed_panel(spot, cycle, panel, after, base, count):
     steps = count // GROUP
+    specs = []
+    for g in range(steps):
+        specs += panel_specs(base // GROUP + g, lambda blk: 1 - blk // 2)
     return pl.pallas_call(
-        pack_panel,
+        functools.partial(pack_panel, steps=steps),
         out_shape=jax.ShapeDtypeStruct((steps, 16, PANEL_LANES), jnp.bfloat16),
         grid_spec=pltpu.PrefetchScalarGridSpec(
             num_scalar_prefetch=1,
-            grid=(steps,),
-            in_specs=[pl.BlockSpec(memory_space=pltpu.SMEM)]
-            + panel_specs(base // GROUP, lambda blk: 1 - blk // 2)
+            grid=(1,),
+            in_specs=[pl.BlockSpec(memory_space=pl.ANY)] + specs
             + [pl.BlockSpec(memory_space=pl.ANY)] * len(after),
-            out_specs=pl.BlockSpec((1, 16, PANEL_LANES), lambda i, spot: (i, 0, 0)),
+            out_specs=pl.BlockSpec(memory_space=pltpu.VMEM),
+            scratch_shapes=[pltpu.SMEM((16,), jnp.int32), pltpu.SemaphoreType.DMA(())],
         ),
         compiler_params=pltpu.CompilerParams(vmem_limit_bytes=10 << 20),
         cost_estimate=pl.CostEstimate(flops=0, bytes_accessed=count * 100000, transcendentals=0),
         name="pack_panel",
-    )(spot, cycle, panel, panel, *after)
+    )(spot, cycle, *[panel] * (2 * steps), *after)
 
 
 def packed_gauss(own, after, base, count):
     steps, skip = count // GROUP, base // GROUP
+    specs = []
+    for g in range(steps):
+        for k in range(2):
+            specs.append(pl.BlockSpec(
+                (1, GROUP, 16, QUARTER), lambda i, k=k, at=skip + g: (k, at, 0, 0)))
     return pl.pallas_call(
-        pack_gauss,
+        functools.partial(pack_gauss, steps=steps),
         out_shape=jax.ShapeDtypeStruct((steps, 16, GAUSS_LANES), jnp.bfloat16),
-        grid=(steps,),
-        in_specs=[pl.BlockSpec((2, GROUP, 16, QUARTER), lambda i: (0, i + skip, 0, 0))]
-        + [pl.BlockSpec(memory_space=pl.ANY)] * len(after),
-        out_specs=pl.BlockSpec((1, 16, GAUSS_LANES), lambda i: (i, 0, 0)),
+        grid=(1,),
+        in_specs=specs + [pl.BlockSpec(memory_space=pl.ANY)] * len(after),
+        out_specs=pl.BlockSpec(memory_space=pltpu.VMEM),
         compiler_params=pltpu.CompilerParams(vmem_limit_bytes=10 << 20),
         cost_estimate=pl.CostEstimate(flops=0, bytes_accessed=count * 100000, transcendentals=0),
         name="pack_gauss",
-    )(own, *after)
+    )(*[own] * (2 * steps), *after)
 
 
 def sums_kernel(spot_ref, order_ref, decay_ref, cycle_ref, own_ref, other_ref, main_ref, tail_ref,
@@ -216,6 +232,7 @@
     own = jnp.transpose(gauss, (0, 2, 1, 3))
     own = pltpu.with_memory_space_constraint(own, pltpu.HBM)
     panel = pltpu.with_memory_space_constraint(panel, pltpu.HBM)
+    cycle_hbm = pltpu.with_memory_space_constraint(cycle_map, pltpu.HBM)
     spans = list(zip(CHUNKS[:-1], CHUNKS[1:]))
     orders_int = lax.dynamic_slice_in_dim(order_map, here * count, count, 0)
     degree = (spot // 2 * START + jnp.arange(WIDE)).astype(jnp.float32)[None, :]
@@ -227,7 +244,7 @@
     def start(c):
         a, b = spans[c]
         after = (kept[0:1] if c >= 2 else []) + ([packed[-1][2]] if packed else [])
-        part = packed_panel(spot, cycle_map, panel, after, a, b - a)
+        part = packed_panel(spot, cycle_hbm, panel, after, a, b - a)
         far = lax.ppermute(part, "blk", PANEL_PAIRS)
         coef = packed_gauss(own, [part], a, b - a)
         packed.append((lax.ppermute(coef, "blk", GAUSS_PAIRS), far, coef))

time: 109 us -> 107 us (0.982)
  waiting for transfers between devices: 15.9 us -> 13.9 us
  starting transfers between devices: 9.53 us -> 10.9 us
    ppermute x4, waiting for transfers between devices: 12.2 us -> 10.8 us  [start(): packed.append((lax.ppermute(coef, 'blk', GAUSS_PAIRS), far, coef))]
    ppermute x2, starting transfers between devices: 1.52 us -> 2.89 us  [body(): added.append(lax.ppermute(send, 'blk', PANEL_PAIRS))]
  transfers between devices with their start and end apart: 10 -> 10, of which waited for: 5 -> 6; matrix products, arithmetic and copies ran while one was open for 7% -> 7% of each run, Pallas kernels for 22% -> 22%
where the time goes in v10:
time: 107 us; the launch traced here: 106 us
  blocking collectives  41.1 us (38%)
  Pallas kernels  28.3 us (26%)
  waiting for transfers between devices  13.9 us (13%)
  starting transfers between devices  10.9 us (10%)
  local copies, waits for them, and re-layouts  5.3 us (5%)
  other arithmetic  5.25 us (5%)
  matrix products  1.2 us (1%)
    all_to_all x1, blocking collectives, body(): spread = lax.all_to_all(chunk, 'ord', 0, 0, tiled=True).astype(jnp.float32)  25 us
    all_to_all x1, blocking collectives, body(): field = lax.all_to_all(field, 'ord', 0, 0, tiled=True)  16.1 us
    pallas_call x4, Pallas kernels, partial_sums(): pl.pallas_call(functools.partial(sums_kernel, base=base), out_shape=[jax....  15.6 us
    ppermute x4, waiting for transfers between devices, start(): packed.append((lax.ppermute(coef, 'blk', GAUSS_PAIRS), far, coef))  10.8 us
    pallas_call x4, Pallas kernels, packed_panel(): pl.pallas_call(functools.partial(pack_panel, steps=steps), out_shape=jax....  7.76 us
    ppermute x4, starting transfers between devices, start(): far = lax.ppermute(part, 'blk', PANEL_PAIRS)  7.1 us
    pallas_call x4, Pallas kernels, packed_gauss(): pl.pallas_call(functools.partial(pack_gauss, steps=steps), out_shape=jax....  4.99 us
    ppermute x2, waiting for transfers between devices, body(): added.append(lax.ppermute(send, 'blk', PANEL_PAIRS))  3.15 us
  transfers between devices with their start and end apart: 10, of which 6 were waited for; matrix products, arithmetic and copies ran while one was open for 7% of the time, Pallas kernels for 22%

profile of v10, /device:TPU:1, one launch (start us, length us, event | category | flops | bytes accessed | tf_op | source)
XLA Modules:
  0.0 106.4 jit_solution(16385869873678346389)
XLA Ops:
  0.0 2.0 %pack_panel.4.rest_6_ = bf16[3,16,7424]{2,1,0:T(8,128)(2,1)S(1)} custom-call(s32[1]{0:T(128)} %bitcast.spot_ref, s32[16]{0:T(128)} %cycle_ref.7, bf16[45,16,2880]{2,1,0:T(8,128)(2,1)} %tail_ref.7, bf16[45,16,2880]{2,1,0:T(8,128)(2,1)} %tail_ref.7, bf16[45,16,2880]{2,1,0:T(8,128)(2,1)} %tail_ref.7, bf16[45,16,2880]{2,1,0:T(8,128)(2,1)} %tail_ref.7, ...), custom_call_target="tpu_custom_call" | custom-call | bytes 1500000 | tf_op jit(solution)/shard_map/pack_panel/pallas_call | solution.py:73
  2.0 3.4 %collective-permute-start.1 = (bf16[3,16,7424]{2,1,0:T(8,128)(2,1)S(1)}, bf16[3,16,7424]{2,1,0:T(8,128)(2,1)}, u32[]{:S(2)}, u32[]{:S(2)}) collective-permute-start(bf16[3,16,7424]{2,1,0:T(8,128)(2,1)S(1)} %pack_panel.4.rest_6_), channel_id=1, source_target_pairs={{1,2},{2,1},{3,0},{0,3},{5,6},{6,5},{7,4},{4,7},{9,10},{10,9},{11,... | collective-permute-start | bytes 2138120 | tf_op jit(solution)/shard_map/ppermute | solution.py:248
  5.4 1.4 %pack_gauss.4.rest_6_ = bf16[3,16,7296]{2,1,0:T(8,128)(2,1)S(1)} custom-call(bf16[2,45,16,720]{3,2,1,0:T(8,128)(2,1)} %bitcast.31, bf16[2,45,16,720]{3,2,1,0:T(8,128)(2,1)} %bitcast.32, bf16[2,45,16,720]{3,2,1,0:T(8,128)(2,1)} %bitcast.33, bf16[2,45,16,720]{3,2,1,0:T(8,128)(2,1)} %bitcast.34, bf16[2,45,16,720]{3,2,1,0:T(8,128)(2,1)} %bitcast.35, ...), custom_call_target="tpu_custom_call" | custom-call | bytes 1500000 | tf_op jit(solution)/shard_map/pack_gauss/pallas_call | solution.py:97
  6.9 2.0 %pack_panel.5.rest_6_ = bf16[3,16,7424]{2,1,0:T(8,128)(2,1)S(1)} custom-call(s32[1]{0:T(128)} %bitcast.spot_ref, s32[16]{0:T(128)} %cycle_ref.7, bf16[45,16,2880]{2,1,0:T(8,128)(2,1)} %tail_ref.7, bf16[45,16,2880]{2,1,0:T(8,128)(2,1)} %tail_ref.7, bf16[45,16,2880]{2,1,0:T(8,128)(2,1)} %tail_ref.7, bf16[45,16,2880]{2,1,0:T(8,128)(2,1)} %tail_ref.7, ...), custom_call_target="tpu_custom_call" | custom-call | bytes 1500000 | tf_op jit(solution)/shard_map/pack_panel/pallas_call | solution.py:73
  9.8 1.4 %pack_gauss.5.rest_5_ = bf16[3,16,7296]{2,1,0:T(8,128)(2,1)S(1)} custom-call(bf16[2,45,16,720]{3,2,1,0:T(8,128)(2,1)} %bitcast.37, bf16[2,45,16,720]{3,2,1,0:T(8,128)(2,1)} %bitcast.38, bf16[2,45,16,720]{3,2,1,0:T(8,128)(2,1)} %bitcast.39, bf16[2,45,16,720]{3,2,1,0:T(8,128)(2,1)} %bitcast.40, bf16[2,45,16,720]{3,2,1,0:T(8,128)(2,1)} %bitcast.41, ...), custom_call_target="tpu_custom_call" | custom-call | bytes 1500000 | tf_op jit(solution)/shard_map/pack_gauss/pallas_call | solution.py:97
  13.2 1.4 %slice.19 = s32[64]{0:T(128)} slice(s32[2880]{0:T(1024)} %param.8), slice={[0:2880:45]} | slice | bytes 512 | tf_op jit(solution)/shard_map/slice | solution.py:274
  14.6 1.5 %multiply_exponential_fusion.1 = (f32[1,16,1536]{2,1,0:T(8,128)}, f32[1,16,1536]{2,1,0:T(8,128)}, f32[1,16,1536]{2,1,0:T(8,128)}) fusion(f32[16]{0:T(128)S(1)} %copy-done.2, f32[1536]{0:T(1024)} %get-tuple-element.44, f32[1536]{0:T(1024)} %convert_add_fusion, f32[1536]{0:T(1024)S(1)} %get-tuple-element.43), kind=kLoop, calls=%fused_computation.20 | loop fusion | flops 122880 | bytes 313408 | tf_op jit(solution)/shard_map/exp | solution.py:239
  17.6 1.0 pad_maximum_fusion.decay_ref
  18.6 4.7 %collective-permute-done.other_ref = bf16[3,16,7296]{2,1,0:T(8,128)(2,1)} collective-permute-done((bf16[3,16,7296]{2,1,0:T(8,128)(2,1)S(1)}, bf16[3,16,7296]{2,1,0:T(8,128)(2,1)}, u32[]{:S(2)}, u32[]{:S(2)}) %collective-permute-start) | collective-permute-done | bytes 700448 | tf_op jit(solution)/shard_map/ppermute | solution.py:250
  23.2 5.0 %partial_sums.4 = (f32[15,16,96]{2,1,0:T(8,128)S(1)}, bf16[15,16,96]{2,1,0:T(8,128)(2,1)S(1)}) custom-call(s32[1]{0:T(128)} %bitcast.spot_ref, s32[45]{0:T(128)S(1)} %dynamic_slice.3.order_ref, f32[3,16,1536]{2,1,0:T(8,128)S(1)} %pad_maximum_fusion.decay_ref, s32[16]{0:T(128)S(1)} %copy-done, bf16[2,45,16,720]{3,2,1,0:T(8,128)(2,1)} %bitcast.43, ...), custom_call_target="tpu_custom_call" | custom-call | flops 188743680 | bytes 3000000 | tf_op jit(solution)/shard_map/partial_sums/pallas_call | solution.py:191
  28.2 1.9 %pack_panel.6.rest_4_ = bf16[2,16,7424]{2,1,0:T(8,128)(2,1)S(1)} custom-call(s32[1]{0:T(128)} %bitcast.spot_ref, s32[16]{0:T(128)} %cycle_ref.7, bf16[45,16,2880]{2,1,0:T(8,128)(2,1)} %tail_ref.7, bf16[45,16,2880]{2,1,0:T(8,128)(2,1)} %tail_ref.7, bf16[45,16,2880]{2,1,0:T(8,128)(2,1)} %tail_ref.7, bf16[45,16,2880]{2,1,0:T(8,128)(2,1)} %tail_ref.7, ...), custom_call_target="tpu_custom_call" | custom-call | bytes 1000000 | tf_op jit(solution)/shard_map/pack_panel/pallas_call | solution.py:73
  30.1 1.2 %pack_gauss.6.rest_3_ = bf16[2,16,7296]{2,1,0:T(8,128)(2,1)S(1)} custom-call(bf16[2,45,16,720]{3,2,1,0:T(8,128)(2,1)} %bitcast.44, bf16[2,45,16,720]{3,2,1,0:T(8,128)(2,1)} %bitcast.45, bf16[2,45,16,720]{3,2,1,0:T(8,128)(2,1)} %bitcast.46, bf16[2,45,16,720]{3,2,1,0:T(8,128)(2,1)} %bitcast.47, bf16[2,16,7424]{2,1,0:T(8,128)(2,1)S(1)} %pack_panel.6.rest_4_), custom_call_target="tpu_custom_call" | custom-call | bytes 1000000 | tf_op jit(solution)/shard_map/pack_gauss/pallas_call | solution.py:97
  32.2 1.8 %pack_panel.7.rest_2_ = bf16[1,16,7424]{2,1,0:T(8,128)(2,1)S(1)} custom-call(s32[1]{0:T(128)} %bitcast.spot_ref, s32[16]{0:T(128)} %cycle_ref.7, bf16[45,16,2880]{2,1,0:T(8,128)(2,1)} %tail_ref.7, bf16[45,16,2880]{2,1,0:T(8,128)(2,1)} %tail_ref.7, f32[15,16,96]{2,1,0:T(8,128)S(1)} %get-tuple-element.18.rest_4_.rest_2_.rest_0_, ...), custom_call_target="tpu_custom_call" | custom-call | bytes 500000 | tf_op jit(solution)/shard_map/pack_panel/pallas_call | solution.py:73
  34.0 1.1 pack_gauss.7
  35.1 2.4 %collective-permute-start.3 = (bf16[1,16,7424]{2,1,0:T(8,128)(2,1)S(1)}, bf16[1,16,7424]{2,1,0:T(8,128)(2,1)S(1)}, u32[]{:S(2)}, u32[]{:S(2)}) collective-permute-start(bf16[1,16,7424]{2,1,0:T(8,128)(2,1)S(1)} %pack_panel.7.rest_2_), channel_id=1, source_target_pairs={{1,2},{2,1},{3,0},{0,3},{5,6},{6,5},{7,4},{4,7},{9,10},{10,9},{11,... | collective-permute-start | bytes 712712 | tf_op jit(solution)/shard_map/ppermute | solution.py:248
  39.4 4.7 %partial_sums.5 = (f32[30,16,96]{2,1,0:T(8,128)S(1)}, bf16[30,16,96]{2,1,0:T(8,128)(2,1)S(1)}) custom-call(s32[1]{0:T(128)} %bitcast.spot_ref, s32[45]{0:T(128)S(1)} %dynamic_slice.3.order_ref, f32[3,16,1536]{2,1,0:T(8,128)S(1)} %pad_maximum_fusion.decay_ref, s32[16]{0:T(128)S(1)} %copy-done.1, bf16[2,45,16,720]{3,2,1,0:T(8,128)(2,1)} %bitcast.50, ...), custom_call_target="tpu_custom_call" | custom-call | flops 188743680 | bytes 3000000 | tf_op jit(solution)/shard_map/partial_sums/pallas_call | solution.py:191
  44.1 4.0 %collective-permute-done.4.other_ref = bf16[2,16,7296]{2,1,0:T(8,128)(2,1)S(1)} collective-permute-done((bf16[2,16,7296]{2,1,0:T(8,128)(2,1)S(1)}, bf16[2,16,7296]{2,1,0:T(8,128)(2,1)S(1)}, u32[]{:S(2)}, u32[]{:S(2)}) %collective-permute-start.4) | collective-permute-done | bytes 466976 | tf_op jit(solution)/shard_map/ppermute | solution.py:250
  48.1 3.4 %partial_sums.6 = (f32[30,16,96]{2,1,0:T(8,128)S(1)}, bf16[30,16,96]{2,1,0:T(8,128)(2,1)S(1)}) custom-call(s32[1]{0:T(128)} %bitcast.spot_ref, s32[45]{0:T(128)S(1)} %dynamic_slice.3.order_ref, f32[3,16,1536]{2,1,0:T(8,128)S(1)} %pad_maximum_fusion.decay_ref, s32[16]{0:T(128)S(1)} %copy-done.1, ...), custom_call_target="tpu_custom_call", output_to_operand_aliasing={{0}: (9, {}), {1}: (10, {})} | custom-call | flops 125829120 | bytes 2000000 | tf_op jit(solution)/shard_map/partial_sums/pallas_call | solution.py:191
  51.8 1.3 %collective-permute-done.2.other_ref = bf16[1,16,7296]{2,1,0:T(8,128)(2,1)S(1)} collective-permute-done((bf16[1,16,7296]{2,1,0:T(8,128)(2,1)S(1)}, bf16[1,16,7296]{2,1,0:T(8,128)(2,1)S(1)}, u32[]{:S(2)}, u32[]{:S(2)}) %collective-permute-start.2) | collective-permute-done | bytes 233504 | tf_op jit(solution)/shard_map/ppermute | solution.py:250
  53.1 2.5 %partial_sums.7 = (f32[30,16,96]{2,1,0:T(8,128)S(1)}, bf16[30,16,96]{2,1,0:T(8,128)(2,1)S(1)}) custom-call(s32[1]{0:T(128)} %bitcast.spot_ref, s32[45]{0:T(128)S(1)} %dynamic_slice.3.order_ref, f32[3,16,1536]{2,1,0:T(8,128)S(1)} %pad_maximum_fusion.decay_ref, s32[16]{0:T(128)S(1)} %copy-done.1, ...), custom_call_target="tpu_custom_call", output_to_operand_aliasing={{0}: (9, {}), {1}: (10, {})} | custom-call | flops 62914560 | bytes 1000000 | tf_op jit(solution)/shard_map/partial_sums/pallas_call | solution.py:191
  55.7 2.1 %collective-permute-start.9 = (bf16[30,16,96]{2,1,0:T(8,128)(2,1)S(1)}, bf16[30,16,96]{2,1,0:T(8,128)(2,1)S(1)}, u32[]{:S(2)}, u32[]{:S(2)}) collective-permute-start(bf16[30,16,96]{2,1,0:T(8,128)(2,1)S(1)} %get-tuple-element.25), channel_id=1, source_target_pairs={{1,2},{2,1},{3,0},{0,3},{5,6},{6,5},{7,4},{4,7},{9,10},{10,9},{11,... | collective-permute-start | bytes 276488 | tf_op jit(solution)/shard_map/ppermute | solution.py:264
  57.8 2.9 %collective-permute-done.9 = bf16[30,16,96]{2,1,0:T(8,128)(2,1)S(1)} collective-permute-done((bf16[30,16,96]{2,1,0:T(8,128)(2,1)S(1)}, bf16[30,16,96]{2,1,0:T(8,128)(2,1)S(1)}, u32[]{:S(2)}, u32[]{:S(2)}) %collective-permute-start.9) | collective-permute-done | bytes 92192 | tf_op jit(solution)/shard_map/ppermute | solution.py:264
  61.8 25.0 %all_to_all.10 = bf16[64,2,540]{2,1,0:T(2,128)(2,1)S(1)} all-to-all(bf16[64,2,540]{2,1,0:T(2,128)(2,1)S(1)} %copy.18), channel_id=1, replica_groups=mesh['ord'=64,'blk'=4] {'ord'}, dimensions={0} | all-to-all | bytes 276480 | tf_op jit(solution)/shard_map/all_to_all | solution.py:286
  89.4 16.1 %all_to_all.11 = bf16[192,4,90]{2,1,0:T(4,128)(2,1)S(1)} all-to-all(bf16[192,4,90]{2,1,0:T(4,128)(2,1)S(1)} %bitcast.54), channel_id=1, replica_groups=mesh['ord'=64,'blk'=4] {'ord'}, dimensions={0} | all-to-all | bytes 276480 | tf_op jit(solution)/shard_map/all_to_all | solution.py:297
  (46 shorter events, 12.0 us)
Async XLA Ops:
  2.0 21.2 %collective-permute-start.1 = (bf16[3,16,7424]{2,1,0:T(8,128)(2,1)S(1)}, bf16[3,16,7424]{2,1,0:T(8,128)(2,1)}, u32[]{:S(2)}, u32[]{:S(2)}) collective-permute-start(bf16[3,16,7424]{2,1,0:T(8,128)(2,1)S(1)} %pack_panel.4.rest_6_), channel_id=1, source_target_pairs={{1,2},{2,1},{3,0},{0,3},{5,6},{6,5},{7,4},{4,7},{9,10},{10,9},{11,... | collective-permute-start | bytes 2138120 | tf_op jit(solution)/shard_map/ppermute | solution.py:248
  6.8 16.4 %collective-permute-start = (bf16[3,16,7296]{2,1,0:T(8,128)(2,1)S(1)}, bf16[3,16,7296]{2,1,0:T(8,128)(2,1)}, u32[]{:S(2)}, u32[]{:S(2)}) collective-permute-start(bf16[3,16,7296]{2,1,0:T(8,128)(2,1)S(1)} %pack_gauss.4.rest_6_), channel_id=1, source_target_pairs={{0,1},{1,0},{2,3},{3,2},{4,5},{5,4},{6,7},{7,6},{8,9},{9,8},{10,11... | collective-permute-start | bytes 2101256 | tf_op jit(solution)/shard_map/ppermute | solution.py:250
  8.9 5.6 %copy-start.2 = (f32[16]{0:T(128)S(1)}, f32[16]{0:T(128)}, u32[]{:S(2)}) copy-start(f32[16]{0:T(128)} %param.7) | copy-start | bytes 196
  9.0 14.3 %copy-start = (s32[16]{0:T(128)S(1)}, s32[16]{0:T(128)}, u32[]{:S(2)}) copy-start(s32[16]{0:T(128)} %cycle_ref.7) | copy-start | bytes 196
  9.0 29.5 %collective-permute-start.7 = (bf16[3,16,7424]{2,1,0:T(8,128)(2,1)S(1)}, bf16[3,16,7424]{2,1,0:T(8,128)(2,1)S(1)}, u32[]{:S(2)}, u32[]{:S(2)}) collective-permute-start(bf16[3,16,7424]{2,1,0:T(8,128)(2,1)S(1)} %pack_panel.5.rest_6_), channel_id=1, source_target_pairs={{1,2},{2,1},{3,0},{0,3},{5,6},{6,5},{7,4},{4,7},{9,10},{10,9},{11,... | collective-permute-start | bytes 2138120 | tf_op jit(solution)/shard_map/ppermute | solution.py:248
  11.2 27.1 %collective-permute-start.6 = (bf16[3,16,7296]{2,1,0:T(8,128)(2,1)S(1)}, bf16[3,16,7296]{2,1,0:T(8,128)(2,1)}, u32[]{:S(2)}, u32[]{:S(2)}) collective-permute-start(bf16[3,16,7296]{2,1,0:T(8,128)(2,1)S(1)} %pack_gauss.5.rest_5_), channel_id=1, source_target_pairs={{0,1},{1,0},{2,3},{3,2},{4,5},{5,4},{6,7},{7,6},{8,9},{9,8},{10,11... | collective-permute-start | bytes 2101256 | tf_op jit(solution)/shard_map/ppermute | solution.py:250
  31.3 16.8 %collective-permute-start.5 = (bf16[2,16,7424]{2,1,0:T(8,128)(2,1)S(1)}, bf16[2,16,7424]{2,1,0:T(8,128)(2,1)S(1)}, u32[]{:S(2)}, u32[]{:S(2)}) collective-permute-start(bf16[2,16,7424]{2,1,0:T(8,128)(2,1)S(1)} %pack_panel.6.rest_4_), channel_id=1, source_target_pairs={{1,2},{2,1},{3,0},{0,3},{5,6},{6,5},{7,4},{4,7},{9,10},{10,9},{11,... | collective-permute-start | bytes 1425416 | tf_op jit(solution)/shard_map/ppermute | solution.py:248
  31.8 16.3 %collective-permute-start.4 = (bf16[2,16,7296]{2,1,0:T(8,128)(2,1)S(1)}, bf16[2,16,7296]{2,1,0:T(8,128)(2,1)S(1)}, u32[]{:S(2)}, u32[]{:S(2)}) collective-permute-start(bf16[2,16,7296]{2,1,0:T(8,128)(2,1)S(1)} %pack_gauss.6.rest_3_), channel_id=1, source_target_pairs={{0,1},{1,0},{2,3},{3,2},{4,5},{5,4},{6,7},{7,6},{8,9},{9,8},{10,11... | collective-permute-start | bytes 1400840 | tf_op jit(solution)/shard_map/ppermute | solution.py:250
  34.0 5.4 %copy-start.1 = (s32[16]{0:T(128)S(1)}, s32[16]{0:T(128)}, u32[]{:S(2)}) copy-start(s32[16]{0:T(128)} %cycle_ref.7) | copy-start | bytes 196
  35.1 18.0 %collective-permute-start.3 = (bf16[1,16,7424]{2,1,0:T(8,128)(2,1)S(1)}, bf16[1,16,7424]{2,1,0:T(8,128)(2,1)S(1)}, u32[]{:S(2)}, u32[]{:S(2)}) collective-permute-start(bf16[1,16,7424]{2,1,0:T(8,128)(2,1)S(1)} %pack_panel.7.rest_2_), channel_id=1, source_target_pairs={{1,2},{2,1},{3,0},{0,3},{5,6},{6,5},{7,4},{4,7},{9,10},{10,9},{11,... | collective-permute-start | bytes 712712 | tf_op jit(solution)/shard_map/ppermute | solution.py:248
  38.2 14.9 %collective-permute-start.2 = (bf16[1,16,7296]{2,1,0:T(8,128)(2,1)S(1)}, bf16[1,16,7296]{2,1,0:T(8,128)(2,1)S(1)}, u32[]{:S(2)}, u32[]{:S(2)}) collective-permute-start(bf16[1,16,7296]{2,1,0:T(8,128)(2,1)S(1)} %pack_gauss.7), channel_id=1, source_target_pairs={{0,1},{1,0},{2,3},{3,2},{4,5},{5,4},{6,7},{7,6},{8,9},{9,8},{10,11... | collective-permute-start | bytes 700424 | tf_op jit(solution)/shard_map/ppermute | solution.py:250
  38.5 13.4 %collective-permute-start.8 = (bf16[15,16,96]{2,1,0:T(8,128)(2,1)S(1)}, bf16[15,16,96]{2,1,0:T(8,128)(2,1)S(1)}, u32[]{:S(2)}, u32[]{:S(2)}) collective-permute-start(bf16[15,16,96]{2,1,0:T(8,128)(2,1)S(1)} %get-tuple-element.23), channel_id=1, source_target_pairs={{1,2},{2,1},{3,0},{0,3},{5,6},{6,5},{7,4},{4,7},{9,10},{10,9},{11,... | collective-permute-start | bytes 138248 | tf_op jit(solution)/shard_map/ppermute | solution.py:264
  55.7 5.0 %collective-permute-start.9 = (bf16[30,16,96]{2,1,0:T(8,128)(2,1)S(1)}, bf16[30,16,96]{2,1,0:T(8,128)(2,1)S(1)}, u32[]{:S(2)}, u32[]{:S(2)}) collective-permute-start(bf16[30,16,96]{2,1,0:T(8,128)(2,1)S(1)} %get-tuple-element.25), channel_id=1, source_target_pairs={{1,2},{2,1},{3,0},{0,3},{5,6},{6,5},{7,4},{4,7},{9,10},{10,9},{11,... | collective-permute-start | bytes 276488 | tf_op jit(solution)/shard_map/ppermute | solution.py:264

commit v11 on v10

--- a/solution.py
+++ b/solution.py
@@ -26,25 +26,22 @@
 PANEL_PAIRS = [(1, 2), (2, 1), (3, 0), (0, 3)]
 
 
-def pack_panel(spot_ref, cycle_hbm, *rest, steps):
-    out_ref, cycle_ref, sem = rest[-3:]
-    copy = pltpu.make_async_copy(cycle_hbm, cycle_ref, sem)
-    copy.start()
+def pack_panel(spot_ref, cycle_ref, *rest, steps):
+    out_ref = rest[-1]
+    cycle = cycle_ref[...]
+    row = lax.broadcasted_iota(jnp.int32, (16, 16), 0)
+    lane = lax.broadcasted_iota(jnp.int32, (16, 16), 1)
+    digits = []
+    for digit in (cycle // 64, cycle % 64):
+        spread = jnp.broadcast_to(digit.astype(jnp.float32), (16, 16))
+        digits.append(jnp.sum(jnp.where(row == lane, spread, 0.0), 1, keepdims=True))
+    digits = jnp.concatenate(digits, 1).astype(jnp.bfloat16)
     for g in range(steps):
         main_ref, tail_ref = rest[2 * g:2 * g + 2]
+        out_ref[g, :, CYCLE_LANE:CYCLE_LANE + 2] = digits
         for o in range(GROUP):
             out_ref[g, :, START * o:START * (o + 1)] = main_ref[o]
             out_ref[g, :, PANEL_TAIL + 64 * o:PANEL_TAIL + 64 * (o + 1)] = tail_ref[o, :, 0:64]
-    copy.wait()
-    row = lax.broadcasted_iota(jnp.int32, (16, 2), 0)
-    column = lax.broadcasted_iota(jnp.int32, (16, 2), 1)
-    digits = jnp.zeros((16, 2), jnp.int32)
-    for i in range(16):
-        value = jnp.where(column == 0, cycle_ref[i] // 64, cycle_ref[i] % 64)
-        digits = jnp.where(row == i, value, digits)
-    digits = digits.astype(jnp.float32).astype(jnp.bfloat16)
-    for g in range(steps):
-        out_ref[g, :, CYCLE_LANE:CYCLE_LANE + 2] = digits
 
 
 def pack_gauss(*rest, steps):
@@ -76,10 +73,9 @@
         grid_spec=pltpu.PrefetchScalarGridSpec(
             num_scalar_prefetch=1,
             grid=(1,),
-            in_specs=[pl.BlockSpec(memory_space=pl.ANY)] + specs
+            in_specs=[pl.BlockSpec((1, 16), lambda i, spot: (0, 0))] + specs
             + [pl.BlockSpec(memory_space=pl.ANY)] * len(after),
             out_specs=pl.BlockSpec(memory_space=pltpu.VMEM),
-            scratch_shapes=[pltpu.SMEM((16,), jnp.int32), pltpu.SemaphoreType.DMA(())],
         ),
         compiler_params=pltpu.CompilerParams(vmem_limit_bytes=10 << 20),
         cost_estimate=pl.CostEstimate(flops=0, bytes_accessed=count * 100000, transcendentals=0),
@@ -187,6 +183,7 @@
     into = place // GROUP
     total = begun[0].shape[0] if begun else size
     smem = pl.BlockSpec(memory_space=pltpu.SMEM)
+    here = pl.BlockSpec(memory_space=pltpu.VMEM)
     out = pl.BlockSpec((GROUP, 16, 96), lambda i, spot: (i + into, 0, 0))
     return pl.pallas_call(
         functools.partial(sums_kernel, base=base),
@@ -197,11 +194,11 @@
             num_scalar_prefetch=1,
             grid=(count // GROUP,),
             in_specs=[
-                smem, pl.BlockSpec((3, 16, WIDE), lambda i, spot: (0, 0, 0)), smem,
+                smem, here, smem,
                 pl.BlockSpec((2, GROUP, 16, QUARTER), lambda i, spot: (0, i + skip, 0, 0)),
-                pl.BlockSpec((1, 16, GAUSS_LANES), lambda i, spot: (i, 0, 0)),
+                here if count == GROUP else pl.BlockSpec((1, 16, GAUSS_LANES), lambda i, spot: (i, 0, 0)),
             ] + panel_specs(skip, lambda blk: blk // 2)
-            + [pl.BlockSpec((1, 16, PANEL_LANES), lambda i, spot: (i, 0, 0))]
+            + [here if count == GROUP else pl.BlockSpec((1, 16, PANEL_LANES), lambda i, spot: (i, 0, 0))]
             + [pl.BlockSpec(memory_space=pl.ANY)] * (len(begun) + len(after)),
             out_specs=[out, out],
             scratch_shapes=[
@@ -232,7 +229,7 @@
     own = jnp.transpose(gauss, (0, 2, 1, 3))
     own = pltpu.with_memory_space_constraint(own, pltpu.HBM)
     panel = pltpu.with_memory_space_constraint(panel, pltpu.HBM)
-    cycle_hbm = pltpu.with_memory_space_constraint(cycle_map, pltpu.HBM)
+    cycle_row = pltpu.with_memory_space_constraint(cycle_map[None, :], pltpu.HBM)
     spans = list(zip(CHUNKS[:-1], CHUNKS[1:]))
     orders_int = lax.dynamic_slice_in_dim(order_map, here * count, count, 0)
     degree = (spot // 2 * START + jnp.arange(WIDE)).astype(jnp.float32)[None, :]
@@ -244,7 +241,7 @@
     def start(c):
         a, b = spans[c]
         after = (kept[0:1] if c >= 2 else []) + ([packed[-1][2]] if packed else [])
-        part = packed_panel(spot, cycle_hbm, panel, after, a, b - a)
+        part = packed_panel(spot, cycle_row, panel, after, a, b - a)
         far = lax.ppermute(part, "blk", PANEL_PAIRS)
         coef = packed_gauss(own, [part], a, b - a)
         packed.append((lax.ppermute(coef, "blk", GAUSS_PAIRS), far, coef))

time: 107 us -> 106 us (level)
  Pallas kernels: 28.3 us -> 25.6 us
  waiting for transfers between devices: 13.9 us -> 16.1 us
    pallas_call x4, Pallas kernels: 7.76 us -> 5.18 us  [packed_panel(): pl.pallas_call(functools.partial(pack_panel, steps=steps), out_shape=jax....]
    ppermute x4, waiting for transfers between devices: 10.8 us -> 13.2 us  [start(): packed.append((lax.ppermute(coef, 'blk', GAUSS_PAIRS), far, coef))]
  transfers between devices with their start and end apart: 10 -> 10, of which waited for: 6 -> 6; matrix products, arithmetic and copies ran while one was open for 7% -> 7% of each run, Pallas kernels for 22% -> 21%
where the time goes in v11:
time: 106 us
  blocking collectives  41.2 us (39%)
  Pallas kernels  25.6 us (24%)
  waiting for transfers between devices  16.1 us (15%)
  starting transfers between devices  10.8 us (10%)
  local copies, waits for them, and re-layouts  5.31 us (5%)
  other arithmetic  5.25 us (5%)
  matrix products  1.19 us (1%)
    all_to_all x1, blocking collectives, body(): spread = lax.all_to_all(chunk, 'ord', 0, 0, tiled=True).astype(jnp.float32)  25.1 us
    all_to_all x1, blocking collectives, body(): field = lax.all_to_all(field, 'ord', 0, 0, tiled=True)  16.1 us
    pallas_call x4, Pallas kernels, partial_sums(): pl.pallas_call(functools.partial(sums_kernel, base=base), out_shape=[jax....  15.4 us
    ppermute x4, waiting for transfers between devices, start(): packed.append((lax.ppermute(coef, 'blk', GAUSS_PAIRS), far, coef))  13.2 us
    ppermute x4, starting transfers between devices, start(): far = lax.ppermute(part, 'blk', PANEL_PAIRS)  7.09 us
    pallas_call x4, Pallas kernels, packed_panel(): pl.pallas_call(functools.partial(pack_panel, steps=steps), out_shape=jax....  5.18 us
    pallas_call x4, Pallas kernels, packed_gauss(): pl.pallas_call(functools.partial(pack_gauss, steps=steps), out_shape=jax....  5.02 us
    ppermute x2, waiting for transfers between devices, body(): added.append(lax.ppermute(send, 'blk', PANEL_PAIRS))  2.97 us
  transfers between devices with their start and end apart: 10, of which 6 were waited for; matrix products, arithmetic and copies ran while one was open for 7% of the time, Pallas kernels for 21%

profile of v11, /device:TPU:1, one launch (start us, length us, event | category | flops | bytes accessed | tf_op | source)
XLA Modules:
  0.0 105.7 jit_solution(3048120612774930017)
XLA Ops:
  0.0 1.4 %pack_panel.4.rest_6_ = bf16[3,16,7424]{2,1,0:T(8,128)(2,1)S(1)} custom-call(s32[1]{0:T(128)} %bitcast.spot_ref, s32[1,16]{1,0:T(1,128)} %bitcast.32, bf16[45,16,2880]{2,1,0:T(8,128)(2,1)} %tail_ref.7, bf16[45,16,2880]{2,1,0:T(8,128)(2,1)} %tail_ref.7, bf16[45,16,2880]{2,1,0:T(8,128)(2,1)} %tail_ref.7, bf16[45,16,2880]{2,1,0:T(8,128)(2,1)} %tail_ref.7, ...), custom_call_target="tpu_custom_call" | custom-call | bytes 1500000 | tf_op jit(solution)/shard_map/pack_panel/pallas_call | solution.py:70
  1.4 3.4 %collective-permute-start.1 = (bf16[3,16,7424]{2,1,0:T(8,128)(2,1)S(1)}, bf16[3,16,7424]{2,1,0:T(8,128)(2,1)}, u32[]{:S(2)}, u32[]{:S(2)}) collective-permute-start(bf16[3,16,7424]{2,1,0:T(8,128)(2,1)S(1)} %pack_panel.4.rest_6_), channel_id=1, source_target_pairs={{1,2},{2,1},{3,0},{0,3},{5,6},{6,5},{7,4},{4,7},{9,10},{10,9},{11,... | collective-permute-start | bytes 2138120 | tf_op jit(solution)/shard_map/ppermute | solution.py:245
  4.8 1.4 %pack_gauss.4.rest_6_ = bf16[3,16,7296]{2,1,0:T(8,128)(2,1)S(1)} custom-call(bf16[2,45,16,720]{3,2,1,0:T(8,128)(2,1)} %bitcast.36, bf16[2,45,16,720]{3,2,1,0:T(8,128)(2,1)} %bitcast.37, bf16[2,45,16,720]{3,2,1,0:T(8,128)(2,1)} %bitcast.38, bf16[2,45,16,720]{3,2,1,0:T(8,128)(2,1)} %bitcast.39, bf16[2,45,16,720]{3,2,1,0:T(8,128)(2,1)} %bitcast.40, ...), custom_call_target="tpu_custom_call" | custom-call | bytes 1500000 | tf_op jit(solution)/shard_map/pack_gauss/pallas_call | solution.py:93
  6.2 1.4 %pack_panel.5.rest_6_ = bf16[3,16,7424]{2,1,0:T(8,128)(2,1)S(1)} custom-call(s32[1]{0:T(128)} %bitcast.spot_ref, s32[1,16]{1,0:T(1,128)} %bitcast.33, bf16[45,16,2880]{2,1,0:T(8,128)(2,1)} %tail_ref.7, bf16[45,16,2880]{2,1,0:T(8,128)(2,1)} %tail_ref.7, bf16[45,16,2880]{2,1,0:T(8,128)(2,1)} %tail_ref.7, bf16[45,16,2880]{2,1,0:T(8,128)(2,1)} %tail_ref.7, ...), custom_call_target="tpu_custom_call" | custom-call | bytes 1500000 | tf_op jit(solution)/shard_map/pack_panel/pallas_call | solution.py:70
  8.5 1.4 %pack_gauss.5.rest_5_ = bf16[3,16,7296]{2,1,0:T(8,128)(2,1)S(1)} custom-call(bf16[2,45,16,720]{3,2,1,0:T(8,128)(2,1)} %bitcast.42, bf16[2,45,16,720]{3,2,1,0:T(8,128)(2,1)} %bitcast.43, bf16[2,45,16,720]{3,2,1,0:T(8,128)(2,1)} %bitcast.44, bf16[2,45,16,720]{3,2,1,0:T(8,128)(2,1)} %bitcast.45, bf16[2,45,16,720]{3,2,1,0:T(8,128)(2,1)} %bitcast.46, ...), custom_call_target="tpu_custom_call" | custom-call | bytes 1500000 | tf_op jit(solution)/shard_map/pack_gauss/pallas_call | solution.py:93
  11.9 1.4 %slice.19 = s32[64]{0:T(128)} slice(s32[2880]{0:T(1024)} %param.8), slice={[0:2880:45]} | slice | bytes 512 | tf_op jit(solution)/shard_map/slice | solution.py:271
  13.3 1.5 %multiply_exponential_fusion.1 = (f32[1,16,1536]{2,1,0:T(8,128)}, f32[1,16,1536]{2,1,0:T(8,128)}, f32[1,16,1536]{2,1,0:T(8,128)}) fusion(f32[16]{0:T(128)S(1)} %copy-done.2, f32[1536]{0:T(1024)} %get-tuple-element.44, f32[1536]{0:T(1024)} %convert_add_fusion, f32[1536]{0:T(1024)S(1)} %get-tuple-element.43), kind=kLoop, calls=%fused_computation.20 | loop fusion | flops 122880 | bytes 313408 | tf_op jit(solution)/shard_map/exp | solution.py:236
  17.3 5.3 %collective-permute-done.other_ref = bf16[3,16,7296]{2,1,0:T(8,128)(2,1)} collective-permute-done((bf16[3,16,7296]{2,1,0:T(8,128)(2,1)S(1)}, bf16[3,16,7296]{2,1,0:T(8,128)(2,1)}, u32[]{:S(2)}, u32[]{:S(2)}) %collective-permute-start) | collective-permute-done | bytes 700448 | tf_op jit(solution)/shard_map/ppermute | solution.py:247
  22.6 4.9 %partial_sums.4 = (f32[15,16,96]{2,1,0:T(8,128)S(1)}, bf16[15,16,96]{2,1,0:T(8,128)(2,1)S(1)}) custom-call(s32[1]{0:T(128)} %bitcast.spot_ref, s32[45]{0:T(128)S(1)} %dynamic_slice.3.order_ref, f32[3,16,1536]{2,1,0:T(8,128)S(1)} %pad_maximum_fusion.decay_ref, s32[16]{0:T(128)S(1)} %copy-done, bf16[2,45,16,720]{3,2,1,0:T(8,128)(2,1)} %bitcast.48, ...), custom_call_target="tpu_custom_call" | custom-call | flops 188743680 | bytes 3000000 | tf_op jit(solution)/shard_map/partial_sums/pallas_call | solution.py:188
  27.5 1.3 %pack_panel.6.rest_4_ = bf16[2,16,7424]{2,1,0:T(8,128)(2,1)S(1)} custom-call(s32[1]{0:T(128)} %bitcast.spot_ref, s32[1,16]{1,0:T(1,128)} %bitcast.34, bf16[45,16,2880]{2,1,0:T(8,128)(2,1)} %tail_ref.7, bf16[45,16,2880]{2,1,0:T(8,128)(2,1)} %tail_ref.7, bf16[45,16,2880]{2,1,0:T(8,128)(2,1)} %tail_ref.7, bf16[45,16,2880]{2,1,0:T(8,128)(2,1)} %tail_ref.7, ...), custom_call_target="tpu_custom_call" | custom-call | bytes 1000000 | tf_op jit(solution)/shard_map/pack_panel/pallas_call | solution.py:70
  28.8 1.2 %pack_gauss.6.rest_3_ = bf16[2,16,7296]{2,1,0:T(8,128)(2,1)S(1)} custom-call(bf16[2,45,16,720]{3,2,1,0:T(8,128)(2,1)} %bitcast.49, bf16[2,45,16,720]{3,2,1,0:T(8,128)(2,1)} %bitcast.50, bf16[2,45,16,720]{3,2,1,0:T(8,128)(2,1)} %bitcast.51, bf16[2,45,16,720]{3,2,1,0:T(8,128)(2,1)} %bitcast.52, bf16[2,16,7424]{2,1,0:T(8,128)(2,1)S(1)} %pack_panel.6.rest_4_), custom_call_target="tpu_custom_call" | custom-call | bytes 1000000 | tf_op jit(solution)/shard_map/pack_gauss/pallas_call | solution.py:93
  30.9 1.1 %pack_panel.7.rest_2_ = bf16[1,16,7424]{2,1,0:T(8,128)(2,1)S(1)} custom-call(s32[1]{0:T(128)} %bitcast.spot_ref, s32[1,16]{1,0:T(1,128)} %bitcast.35, bf16[45,16,2880]{2,1,0:T(8,128)(2,1)} %tail_ref.7, bf16[45,16,2880]{2,1,0:T(8,128)(2,1)} %tail_ref.7, f32[15,16,96]{2,1,0:T(8,128)S(1)} %get-tuple-element.18.rest_4_.rest_2_.rest_0_, ...), custom_call_target="tpu_custom_call" | custom-call | bytes 500000 | tf_op jit(solution)/shard_map/pack_panel/pallas_call | solution.py:70
  32.1 1.1 %pack_gauss.7 = bf16[1,16,7296]{2,1,0:T(8,128)(2,1)S(1)} custom-call(bf16[2,45,16,720]{3,2,1,0:T(8,128)(2,1)} %bitcast.53, bf16[2,45,16,720]{3,2,1,0:T(8,128)(2,1)} %bitcast.54, bf16[1,16,7424]{2,1,0:T(8,128)(2,1)S(1)} %pack_panel.7.rest_2_), custom_call_target="tpu_custom_call" | custom-call | bytes 500000 | tf_op jit(solution)/shard_map/pack_gauss/pallas_call | solution.py:93
  33.1 2.3 %collective-permute-start.3 = (bf16[1,16,7424]{2,1,0:T(8,128)(2,1)S(1)}, bf16[1,16,7424]{2,1,0:T(8,128)(2,1)S(1)}, u32[]{:S(2)}, u32[]{:S(2)}) collective-permute-start(bf16[1,16,7424]{2,1,0:T(8,128)(2,1)S(1)} %pack_panel.7.rest_2_), channel_id=1, source_target_pairs={{1,2},{2,1},{3,0},{0,3},{5,6},{6,5},{7,4},{4,7},{9,10},{10,9},{11,... | collective-permute-start | bytes 712712 | tf_op jit(solution)/shard_map/ppermute | solution.py:245
  35.5 2.1 %collective-permute-done.6.other_ref = bf16[3,16,7296]{2,1,0:T(8,128)(2,1)} collective-permute-done((bf16[3,16,7296]{2,1,0:T(8,128)(2,1)S(1)}, bf16[3,16,7296]{2,1,0:T(8,128)(2,1)}, u32[]{:S(2)}, u32[]{:S(2)}) %collective-permute-start.6) | collective-permute-done | bytes 700448 | tf_op jit(solution)/shard_map/ppermute | solution.py:247
  38.2 4.7 %partial_sums.5 = (f32[30,16,96]{2,1,0:T(8,128)S(1)}, bf16[30,16,96]{2,1,0:T(8,128)(2,1)S(1)}) custom-call(s32[1]{0:T(128)} %bitcast.spot_ref, s32[45]{0:T(128)S(1)} %dynamic_slice.3.order_ref, f32[3,16,1536]{2,1,0:T(8,128)S(1)} %pad_maximum_fusion.decay_ref, s32[16]{0:T(128)S(1)} %copy-done.1, bf16[2,45,16,720]{3,2,1,0:T(8,128)(2,1)} %bitcast.55, ...), custom_call_target="tpu_custom_call" | custom-call | flops 188743680 | bytes 3000000 | tf_op jit(solution)/shard_map/partial_sums/pallas_call | solution.py:188
  42.9 4.5 %collective-permute-done.4.other_ref = bf16[2,16,7296]{2,1,0:T(8,128)(2,1)S(1)} collective-permute-done((bf16[2,16,7296]{2,1,0:T(8,128)(2,1)S(1)}, bf16[2,16,7296]{2,1,0:T(8,128)(2,1)S(1)}, u32[]{:S(2)}, u32[]{:S(2)}) %collective-permute-start.4) | collective-permute-done | bytes 466976 | tf_op jit(solution)/shard_map/ppermute | solution.py:247
  47.5 3.4 %partial_sums.6 = (f32[30,16,96]{2,1,0:T(8,128)S(1)}, bf16[30,16,96]{2,1,0:T(8,128)(2,1)S(1)}) custom-call(s32[1]{0:T(128)} %bitcast.spot_ref, s32[45]{0:T(128)S(1)} %dynamic_slice.3.order_ref, f32[3,16,1536]{2,1,0:T(8,128)S(1)} %pad_maximum_fusion.decay_ref, s32[16]{0:T(128)S(1)} %copy-done.1, ...), custom_call_target="tpu_custom_call", output_to_operand_aliasing={{0}: (9, {}), {1}: (10, {})} | custom-call | flops 125829120 | bytes 2000000 | tf_op jit(solution)/shard_map/partial_sums/pallas_call | solution.py:188
  51.3 1.2 %collective-permute-done.2.other_ref = bf16[1,16,7296]{2,1,0:T(8,128)(2,1)S(1)} collective-permute-done((bf16[1,16,7296]{2,1,0:T(8,128)(2,1)S(1)}, bf16[1,16,7296]{2,1,0:T(8,128)(2,1)S(1)}, u32[]{:S(2)}, u32[]{:S(2)}) %collective-permute-start.2) | collective-permute-done | bytes 233504 | tf_op jit(solution)/shard_map/ppermute | solution.py:247
  52.5 2.3 %partial_sums.7 = (f32[30,16,96]{2,1,0:T(8,128)S(1)}, bf16[30,16,96]{2,1,0:T(8,128)(2,1)S(1)}) custom-call(s32[1]{0:T(128)} %bitcast.spot_ref, s32[45]{0:T(128)S(1)} %dynamic_slice.3.order_ref, f32[3,16,1536]{2,1,0:T(8,128)S(1)} %pad_maximum_fusion.decay_ref, s32[16]{0:T(128)S(1)} %copy-done.1, ...), custom_call_target="tpu_custom_call", output_to_operand_aliasing={{0}: (9, {}), {1}: (10, {})} | custom-call | flops 62914560 | bytes 1000000 | tf_op jit(solution)/shard_map/partial_sums/pallas_call | solution.py:188
  54.8 2.5 %collective-permute-start.9 = (bf16[30,16,96]{2,1,0:T(8,128)(2,1)S(1)}, bf16[30,16,96]{2,1,0:T(8,128)(2,1)S(1)}, u32[]{:S(2)}, u32[]{:S(2)}) collective-permute-start(bf16[30,16,96]{2,1,0:T(8,128)(2,1)S(1)} %get-tuple-element.25), channel_id=1, source_target_pairs={{1,2},{2,1},{3,0},{0,3},{5,6},{6,5},{7,4},{4,7},{9,10},{10,9},{11,... | collective-permute-start | bytes 276488 | tf_op jit(solution)/shard_map/ppermute | solution.py:261
  57.4 2.6 %collective-permute-done.9 = bf16[30,16,96]{2,1,0:T(8,128)(2,1)S(1)} collective-permute-done((bf16[30,16,96]{2,1,0:T(8,128)(2,1)S(1)}, bf16[30,16,96]{2,1,0:T(8,128)(2,1)S(1)}, u32[]{:S(2)}, u32[]{:S(2)}) %collective-permute-start.9) | collective-permute-done | bytes 92192 | tf_op jit(solution)/shard_map/ppermute | solution.py:261
  61.1 25.1 %all_to_all.10 = bf16[64,2,540]{2,1,0:T(2,128)(2,1)S(1)} all-to-all(bf16[64,2,540]{2,1,0:T(2,128)(2,1)S(1)} %copy.18), channel_id=1, replica_groups=mesh['ord'=64,'blk'=4] {'ord'}, dimensions={0} | all-to-all | bytes 276480 | tf_op jit(solution)/shard_map/all_to_all | solution.py:283
  88.7 16.1 %all_to_all.11 = bf16[192,4,90]{2,1,0:T(4,128)(2,1)S(1)} all-to-all(bf16[192,4,90]{2,1,0:T(4,128)(2,1)S(1)} %bitcast.59), channel_id=1, replica_groups=mesh['ord'=64,'blk'=4] {'ord'}, dimensions={0} | all-to-all | bytes 276480 | tf_op jit(solution)/shard_map/all_to_all | solution.py:294
  (46 shorter events, 11.8 us)
Async XLA Ops:
  1.4 21.2 %collective-permute-start.1 = (bf16[3,16,7424]{2,1,0:T(8,128)(2,1)S(1)}, bf16[3,16,7424]{2,1,0:T(8,128)(2,1)}, u32[]{:S(2)}, u32[]{:S(2)}) collective-permute-start(bf16[3,16,7424]{2,1,0:T(8,128)(2,1)S(1)} %pack_panel.4.rest_6_), channel_id=1, source_target_pairs={{1,2},{2,1},{3,0},{0,3},{5,6},{6,5},{7,4},{4,7},{9,10},{10,9},{11,... | collective-permute-start | bytes 2138120 | tf_op jit(solution)/shard_map/ppermute | solution.py:245
  6.1 16.4 %collective-permute-start = (bf16[3,16,7296]{2,1,0:T(8,128)(2,1)S(1)}, bf16[3,16,7296]{2,1,0:T(8,128)(2,1)}, u32[]{:S(2)}, u32[]{:S(2)}) collective-permute-start(bf16[3,16,7296]{2,1,0:T(8,128)(2,1)S(1)} %pack_gauss.4.rest_6_), channel_id=1, source_target_pairs={{0,1},{1,0},{2,3},{3,2},{4,5},{5,4},{6,7},{7,6},{8,9},{9,8},{10,11... | collective-permute-start | bytes 2101256 | tf_op jit(solution)/shard_map/ppermute | solution.py:247
  7.6 5.6 %copy-start.2 = (f32[16]{0:T(128)S(1)}, f32[16]{0:T(128)}, u32[]{:S(2)}) copy-start(f32[16]{0:T(128)} %param.7) | copy-start | bytes 196
  7.7 14.9 %copy-start = (s32[16]{0:T(128)S(1)}, s32[16]{0:T(128)}, u32[]{:S(2)}) copy-start(s32[16]{0:T(128)} %cycle_ref.7) | copy-start | bytes 196
  7.7 30.1 %collective-permute-start.7 = (bf16[3,16,7424]{2,1,0:T(8,128)(2,1)S(1)}, bf16[3,16,7424]{2,1,0:T(8,128)(2,1)S(1)}, u32[]{:S(2)}, u32[]{:S(2)}) collective-permute-start(bf16[3,16,7424]{2,1,0:T(8,128)(2,1)S(1)} %pack_panel.5.rest_6_), channel_id=1, source_target_pairs={{1,2},{2,1},{3,0},{0,3},{5,6},{6,5},{7,4},{4,7},{9,10},{10,9},{11,... | collective-permute-start | bytes 2138120 | tf_op jit(solution)/shard_map/ppermute | solution.py:245
  9.9 27.7 %collective-permute-start.6 = (bf16[3,16,7296]{2,1,0:T(8,128)(2,1)S(1)}, bf16[3,16,7296]{2,1,0:T(8,128)(2,1)}, u32[]{:S(2)}, u32[]{:S(2)}) collective-permute-start(bf16[3,16,7296]{2,1,0:T(8,128)(2,1)S(1)} %pack_gauss.5.rest_5_), channel_id=1, source_target_pairs={{0,1},{1,0},{2,3},{3,2},{4,5},{5,4},{6,7},{7,6},{8,9},{9,8},{10,11... | collective-permute-start | bytes 2101256 | tf_op jit(solution)/shard_map/ppermute | solution.py:247
  30.0 17.5 %collective-permute-start.5 = (bf16[2,16,7424]{2,1,0:T(8,128)(2,1)S(1)}, bf16[2,16,7424]{2,1,0:T(8,128)(2,1)S(1)}, u32[]{:S(2)}, u32[]{:S(2)}) collective-permute-start(bf16[2,16,7424]{2,1,0:T(8,128)(2,1)S(1)} %pack_panel.6.rest_4_), channel_id=1, source_target_pairs={{1,2},{2,1},{3,0},{0,3},{5,6},{6,5},{7,4},{4,7},{9,10},{10,9},{11,... | collective-permute-start | bytes 1425416 | tf_op jit(solution)/shard_map/ppermute | solution.py:245
  30.5 17.0 %collective-permute-start.4 = (bf16[2,16,7296]{2,1,0:T(8,128)(2,1)S(1)}, bf16[2,16,7296]{2,1,0:T(8,128)(2,1)S(1)}, u32[]{:S(2)}, u32[]{:S(2)}) collective-permute-start(bf16[2,16,7296]{2,1,0:T(8,128)(2,1)S(1)} %pack_gauss.6.rest_3_), channel_id=1, source_target_pairs={{0,1},{1,0},{2,3},{3,2},{4,5},{5,4},{6,7},{7,6},{8,9},{9,8},{10,11... | collective-permute-start | bytes 1400840 | tf_op jit(solution)/shard_map/ppermute | solution.py:247
  32.0 6.2 %copy-start.1 = (s32[16]{0:T(128)S(1)}, s32[16]{0:T(128)}, u32[]{:S(2)}) copy-start(s32[16]{0:T(128)} %cycle_ref.7) | copy-start | bytes 196
  33.1 19.3 %collective-permute-start.3 = (bf16[1,16,7424]{2,1,0:T(8,128)(2,1)S(1)}, bf16[1,16,7424]{2,1,0:T(8,128)(2,1)S(1)}, u32[]{:S(2)}, u32[]{:S(2)}) collective-permute-start(bf16[1,16,7424]{2,1,0:T(8,128)(2,1)S(1)} %pack_panel.7.rest_2_), channel_id=1, source_target_pairs={{1,2},{2,1},{3,0},{0,3},{5,6},{6,5},{7,4},{4,7},{9,10},{10,9},{11,... | collective-permute-start | bytes 712712 | tf_op jit(solution)/shard_map/ppermute | solution.py:245
  37.6 14.9 %collective-permute-start.2 = (bf16[1,16,7296]{2,1,0:T(8,128)(2,1)S(1)}, bf16[1,16,7296]{2,1,0:T(8,128)(2,1)S(1)}, u32[]{:S(2)}, u32[]{:S(2)}) collective-permute-start(bf16[1,16,7296]{2,1,0:T(8,128)(2,1)S(1)} %pack_gauss.7), channel_id=1, source_target_pairs={{0,1},{1,0},{2,3},{3,2},{4,5},{5,4},{6,7},{7,6},{8,9},{9,8},{10,11... | collective-permute-start | bytes 700424 | tf_op jit(solution)/shard_map/ppermute | solution.py:247
  37.8 13.5 %collective-permute-start.8 = (bf16[15,16,96]{2,1,0:T(8,128)(2,1)S(1)}, bf16[15,16,96]{2,1,0:T(8,128)(2,1)S(1)}, u32[]{:S(2)}, u32[]{:S(2)}) collective-permute-start(bf16[15,16,96]{2,1,0:T(8,128)(2,1)S(1)} %get-tuple-element.23), channel_id=1, source_target_pairs={{1,2},{2,1},{3,0},{0,3},{5,6},{6,5},{7,4},{4,7},{9,10},{10,9},{11,... | collective-permute-start | bytes 138248 | tf_op jit(solution)/shard_map/ppermute | solution.py:261
  54.8 5.2 %collective-permute-start.9 = (bf16[30,16,96]{2,1,0:T(8,128)(2,1)S(1)}, bf16[30,16,96]{2,1,0:T(8,128)(2,1)S(1)}, u32[]{:S(2)}, u32[]{:S(2)}) collective-permute-start(bf16[30,16,96]{2,1,0:T(8,128)(2,1)S(1)} %get-tuple-element.25), channel_id=1, source_target_pairs={{1,2},{2,1},{3,0},{0,3},{5,6},{6,5},{7,4},{4,7},{9,10},{10,9},{11,... | collective-permute-start | bytes 276488 | tf_op jit(solution)/shard_map/ppermute | solution.py:261

commit v12 on v11

--- a/solution.py
+++ b/solution.py
@@ -272,23 +272,22 @@
     b = jnp.arange(128)
     q = jnp.arange(RUN)
     cos1, sin1 = turn(b[:, None] * runs[None, :], 128)
-    table = jnp.concatenate(
-        [jnp.concatenate([cos1, sin1], 1), jnp.concatenate([sin1, -cos1], 1)], 0)
+    table = jnp.concatenate([jnp.stack([cos1, sin1], 2), jnp.stack([sin1, -cos1], 2)], 0)
+    table = table.reshape(256, 2 * parts).astype(jnp.bfloat16)
     cos2, sin2 = turn(b[:, None] * q[None, :], NLON)
     cos3, sin3 = turn(q[:, None] * q[None, :], RUN)
     last = jnp.concatenate([cos3, -sin3], 1)
 
     chunk = chunk.reshape(parts, 2, items * count)
     chunk, table, cos2, sin2, last = lax.optimization_barrier((chunk, table, cos2, sin2, last))
-    spread = lax.all_to_all(chunk, "ord", 0, 0, tiled=True).astype(jnp.float32)
-    flat = jnp.concatenate([spread[:, 0], spread[:, 1]], 0)
-    mid = jnp.dot(table, flat, precision=lax.Precision.HIGHEST).reshape(2, 128, items, count)
+    flat = lax.all_to_all(chunk, "ord", 0, 0, tiled=True).reshape(2 * parts, items * count)
+    mid = jnp.dot(table, flat, preferred_element_type=jnp.float32).reshape(2, 128, items, count)
     cos2, sin2 = cos2[:, None, :], sin2[:, None, :]
     real = mid[0] * cos2 - mid[1] * sin2
     imag = mid[0] * sin2 + mid[1] * cos2
     field = lax.dot_general(
         last, jnp.concatenate([real, imag], 2),
-        (((1,), (2,)), ((), ())), precision=lax.Precision.HIGHEST)
+        (((1,), (2,)), ((), ())), precision=lax.Precision.HIGH)
     field = field.reshape(parts, NLON // parts, 3, shells // 4).astype(jnp.bfloat16)
     field = jnp.transpose(field, (0, 2, 3, 1)).reshape(parts * 3, shells // 4, NLON // parts)
     field = lax.all_to_all(field, "ord", 0, 0, tiled=True)

time: 106 us -> 106 us (level)
  other arithmetic: 5.25 us -> 0.85 us
  waiting for transfers between devices: 16.1 us -> 19.8 us
  Pallas kernels: 25.6 us -> 26.8 us
    ppermute x4, waiting for transfers between devices: 13.2 us -> 17.2 us  [start(): packed.append((lax.ppermute(coef, 'blk', GAUSS_PAIRS), far, coef))]
    exp x1, other arithmetic: 1.5 us -> 0.11 us  [body(): here_ = jnp.exp(-(degree + 2.0) * height[:, None] / ORDERS)]
  transfers between devices with their start and end apart: 10 -> 10, of which waited for: 6 -> 5; matrix products, arithmetic and copies ran while one was open for 7% -> 2% of each run, Pallas kernels for 21% -> 22%
where the time goes in v12:
time: 106 us; the launch traced here: 105 us
  blocking collectives  41.4 us (39%)
  Pallas kernels  26.8 us (25%)
  waiting for transfers between devices  19.8 us (19%)
  starting transfers between devices  10.9 us (10%)
  local copies, waits for them, and re-layouts  4.7 us (4%)
    all_to_all x1, blocking collectives, body(): lax.all_to_all(chunk, 'ord', 0, 0, tiled=True)  25.3 us
    ppermute x4, waiting for transfers between devices, start(): packed.append((lax.ppermute(coef, 'blk', GAUSS_PAIRS), far, coef))  17.2 us
    all_to_all x1, blocking collectives, body(): field = lax.all_to_all(field, 'ord', 0, 0, tiled=True)  16.1 us
    pallas_call x4, Pallas kernels, partial_sums(): pl.pallas_call(functools.partial(sums_kernel, base=base), out_shape=[jax....  15.9 us
    ppermute x4, starting transfers between devices, start(): far = lax.ppermute(part, 'blk', PANEL_PAIRS)  7 us
    pallas_call x4, Pallas kernels, packed_gauss(): pl.pallas_call(functools.partial(pack_gauss, steps=steps), out_shape=jax....  5.71 us
    pallas_call x4, Pallas kernels, packed_panel(): pl.pallas_call(functools.partial(pack_panel, steps=steps), out_shape=jax....  5.18 us
    ppermute x2, starting transfers between devices, body(): added.append(lax.ppermute(send, 'blk', PANEL_PAIRS))  2.91 us
  transfers between devices with their start and end apart: 10, of which 5 were waited for; matrix products, arithmetic and copies ran while one was open for 2% of the time, Pallas kernels for 22%

profile of v12, /device:TPU:1, one launch (start us, length us, event | category | flops | bytes accessed | tf_op | source)
XLA Modules:
  0.0 105.2 jit_solution(11885389569384093964)
XLA Ops:
  0.0 1.4 %pack_panel.4.rest_6_ = bf16[3,16,7424]{2,1,0:T(8,128)(2,1)S(1)} custom-call(s32[1]{0:T(128)} %bitcast.spot_ref, s32[1,16]{1,0:T(1,128)} %bitcast.29, bf16[45,16,2880]{2,1,0:T(8,128)(2,1)} %tail_ref.7, bf16[45,16,2880]{2,1,0:T(8,128)(2,1)} %tail_ref.7, bf16[45,16,2880]{2,1,0:T(8,128)(2,1)} %tail_ref.7, bf16[45,16,2880]{2,1,0:T(8,128)(2,1)} %tail_ref.7, ...), custom_call_target="tpu_custom_call" | custom-call | bytes 1500000 | tf_op jit(solution)/shard_map/pack_panel/pallas_call | solution.py:70
  1.4 3.4 %collective-permute-start.1 = (bf16[3,16,7424]{2,1,0:T(8,128)(2,1)S(1)}, bf16[3,16,7424]{2,1,0:T(8,128)(2,1)}, u32[]{:S(2)}, u32[]{:S(2)}) collective-permute-start(bf16[3,16,7424]{2,1,0:T(8,128)(2,1)S(1)} %pack_panel.4.rest_6_), channel_id=1, source_target_pairs={{1,2},{2,1},{3,0},{0,3},{5,6},{6,5},{7,4},{4,7},{9,10},{10,9},{11,... | collective-permute-start | bytes 2138120 | tf_op jit(solution)/shard_map/ppermute | solution.py:245
  4.8 1.4 %pack_gauss.4.rest_6_ = bf16[3,16,7296]{2,1,0:T(8,128)(2,1)S(1)} custom-call(bf16[2,45,16,720]{3,2,1,0:T(8,128)(2,1)} %bitcast.33, bf16[2,45,16,720]{3,2,1,0:T(8,128)(2,1)} %bitcast.34, bf16[2,45,16,720]{3,2,1,0:T(8,128)(2,1)} %bitcast.35, bf16[2,45,16,720]{3,2,1,0:T(8,128)(2,1)} %bitcast.36, bf16[2,45,16,720]{3,2,1,0:T(8,128)(2,1)} %bitcast.37, ...), custom_call_target="tpu_custom_call" | custom-call | bytes 1500000 | tf_op jit(solution)/shard_map/pack_gauss/pallas_call | solution.py:93
  6.2 1.4 %pack_panel.5.rest_6_ = bf16[3,16,7424]{2,1,0:T(8,128)(2,1)S(1)} custom-call(s32[1]{0:T(128)} %bitcast.spot_ref, s32[1,16]{1,0:T(1,128)} %bitcast.30, bf16[45,16,2880]{2,1,0:T(8,128)(2,1)} %tail_ref.7, bf16[45,16,2880]{2,1,0:T(8,128)(2,1)} %tail_ref.7, bf16[45,16,2880]{2,1,0:T(8,128)(2,1)} %tail_ref.7, bf16[45,16,2880]{2,1,0:T(8,128)(2,1)} %tail_ref.7, ...), custom_call_target="tpu_custom_call" | custom-call | bytes 1500000 | tf_op jit(solution)/shard_map/pack_panel/pallas_call | solution.py:70
  7.7 0.9 collective-permute-start.7
  8.5 1.4 %pack_gauss.5.rest_5_ = bf16[3,16,7296]{2,1,0:T(8,128)(2,1)S(1)} custom-call(bf16[2,45,16,720]{3,2,1,0:T(8,128)(2,1)} %bitcast.39, bf16[2,45,16,720]{3,2,1,0:T(8,128)(2,1)} %bitcast.40, bf16[2,45,16,720]{3,2,1,0:T(8,128)(2,1)} %bitcast.41, bf16[2,45,16,720]{3,2,1,0:T(8,128)(2,1)} %bitcast.42, bf16[2,45,16,720]{3,2,1,0:T(8,128)(2,1)} %bitcast.43, ...), custom_call_target="tpu_custom_call" | custom-call | bytes 1500000 | tf_op jit(solution)/shard_map/pack_gauss/pallas_call | solution.py:93
  12.5 10.1 %collective-permute-done.other_ref = bf16[3,16,7296]{2,1,0:T(8,128)(2,1)} collective-permute-done((bf16[3,16,7296]{2,1,0:T(8,128)(2,1)S(1)}, bf16[3,16,7296]{2,1,0:T(8,128)(2,1)}, u32[]{:S(2)}, u32[]{:S(2)}) %collective-permute-start) | collective-permute-done | bytes 700448 | tf_op jit(solution)/shard_map/ppermute | solution.py:247
  22.6 4.9 %partial_sums.4 = (f32[15,16,96]{2,1,0:T(8,128)S(1)}, bf16[15,16,96]{2,1,0:T(8,128)(2,1)S(1)}) custom-call(s32[1]{0:T(128)} %bitcast.spot_ref, s32[45]{0:T(128)S(1)} %dynamic_slice.3.order_ref, f32[3,16,1536]{2,1,0:T(8,128)S(1)} %pad_maximum_fusion.decay_ref, s32[16]{0:T(128)S(1)} %copy-done, bf16[2,45,16,720]{3,2,1,0:T(8,128)(2,1)} %bitcast.45, ...), custom_call_target="tpu_custom_call" | custom-call | flops 188743680 | bytes 3000000 | tf_op jit(solution)/shard_map/partial_sums/pallas_call | solution.py:188
  27.5 1.3 %pack_panel.6.rest_4_ = bf16[2,16,7424]{2,1,0:T(8,128)(2,1)S(1)} custom-call(s32[1]{0:T(128)} %bitcast.spot_ref, s32[1,16]{1,0:T(1,128)} %bitcast.31, bf16[45,16,2880]{2,1,0:T(8,128)(2,1)} %tail_ref.7, bf16[45,16,2880]{2,1,0:T(8,128)(2,1)} %tail_ref.7, bf16[45,16,2880]{2,1,0:T(8,128)(2,1)} %tail_ref.7, bf16[45,16,2880]{2,1,0:T(8,128)(2,1)} %tail_ref.7, ...), custom_call_target="tpu_custom_call" | custom-call | bytes 1000000 | tf_op jit(solution)/shard_map/pack_panel/pallas_call | solution.py:70
  28.8 1.2 %pack_gauss.6.rest_3_ = bf16[2,16,7296]{2,1,0:T(8,128)(2,1)S(1)} custom-call(bf16[2,45,16,720]{3,2,1,0:T(8,128)(2,1)} %bitcast.46, bf16[2,45,16,720]{3,2,1,0:T(8,128)(2,1)} %bitcast.47, bf16[2,45,16,720]{3,2,1,0:T(8,128)(2,1)} %bitcast.48, bf16[2,45,16,720]{3,2,1,0:T(8,128)(2,1)} %bitcast.49, bf16[2,16,7424]{2,1,0:T(8,128)(2,1)S(1)} %pack_panel.6.rest_4_), custom_call_target="tpu_custom_call" | custom-call | bytes 1000000 | tf_op jit(solution)/shard_map/pack_gauss/pallas_call | solution.py:93
  30.8 1.1 %pack_panel.7.rest_2_ = bf16[1,16,7424]{2,1,0:T(8,128)(2,1)S(1)} custom-call(s32[1]{0:T(128)} %bitcast.spot_ref, s32[1,16]{1,0:T(1,128)} %bitcast.32, bf16[45,16,2880]{2,1,0:T(8,128)(2,1)} %tail_ref.7, bf16[45,16,2880]{2,1,0:T(8,128)(2,1)} %tail_ref.7, f32[15,16,96]{2,1,0:T(8,128)S(1)} %get-tuple-element.18.rest_4_.rest_2_.rest_0_, ...), custom_call_target="tpu_custom_call" | custom-call | bytes 500000 | tf_op jit(solution)/shard_map/pack_panel/pallas_call | solution.py:70
  31.9 1.8 %pack_gauss.7 = bf16[1,16,7296]{2,1,0:T(8,128)(2,1)} custom-call(bf16[2,45,16,720]{3,2,1,0:T(8,128)(2,1)} %bitcast.50, bf16[2,45,16,720]{3,2,1,0:T(8,128)(2,1)} %bitcast.51, bf16[1,16,7424]{2,1,0:T(8,128)(2,1)S(1)} %pack_panel.7.rest_2_), custom_call_target="tpu_custom_call" | custom-call | bytes 500000 | tf_op jit(solution)/shard_map/pack_gauss/pallas_call | solution.py:93
  33.7 2.2 %collective-permute-start.3 = (bf16[1,16,7424]{2,1,0:T(8,128)(2,1)S(1)}, bf16[1,16,7424]{2,1,0:T(8,128)(2,1)S(1)}, u32[]{:S(2)}, u32[]{:S(2)}) collective-permute-start(bf16[1,16,7424]{2,1,0:T(8,128)(2,1)S(1)} %pack_panel.7.rest_2_), channel_id=1, source_target_pairs={{1,2},{2,1},{3,0},{0,3},{5,6},{6,5},{7,4},{4,7},{9,10},{10,9},{11,... | collective-permute-start | bytes 712712 | tf_op jit(solution)/shard_map/ppermute | solution.py:245
  35.9 1.7 %collective-permute-done.6.other_ref = bf16[3,16,7296]{2,1,0:T(8,128)(2,1)} collective-permute-done((bf16[3,16,7296]{2,1,0:T(8,128)(2,1)S(1)}, bf16[3,16,7296]{2,1,0:T(8,128)(2,1)}, u32[]{:S(2)}, u32[]{:S(2)}) %collective-permute-start.6) | collective-permute-done | bytes 700448 | tf_op jit(solution)/shard_map/ppermute | solution.py:247
  38.4 5.0 %partial_sums.5 = (f32[30,16,96]{2,1,0:T(8,128)S(1)}, bf16[30,16,96]{2,1,0:T(8,128)(2,1)S(1)}) custom-call(s32[1]{0:T(128)} %bitcast.spot_ref, s32[45]{0:T(128)S(1)} %dynamic_slice.3.order_ref, f32[3,16,1536]{2,1,0:T(8,128)S(1)} %pad_maximum_fusion.decay_ref, s32[16]{0:T(128)S(1)} %copy-done.1, bf16[2,45,16,720]{3,2,1,0:T(8,128)(2,1)} %bitcast.52, ...), custom_call_target="tpu_custom_call" | custom-call | flops 188743680 | bytes 3000000 | tf_op jit(solution)/shard_map/partial_sums/pallas_call | solution.py:188
  43.4 4.2 %collective-permute-done.4.other_ref = bf16[2,16,7296]{2,1,0:T(8,128)(2,1)} collective-permute-done((bf16[2,16,7296]{2,1,0:T(8,128)(2,1)S(1)}, bf16[2,16,7296]{2,1,0:T(8,128)(2,1)}, u32[]{:S(2)}, u32[]{:S(2)}) %collective-permute-start.4) | collective-permute-done | bytes 466976 | tf_op jit(solution)/shard_map/ppermute | solution.py:247
  47.6 3.7 %partial_sums.6 = (f32[30,16,96]{2,1,0:T(8,128)S(1)}, bf16[30,16,96]{2,1,0:T(8,128)(2,1)S(1)}) custom-call(s32[1]{0:T(128)} %bitcast.spot_ref, s32[45]{0:T(128)S(1)} %dynamic_slice.3.order_ref, f32[3,16,1536]{2,1,0:T(8,128)S(1)} %pad_maximum_fusion.decay_ref, s32[16]{0:T(128)S(1)} %copy-done.1, ...), custom_call_target="tpu_custom_call", output_to_operand_aliasing={{0}: (9, {}), {1}: (10, {})} | custom-call | flops 125829120 | bytes 2000000 | tf_op jit(solution)/shard_map/partial_sums/pallas_call | solution.py:188
  51.3 1.2 %collective-permute-done.2.other_ref = bf16[1,16,7296]{2,1,0:T(8,128)(2,1)S(1)} collective-permute-done((bf16[1,16,7296]{2,1,0:T(8,128)(2,1)}, bf16[1,16,7296]{2,1,0:T(8,128)(2,1)S(1)}, u32[]{:S(2)}, u32[]{:S(2)}) %collective-permute-start.2) | collective-permute-done | bytes 233504 | tf_op jit(solution)/shard_map/ppermute | solution.py:247
  52.5 2.3 %partial_sums.7 = (f32[30,16,96]{2,1,0:T(8,128)S(1)}, bf16[30,16,96]{2,1,0:T(8,128)(2,1)S(1)}) custom-call(s32[1]{0:T(128)} %bitcast.spot_ref, s32[45]{0:T(128)S(1)} %dynamic_slice.3.order_ref, f32[3,16,1536]{2,1,0:T(8,128)S(1)} %pad_maximum_fusion.decay_ref, s32[16]{0:T(128)S(1)} %copy-done.1, ...), custom_call_target="tpu_custom_call", output_to_operand_aliasing={{0}: (9, {}), {1}: (10, {})} | custom-call | flops 62914560 | bytes 1000000 | tf_op jit(solution)/shard_map/partial_sums/pallas_call | solution.py:188
  54.8 2.5 %collective-permute-start.9 = (bf16[30,16,96]{2,1,0:T(8,128)(2,1)S(1)}, bf16[30,16,96]{2,1,0:T(8,128)(2,1)S(1)}, u32[]{:S(2)}, u32[]{:S(2)}) collective-permute-start(bf16[30,16,96]{2,1,0:T(8,128)(2,1)S(1)} %get-tuple-element.25), channel_id=1, source_target_pairs={{1,2},{2,1},{3,0},{0,3},{5,6},{6,5},{7,4},{4,7},{9,10},{10,9},{11,... | collective-permute-start | bytes 276488 | tf_op jit(solution)/shard_map/ppermute | solution.py:261
  57.4 2.6 %collective-permute-done.9 = bf16[30,16,96]{2,1,0:T(8,128)(2,1)S(1)} collective-permute-done((bf16[30,16,96]{2,1,0:T(8,128)(2,1)S(1)}, bf16[30,16,96]{2,1,0:T(8,128)(2,1)S(1)}, u32[]{:S(2)}, u32[]{:S(2)}) %collective-permute-start.9) | collective-permute-done | bytes 92192 | tf_op jit(solution)/shard_map/ppermute | solution.py:261
  61.1 25.3 %all_to_all.10 = bf16[64,2,540]{2,1,0:T(2,128)(2,1)S(1)} all-to-all(bf16[64,2,540]{2,1,0:T(2,128)(2,1)S(1)} %copy.25), channel_id=1, replica_groups=mesh['ord'=64,'blk'=4] {'ord'}, dimensions={0} | all-to-all | bytes 276480 | tf_op jit(solution)/shard_map/all_to_all | solution.py:283
  88.3 16.1 %all_to_all.11 = bf16[192,4,90]{2,1,0:T(4,128)(2,1)S(1)} all-to-all(bf16[192,4,90]{2,1,0:T(4,128)(2,1)S(1)} %bitcast.56), channel_id=1, replica_groups=mesh['ord'=64,'blk'=4] {'ord'}, dimensions={0} | all-to-all | bytes 276480 | tf_op jit(solution)/shard_map/all_to_all | solution.py:293
  104.4 0.8 copy.28
  (46 shorter events, 7.2 us)
Async XLA Ops:
  1.4 21.2 %collective-permute-start.1 = (bf16[3,16,7424]{2,1,0:T(8,128)(2,1)S(1)}, bf16[3,16,7424]{2,1,0:T(8,128)(2,1)}, u32[]{:S(2)}, u32[]{:S(2)}) collective-permute-start(bf16[3,16,7424]{2,1,0:T(8,128)(2,1)S(1)} %pack_panel.4.rest_6_), channel_id=1, source_target_pairs={{1,2},{2,1},{3,0},{0,3},{5,6},{6,5},{7,4},{4,7},{9,10},{10,9},{11,... | collective-permute-start | bytes 2138120 | tf_op jit(solution)/shard_map/ppermute | solution.py:245
  6.1 16.4 %collective-permute-start = (bf16[3,16,7296]{2,1,0:T(8,128)(2,1)S(1)}, bf16[3,16,7296]{2,1,0:T(8,128)(2,1)}, u32[]{:S(2)}, u32[]{:S(2)}) collective-permute-start(bf16[3,16,7296]{2,1,0:T(8,128)(2,1)S(1)} %pack_gauss.4.rest_6_), channel_id=1, source_target_pairs={{0,1},{1,0},{2,3},{3,2},{4,5},{5,4},{6,7},{7,6},{8,9},{9,8},{10,11... | collective-permute-start | bytes 2101256 | tf_op jit(solution)/shard_map/ppermute | solution.py:247
  7.6 3.9 %copy-start.2 = (f32[16]{0:T(128)S(1)}, f32[16]{0:T(128)}, u32[]{:S(2)}) copy-start(f32[16]{0:T(128)} %param.7) | copy-start | bytes 196
  7.7 14.9 %copy-start = (s32[16]{0:T(128)S(1)}, s32[16]{0:T(128)}, u32[]{:S(2)}) copy-start(s32[16]{0:T(128)} %cycle_ref.7) | copy-start | bytes 196
  7.7 30.1 %collective-permute-start.7 = (bf16[3,16,7424]{2,1,0:T(8,128)(2,1)S(1)}, bf16[3,16,7424]{2,1,0:T(8,128)(2,1)}, u32[]{:S(2)}, u32[]{:S(2)}) collective-permute-start(bf16[3,16,7424]{2,1,0:T(8,128)(2,1)S(1)} %pack_panel.5.rest_6_), channel_id=1, source_target_pairs={{1,2},{2,1},{3,0},{0,3},{5,6},{6,5},{7,4},{4,7},{9,10},{10,9},{11,... | collective-permute-start | bytes 2138120 | tf_op jit(solution)/shard_map/ppermute | solution.py:245
  9.9 27.7 %collective-permute-start.6 = (bf16[3,16,7296]{2,1,0:T(8,128)(2,1)S(1)}, bf16[3,16,7296]{2,1,0:T(8,128)(2,1)}, u32[]{:S(2)}, u32[]{:S(2)}) collective-permute-start(bf16[3,16,7296]{2,1,0:T(8,128)(2,1)S(1)} %pack_gauss.5.rest_5_), channel_id=1, source_target_pairs={{0,1},{1,0},{2,3},{3,2},{4,5},{5,4},{6,7},{7,6},{8,9},{9,8},{10,11... | collective-permute-start | bytes 2101256 | tf_op jit(solution)/shard_map/ppermute | solution.py:247
  30.0 17.6 %collective-permute-start.5 = (bf16[2,16,7424]{2,1,0:T(8,128)(2,1)S(1)}, bf16[2,16,7424]{2,1,0:T(8,128)(2,1)}, u32[]{:S(2)}, u32[]{:S(2)}) collective-permute-start(bf16[2,16,7424]{2,1,0:T(8,128)(2,1)S(1)} %pack_panel.6.rest_4_), channel_id=1, source_target_pairs={{1,2},{2,1},{3,0},{0,3},{5,6},{6,5},{7,4},{4,7},{9,10},{10,9},{11,... | collective-permute-start | bytes 1425416 | tf_op jit(solution)/shard_map/ppermute | solution.py:245
  30.5 17.0 %collective-permute-start.4 = (bf16[2,16,7296]{2,1,0:T(8,128)(2,1)S(1)}, bf16[2,16,7296]{2,1,0:T(8,128)(2,1)}, u32[]{:S(2)}, u32[]{:S(2)}) collective-permute-start(bf16[2,16,7296]{2,1,0:T(8,128)(2,1)S(1)} %pack_gauss.6.rest_3_), channel_id=1, source_target_pairs={{0,1},{1,0},{2,3},{3,2},{4,5},{5,4},{6,7},{7,6},{8,9},{9,8},{10,11... | collective-permute-start | bytes 1400840 | tf_op jit(solution)/shard_map/ppermute | solution.py:247
  31.9 6.5 %copy-start.1 = (s32[16]{0:T(128)S(1)}, s32[16]{0:T(128)}, u32[]{:S(2)}) copy-start(s32[16]{0:T(128)} %cycle_ref.7) | copy-start | bytes 196
  33.7 18.8 %collective-permute-start.3 = (bf16[1,16,7424]{2,1,0:T(8,128)(2,1)S(1)}, bf16[1,16,7424]{2,1,0:T(8,128)(2,1)S(1)}, u32[]{:S(2)}, u32[]{:S(2)}) collective-permute-start(bf16[1,16,7424]{2,1,0:T(8,128)(2,1)S(1)} %pack_panel.7.rest_2_), channel_id=1, source_target_pairs={{1,2},{2,1},{3,0},{0,3},{5,6},{6,5},{7,4},{4,7},{9,10},{10,9},{11,... | collective-permute-start | bytes 712712 | tf_op jit(solution)/shard_map/ppermute | solution.py:245
  37.6 14.9 %collective-permute-start.2 = (bf16[1,16,7296]{2,1,0:T(8,128)(2,1)}, bf16[1,16,7296]{2,1,0:T(8,128)(2,1)S(1)}, u32[]{:S(2)}, u32[]{:S(2)}) collective-permute-start(bf16[1,16,7296]{2,1,0:T(8,128)(2,1)} %pack_gauss.7), channel_id=1, source_target_pairs={{0,1},{1,0},{2,3},{3,2},{4,5},{5,4},{6,7},{7,6},{8,9},{9,8},{10,11... | collective-permute-start | bytes 700424 | tf_op jit(solution)/shard_map/ppermute | solution.py:247
  37.8 13.5 %collective-permute-start.8 = (bf16[15,16,96]{2,1,0:T(8,128)(2,1)S(1)}, bf16[15,16,96]{2,1,0:T(8,128)(2,1)S(1)}, u32[]{:S(2)}, u32[]{:S(2)}) collective-permute-start(bf16[15,16,96]{2,1,0:T(8,128)(2,1)S(1)} %get-tuple-element.23), channel_id=1, source_target_pairs={{1,2},{2,1},{3,0},{0,3},{5,6},{6,5},{7,4},{4,7},{9,10},{10,9},{11,... | collective-permute-start | bytes 138248 | tf_op jit(solution)/shard_map/ppermute | solution.py:261
  54.8 5.2 %collective-permute-start.9 = (bf16[30,16,96]{2,1,0:T(8,128)(2,1)S(1)}, bf16[30,16,96]{2,1,0:T(8,128)(2,1)S(1)}, u32[]{:S(2)}, u32[]{:S(2)}) collective-permute-start(bf16[30,16,96]{2,1,0:T(8,128)(2,1)S(1)} %get-tuple-element.25), channel_id=1, source_target_pairs={{1,2},{2,1},{3,0},{0,3},{5,6},{6,5},{7,4},{4,7},{9,10},{10,9},{11,... | collective-permute-start | bytes 276488 | tf_op jit(solution)/shard_map/ppermute | solution.py:261

commit v13 on v12

--- a/solution.py
+++ b/solution.py
@@ -172,7 +172,8 @@
         main, bare, tilt = sums[o][0:32], sums[o][32:64], sums[o][64:96]
         polar = (tilt - cosine * (main - bare)) * inverse
         bare = orders[o] * inverse * bare
-        mixed.append(jnp.concatenate([main, polar, -bare[16:32], bare[0:16]], 0).T)
+        mixed.append(jnp.concatenate(
+            [main[0:16], polar[0:16], -bare[16:32], main[16:32], polar[16:32], bare[0:16]], 0).T)
     for o in range(GROUP):
         keep_ref[o] = mixed[o][:16]
         send_ref[o] = mixed[o][16:].astype(jnp.bfloat16)
@@ -263,8 +264,7 @@
             start(c + 2)
     total = jnp.concatenate(kept, 0) + jnp.concatenate(added, 0).astype(jnp.float32)
     total = lax.optimization_barrier(total.astype(jnp.bfloat16))
-    split = (count, cycles, 3, 2, 4, shells // 4)
-    chunk = jnp.transpose(total.reshape(split), (1, 4, 3, 2, 5, 0))
+    chunk = jnp.transpose(total.reshape(count, cycles, 2, 4, 12), (1, 3, 2, 4, 0))
 
     parts = ORDERS // count
     items = cycles * 3 * shells // parts
@@ -288,11 +288,10 @@
     field = lax.dot_general(
         last, jnp.concatenate([real, imag], 2),
         (((1,), (2,)), ((), ())), precision=lax.Precision.HIGH)
-    field = field.reshape(parts, NLON // parts, 3, shells // 4).astype(jnp.bfloat16)
-    field = jnp.transpose(field, (0, 2, 3, 1)).reshape(parts * 3, shells // 4, NLON // parts)
+    field = field.reshape(parts, NLON // parts, 3, 4).astype(jnp.bfloat16)
+    field = jnp.transpose(field, (0, 2, 3, 1)).reshape(parts * 3, 4, NLON // parts)
     field = lax.all_to_all(field, "ord", 0, 0, tiled=True)
-    field = field.reshape(cycles, 4, 3, shells // 4, NLON // parts)
-    return jnp.transpose(field, (4, 0, 2, 1, 3)).reshape(NLON // parts, cycles * 3 * shells)
+    return jnp.transpose(field, (2, 0, 1)).reshape(NLON // parts, cycles * 3 * shells)
 
 
 def solution(mesh):

time: 106 us -> 106 us (level)
  no operation moved by 1% of the time
where the time goes in v13:
time: 106 us; the launch traced here: 105 us
  blocking collectives  41.4 us (39%)
  Pallas kernels  26.8 us (25%)
  waiting for transfers between devices  19.8 us (19%)
  starting transfers between devices  10.9 us (10%)
  local copies, waits for them, and re-layouts  4.77 us (4%)
    all_to_all x1, blocking collectives, body(): lax.all_to_all(chunk, 'ord', 0, 0, tiled=True)  25.3 us
    ppermute x4, waiting for transfers between devices, start(): packed.append((lax.ppermute(coef, 'blk', GAUSS_PAIRS), far, coef))  17.2 us
    all_to_all x1, blocking collectives, body(): field = lax.all_to_all(field, 'ord', 0, 0, tiled=True)  16.1 us
    pallas_call x4, Pallas kernels, partial_sums(): pl.pallas_call(functools.partial(sums_kernel, base=base), out_shape=[jax....  15.9 us
    ppermute x4, starting transfers between devices, start(): far = lax.ppermute(part, 'blk', PANEL_PAIRS)  7 us
    pallas_call x4, Pallas kernels, packed_gauss(): pl.pallas_call(functools.partial(pack_gauss, steps=steps), out_shape=jax....  5.71 us
    pallas_call x4, Pallas kernels, packed_panel(): pl.pallas_call(functools.partial(pack_panel, steps=steps), out_shape=jax....  5.18 us
    ppermute x2, starting transfers between devices, body(): added.append(lax.ppermute(send, 'blk', PANEL_PAIRS))  2.91 us
  transfers between devices with their start and end apart: 10, of which 5 were waited for; matrix products, arithmetic and copies ran while one was open for 2% of the time, Pallas kernels for 22%

profile of v13, /device:TPU:1, one launch (start us, length us, event | category | flops | bytes accessed | tf_op | source)
XLA Modules:
  0.0 105.3 jit_solution(1618316898689702521)
XLA Ops:
  0.0 1.4 %pack_panel.4.rest_6_ = bf16[3,16,7424]{2,1,0:T(8,128)(2,1)S(1)} custom-call(s32[1]{0:T(128)} %bitcast.spot_ref, s32[1,16]{1,0:T(1,128)} %bitcast.28, bf16[45,16,2880]{2,1,0:T(8,128)(2,1)} %tail_ref.7, bf16[45,16,2880]{2,1,0:T(8,128)(2,1)} %tail_ref.7, bf16[45,16,2880]{2,1,0:T(8,128)(2,1)} %tail_ref.7, bf16[45,16,2880]{2,1,0:T(8,128)(2,1)} %tail_ref.7, ...), custom_call_target="tpu_custom_call" | custom-call | bytes 1500000 | tf_op jit(solution)/shard_map/pack_panel/pallas_call | solution.py:70
  1.4 3.4 %collective-permute-start.1 = (bf16[3,16,7424]{2,1,0:T(8,128)(2,1)S(1)}, bf16[3,16,7424]{2,1,0:T(8,128)(2,1)}, u32[]{:S(2)}, u32[]{:S(2)}) collective-permute-start(bf16[3,16,7424]{2,1,0:T(8,128)(2,1)S(1)} %pack_panel.4.rest_6_), channel_id=1, source_target_pairs={{1,2},{2,1},{3,0},{0,3},{5,6},{6,5},{7,4},{4,7},{9,10},{10,9},{11,... | collective-permute-start | bytes 2138120 | tf_op jit(solution)/shard_map/ppermute | solution.py:246
  4.8 1.4 %pack_gauss.4.rest_6_ = bf16[3,16,7296]{2,1,0:T(8,128)(2,1)S(1)} custom-call(bf16[2,45,16,720]{3,2,1,0:T(8,128)(2,1)} %bitcast.32, bf16[2,45,16,720]{3,2,1,0:T(8,128)(2,1)} %bitcast.33, bf16[2,45,16,720]{3,2,1,0:T(8,128)(2,1)} %bitcast.34, bf16[2,45,16,720]{3,2,1,0:T(8,128)(2,1)} %bitcast.35, bf16[2,45,16,720]{3,2,1,0:T(8,128)(2,1)} %bitcast.36, ...), custom_call_target="tpu_custom_call" | custom-call | bytes 1500000 | tf_op jit(solution)/shard_map/pack_gauss/pallas_call | solution.py:93
  6.2 1.4 %pack_panel.5.rest_6_ = bf16[3,16,7424]{2,1,0:T(8,128)(2,1)S(1)} custom-call(s32[1]{0:T(128)} %bitcast.spot_ref, s32[1,16]{1,0:T(1,128)} %bitcast.29, bf16[45,16,2880]{2,1,0:T(8,128)(2,1)} %tail_ref.7, bf16[45,16,2880]{2,1,0:T(8,128)(2,1)} %tail_ref.7, bf16[45,16,2880]{2,1,0:T(8,128)(2,1)} %tail_ref.7, bf16[45,16,2880]{2,1,0:T(8,128)(2,1)} %tail_ref.7, ...), custom_call_target="tpu_custom_call" | custom-call | bytes 1500000 | tf_op jit(solution)/shard_map/pack_panel/pallas_call | solution.py:70
  7.7 0.9 collective-permute-start.7
  8.5 1.4 %pack_gauss.5.rest_5_ = bf16[3,16,7296]{2,1,0:T(8,128)(2,1)S(1)} custom-call(bf16[2,45,16,720]{3,2,1,0:T(8,128)(2,1)} %bitcast.38, bf16[2,45,16,720]{3,2,1,0:T(8,128)(2,1)} %bitcast.39, bf16[2,45,16,720]{3,2,1,0:T(8,128)(2,1)} %bitcast.40, bf16[2,45,16,720]{3,2,1,0:T(8,128)(2,1)} %bitcast.41, bf16[2,45,16,720]{3,2,1,0:T(8,128)(2,1)} %bitcast.42, ...), custom_call_target="tpu_custom_call" | custom-call | bytes 1500000 | tf_op jit(solution)/shard_map/pack_gauss/pallas_call | solution.py:93
  12.5 10.1 %collective-permute-done.other_ref = bf16[3,16,7296]{2,1,0:T(8,128)(2,1)} collective-permute-done((bf16[3,16,7296]{2,1,0:T(8,128)(2,1)S(1)}, bf16[3,16,7296]{2,1,0:T(8,128)(2,1)}, u32[]{:S(2)}, u32[]{:S(2)}) %collective-permute-start) | collective-permute-done | bytes 700448 | tf_op jit(solution)/shard_map/ppermute | solution.py:248
  22.6 4.9 %partial_sums.4 = (f32[15,16,96]{2,1,0:T(8,128)S(1)}, bf16[15,16,96]{2,1,0:T(8,128)(2,1)S(1)}) custom-call(s32[1]{0:T(128)} %bitcast.spot_ref, s32[45]{0:T(128)S(1)} %dynamic_slice.3.order_ref, f32[3,16,1536]{2,1,0:T(8,128)S(1)} %pad_maximum_fusion.decay_ref, s32[16]{0:T(128)S(1)} %copy-done, bf16[2,45,16,720]{3,2,1,0:T(8,128)(2,1)} %bitcast.44, ...), custom_call_target="tpu_custom_call" | custom-call | flops 188743680 | bytes 3000000 | tf_op jit(solution)/shard_map/partial_sums/pallas_call | solution.py:189
  27.5 1.3 %pack_panel.6.rest_4_ = bf16[2,16,7424]{2,1,0:T(8,128)(2,1)S(1)} custom-call(s32[1]{0:T(128)} %bitcast.spot_ref, s32[1,16]{1,0:T(1,128)} %bitcast.30, bf16[45,16,2880]{2,1,0:T(8,128)(2,1)} %tail_ref.7, bf16[45,16,2880]{2,1,0:T(8,128)(2,1)} %tail_ref.7, bf16[45,16,2880]{2,1,0:T(8,128)(2,1)} %tail_ref.7, bf16[45,16,2880]{2,1,0:T(8,128)(2,1)} %tail_ref.7, ...), custom_call_target="tpu_custom_call" | custom-call | bytes 1000000 | tf_op jit(solution)/shard_map/pack_panel/pallas_call | solution.py:70
  28.8 1.2 %pack_gauss.6.rest_3_ = bf16[2,16,7296]{2,1,0:T(8,128)(2,1)S(1)} custom-call(bf16[2,45,16,720]{3,2,1,0:T(8,128)(2,1)} %bitcast.45, bf16[2,45,16,720]{3,2,1,0:T(8,128)(2,1)} %bitcast.46, bf16[2,45,16,720]{3,2,1,0:T(8,128)(2,1)} %bitcast.47, bf16[2,45,16,720]{3,2,1,0:T(8,128)(2,1)} %bitcast.48, bf16[2,16,7424]{2,1,0:T(8,128)(2,1)S(1)} %pack_panel.6.rest_4_), custom_call_target="tpu_custom_call" | custom-call | bytes 1000000 | tf_op jit(solution)/shard_map/pack_gauss/pallas_call | solution.py:93
  30.8 1.1 %pack_panel.7.rest_2_ = bf16[1,16,7424]{2,1,0:T(8,128)(2,1)S(1)} custom-call(s32[1]{0:T(128)} %bitcast.spot_ref, s32[1,16]{1,0:T(1,128)} %bitcast.31, bf16[45,16,2880]{2,1,0:T(8,128)(2,1)} %tail_ref.7, bf16[45,16,2880]{2,1,0:T(8,128)(2,1)} %tail_ref.7, f32[15,16,96]{2,1,0:T(8,128)S(1)} %get-tuple-element.18.rest_4_.rest_2_.rest_0_, ...), custom_call_target="tpu_custom_call" | custom-call | bytes 500000 | tf_op jit(solution)/shard_map/pack_panel/pallas_call | solution.py:70
  31.9 1.8 %pack_gauss.7 = bf16[1,16,7296]{2,1,0:T(8,128)(2,1)} custom-call(bf16[2,45,16,720]{3,2,1,0:T(8,128)(2,1)} %bitcast.49, bf16[2,45,16,720]{3,2,1,0:T(8,128)(2,1)} %bitcast.50, bf16[1,16,7424]{2,1,0:T(8,128)(2,1)S(1)} %pack_panel.7.rest_2_), custom_call_target="tpu_custom_call" | custom-call | bytes 500000 | tf_op jit(solution)/shard_map/pack_gauss/pallas_call | solution.py:93
  33.7 2.2 %collective-permute-start.3 = (bf16[1,16,7424]{2,1,0:T(8,128)(2,1)S(1)}, bf16[1,16,7424]{2,1,0:T(8,128)(2,1)S(1)}, u32[]{:S(2)}, u32[]{:S(2)}) collective-permute-start(bf16[1,16,7424]{2,1,0:T(8,128)(2,1)S(1)} %pack_panel.7.rest_2_), channel_id=1, source_target_pairs={{1,2},{2,1},{3,0},{0,3},{5,6},{6,5},{7,4},{4,7},{9,10},{10,9},{11,... | collective-permute-start | bytes 712712 | tf_op jit(solution)/shard_map/ppermute | solution.py:246
  35.9 1.7 %collective-permute-done.6.other_ref = bf16[3,16,7296]{2,1,0:T(8,128)(2,1)} collective-permute-done((bf16[3,16,7296]{2,1,0:T(8,128)(2,1)S(1)}, bf16[3,16,7296]{2,1,0:T(8,128)(2,1)}, u32[]{:S(2)}, u32[]{:S(2)}) %collective-permute-start.6) | collective-permute-done | bytes 700448 | tf_op jit(solution)/shard_map/ppermute | solution.py:248
  38.4 5.0 %partial_sums.5 = (f32[30,16,96]{2,1,0:T(8,128)S(1)}, bf16[30,16,96]{2,1,0:T(8,128)(2,1)S(1)}) custom-call(s32[1]{0:T(128)} %bitcast.spot_ref, s32[45]{0:T(128)S(1)} %dynamic_slice.3.order_ref, f32[3,16,1536]{2,1,0:T(8,128)S(1)} %pad_maximum_fusion.decay_ref, s32[16]{0:T(128)S(1)} %copy-done.1, bf16[2,45,16,720]{3,2,1,0:T(8,128)(2,1)} %bitcast.51, ...), custom_call_target="tpu_custom_call" | custom-call | flops 188743680 | bytes 3000000 | tf_op jit(solution)/shard_map/partial_sums/pallas_call | solution.py:189
  43.4 4.2 %collective-permute-done.4.other_ref = bf16[2,16,7296]{2,1,0:T(8,128)(2,1)} collective-permute-done((bf16[2,16,7296]{2,1,0:T(8,128)(2,1)S(1)}, bf16[2,16,7296]{2,1,0:T(8,128)(2,1)}, u32[]{:S(2)}, u32[]{:S(2)}) %collective-permute-start.4) | collective-permute-done | bytes 466976 | tf_op jit(solution)/shard_map/ppermute | solution.py:248
  47.6 3.7 %partial_sums.6 = (f32[30,16,96]{2,1,0:T(8,128)S(1)}, bf16[30,16,96]{2,1,0:T(8,128)(2,1)S(1)}) custom-call(s32[1]{0:T(128)} %bitcast.spot_ref, s32[45]{0:T(128)S(1)} %dynamic_slice.3.order_ref, f32[3,16,1536]{2,1,0:T(8,128)S(1)} %pad_maximum_fusion.decay_ref, s32[16]{0:T(128)S(1)} %copy-done.1, ...), custom_call_target="tpu_custom_call", output_to_operand_aliasing={{0}: (9, {}), {1}: (10, {})} | custom-call | flops 125829120 | bytes 2000000 | tf_op jit(solution)/shard_map/partial_sums/pallas_call | solution.py:189
  51.3 1.2 %collective-permute-done.2.other_ref = bf16[1,16,7296]{2,1,0:T(8,128)(2,1)S(1)} collective-permute-done((bf16[1,16,7296]{2,1,0:T(8,128)(2,1)}, bf16[1,16,7296]{2,1,0:T(8,128)(2,1)S(1)}, u32[]{:S(2)}, u32[]{:S(2)}) %collective-permute-start.2) | collective-permute-done | bytes 233504 | tf_op jit(solution)/shard_map/ppermute | solution.py:248
  52.5 2.3 %partial_sums.7 = (f32[30,16,96]{2,1,0:T(8,128)S(1)}, bf16[30,16,96]{2,1,0:T(8,128)(2,1)S(1)}) custom-call(s32[1]{0:T(128)} %bitcast.spot_ref, s32[45]{0:T(128)S(1)} %dynamic_slice.3.order_ref, f32[3,16,1536]{2,1,0:T(8,128)S(1)} %pad_maximum_fusion.decay_ref, s32[16]{0:T(128)S(1)} %copy-done.1, ...), custom_call_target="tpu_custom_call", output_to_operand_aliasing={{0}: (9, {}), {1}: (10, {})} | custom-call | flops 62914560 | bytes 1000000 | tf_op jit(solution)/shard_map/partial_sums/pallas_call | solution.py:189
  54.8 2.5 %collective-permute-start.9 = (bf16[30,16,96]{2,1,0:T(8,128)(2,1)S(1)}, bf16[30,16,96]{2,1,0:T(8,128)(2,1)S(1)}, u32[]{:S(2)}, u32[]{:S(2)}) collective-permute-start(bf16[30,16,96]{2,1,0:T(8,128)(2,1)S(1)} %get-tuple-element.25), channel_id=1, source_target_pairs={{1,2},{2,1},{3,0},{0,3},{5,6},{6,5},{7,4},{4,7},{9,10},{10,9},{11,... | collective-permute-start | bytes 276488 | tf_op jit(solution)/shard_map/ppermute | solution.py:262
  57.4 2.6 %collective-permute-done.9 = bf16[30,16,96]{2,1,0:T(8,128)(2,1)S(1)} collective-permute-done((bf16[30,16,96]{2,1,0:T(8,128)(2,1)S(1)}, bf16[30,16,96]{2,1,0:T(8,128)(2,1)S(1)}, u32[]{:S(2)}, u32[]{:S(2)}) %collective-permute-start.9) | collective-permute-done | bytes 92192 | tf_op jit(solution)/shard_map/ppermute | solution.py:262
  61.2 25.3 %all_to_all.10 = bf16[64,2,540]{2,1,0:T(2,128)(2,1)S(1)} all-to-all(bf16[64,2,540]{2,1,0:T(2,128)(2,1)S(1)} %copy.23), channel_id=1, replica_groups=mesh['ord'=64,'blk'=4] {'ord'}, dimensions={0} | all-to-all | bytes 276480 | tf_op jit(solution)/shard_map/all_to_all | solution.py:283
  88.4 16.1 %all_to_all.11 = bf16[192,4,90]{2,1,0:T(4,128)(2,1)S(1)} all-to-all(bf16[192,4,90]{2,1,0:T(4,128)(2,1)S(1)} %bitcast.55), channel_id=1, replica_groups=mesh['ord'=64,'blk'=4] {'ord'}, dimensions={0} | all-to-all | bytes 276480 | tf_op jit(solution)/shard_map/all_to_all | solution.py:293
  104.5 0.8 copy.25
  (45 shorter events, 7.3 us)
Async XLA Ops:
  1.4 21.2 %collective-permute-start.1 = (bf16[3,16,7424]{2,1,0:T(8,128)(2,1)S(1)}, bf16[3,16,7424]{2,1,0:T(8,128)(2,1)}, u32[]{:S(2)}, u32[]{:S(2)}) collective-permute-start(bf16[3,16,7424]{2,1,0:T(8,128)(2,1)S(1)} %pack_panel.4.rest_6_), channel_id=1, source_target_pairs={{1,2},{2,1},{3,0},{0,3},{5,6},{6,5},{7,4},{4,7},{9,10},{10,9},{11,... | collective-permute-start | bytes 2138120 | tf_op jit(solution)/shard_map/ppermute | solution.py:246
  6.1 16.4 %collective-permute-start = (bf16[3,16,7296]{2,1,0:T(8,128)(2,1)S(1)}, bf16[3,16,7296]{2,1,0:T(8,128)(2,1)}, u32[]{:S(2)}, u32[]{:S(2)}) collective-permute-start(bf16[3,16,7296]{2,1,0:T(8,128)(2,1)S(1)} %pack_gauss.4.rest_6_), channel_id=1, source_target_pairs={{0,1},{1,0},{2,3},{3,2},{4,5},{5,4},{6,7},{7,6},{8,9},{9,8},{10,11... | collective-permute-start | bytes 2101256 | tf_op jit(solution)/shard_map/ppermute | solution.py:248
  7.6 3.9 %copy-start.2 = (f32[16]{0:T(128)S(1)}, f32[16]{0:T(128)}, u32[]{:S(2)}) copy-start(f32[16]{0:T(128)} %param.7) | copy-start | bytes 196
  7.7 14.9 %copy-start = (s32[16]{0:T(128)S(1)}, s32[16]{0:T(128)}, u32[]{:S(2)}) copy-start(s32[16]{0:T(128)} %cycle_ref.7) | copy-start | bytes 196
  7.7 30.1 %collective-permute-start.7 = (bf16[3,16,7424]{2,1,0:T(8,128)(2,1)S(1)}, bf16[3,16,7424]{2,1,0:T(8,128)(2,1)}, u32[]{:S(2)}, u32[]{:S(2)}) collective-permute-start(bf16[3,16,7424]{2,1,0:T(8,128)(2,1)S(1)} %pack_panel.5.rest_6_), channel_id=1, source_target_pairs={{1,2},{2,1},{3,0},{0,3},{5,6},{6,5},{7,4},{4,7},{9,10},{10,9},{11,... | collective-permute-start | bytes 2138120 | tf_op jit(solution)/shard_map/ppermute | solution.py:246
  9.9 27.7 %collective-permute-start.6 = (bf16[3,16,7296]{2,1,0:T(8,128)(2,1)S(1)}, bf16[3,16,7296]{2,1,0:T(8,128)(2,1)}, u32[]{:S(2)}, u32[]{:S(2)}) collective-permute-start(bf16[3,16,7296]{2,1,0:T(8,128)(2,1)S(1)} %pack_gauss.5.rest_5_), channel_id=1, source_target_pairs={{0,1},{1,0},{2,3},{3,2},{4,5},{5,4},{6,7},{7,6},{8,9},{9,8},{10,11... | collective-permute-start | bytes 2101256 | tf_op jit(solution)/shard_map/ppermute | solution.py:248
  30.0 17.6 %collective-permute-start.5 = (bf16[2,16,7424]{2,1,0:T(8,128)(2,1)S(1)}, bf16[2,16,7424]{2,1,0:T(8,128)(2,1)}, u32[]{:S(2)}, u32[]{:S(2)}) collective-permute-start(bf16[2,16,7424]{2,1,0:T(8,128)(2,1)S(1)} %pack_panel.6.rest_4_), channel_id=1, source_target_pairs={{1,2},{2,1},{3,0},{0,3},{5,6},{6,5},{7,4},{4,7},{9,10},{10,9},{11,... | collective-permute-start | bytes 1425416 | tf_op jit(solution)/shard_map/ppermute | solution.py:246
  30.5 17.1 %collective-permute-start.4 = (bf16[2,16,7296]{2,1,0:T(8,128)(2,1)S(1)}, bf16[2,16,7296]{2,1,0:T(8,128)(2,1)}, u32[]{:S(2)}, u32[]{:S(2)}) collective-permute-start(bf16[2,16,7296]{2,1,0:T(8,128)(2,1)S(1)} %pack_gauss.6.rest_3_), channel_id=1, source_target_pairs={{0,1},{1,0},{2,3},{3,2},{4,5},{5,4},{6,7},{7,6},{8,9},{9,8},{10,11... | collective-permute-start | bytes 1400840 | tf_op jit(solution)/shard_map/ppermute | solution.py:248
  31.9 6.5 %copy-start.1 = (s32[16]{0:T(128)S(1)}, s32[16]{0:T(128)}, u32[]{:S(2)}) copy-start(s32[16]{0:T(128)} %cycle_ref.7) | copy-start | bytes 196
  33.7 18.8 %collective-permute-start.3 = (bf16[1,16,7424]{2,1,0:T(8,128)(2,1)S(1)}, bf16[1,16,7424]{2,1,0:T(8,128)(2,1)S(1)}, u32[]{:S(2)}, u32[]{:S(2)}) collective-permute-start(bf16[1,16,7424]{2,1,0:T(8,128)(2,1)S(1)} %pack_panel.7.rest_2_), channel_id=1, source_target_pairs={{1,2},{2,1},{3,0},{0,3},{5,6},{6,5},{7,4},{4,7},{9,10},{10,9},{11,... | collective-permute-start | bytes 712712 | tf_op jit(solution)/shard_map/ppermute | solution.py:246
  37.6 14.9 %collective-permute-start.2 = (bf16[1,16,7296]{2,1,0:T(8,128)(2,1)}, bf16[1,16,7296]{2,1,0:T(8,128)(2,1)S(1)}, u32[]{:S(2)}, u32[]{:S(2)}) collective-permute-start(bf16[1,16,7296]{2,1,0:T(8,128)(2,1)} %pack_gauss.7), channel_id=1, source_target_pairs={{0,1},{1,0},{2,3},{3,2},{4,5},{5,4},{6,7},{7,6},{8,9},{9,8},{10,11... | collective-permute-start | bytes 700424 | tf_op jit(solution)/shard_map/ppermute | solution.py:248
  37.8 13.5 %collective-permute-start.8 = (bf16[15,16,96]{2,1,0:T(8,128)(2,1)S(1)}, bf16[15,16,96]{2,1,0:T(8,128)(2,1)S(1)}, u32[]{:S(2)}, u32[]{:S(2)}) collective-permute-start(bf16[15,16,96]{2,1,0:T(8,128)(2,1)S(1)} %get-tuple-element.23), channel_id=1, source_target_pairs={{1,2},{2,1},{3,0},{0,3},{5,6},{6,5},{7,4},{4,7},{9,10},{10,9},{11,... | collective-permute-start | bytes 138248 | tf_op jit(solution)/shard_map/ppermute | solution.py:262
  54.8 5.2 %collective-permute-start.9 = (bf16[30,16,96]{2,1,0:T(8,128)(2,1)S(1)}, bf16[30,16,96]{2,1,0:T(8,128)(2,1)S(1)}, u32[]{:S(2)}, u32[]{:S(2)}) collective-permute-start(bf16[30,16,96]{2,1,0:T(8,128)(2,1)S(1)} %get-tuple-element.25), channel_id=1, source_target_pairs={{1,2},{2,1},{3,0},{0,3},{5,6},{6,5},{7,4},{4,7},{9,10},{10,9},{11,... | collective-permute-start | bytes 276488 | tf_op jit(solution)/shard_map/ppermute | solution.py:262

commit v14 on v13

--- a/solution.py
+++ b/solution.py
@@ -113,9 +113,11 @@
 
     @pl.when(step == 0)
     def _():
-        gs_ref[...] = jnp.zeros_like(gs_ref)
-        gn_ref[...] = jnp.zeros_like(gn_ref)
-        table_ref[...] = jnp.zeros_like(table_ref)
+        edge = jnp.zeros((2, GROUP, 16, 128), jnp.bfloat16)
+        for ref in (gs_ref, gn_ref):
+            ref[:, :, :, 0:128] = edge
+            ref[:, :, :, START:WIDE] = edge
+        table_ref[:, :, START:WIDE] = jnp.zeros((GROUP, 32, 128), jnp.bfloat16)
         digits = far_ref[0, :, CYCLE_LANE:CYCLE_LANE + 2].astype(jnp.float32)
         mates = digits[:, 0:1] * 64.0 + digits[:, 1:2]
         cycles = jnp.broadcast_to(mates, (16, 128)).T[0:8, :]

time: 106 us -> 106 us (level)
  no operation moved by 1% of the time
where the time goes in v14:
time: 106 us; the launch traced here: 105 us
  blocking collectives  41.4 us (39%)
  Pallas kernels  26.8 us (25%)
  waiting for transfers between devices  19.8 us (19%)
  starting transfers between devices  10.9 us (10%)
  local copies, waits for them, and re-layouts  4.77 us (4%)
    all_to_all x1, blocking collectives, body(): lax.all_to_all(chunk, 'ord', 0, 0, tiled=True)  25.3 us
    ppermute x4, waiting for transfers between devices, start(): packed.append((lax.ppermute(coef, 'blk', GAUSS_PAIRS), far, coef))  17.2 us
    all_to_all x1, blocking collectives, body(): field = lax.all_to_all(field, 'ord', 0, 0, tiled=True)  16.1 us
    pallas_call x4, Pallas kernels, partial_sums(): pl.pallas_call(functools.partial(sums_kernel, base=base), out_shape=[jax....  15.9 us
    ppermute x4, starting transfers between devices, start(): far = lax.ppermute(part, 'blk', PANEL_PAIRS)  7 us
    pallas_call x4, Pallas kernels, packed_gauss(): pl.pallas_call(functools.partial(pack_gauss, steps=steps), out_shape=jax....  5.71 us
    pallas_call x4, Pallas kernels, packed_panel(): pl.pallas_call(functools.partial(pack_panel, steps=steps), out_shape=jax....  5.18 us
    ppermute x2, starting transfers between devices, body(): added.append(lax.ppermute(send, 'blk', PANEL_PAIRS))  2.91 us
  transfers between devices with their start and end apart: 10, of which 5 were waited for; matrix products, arithmetic and copies ran while one was open for 2% of the time, Pallas kernels for 22%

profile of v14, /device:TPU:1, one launch (start us, length us, event | category | flops | bytes accessed | tf_op | source)
XLA Modules:
  0.0 105.3 jit_solution(16194794995878763597)
XLA Ops:
  0.0 1.4 %pack_panel.4.rest_6_ = bf16[3,16,7424]{2,1,0:T(8,128)(2,1)S(1)} custom-call(s32[1]{0:T(128)} %bitcast.spot_ref, s32[1,16]{1,0:T(1,128)} %bitcast.28, bf16[45,16,2880]{2,1,0:T(8,128)(2,1)} %tail_ref.7, bf16[45,16,2880]{2,1,0:T(8,128)(2,1)} %tail_ref.7, bf16[45,16,2880]{2,1,0:T(8,128)(2,1)} %tail_ref.7, bf16[45,16,2880]{2,1,0:T(8,128)(2,1)} %tail_ref.7, ...), custom_call_target="tpu_custom_call" | custom-call | bytes 1500000 | tf_op jit(solution)/shard_map/pack_panel/pallas_call | solution.py:70
  1.4 3.4 %collective-permute-start.1 = (bf16[3,16,7424]{2,1,0:T(8,128)(2,1)S(1)}, bf16[3,16,7424]{2,1,0:T(8,128)(2,1)}, u32[]{:S(2)}, u32[]{:S(2)}) collective-permute-start(bf16[3,16,7424]{2,1,0:T(8,128)(2,1)S(1)} %pack_panel.4.rest_6_), channel_id=1, source_target_pairs={{1,2},{2,1},{3,0},{0,3},{5,6},{6,5},{7,4},{4,7},{9,10},{10,9},{11,... | collective-permute-start | bytes 2138120 | tf_op jit(solution)/shard_map/ppermute | solution.py:248
  4.8 1.4 %pack_gauss.4.rest_6_ = bf16[3,16,7296]{2,1,0:T(8,128)(2,1)S(1)} custom-call(bf16[2,45,16,720]{3,2,1,0:T(8,128)(2,1)} %bitcast.32, bf16[2,45,16,720]{3,2,1,0:T(8,128)(2,1)} %bitcast.33, bf16[2,45,16,720]{3,2,1,0:T(8,128)(2,1)} %bitcast.34, bf16[2,45,16,720]{3,2,1,0:T(8,128)(2,1)} %bitcast.35, bf16[2,45,16,720]{3,2,1,0:T(8,128)(2,1)} %bitcast.36, ...), custom_call_target="tpu_custom_call" | custom-call | bytes 1500000 | tf_op jit(solution)/shard_map/pack_gauss/pallas_call | solution.py:93
  6.2 1.4 %pack_panel.5.rest_6_ = bf16[3,16,7424]{2,1,0:T(8,128)(2,1)S(1)} custom-call(s32[1]{0:T(128)} %bitcast.spot_ref, s32[1,16]{1,0:T(1,128)} %bitcast.29, bf16[45,16,2880]{2,1,0:T(8,128)(2,1)} %tail_ref.7, bf16[45,16,2880]{2,1,0:T(8,128)(2,1)} %tail_ref.7, bf16[45,16,2880]{2,1,0:T(8,128)(2,1)} %tail_ref.7, bf16[45,16,2880]{2,1,0:T(8,128)(2,1)} %tail_ref.7, ...), custom_call_target="tpu_custom_call" | custom-call | bytes 1500000 | tf_op jit(solution)/shard_map/pack_panel/pallas_call | solution.py:70
  7.7 0.9 collective-permute-start.7
  8.5 1.4 %pack_gauss.5.rest_5_ = bf16[3,16,7296]{2,1,0:T(8,128)(2,1)S(1)} custom-call(bf16[2,45,16,720]{3,2,1,0:T(8,128)(2,1)} %bitcast.38, bf16[2,45,16,720]{3,2,1,0:T(8,128)(2,1)} %bitcast.39, bf16[2,45,16,720]{3,2,1,0:T(8,128)(2,1)} %bitcast.40, bf16[2,45,16,720]{3,2,1,0:T(8,128)(2,1)} %bitcast.41, bf16[2,45,16,720]{3,2,1,0:T(8,128)(2,1)} %bitcast.42, ...), custom_call_target="tpu_custom_call" | custom-call | bytes 1500000 | tf_op jit(solution)/shard_map/pack_gauss/pallas_call | solution.py:93
  12.5 10.1 %collective-permute-done.other_ref = bf16[3,16,7296]{2,1,0:T(8,128)(2,1)} collective-permute-done((bf16[3,16,7296]{2,1,0:T(8,128)(2,1)S(1)}, bf16[3,16,7296]{2,1,0:T(8,128)(2,1)}, u32[]{:S(2)}, u32[]{:S(2)}) %collective-permute-start) | collective-permute-done | bytes 700448 | tf_op jit(solution)/shard_map/ppermute | solution.py:250
  22.6 4.9 %partial_sums.4 = (f32[15,16,96]{2,1,0:T(8,128)S(1)}, bf16[15,16,96]{2,1,0:T(8,128)(2,1)S(1)}) custom-call(s32[1]{0:T(128)} %bitcast.spot_ref, s32[45]{0:T(128)S(1)} %dynamic_slice.3.order_ref, f32[3,16,1536]{2,1,0:T(8,128)S(1)} %pad_maximum_fusion.decay_ref, s32[16]{0:T(128)S(1)} %copy-done, bf16[2,45,16,720]{3,2,1,0:T(8,128)(2,1)} %bitcast.44, ...), custom_call_target="tpu_custom_call" | custom-call | flops 188743680 | bytes 3000000 | tf_op jit(solution)/shard_map/partial_sums/pallas_call | solution.py:191
  27.5 1.3 %pack_panel.6.rest_4_ = bf16[2,16,7424]{2,1,0:T(8,128)(2,1)S(1)} custom-call(s32[1]{0:T(128)} %bitcast.spot_ref, s32[1,16]{1,0:T(1,128)} %bitcast.30, bf16[45,16,2880]{2,1,0:T(8,128)(2,1)} %tail_ref.7, bf16[45,16,2880]{2,1,0:T(8,128)(2,1)} %tail_ref.7, bf16[45,16,2880]{2,1,0:T(8,128)(2,1)} %tail_ref.7, bf16[45,16,2880]{2,1,0:T(8,128)(2,1)} %tail_ref.7, ...), custom_call_target="tpu_custom_call" | custom-call | bytes 1000000 | tf_op jit(solution)/shard_map/pack_panel/pallas_call | solution.py:70
  28.8 1.2 %pack_gauss.6.rest_3_ = bf16[2,16,7296]{2,1,0:T(8,128)(2,1)S(1)} custom-call(bf16[2,45,16,720]{3,2,1,0:T(8,128)(2,1)} %bitcast.45, bf16[2,45,16,720]{3,2,1,0:T(8,128)(2,1)} %bitcast.46, bf16[2,45,16,720]{3,2,1,0:T(8,128)(2,1)} %bitcast.47, bf16[2,45,16,720]{3,2,1,0:T(8,128)(2,1)} %bitcast.48, bf16[2,16,7424]{2,1,0:T(8,128)(2,1)S(1)} %pack_panel.6.rest_4_), custom_call_target="tpu_custom_call" | custom-call | bytes 1000000 | tf_op jit(solution)/shard_map/pack_gauss/pallas_call | solution.py:93
  30.8 1.1 %pack_panel.7.rest_2_ = bf16[1,16,7424]{2,1,0:T(8,128)(2,1)S(1)} custom-call(s32[1]{0:T(128)} %bitcast.spot_ref, s32[1,16]{1,0:T(1,128)} %bitcast.31, bf16[45,16,2880]{2,1,0:T(8,128)(2,1)} %tail_ref.7, bf16[45,16,2880]{2,1,0:T(8,128)(2,1)} %tail_ref.7, f32[15,16,96]{2,1,0:T(8,128)S(1)} %get-tuple-element.18.rest_4_.rest_2_.rest_0_, ...), custom_call_target="tpu_custom_call" | custom-call | bytes 500000 | tf_op jit(solution)/shard_map/pack_panel/pallas_call | solution.py:70
  31.9 1.8 %pack_gauss.7 = bf16[1,16,7296]{2,1,0:T(8,128)(2,1)} custom-call(bf16[2,45,16,720]{3,2,1,0:T(8,128)(2,1)} %bitcast.49, bf16[2,45,16,720]{3,2,1,0:T(8,128)(2,1)} %bitcast.50, bf16[1,16,7424]{2,1,0:T(8,128)(2,1)S(1)} %pack_panel.7.rest_2_), custom_call_target="tpu_custom_call" | custom-call | bytes 500000 | tf_op jit(solution)/shard_map/pack_gauss/pallas_call | solution.py:93
  33.7 2.2 %collective-permute-start.3 = (bf16[1,16,7424]{2,1,0:T(8,128)(2,1)S(1)}, bf16[1,16,7424]{2,1,0:T(8,128)(2,1)S(1)}, u32[]{:S(2)}, u32[]{:S(2)}) collective-permute-start(bf16[1,16,7424]{2,1,0:T(8,128)(2,1)S(1)} %pack_panel.7.rest_2_), channel_id=1, source_target_pairs={{1,2},{2,1},{3,0},{0,3},{5,6},{6,5},{7,4},{4,7},{9,10},{10,9},{11,... | collective-permute-start | bytes 712712 | tf_op jit(solution)/shard_map/ppermute | solution.py:248
  35.9 1.7 %collective-permute-done.6.other_ref = bf16[3,16,7296]{2,1,0:T(8,128)(2,1)} collective-permute-done((bf16[3,16,7296]{2,1,0:T(8,128)(2,1)S(1)}, bf16[3,16,7296]{2,1,0:T(8,128)(2,1)}, u32[]{:S(2)}, u32[]{:S(2)}) %collective-permute-start.6) | collective-permute-done | bytes 700448 | tf_op jit(solution)/shard_map/ppermute | solution.py:250
  38.4 5.0 %partial_sums.5 = (f32[30,16,96]{2,1,0:T(8,128)S(1)}, bf16[30,16,96]{2,1,0:T(8,128)(2,1)S(1)}) custom-call(s32[1]{0:T(128)} %bitcast.spot_ref, s32[45]{0:T(128)S(1)} %dynamic_slice.3.order_ref, f32[3,16,1536]{2,1,0:T(8,128)S(1)} %pad_maximum_fusion.decay_ref, s32[16]{0:T(128)S(1)} %copy-done.1, bf16[2,45,16,720]{3,2,1,0:T(8,128)(2,1)} %bitcast.51, ...), custom_call_target="tpu_custom_call" | custom-call | flops 188743680 | bytes 3000000 | tf_op jit(solution)/shard_map/partial_sums/pallas_call | solution.py:191
  43.4 4.2 %collective-permute-done.4.other_ref = bf16[2,16,7296]{2,1,0:T(8,128)(2,1)} collective-permute-done((bf16[2,16,7296]{2,1,0:T(8,128)(2,1)S(1)}, bf16[2,16,7296]{2,1,0:T(8,128)(2,1)}, u32[]{:S(2)}, u32[]{:S(2)}) %collective-permute-start.4) | collective-permute-done | bytes 466976 | tf_op jit(solution)/shard_map/ppermute | solution.py:250
  47.6 3.7 %partial_sums.6 = (f32[30,16,96]{2,1,0:T(8,128)S(1)}, bf16[30,16,96]{2,1,0:T(8,128)(2,1)S(1)}) custom-call(s32[1]{0:T(128)} %bitcast.spot_ref, s32[45]{0:T(128)S(1)} %dynamic_slice.3.order_ref, f32[3,16,1536]{2,1,0:T(8,128)S(1)} %pad_maximum_fusion.decay_ref, s32[16]{0:T(128)S(1)} %copy-done.1, ...), custom_call_target="tpu_custom_call", output_to_operand_aliasing={{0}: (9, {}), {1}: (10, {})} | custom-call | flops 125829120 | bytes 2000000 | tf_op jit(solution)/shard_map/partial_sums/pallas_call | solution.py:191
  51.3 1.2 %collective-permute-done.2.other_ref = bf16[1,16,7296]{2,1,0:T(8,128)(2,1)S(1)} collective-permute-done((bf16[1,16,7296]{2,1,0:T(8,128)(2,1)}, bf16[1,16,7296]{2,1,0:T(8,128)(2,1)S(1)}, u32[]{:S(2)}, u32[]{:S(2)}) %collective-permute-start.2) | collective-permute-done | bytes 233504 | tf_op jit(solution)/shard_map/ppermute | solution.py:250
  52.5 2.3 %partial_sums.7 = (f32[30,16,96]{2,1,0:T(8,128)S(1)}, bf16[30,16,96]{2,1,0:T(8,128)(2,1)S(1)}) custom-call(s32[1]{0:T(128)} %bitcast.spot_ref, s32[45]{0:T(128)S(1)} %dynamic_slice.3.order_ref, f32[3,16,1536]{2,1,0:T(8,128)S(1)} %pad_maximum_fusion.decay_ref, s32[16]{0:T(128)S(1)} %copy-done.1, ...), custom_call_target="tpu_custom_call", output_to_operand_aliasing={{0}: (9, {}), {1}: (10, {})} | custom-call | flops 62914560 | bytes 1000000 | tf_op jit(solution)/shard_map/partial_sums/pallas_call | solution.py:191
  54.8 2.5 %collective-permute-start.9 = (bf16[30,16,96]{2,1,0:T(8,128)(2,1)S(1)}, bf16[30,16,96]{2,1,0:T(8,128)(2,1)S(1)}, u32[]{:S(2)}, u32[]{:S(2)}) collective-permute-start(bf16[30,16,96]{2,1,0:T(8,128)(2,1)S(1)} %get-tuple-element.25), channel_id=1, source_target_pairs={{1,2},{2,1},{3,0},{0,3},{5,6},{6,5},{7,4},{4,7},{9,10},{10,9},{11,... | collective-permute-start | bytes 276488 | tf_op jit(solution)/shard_map/ppermute | solution.py:264
  57.4 2.6 %collective-permute-done.9 = bf16[30,16,96]{2,1,0:T(8,128)(2,1)S(1)} collective-permute-done((bf16[30,16,96]{2,1,0:T(8,128)(2,1)S(1)}, bf16[30,16,96]{2,1,0:T(8,128)(2,1)S(1)}, u32[]{:S(2)}, u32[]{:S(2)}) %collective-permute-start.9) | collective-permute-done | bytes 92192 | tf_op jit(solution)/shard_map/ppermute | solution.py:264
  61.2 25.3 %all_to_all.10 = bf16[64,2,540]{2,1,0:T(2,128)(2,1)S(1)} all-to-all(bf16[64,2,540]{2,1,0:T(2,128)(2,1)S(1)} %copy.23), channel_id=1, replica_groups=mesh['ord'=64,'blk'=4] {'ord'}, dimensions={0} | all-to-all | bytes 276480 | tf_op jit(solution)/shard_map/all_to_all | solution.py:285
  88.4 16.1 %all_to_all.11 = bf16[192,4,90]{2,1,0:T(4,128)(2,1)S(1)} all-to-all(bf16[192,4,90]{2,1,0:T(4,128)(2,1)S(1)} %bitcast.55), channel_id=1, replica_groups=mesh['ord'=64,'blk'=4] {'ord'}, dimensions={0} | all-to-all | bytes 276480 | tf_op jit(solution)/shard_map/all_to_all | solution.py:295
  104.5 0.8 copy.25
  (45 shorter events, 7.3 us)
Async XLA Ops:
  1.4 21.2 %collective-permute-start.1 = (bf16[3,16,7424]{2,1,0:T(8,128)(2,1)S(1)}, bf16[3,16,7424]{2,1,0:T(8,128)(2,1)}, u32[]{:S(2)}, u32[]{:S(2)}) collective-permute-start(bf16[3,16,7424]{2,1,0:T(8,128)(2,1)S(1)} %pack_panel.4.rest_6_), channel_id=1, source_target_pairs={{1,2},{2,1},{3,0},{0,3},{5,6},{6,5},{7,4},{4,7},{9,10},{10,9},{11,... | collective-permute-start | bytes 2138120 | tf_op jit(solution)/shard_map/ppermute | solution.py:248
  6.1 16.4 %collective-permute-start = (bf16[3,16,7296]{2,1,0:T(8,128)(2,1)S(1)}, bf16[3,16,7296]{2,1,0:T(8,128)(2,1)}, u32[]{:S(2)}, u32[]{:S(2)}) collective-permute-start(bf16[3,16,7296]{2,1,0:T(8,128)(2,1)S(1)} %pack_gauss.4.rest_6_), channel_id=1, source_target_pairs={{0,1},{1,0},{2,3},{3,2},{4,5},{5,4},{6,7},{7,6},{8,9},{9,8},{10,11... | collective-permute-start | bytes 2101256 | tf_op jit(solution)/shard_map/ppermute | solution.py:250
  7.6 3.9 %copy-start.2 = (f32[16]{0:T(128)S(1)}, f32[16]{0:T(128)}, u32[]{:S(2)}) copy-start(f32[16]{0:T(128)} %param.7) | copy-start | bytes 196
  7.7 14.9 %copy-start = (s32[16]{0:T(128)S(1)}, s32[16]{0:T(128)}, u32[]{:S(2)}) copy-start(s32[16]{0:T(128)} %cycle_ref.7) | copy-start | bytes 196
  7.7 30.1 %collective-permute-start.7 = (bf16[3,16,7424]{2,1,0:T(8,128)(2,1)S(1)}, bf16[3,16,7424]{2,1,0:T(8,128)(2,1)}, u32[]{:S(2)}, u32[]{:S(2)}) collective-permute-start(bf16[3,16,7424]{2,1,0:T(8,128)(2,1)S(1)} %pack_panel.5.rest_6_), channel_id=1, source_target_pairs={{1,2},{2,1},{3,0},{0,3},{5,6},{6,5},{7,4},{4,7},{9,10},{10,9},{11,... | collective-permute-start | bytes 2138120 | tf_op jit(solution)/shard_map/ppermute | solution.py:248
  9.9 27.7 %collective-permute-start.6 = (bf16[3,16,7296]{2,1,0:T(8,128)(2,1)S(1)}, bf16[3,16,7296]{2,1,0:T(8,128)(2,1)}, u32[]{:S(2)}, u32[]{:S(2)}) collective-permute-start(bf16[3,16,7296]{2,1,0:T(8,128)(2,1)S(1)} %pack_gauss.5.rest_5_), channel_id=1, source_target_pairs={{0,1},{1,0},{2,3},{3,2},{4,5},{5,4},{6,7},{7,6},{8,9},{9,8},{10,11... | collective-permute-start | bytes 2101256 | tf_op jit(solution)/shard_map/ppermute | solution.py:250
  30.0 17.6 %collective-permute-start.5 = (bf16[2,16,7424]{2,1,0:T(8,128)(2,1)S(1)}, bf16[2,16,7424]{2,1,0:T(8,128)(2,1)}, u32[]{:S(2)}, u32[]{:S(2)}) collective-permute-start(bf16[2,16,7424]{2,1,0:T(8,128)(2,1)S(1)} %pack_panel.6.rest_4_), channel_id=1, source_target_pairs={{1,2},{2,1},{3,0},{0,3},{5,6},{6,5},{7,4},{4,7},{9,10},{10,9},{11,... | collective-permute-start | bytes 1425416 | tf_op jit(solution)/shard_map/ppermute | solution.py:248
  30.5 17.1 %collective-permute-start.4 = (bf16[2,16,7296]{2,1,0:T(8,128)(2,1)S(1)}, bf16[2,16,7296]{2,1,0:T(8,128)(2,1)}, u32[]{:S(2)}, u32[]{:S(2)}) collective-permute-start(bf16[2,16,7296]{2,1,0:T(8,128)(2,1)S(1)} %pack_gauss.6.rest_3_), channel_id=1, source_target_pairs={{0,1},{1,0},{2,3},{3,2},{4,5},{5,4},{6,7},{7,6},{8,9},{9,8},{10,11... | collective-permute-start | bytes 1400840 | tf_op jit(solution)/shard_map/ppermute | solution.py:250
  31.9 6.5 %copy-start.1 = (s32[16]{0:T(128)S(1)}, s32[16]{0:T(128)}, u32[]{:S(2)}) copy-start(s32[16]{0:T(128)} %cycle_ref.7) | copy-start | bytes 196
  33.7 18.8 %collective-permute-start.3 = (bf16[1,16,7424]{2,1,0:T(8,128)(2,1)S(1)}, bf16[1,16,7424]{2,1,0:T(8,128)(2,1)S(1)}, u32[]{:S(2)}, u32[]{:S(2)}) collective-permute-start(bf16[1,16,7424]{2,1,0:T(8,128)(2,1)S(1)} %pack_panel.7.rest_2_), channel_id=1, source_target_pairs={{1,2},{2,1},{3,0},{0,3},{5,6},{6,5},{7,4},{4,7},{9,10},{10,9},{11,... | collective-permute-start | bytes 712712 | tf_op jit(solution)/shard_map/ppermute | solution.py:248
  37.6 14.9 %collective-permute-start.2 = (bf16[1,16,7296]{2,1,0:T(8,128)(2,1)}, bf16[1,16,7296]{2,1,0:T(8,128)(2,1)S(1)}, u32[]{:S(2)}, u32[]{:S(2)}) collective-permute-start(bf16[1,16,7296]{2,1,0:T(8,128)(2,1)} %pack_gauss.7), channel_id=1, source_target_pairs={{0,1},{1,0},{2,3},{3,2},{4,5},{5,4},{6,7},{7,6},{8,9},{9,8},{10,11... | collective-permute-start | bytes 700424 | tf_op jit(solution)/shard_map/ppermute | solution.py:250
  37.8 13.5 %collective-permute-start.8 = (bf16[15,16,96]{2,1,0:T(8,128)(2,1)S(1)}, bf16[15,16,96]{2,1,0:T(8,128)(2,1)S(1)}, u32[]{:S(2)}, u32[]{:S(2)}) collective-permute-start(bf16[15,16,96]{2,1,0:T(8,128)(2,1)S(1)} %get-tuple-element.23), channel_id=1, source_target_pairs={{1,2},{2,1},{3,0},{0,3},{5,6},{6,5},{7,4},{4,7},{9,10},{10,9},{11,... | collective-permute-start | bytes 138248 | tf_op jit(solution)/shard_map/ppermute | solution.py:264
  54.8 5.2 %collective-permute-start.9 = (bf16[30,16,96]{2,1,0:T(8,128)(2,1)S(1)}, bf16[30,16,96]{2,1,0:T(8,128)(2,1)S(1)}, u32[]{:S(2)}, u32[]{:S(2)}) collective-permute-start(bf16[30,16,96]{2,1,0:T(8,128)(2,1)S(1)} %get-tuple-element.25), channel_id=1, source_target_pairs={{1,2},{2,1},{3,0},{0,3},{5,6},{6,5},{7,4},{4,7},{9,10},{10,9},{11,... | collective-permute-start | bytes 276488 | tf_op jit(solution)/shard_map/ppermute | solution.py:264

commit v15 on v14

--- a/solution.py
+++ b/solution.py
@@ -16,7 +16,7 @@
 KEPT = 1472
 NLON = 5760
 GROUP = 5
-CHUNKS = (0, 15, 30, 40, 45)
+CHUNKS = (0, 20, 30, 40, 45)
 GAUSS_TAIL = 2 * GROUP * 640
 GAUSS_LANES = GAUSS_TAIL + 896
 PANEL_TAIL = GROUP * START

time: 106 us -> 109 us (1.028)
  blocking collectives: 41.4 us -> 43.6 us
  waiting for transfers between devices: 19.8 us -> 21.8 us
    ppermute x2, waiting for transfers between devices: 2.62 us -> 6.39 us  [body(): added.append(lax.ppermute(send, 'blk', PANEL_PAIRS))]
    all_to_all x1, blocking collectives: 25.3 us -> 27.6 us  [body(): lax.all_to_all(chunk, 'ord', 0, 0, tiled=True)]
    ppermute x4, waiting for transfers between devices: 17.2 us -> 15.4 us  [start(): packed.append((lax.ppermute(coef, 'blk', GAUSS_PAIRS), far, coef))]
    ppermute x2, starting transfers between devices: 2.91 us -> 1.29 us  [body(): added.append(lax.ppermute(send, 'blk', PANEL_PAIRS))]
  transfers between devices with their start and end apart: 10 -> 10, of which waited for: 5 -> 3; matrix products, arithmetic and copies ran while one was open for 2% -> 2% of each run, Pallas kernels for 22% -> 21%
where the time goes in v15:
time: 109 us; the launch traced here: 108 us
  blocking collectives  43.6 us (40%)
  Pallas kernels  26.3 us (24%)
  waiting for transfers between devices  21.8 us (20%)
  starting transfers between devices  10 us (9%)
  local copies, waits for them, and re-layouts  4.76 us (4%)
    all_to_all x1, blocking collectives, body(): lax.all_to_all(chunk, 'ord', 0, 0, tiled=True)  27.6 us
    all_to_all x1, blocking collectives, body(): field = lax.all_to_all(field, 'ord', 0, 0, tiled=True)  16.1 us
    pallas_call x4, Pallas kernels, partial_sums(): pl.pallas_call(functools.partial(sums_kernel, base=base), out_shape=[jax....  15.5 us
    ppermute x4, waiting for transfers between devices, start(): packed.append((lax.ppermute(coef, 'blk', GAUSS_PAIRS), far, coef))  15.4 us
    ppermute x4, starting transfers between devices, start(): far = lax.ppermute(part, 'blk', PANEL_PAIRS)  7.01 us
    ppermute x2, waiting for transfers between devices, body(): added.append(lax.ppermute(send, 'blk', PANEL_PAIRS))  6.39 us
    pallas_call x4, Pallas kernels, packed_gauss(): pl.pallas_call(functools.partial(pack_gauss, steps=steps), out_shape=jax....  5.65 us
    pallas_call x4, Pallas kernels, packed_panel(): pl.pallas_call(functools.partial(pack_panel, steps=steps), out_shape=jax....  5.2 us
  transfers between devices with their start and end apart: 10, of which 3 were waited for; matrix products, arithmetic and copies ran while one was open for 2% of the time, Pallas kernels for 21%

profile of v15, /device:TPU:1, one launch (start us, length us, event | category | flops | bytes accessed | tf_op | source)
XLA Modules:
  0.0 108.3 jit_solution(12437703645198216407)
XLA Ops:
  0.0 1.5 %pack_panel.4.rest_8_ = bf16[4,16,7424]{2,1,0:T(8,128)(2,1)S(1)} custom-call(s32[1]{0:T(128)} %bitcast.spot_ref, s32[1,16]{1,0:T(1,128)} %bitcast.28, bf16[45,16,2880]{2,1,0:T(8,128)(2,1)} %tail_ref.7, bf16[45,16,2880]{2,1,0:T(8,128)(2,1)} %tail_ref.7, bf16[45,16,2880]{2,1,0:T(8,128)(2,1)} %tail_ref.7, bf16[45,16,2880]{2,1,0:T(8,128)(2,1)} %tail_ref.7, ...), custom_call_target="tpu_custom_call" | custom-call | bytes 2000000 | tf_op jit(solution)/shard_map/pack_panel/pallas_call | solution.py:70
  1.5 3.4 %collective-permute-start.1 = (bf16[4,16,7424]{2,1,0:T(8,128)(2,1)S(1)}, bf16[4,16,7424]{2,1,0:T(8,128)(2,1)}, u32[]{:S(2)}, u32[]{:S(2)}) collective-permute-start(bf16[4,16,7424]{2,1,0:T(8,128)(2,1)S(1)} %pack_panel.4.rest_8_), channel_id=1, source_target_pairs={{1,2},{2,1},{3,0},{0,3},{5,6},{6,5},{7,4},{4,7},{9,10},{10,9},{11,... | collective-permute-start | bytes 2850824 | tf_op jit(solution)/shard_map/ppermute | solution.py:248
  4.9 1.5 %pack_gauss.4.rest_4_ = bf16[4,16,7296]{2,1,0:T(8,128)(2,1)S(1)} custom-call(bf16[2,45,16,720]{3,2,1,0:T(8,128)(2,1)} %bitcast.32, bf16[2,45,16,720]{3,2,1,0:T(8,128)(2,1)} %bitcast.33, bf16[2,45,16,720]{3,2,1,0:T(8,128)(2,1)} %bitcast.34, bf16[2,45,16,720]{3,2,1,0:T(8,128)(2,1)} %bitcast.35, bf16[2,45,16,720]{3,2,1,0:T(8,128)(2,1)} %bitcast.36, ...), custom_call_target="tpu_custom_call" | custom-call | bytes 2000000 | tf_op jit(solution)/shard_map/pack_gauss/pallas_call | solution.py:93
  6.5 1.3 %pack_panel.5.rest_4_ = bf16[2,16,7424]{2,1,0:T(8,128)(2,1)S(1)} custom-call(s32[1]{0:T(128)} %bitcast.spot_ref, s32[1,16]{1,0:T(1,128)} %bitcast.29, bf16[45,16,2880]{2,1,0:T(8,128)(2,1)} %tail_ref.7, bf16[45,16,2880]{2,1,0:T(8,128)(2,1)} %tail_ref.7, bf16[45,16,2880]{2,1,0:T(8,128)(2,1)} %tail_ref.7, bf16[45,16,2880]{2,1,0:T(8,128)(2,1)} %tail_ref.7, ...), custom_call_target="tpu_custom_call" | custom-call | bytes 1000000 | tf_op jit(solution)/shard_map/pack_panel/pallas_call | solution.py:70
  7.8 0.9 collective-permute-start.7
  8.7 1.2 %pack_gauss.5.rest_5_ = bf16[2,16,7296]{2,1,0:T(8,128)(2,1)S(1)} custom-call(bf16[2,45,16,720]{3,2,1,0:T(8,128)(2,1)} %bitcast.40, bf16[2,45,16,720]{3,2,1,0:T(8,128)(2,1)} %bitcast.41, bf16[2,45,16,720]{3,2,1,0:T(8,128)(2,1)} %bitcast.42, bf16[2,45,16,720]{3,2,1,0:T(8,128)(2,1)} %bitcast.43, bf16[2,16,7424]{2,1,0:T(8,128)(2,1)S(1)} %pack_panel.5.rest_4_), custom_call_target="tpu_custom_call" | custom-call | bytes 1000000 | tf_op jit(solution)/shard_map/pack_gauss/pallas_call | solution.py:93
  10.7 0.8 slice.13
  11.6 0.8 dynamic_slice.3.order_ref
  12.4 15.4 %collective-permute-done.other_ref = bf16[4,16,7296]{2,1,0:T(8,128)(2,1)} collective-permute-done((bf16[4,16,7296]{2,1,0:T(8,128)(2,1)S(1)}, bf16[4,16,7296]{2,1,0:T(8,128)(2,1)}, u32[]{:S(2)}, u32[]{:S(2)}) %collective-permute-start) | collective-permute-done | bytes 933920 | tf_op jit(solution)/shard_map/ppermute | solution.py:250
  27.9 6.0 %partial_sums.4 = (f32[20,16,96]{2,1,0:T(8,128)S(1)}, bf16[20,16,96]{2,1,0:T(8,128)(2,1)S(1)}) custom-call(s32[1]{0:T(128)} %bitcast.spot_ref, s32[45]{0:T(128)S(1)} %dynamic_slice.3.order_ref, f32[3,16,1536]{2,1,0:T(8,128)S(1)} %pad_maximum_fusion.decay_ref, s32[16]{0:T(128)S(1)} %copy-done, bf16[2,45,16,720]{3,2,1,0:T(8,128)(2,1)} %bitcast.44, ...), custom_call_target="tpu_custom_call" | custom-call | flops 251658240 | bytes 4000000 | tf_op jit(solution)/shard_map/partial_sums/pallas_call | solution.py:191
  33.8 1.3 %pack_panel.6.rest_4_ = bf16[2,16,7424]{2,1,0:T(8,128)(2,1)S(1)} custom-call(s32[1]{0:T(128)} %bitcast.spot_ref, s32[1,16]{1,0:T(1,128)} %bitcast.30, bf16[45,16,2880]{2,1,0:T(8,128)(2,1)} %tail_ref.7, bf16[45,16,2880]{2,1,0:T(8,128)(2,1)} %tail_ref.7, bf16[45,16,2880]{2,1,0:T(8,128)(2,1)} %tail_ref.7, bf16[45,16,2880]{2,1,0:T(8,128)(2,1)} %tail_ref.7, ...), custom_call_target="tpu_custom_call" | custom-call | bytes 1000000 | tf_op jit(solution)/shard_map/pack_panel/pallas_call | solution.py:70
  35.1 1.2 %pack_gauss.6.rest_3_ = bf16[2,16,7296]{2,1,0:T(8,128)(2,1)S(1)} custom-call(bf16[2,45,16,720]{3,2,1,0:T(8,128)(2,1)} %bitcast.45, bf16[2,45,16,720]{3,2,1,0:T(8,128)(2,1)} %bitcast.46, bf16[2,45,16,720]{3,2,1,0:T(8,128)(2,1)} %bitcast.47, bf16[2,45,16,720]{3,2,1,0:T(8,128)(2,1)} %bitcast.48, bf16[2,16,7424]{2,1,0:T(8,128)(2,1)S(1)} %pack_panel.6.rest_4_), custom_call_target="tpu_custom_call" | custom-call | bytes 1000000 | tf_op jit(solution)/shard_map/pack_gauss/pallas_call | solution.py:93
  37.1 1.1 %pack_panel.7.rest_2_ = bf16[1,16,7424]{2,1,0:T(8,128)(2,1)S(1)} custom-call(s32[1]{0:T(128)} %bitcast.spot_ref, s32[1,16]{1,0:T(1,128)} %bitcast.31, bf16[45,16,2880]{2,1,0:T(8,128)(2,1)} %tail_ref.7, bf16[45,16,2880]{2,1,0:T(8,128)(2,1)} %tail_ref.7, f32[20,16,96]{2,1,0:T(8,128)S(1)} %get-tuple-element.18.rest_4_.rest_2_.rest_0_, ...), custom_call_target="tpu_custom_call" | custom-call | bytes 500000 | tf_op jit(solution)/shard_map/pack_panel/pallas_call | solution.py:70
  38.2 1.8 %pack_gauss.7 = bf16[1,16,7296]{2,1,0:T(8,128)(2,1)} custom-call(bf16[2,45,16,720]{3,2,1,0:T(8,128)(2,1)} %bitcast.49, bf16[2,45,16,720]{3,2,1,0:T(8,128)(2,1)} %bitcast.50, bf16[1,16,7424]{2,1,0:T(8,128)(2,1)S(1)} %pack_panel.7.rest_2_), custom_call_target="tpu_custom_call" | custom-call | bytes 500000 | tf_op jit(solution)/shard_map/pack_gauss/pallas_call | solution.py:93
  40.0 2.2 %collective-permute-start.3 = (bf16[1,16,7424]{2,1,0:T(8,128)(2,1)S(1)}, bf16[1,16,7424]{2,1,0:T(8,128)(2,1)S(1)}, u32[]{:S(2)}, u32[]{:S(2)}) collective-permute-start(bf16[1,16,7424]{2,1,0:T(8,128)(2,1)S(1)} %pack_panel.7.rest_2_), channel_id=1, source_target_pairs={{1,2},{2,1},{3,0},{0,3},{5,6},{6,5},{7,4},{4,7},{9,10},{10,9},{11,... | collective-permute-start | bytes 712712 | tf_op jit(solution)/shard_map/ppermute | solution.py:248
  42.2 0.9 collective-permute-start.2
  44.1 3.7 %partial_sums.5 = (f32[25,16,96]{2,1,0:T(8,128)S(1)}, bf16[25,16,96]{2,1,0:T(8,128)(2,1)S(1)}) custom-call(s32[1]{0:T(128)} %bitcast.spot_ref, s32[45]{0:T(128)S(1)} %dynamic_slice.3.order_ref, f32[3,16,1536]{2,1,0:T(8,128)S(1)} %pad_maximum_fusion.decay_ref, s32[16]{0:T(128)S(1)} %copy-done.1, bf16[2,45,16,720]{3,2,1,0:T(8,128)(2,1)} %bitcast.51, ...), custom_call_target="tpu_custom_call" | custom-call | flops 125829120 | bytes 2000000 | tf_op jit(solution)/shard_map/partial_sums/pallas_call | solution.py:191
  47.9 3.5 %partial_sums.6 = (f32[25,16,96]{2,1,0:T(8,128)S(1)}, bf16[25,16,96]{2,1,0:T(8,128)(2,1)S(1)}) custom-call(s32[1]{0:T(128)} %bitcast.spot_ref, s32[45]{0:T(128)S(1)} %dynamic_slice.3.order_ref, f32[3,16,1536]{2,1,0:T(8,128)S(1)} %pad_maximum_fusion.decay_ref, s32[16]{0:T(128)S(1)} %copy-done.1, ...), custom_call_target="tpu_custom_call", output_to_operand_aliasing={{0}: (9, {}), {1}: (10, {})} | custom-call | flops 125829120 | bytes 2000000 | tf_op jit(solution)/shard_map/partial_sums/pallas_call | solution.py:191
  51.4 2.1 %collective-permute-done.8.rest_3_ = bf16[20,16,96]{2,1,0:T(8,128)(2,1)S(1)} collective-permute-done((bf16[20,16,96]{2,1,0:T(8,128)(2,1)S(1)}, bf16[20,16,96]{2,1,0:T(8,128)(2,1)S(1)}, u32[]{:S(2)}, u32[]{:S(2)}) %collective-permute-start.8) | collective-permute-done | bytes 61472 | tf_op jit(solution)/shard_map/ppermute | solution.py:264
  53.5 2.3 %partial_sums.7 = (f32[25,16,96]{2,1,0:T(8,128)S(1)}, bf16[25,16,96]{2,1,0:T(8,128)(2,1)S(1)}) custom-call(s32[1]{0:T(128)} %bitcast.spot_ref, s32[45]{0:T(128)S(1)} %dynamic_slice.3.order_ref, f32[3,16,1536]{2,1,0:T(8,128)S(1)} %pad_maximum_fusion.decay_ref, s32[16]{0:T(128)S(1)} %copy-done.1, ...), custom_call_target="tpu_custom_call", output_to_operand_aliasing={{0}: (9, {}), {1}: (10, {})} | custom-call | flops 62914560 | bytes 1000000 | tf_op jit(solution)/shard_map/partial_sums/pallas_call | solution.py:191
  56.5 4.3 %collective-permute-done.9 = bf16[25,16,96]{2,1,0:T(8,128)(2,1)S(1)} collective-permute-done((bf16[25,16,96]{2,1,0:T(8,128)(2,1)S(1)}, bf16[25,16,96]{2,1,0:T(8,128)(2,1)S(1)}, u32[]{:S(2)}, u32[]{:S(2)}) %collective-permute-start.9) | collective-permute-done | bytes 76832 | tf_op jit(solution)/shard_map/ppermute | solution.py:264
  62.0 27.6 %all_to_all.10 = bf16[64,2,540]{2,1,0:T(2,128)(2,1)S(1)} all-to-all(bf16[64,2,540]{2,1,0:T(2,128)(2,1)S(1)} %copy.23), channel_id=1, replica_groups=mesh['ord'=64,'blk'=4] {'ord'}, dimensions={0} | all-to-all | bytes 276480 | tf_op jit(solution)/shard_map/all_to_all | solution.py:285
  91.4 16.1 %all_to_all.11 = bf16[192,4,90]{2,1,0:T(4,128)(2,1)S(1)} all-to-all(bf16[192,4,90]{2,1,0:T(4,128)(2,1)S(1)} %bitcast.55), channel_id=1, replica_groups=mesh['ord'=64,'blk'=4] {'ord'}, dimensions={0} | all-to-all | bytes 276480 | tf_op jit(solution)/shard_map/all_to_all | solution.py:295
  107.5 0.8 copy.25
  (45 shorter events, 6.5 us)
Async XLA Ops:
  1.5 26.3 %collective-permute-start.1 = (bf16[4,16,7424]{2,1,0:T(8,128)(2,1)S(1)}, bf16[4,16,7424]{2,1,0:T(8,128)(2,1)}, u32[]{:S(2)}, u32[]{:S(2)}) collective-permute-start(bf16[4,16,7424]{2,1,0:T(8,128)(2,1)S(1)} %pack_panel.4.rest_8_), channel_id=1, source_target_pairs={{1,2},{2,1},{3,0},{0,3},{5,6},{6,5},{7,4},{4,7},{9,10},{10,9},{11,... | collective-permute-start | bytes 2850824 | tf_op jit(solution)/shard_map/ppermute | solution.py:248
  6.4 21.4 %collective-permute-start = (bf16[4,16,7296]{2,1,0:T(8,128)(2,1)S(1)}, bf16[4,16,7296]{2,1,0:T(8,128)(2,1)}, u32[]{:S(2)}, u32[]{:S(2)}) collective-permute-start(bf16[4,16,7296]{2,1,0:T(8,128)(2,1)S(1)} %pack_gauss.4.rest_4_), channel_id=1, source_target_pairs={{0,1},{1,0},{2,3},{3,2},{4,5},{5,4},{6,7},{7,6},{8,9},{9,8},{10,11... | collective-permute-start | bytes 2801672 | tf_op jit(solution)/shard_map/ppermute | solution.py:250
  7.8 3.7 %copy-start.2 = (f32[16]{0:T(128)S(1)}, f32[16]{0:T(128)}, u32[]{:S(2)}) copy-start(f32[16]{0:T(128)} %param.7) | copy-start | bytes 196
  7.8 20.1 %copy-start = (s32[16]{0:T(128)S(1)}, s32[16]{0:T(128)}, u32[]{:S(2)}) copy-start(s32[16]{0:T(128)} %cycle_ref.7) | copy-start | bytes 196
  7.8 35.4 %collective-permute-start.7 = (bf16[2,16,7424]{2,1,0:T(8,128)(2,1)S(1)}, bf16[2,16,7424]{2,1,0:T(8,128)(2,1)}, u32[]{:S(2)}, u32[]{:S(2)}) collective-permute-start(bf16[2,16,7424]{2,1,0:T(8,128)(2,1)S(1)} %pack_panel.5.rest_4_), channel_id=1, source_target_pairs={{1,2},{2,1},{3,0},{0,3},{5,6},{6,5},{7,4},{4,7},{9,10},{10,9},{11,... | collective-permute-start | bytes 1425416 | tf_op jit(solution)/shard_map/ppermute | solution.py:248
  9.9 32.3 %collective-permute-start.6 = (bf16[2,16,7296]{2,1,0:T(8,128)(2,1)S(1)}, bf16[2,16,7296]{2,1,0:T(8,128)(2,1)}, u32[]{:S(2)}, u32[]{:S(2)}) collective-permute-start(bf16[2,16,7296]{2,1,0:T(8,128)(2,1)S(1)} %pack_gauss.5.rest_5_), channel_id=1, source_target_pairs={{0,1},{1,0},{2,3},{3,2},{4,5},{5,4},{6,7},{7,6},{8,9},{9,8},{10,11... | collective-permute-start | bytes 1400840 | tf_op jit(solution)/shard_map/ppermute | solution.py:250
  36.3 11.5 %collective-permute-start.5 = (bf16[2,16,7424]{2,1,0:T(8,128)(2,1)S(1)}, bf16[2,16,7424]{2,1,0:T(8,128)(2,1)S(1)}, u32[]{:S(2)}, u32[]{:S(2)}) collective-permute-start(bf16[2,16,7424]{2,1,0:T(8,128)(2,1)S(1)} %pack_panel.6.rest_4_), channel_id=1, source_target_pairs={{1,2},{2,1},{3,0},{0,3},{5,6},{6,5},{7,4},{4,7},{9,10},{10,9},{11,... | collective-permute-start | bytes 1425416 | tf_op jit(solution)/shard_map/ppermute | solution.py:248
  36.8 11.0 %collective-permute-start.4 = (bf16[2,16,7296]{2,1,0:T(8,128)(2,1)S(1)}, bf16[2,16,7296]{2,1,0:T(8,128)(2,1)}, u32[]{:S(2)}, u32[]{:S(2)}) collective-permute-start(bf16[2,16,7296]{2,1,0:T(8,128)(2,1)S(1)} %pack_gauss.6.rest_3_), channel_id=1, source_target_pairs={{0,1},{1,0},{2,3},{3,2},{4,5},{5,4},{6,7},{7,6},{8,9},{9,8},{10,11... | collective-permute-start | bytes 1400840 | tf_op jit(solution)/shard_map/ppermute | solution.py:250
  38.2 5.9 %copy-start.1 = (s32[16]{0:T(128)S(1)}, s32[16]{0:T(128)}, u32[]{:S(2)}) copy-start(s32[16]{0:T(128)} %cycle_ref.7) | copy-start | bytes 196
  40.0 13.5 %collective-permute-start.3 = (bf16[1,16,7424]{2,1,0:T(8,128)(2,1)S(1)}, bf16[1,16,7424]{2,1,0:T(8,128)(2,1)S(1)}, u32[]{:S(2)}, u32[]{:S(2)}) collective-permute-start(bf16[1,16,7424]{2,1,0:T(8,128)(2,1)S(1)} %pack_panel.7.rest_2_), channel_id=1, source_target_pairs={{1,2},{2,1},{3,0},{0,3},{5,6},{6,5},{7,4},{4,7},{9,10},{10,9},{11,... | collective-permute-start | bytes 712712 | tf_op jit(solution)/shard_map/ppermute | solution.py:248
  42.2 11.3 %collective-permute-start.2 = (bf16[1,16,7296]{2,1,0:T(8,128)(2,1)}, bf16[1,16,7296]{2,1,0:T(8,128)(2,1)S(1)}, u32[]{:S(2)}, u32[]{:S(2)}) collective-permute-start(bf16[1,16,7296]{2,1,0:T(8,128)(2,1)} %pack_gauss.7), channel_id=1, source_target_pairs={{0,1},{1,0},{2,3},{3,2},{4,5},{5,4},{6,7},{7,6},{8,9},{9,8},{10,11... | collective-permute-start | bytes 700424 | tf_op jit(solution)/shard_map/ppermute | solution.py:250
  43.2 10.3 %collective-permute-start.8 = (bf16[20,16,96]{2,1,0:T(8,128)(2,1)S(1)}, bf16[20,16,96]{2,1,0:T(8,128)(2,1)S(1)}, u32[]{:S(2)}, u32[]{:S(2)}) collective-permute-start(bf16[20,16,96]{2,1,0:T(8,128)(2,1)S(1)} %get-tuple-element.23), channel_id=1, source_target_pairs={{1,2},{2,1},{3,0},{0,3},{5,6},{6,5},{7,4},{4,7},{9,10},{10,9},{11,... | collective-permute-start | bytes 184328 | tf_op jit(solution)/shard_map/ppermute | solution.py:264
  55.8 5.0 %collective-permute-start.9 = (bf16[25,16,96]{2,1,0:T(8,128)(2,1)S(1)}, bf16[25,16,96]{2,1,0:T(8,128)(2,1)S(1)}, u32[]{:S(2)}, u32[]{:S(2)}) collective-permute-start(bf16[25,16,96]{2,1,0:T(8,128)(2,1)S(1)} %get-tuple-element.25), channel_id=1, source_target_pairs={{1,2},{2,1},{3,0},{0,3},{5,6},{6,5},{7,4},{4,7},{9,10},{10,9},{11,... | collective-permute-start | bytes 230408 | tf_op jit(solution)/shard_map/ppermute | solution.py:264
